TPU v7x, 32 devices: a whole 2x2x4 slice. The times are simulated.
32 devices in a mesh: gx: 8 (over z, x), gy: 2 (over y), lvl: 2 (over core).
Axes of the slice: x: 2, y: 2, z: 4, core: 2. Of those that a mesh axis runs over, the one named last changes fastest.
Arguments:
- right_side: float32 [4, 64, 32, 512], P(None, 'gx', 'gy', 'lvl'), may hold values from -6 to 6
- start_field: float32 [4, 64, 32, 512], P(None, 'gx', 'gy', 'lvl'), may hold values from -4 to 4
- mask_blocks: float32 [3072, 1024], P(('gx', 'gy', 'lvl')), may hold values from 0.5 to 20
- block_tile: int32 [3072, 1], replicated, may hold values from 0 to 15; in each aligned block of 96 rows (0 to 95, 96 to 191, ...) at most 12 rows name the same one
- block_slot: int32 [3072], replicated, may hold values from 0 to 31
Outputs:
- solution: float32 [4, 64, 32, 512], P(None, 'gx', 'gy', 'lvl')
Inputs may be any that keep to these rules, and one draw needn't show every extreme that they name: `block_tile`: rows s * 96 to (s + 1) * 96 - 1 are the blocks of the device at position s of the joined gx, gy, lvl order; in each such block of rows no tile is named by more than 12 rows, a bound that some block reaches. `block_slot`: several blocks may name the same slot of a tile; their coefficients add.
All inputs are finite; a program needn't handle non-finite values.
Results may differ from a plain program's by a relative error of at most 0.00002.
Values sent between devices are 32-bit elements; how exact they have to be, the bound alone decides.
No kernel may reach another device: no remote copies, remote signals or barrier semaphores. Data moves between devices by JAX's collectives and lax.ppermute only.
A program may use at most 128 MiB of HBM per device.

v0:
```python
import jax
import jax.numpy as jnp
from jax import lax
from jax.sharding import PartitionSpec as P

SMOOTH_SWEEPS = 2
COARSE_SWEEPS = 4


VEL_SHIFT = 0.05
PRES_SHIFT = 0.05
RELAX = 0.6


def with_halo(cells, sides, width):
    for axis, dim in sides:
        count = lax.axis_size(axis)
        ends = count - 1
        head = lax.slice_in_dim(cells, 0, width, axis=dim)
        tail = lax.slice_in_dim(cells, cells.shape[dim] - width, cells.shape[dim], axis=dim)
        cells = jnp.concatenate(
            [
                lax.ppermute(tail, axis, [(i, (i + 1) % count) for i in range(ends)]),
                cells,
                lax.ppermute(head, axis, [((i + 1) % count, i) for i in range(ends)]),
            ],
            axis=dim,
        )
    return cells


def apply_operator(padded, chi, lap_coef, grad_coef):
    center = padded[:, 1:-1, 1:-1, 1:-1]
    x_next = padded[:, 2:, 1:-1, 1:-1]
    x_prev = padded[:, :-2, 1:-1, 1:-1]
    y_next = padded[:, 1:-1, 2:, 1:-1]
    y_prev = padded[:, 1:-1, :-2, 1:-1]
    z_next = padded[:, 1:-1, 1:-1, 2:]
    z_prev = padded[:, 1:-1, 1:-1, :-2]
    laplace = 6.0 * center - (x_next + x_prev + y_next + y_prev + z_next + z_prev)
    gradients = [x_next[3] - x_prev[3], y_next[3] - y_prev[3], z_next[3] - z_prev[3]]
    rows = [
        (VEL_SHIFT + chi) * center[k] + lap_coef * laplace[k] + grad_coef * gradients[k]
        for k in range(3)
    ]
    spread = x_next[0] - x_prev[0] + (y_next[1] - y_prev[1]) + (z_next[2] - z_prev[2])
    rows.append(PRES_SHIFT * center[3] + lap_coef * laplace[3] + grad_coef * spread)
    return jnp.stack(rows)


def diagonal_of(chi, lap_coef):
    velocity = VEL_SHIFT + chi + 6.0 * lap_coef
    pressure = jnp.zeros_like(chi) + (PRES_SHIFT + 6.0 * lap_coef)
    return jnp.stack([velocity, velocity, velocity, pressure])


def restrict(values):
    lead, size_x, size_y, size_z = values.shape
    shaped = values.reshape(lead, size_x // 2, 2, size_y // 2, 2, size_z // 2, 2)
    return jnp.mean(shaped, axis=(2, 4, 6))


def prolong(values):
    return jnp.repeat(jnp.repeat(jnp.repeat(values, 2, axis=1), 2, axis=2), 2, axis=3)


def fine_residual(state, right_side, chi):
    padded = with_halo(state, (("gx", 1), ("gy", 2), ("lvl", 3)), 1)
    return right_side - apply_operator(padded, chi, 1.0, 0.5)


def smooth(state, right_side, chi, diag):
    for sweep in range(SMOOTH_SWEEPS):
        state = state + RELAX * fine_residual(state, right_side, chi) / diag
    return state


def split_pad(values):
    return with_halo(values, (("gx", 1), ("gy", 2), ("lvl", 3)), 1)


def body(right_side, start_field, mask_blocks, block_tile, block_slot):
    count_x = lax.axis_size("gx")
    count_y = lax.axis_size("gy")
    count_l = lax.axis_size("lvl")
    tiles = count_x * count_y
    index_x = lax.axis_index("gx")
    index_y = lax.axis_index("gy")
    index_l = lax.axis_index("lvl")
    per_device = mask_blocks.shape[0]
    width = mask_blocks.shape[1]
    capacity = max(2, 2 * per_device // tiles)
    size_x = right_side.shape[1]
    size_y = right_side.shape[2]
    size_z = right_side.shape[3]
    slots = size_x // 2 * (size_y // 2)
    my_flat = (index_x * count_y + index_y) * count_l + index_l
    my_tiles = lax.dynamic_slice_in_dim(block_tile[:, 0], my_flat * per_device, per_device)
    same = my_tiles[:, None] == my_tiles[None, :]
    counter = jnp.arange(per_device, dtype=jnp.int32)
    earlier = counter[None, :] < counter[:, None]
    rank = jnp.sum((same & earlier).astype(jnp.int32), axis=1)
    position = my_tiles * capacity + rank
    outgoing = jnp.zeros((tiles * capacity, width), jnp.float32).at[position].set(mask_blocks)
    my_tile = index_x * count_y + index_y
    all_tiles = block_tile[:, 0].reshape(tiles, count_l, per_device)
    all_slots = block_slot.reshape(tiles, count_l, per_device)
    their_tiles = lax.dynamic_index_in_dim(all_tiles, index_l, 1, keepdims=False)
    their_slots = lax.dynamic_index_in_dim(all_slots, index_l, 1, keepdims=False)
    arriving = their_tiles == my_tile
    order = jnp.cumsum(arriving.astype(jnp.int32), axis=1) - 1
    senders = jnp.arange(tiles, dtype=jnp.int32)[:, None]
    target = jnp.where(arriving, senders * capacity + order, tiles * capacity)
    slot_of = (
        jnp.full((tiles * capacity,), slots, jnp.int32)
        .at[target.reshape(-1)]
        .set(their_slots.reshape(-1), mode="drop")
    )
    arrived = lax.all_to_all(outgoing, ("gx", "gy"), split_axis=0, concat_axis=0, tiled=True)
    placed = jax.ops.segment_sum(arrived, slot_of, num_segments=slots + 1)[:slots]
    chi = (
        placed.reshape(size_x // 2, size_y // 2, 2, 2, size_z)
        .transpose(0, 2, 1, 3, 4)
        .reshape(size_x, size_y, size_z)
    )
    diag = diagonal_of(chi, 1.0)
    state = smooth(start_field, right_side, chi, diag)
    residual = fine_residual(state, right_side, chi)
    coarse_source = restrict(residual)
    coarse_chi = restrict(chi[None])[0]
    coarse_diag = diagonal_of(coarse_chi, 0.25)
    correction = RELAX * coarse_source / coarse_diag
    for sweep in range(COARSE_SWEEPS - 1):
        update = coarse_source - apply_operator(split_pad(correction), coarse_chi, 0.25, 0.25)
        correction = correction + RELAX * update / coarse_diag
    state = state + prolong(correction)
    return smooth(state, right_side, chi, diag)


def solution(mesh):
    in_specs = (
        P(None, "gx", "gy", "lvl"),
        P(None, "gx", "gy", "lvl"),
        P(("gx", "gy", "lvl"), None),
        P(),
        P(),
    )
    out_specs = P(None, "gx", "gy", "lvl")
    return jax.shard_map(body, mesh=mesh, in_specs=in_specs, out_specs=out_specs, check_vma=False)
```

profile of v0, /device:TPU:9, one launch (start us, length us, event | category | flops | bytes accessed | tf_op | source)
XLA Modules:
  0.0 254.7 jit_solution(18339793714357900427)
XLA Ops:
  0.9 3.1 %collective-permute-start.1 = (f32[4,1,16,256]{3,2,1,0:T(8,128)S(1)}, f32[4,1,16,256]{3,2,1,0:T(8,128)S(1)}, u32[]{:S(2)}, u32[]{:S(2)}) collective-permute-start(f32[4,1,16,256]{3,2,1,0:T(8,128)S(1)} %get-tuple-element.67), channel_id=1, source_target_pairs={{0,4},{4,8},{8,12},{12,16},{16,20},{20,24},{24,28},{1,5},{5,9},{9,... | collective-permute-start | bytes 196616 | tf_op jit(solution)/shard_map/ppermute | solution.py:23
  4.0 3.1 %collective-permute-start = (f32[4,1,16,256]{3,2,1,0:T(8,128)S(1)}, f32[4,1,16,256]{3,2,1,0:T(8,128)S(1)}, u32[]{:S(2)}, u32[]{:S(2)}) collective-permute-start(f32[4,1,16,256]{3,2,1,0:T(8,128)S(1)} %get-tuple-element.66), channel_id=1, source_target_pairs={{4,0},{8,4},{12,8},{16,12},{20,16},{24,20},{28,24},{5,1},{9,5},{13... | collective-permute-start | bytes 196616 | tf_op jit(solution)/shard_map/ppermute | solution.py:25
  11.4 5.9 %all-to-all-start = ((f32[16,12,1024]{2,1,0:T(8,128)}), f32[16,12,1024]{2,1,0:T(8,128)}, u32[]{:S(2)}, u32[]{:S(2)}) async-start(f32[16,12,1024]{2,1,0:T(8,128)} %all_to_all.8), calls=%async_computation | async-start | bytes 2097152 | tf_op jit(solution)/shard_map/all_to_all | solution.py:119
  21.4 4.0 %collective-permute-start.3 = (f32[4,10,1,256]{3,2,1,0:T(1,128)S(1)}, f32[4,10,1,256]{3,2,1,0:T(1,128)S(1)}, u32[]{:S(2)}, u32[]{:S(2)}) collective-permute-start(f32[4,10,1,256]{3,2,1,0:T(1,128)S(1)} %get-tuple-element.53), channel_id=1, source_target_pairs={{0,2},{1,3},{4,6},{5,7},{8,10},{9,11},{12,14},{13,15},{16,18},{17,... | collective-permute-start | bytes 122888 | tf_op jit(solution)/shard_map/ppermute | solution.py:23
  28.9 7.1 %collective-permute-start.4 = (f32[4,10,18,1]{3,2,1,0:T(8,128)S(1)}, f32[4,10,18,1]{3,2,1,0:T(8,128)S(1)}, u32[]{:S(2)}, u32[]{:S(2)}) collective-permute-start(f32[4,10,18,1]{3,2,1,0:T(8,128)S(1)} %get-tuple-element.25), channel_id=1, source_target_pairs={{1,0},{3,2},{5,4},{7,6},{9,8},{11,10},{13,12},{15,14},{17,16},{19,... | collective-permute-start | bytes 8648 | tf_op jit(solution)/shard_map/ppermute | solution.py:25
  36.7 6.2 %scatter_custom_fusion = s32[192]{0:T(256)S(1)} fusion(s32[1536]{0:T(1024)S(1)} %fusion.211, s32[1536]{0:T(1024)S(1)} %reshape.166, s32[]{:T(128)} %constant.22.clone.1), kind=kCustom, calls=%fused_computation.487 | custom fusion | bytes 772 | tf_op jit(solution)/shard_map/scatter | solution.py:117
  47.5 3.3 %scatter_custom_fusion.2 = f32[33,1024]{1,0:T(8,128)} fusion(s32[192]{0:T(256)S(1)} %scatter_custom_fusion, f32[192,1024]{1,0:T(8,128)} %reshape.182, f32[]{:T(128)} %constant.21.clone.1), kind=kCustom, calls=%fused_computation.298 | custom fusion | flops 196608 | bytes 135680 | tf_op jit(solution)/shard_map/scatter-add | solution.py:120
  65.9 3.7 %collective-permute-done.7 = f32[4,1,16,256]{3,2,1,0:T(8,128)S(1)} collective-permute-done((f32[4,1,16,256]{3,2,1,0:T(8,128)S(1)}, f32[4,1,16,256]{3,2,1,0:T(8,128)S(1)}, u32[]{:S(2)}, u32[]{:S(2)}) %collective-permute-start.7) | collective-permute-done | bytes 65568 | tf_op jit(solution)/shard_map/ppermute | solution.py:23
  71.0 4.2 %collective-permute-start.9 = (f32[4,10,1,256]{3,2,1,0:T(1,128)S(1)}, f32[4,10,1,256]{3,2,1,0:T(1,128)S(1)}, u32[]{:S(2)}, u32[]{:S(2)}) collective-permute-start(f32[4,10,1,256]{3,2,1,0:T(1,128)S(1)} %get-tuple-element.51), channel_id=1, source_target_pairs={{0,2},{1,3},{4,6},{5,7},{8,10},{9,11},{12,14},{13,15},{16,18},{17,... | collective-permute-start | bytes 122888 | tf_op jit(solution)/shard_map/ppermute | solution.py:23
  78.0 3.3 %collective-permute-start.10 = (f32[4,10,18,1]{3,2,1,0:T(8,128)S(1)}, f32[4,10,18,1]{3,2,1,0:T(8,128)S(1)}, u32[]{:S(2)}, u32[]{:S(2)}) collective-permute-start(f32[4,10,18,1]{3,2,1,0:T(8,128)S(1)} %get-tuple-element.23), channel_id=1, source_target_pairs={{1,0},{3,2},{5,4},{7,6},{9,8},{11,10},{13,12},{15,14},{17,16},{19,... | collective-permute-start | bytes 8648 | tf_op jit(solution)/shard_map/ppermute | solution.py:25
  86.7 3.4 %collective-permute-start.13 = (f32[4,1,16,256]{3,2,1,0:T(8,128)S(1)}, f32[4,1,16,256]{3,2,1,0:T(8,128)S(1)}, u32[]{:S(2)}, u32[]{:S(2)}) collective-permute-start(f32[4,1,16,256]{3,2,1,0:T(8,128)S(1)} %get-tuple-element.59), channel_id=1, source_target_pairs={{0,4},{4,8},{8,12},{12,16},{16,20},{20,24},{24,28},{1,5},{5,9},{9,... | collective-permute-start | bytes 196616 | tf_op jit(solution)/shard_map/ppermute | solution.py:23
  93.9 4.2 %collective-permute-start.15 = (f32[4,10,1,256]{3,2,1,0:T(1,128)S(1)}, f32[4,10,1,256]{3,2,1,0:T(1,128)S(1)}, u32[]{:S(2)}, u32[]{:S(2)}) collective-permute-start(f32[4,10,1,256]{3,2,1,0:T(1,128)S(1)} %get-tuple-element.47), channel_id=1, source_target_pairs={{0,2},{1,3},{4,6},{5,7},{8,10},{9,11},{12,14},{13,15},{16,18},{17,... | collective-permute-start | bytes 122888 | tf_op jit(solution)/shard_map/ppermute | solution.py:23
  100.7 4.6 %collective-permute-start.16 = (f32[4,10,18,1]{3,2,1,0:T(8,128)S(1)}, f32[4,10,18,1]{3,2,1,0:T(8,128)S(1)}, u32[]{:S(2)}, u32[]{:S(2)}) collective-permute-start(f32[4,10,18,1]{3,2,1,0:T(8,128)S(1)} %get-tuple-element.21), channel_id=1, source_target_pairs={{1,0},{3,2},{5,4},{7,6},{9,8},{11,10},{13,12},{15,14},{17,16},{19,... | collective-permute-start | bytes 8648 | tf_op jit(solution)/shard_map/ppermute | solution.py:25
  108.6 8.8 %copy.431 = f32[4,8,16,256]{0,3,2,1:T(8,128)} copy(f32[4,8,16,256]{3,2,1,0:T(8,128)S(1)} %maximum_subtract_fusion.2) | data formatting | bytes 1048576 | tf_op jit(solution)/shard_map/sub | solution.py:69
  117.4 11.8 %reduce_sum.38 = f32[4,4,8,128]{0,3,2,1:T(8,128)S(1)} reduce(f32[4,4,2,8,2,128,2]{0,6,5,4,3,2,1:T(2,128)} %bitcast.48, f32[]{:T(128)} %constant.21.clone.1), dimensions={2,4,6}, to_apply=%region_5.6 | reduce | flops 114688 | bytes 589828 | tf_op jit(solution)/shard_map/reduce_sum | solution.py:60
  131.8 3.4 %collective-permute-start.19 = (f32[4,1,8,128]{3,2,1,0:T(8,128)S(1)}, f32[4,1,8,128]{3,2,1,0:T(8,128)S(1)}, u32[]{:S(2)}, u32[]{:S(2)}) collective-permute-start(f32[4,1,8,128]{3,2,1,0:T(8,128)S(1)} %get-tuple-element.123), channel_id=1, source_target_pairs={{0,4},{4,8},{8,12},{12,16},{16,20},{20,24},{24,28},{1,5},{5,9},{9,... | collective-permute-start | bytes 49160 | tf_op jit(solution)/shard_map/ppermute | solution.py:23
  137.2 4.0 %collective-permute-start.21 = (f32[4,6,1,128]{3,2,1,0:T(1,128)S(1)}, f32[4,6,1,128]{3,2,1,0:T(1,128)S(1)}, u32[]{:S(2)}, u32[]{:S(2)}) collective-permute-start(f32[4,6,1,128]{3,2,1,0:T(1,128)S(1)} %get-tuple-element.118), channel_id=1, source_target_pairs={{0,2},{1,3},{4,6},{5,7},{8,10},{9,11},{12,14},{13,15},{16,18},{17,... | collective-permute-start | bytes 36872 | tf_op jit(solution)/shard_map/ppermute | solution.py:23
  142.6 3.1 %collective-permute-done.20 = f32[4,6,1,128]{3,2,1,0:T(1,128)S(1)} collective-permute-done((f32[4,6,1,128]{3,2,1,0:T(1,128)S(1)}, f32[4,6,1,128]{3,2,1,0:T(1,128)S(1)}, u32[]{:S(2)}, u32[]{:S(2)}) %collective-permute-start.20) | collective-permute-done | bytes 12320 | tf_op jit(solution)/shard_map/ppermute | solution.py:25
  145.8 4.9 %collective-permute-start.22 = (f32[4,6,10,1]{3,0,2,1:T(4,128)S(1)}, f32[4,6,10,1]{3,0,2,1:T(4,128)S(1)}, u32[]{:S(2)}, u32[]{:S(2)}) collective-permute-start(f32[4,6,10,1]{3,0,2,1:T(4,128)S(1)} %get-tuple-element.105), channel_id=1, source_target_pairs={{1,0},{3,2},{5,4},{7,6},{9,8},{11,10},{13,12},{15,14},{17,16},{19,... | collective-permute-start | bytes 2888 | tf_op jit(solution)/shard_map/ppermute | solution.py:25
  156.5 3.4 %collective-permute-start.25 = (f32[4,1,8,128]{3,2,1,0:T(8,128)S(1)}, f32[4,1,8,128]{3,2,1,0:T(8,128)S(1)}, u32[]{:S(2)}, u32[]{:S(2)}) collective-permute-start(f32[4,1,8,128]{3,2,1,0:T(8,128)S(1)} %get-tuple-element.121), channel_id=1, source_target_pairs={{0,4},{4,8},{8,12},{12,16},{16,20},{20,24},{24,28},{1,5},{5,9},{9,... | collective-permute-start | bytes 49160 | tf_op jit(solution)/shard_map/ppermute | solution.py:23
  164.6 3.1 %collective-permute-done.26 = f32[4,6,1,128]{3,2,1,0:T(1,128)S(1)} collective-permute-done((f32[4,6,1,128]{3,2,1,0:T(1,128)S(1)}, f32[4,6,1,128]{3,2,1,0:T(1,128)S(1)}, u32[]{:S(2)}, u32[]{:S(2)}) %collective-permute-start.26) | collective-permute-done | bytes 12320 | tf_op jit(solution)/shard_map/ppermute | solution.py:25
  167.8 4.7 %collective-permute-start.28 = (f32[4,6,10,1]{3,0,2,1:T(4,128)S(1)}, f32[4,6,10,1]{3,0,2,1:T(4,128)S(1)}, u32[]{:S(2)}, u32[]{:S(2)}) collective-permute-start(f32[4,6,10,1]{3,0,2,1:T(4,128)S(1)} %get-tuple-element.99), channel_id=1, source_target_pairs={{1,0},{3,2},{5,4},{7,6},{9,8},{11,10},{13,12},{15,14},{17,16},{19,... | collective-permute-start | bytes 2888 | tf_op jit(solution)/shard_map/ppermute | solution.py:25
  178.3 3.4 %collective-permute-start.31 = (f32[4,1,8,128]{3,2,1,0:T(8,128)S(1)}, f32[4,1,8,128]{3,2,1,0:T(8,128)S(1)}, u32[]{:S(2)}, u32[]{:S(2)}) collective-permute-start(f32[4,1,8,128]{3,2,1,0:T(8,128)S(1)} %get-tuple-element.119), channel_id=1, source_target_pairs={{0,4},{4,8},{8,12},{12,16},{16,20},{20,24},{24,28},{1,5},{5,9},{9,... | collective-permute-start | bytes 49160 | tf_op jit(solution)/shard_map/ppermute | solution.py:23
  186.5 3.1 %collective-permute-done.32 = f32[4,6,1,128]{3,2,1,0:T(1,128)S(1)} collective-permute-done((f32[4,6,1,128]{3,2,1,0:T(1,128)S(1)}, f32[4,6,1,128]{3,2,1,0:T(1,128)S(1)}, u32[]{:S(2)}, u32[]{:S(2)}) %collective-permute-start.32) | collective-permute-done | bytes 12320 | tf_op jit(solution)/shard_map/ppermute | solution.py:25
  189.7 4.7 %collective-permute-start.34 = (f32[4,6,10,1]{3,0,2,1:T(4,128)S(1)}, f32[4,6,10,1]{3,0,2,1:T(4,128)S(1)}, u32[]{:S(2)}, u32[]{:S(2)}) collective-permute-start(f32[4,6,10,1]{3,0,2,1:T(4,128)S(1)} %get-tuple-element.93), channel_id=1, source_target_pairs={{1,0},{3,2},{5,4},{7,6},{9,8},{11,10},{13,12},{15,14},{17,16},{19,... | collective-permute-start | bytes 2888 | tf_op jit(solution)/shard_map/ppermute | solution.py:25
  207.8 3.4 %collective-permute-start.37 = (f32[4,1,16,256]{3,2,1,0:T(8,128)S(1)}, f32[4,1,16,256]{3,2,1,0:T(8,128)S(1)}, u32[]{:S(2)}, u32[]{:S(2)}) collective-permute-start(f32[4,1,16,256]{3,2,1,0:T(8,128)S(1)} %get-tuple-element.57), channel_id=1, source_target_pairs={{0,4},{4,8},{8,12},{12,16},{16,20},{20,24},{24,28},{1,5},{5,9},{9,... | collective-permute-start | bytes 196616 | tf_op jit(solution)/shard_map/ppermute | solution.py:23
  211.3 2.8 %collective-permute-done.37 = f32[4,1,16,256]{3,2,1,0:T(8,128)S(1)} collective-permute-done((f32[4,1,16,256]{3,2,1,0:T(8,128)S(1)}, f32[4,1,16,256]{3,2,1,0:T(8,128)S(1)}, u32[]{:S(2)}, u32[]{:S(2)}) %collective-permute-start.37) | collective-permute-done | bytes 65568 | tf_op jit(solution)/shard_map/ppermute | solution.py:23
  215.5 4.0 %collective-permute-start.39 = (f32[4,10,1,256]{3,2,1,0:T(1,128)S(1)}, f32[4,10,1,256]{3,2,1,0:T(1,128)S(1)}, u32[]{:S(2)}, u32[]{:S(2)}) collective-permute-start(f32[4,10,1,256]{3,2,1,0:T(1,128)S(1)} %get-tuple-element.43), channel_id=1, source_target_pairs={{0,2},{1,3},{4,6},{5,7},{8,10},{9,11},{12,14},{13,15},{16,18},{17,... | collective-permute-start | bytes 122888 | tf_op jit(solution)/shard_map/ppermute | solution.py:23
  222.2 4.3 %collective-permute-start.40 = (f32[4,10,18,1]{3,2,1,0:T(8,128)S(1)}, f32[4,10,18,1]{3,2,1,0:T(8,128)S(1)}, u32[]{:S(2)}, u32[]{:S(2)}) collective-permute-start(f32[4,10,18,1]{3,2,1,0:T(8,128)S(1)} %get-tuple-element.19), channel_id=1, source_target_pairs={{1,0},{3,2},{5,4},{7,6},{9,8},{11,10},{13,12},{15,14},{17,16},{19,... | collective-permute-start | bytes 8648 | tf_op jit(solution)/shard_map/ppermute | solution.py:25
  231.9 3.4 %collective-permute-start.43 = (f32[4,1,16,256]{3,2,1,0:T(8,128)S(1)}, f32[4,1,16,256]{3,2,1,0:T(8,128)S(1)}, u32[]{:S(2)}, u32[]{:S(2)}) collective-permute-start(f32[4,1,16,256]{3,2,1,0:T(8,128)S(1)} %get-tuple-element.55), channel_id=1, source_target_pairs={{0,4},{4,8},{8,12},{12,16},{16,20},{20,24},{24,28},{1,5},{5,9},{9,... | collective-permute-start | bytes 196616 | tf_op jit(solution)/shard_map/ppermute | solution.py:23
  239.2 4.0 %collective-permute-start.45 = (f32[4,10,1,256]{3,2,1,0:T(1,128)S(1)}, f32[4,10,1,256]{3,2,1,0:T(1,128)S(1)}, u32[]{:S(2)}, u32[]{:S(2)}) collective-permute-start(f32[4,10,1,256]{3,2,1,0:T(1,128)S(1)} %get-tuple-element.39), channel_id=1, source_target_pairs={{0,2},{1,3},{4,6},{5,7},{8,10},{9,11},{12,14},{13,15},{16,18},{17,... | collective-permute-start | bytes 122888 | tf_op jit(solution)/shard_map/ppermute | solution.py:23
  245.9 4.6 %collective-permute-start.46 = (f32[4,10,18,1]{3,2,1,0:T(8,128)S(1)}, f32[4,10,18,1]{3,2,1,0:T(8,128)S(1)}, u32[]{:S(2)}, u32[]{:S(2)}) collective-permute-start(f32[4,10,18,1]{3,2,1,0:T(8,128)S(1)} %get-tuple-element.17), channel_id=1, source_target_pairs={{1,0},{3,2},{5,4},{7,6},{9,8},{11,10},{13,12},{15,14},{17,16},{19,... | collective-permute-start | bytes 8648 | tf_op jit(solution)/shard_map/ppermute | solution.py:25
  (234 shorter events, 112.8 us)
Async XLA Ops:
  0.9 18.1 %collective-permute-start.1 = (f32[4,1,16,256]{3,2,1,0:T(8,128)S(1)}, f32[4,1,16,256]{3,2,1,0:T(8,128)S(1)}, u32[]{:S(2)}, u32[]{:S(2)}) collective-permute-start(f32[4,1,16,256]{3,2,1,0:T(8,128)S(1)} %get-tuple-element.67), channel_id=1, source_target_pairs={{0,4},{4,8},{8,12},{12,16},{16,20},{20,24},{24,28},{1,5},{5,9},{9,... | collective-permute-start | bytes 196616 | tf_op jit(solution)/shard_map/ppermute | solution.py:23
  4.0 15.2 %collective-permute-start = (f32[4,1,16,256]{3,2,1,0:T(8,128)S(1)}, f32[4,1,16,256]{3,2,1,0:T(8,128)S(1)}, u32[]{:S(2)}, u32[]{:S(2)}) collective-permute-start(f32[4,1,16,256]{3,2,1,0:T(8,128)S(1)} %get-tuple-element.66), channel_id=1, source_target_pairs={{4,0},{8,4},{12,8},{16,12},{20,16},{24,20},{28,24},{5,1},{9,5},{13... | collective-permute-start | bytes 196616 | tf_op jit(solution)/shard_map/ppermute | solution.py:25
  11.4 33.9 %all-to-all-start = ((f32[16,12,1024]{2,1,0:T(8,128)}), f32[16,12,1024]{2,1,0:T(8,128)}, u32[]{:S(2)}, u32[]{:S(2)}) async-start(f32[16,12,1024]{2,1,0:T(8,128)} %all_to_all.8), calls=%async_computation | async-start | bytes 2097152 | tf_op jit(solution)/shard_map/all_to_all | solution.py:119
  20.1 5.5 %collective-permute-start.2 = (f32[4,10,1,256]{3,2,1,0:T(1,128)S(1)}, f32[4,10,1,256]{3,2,1,0:T(1,128)S(1)}, u32[]{:S(2)}, u32[]{:S(2)}) collective-permute-start(f32[4,10,1,256]{3,2,1,0:T(1,128)S(1)} %get-tuple-element.54), channel_id=1, source_target_pairs={{2,0},{3,1},{6,4},{7,5},{10,8},{11,9},{14,12},{15,13},{18,16},{19,... | collective-permute-start | bytes 122888 | tf_op jit(solution)/shard_map/ppermute | solution.py:25
  27.6 15.3 %collective-permute-start.5 = (f32[4,10,18,1]{3,2,1,0:T(8,128)}, f32[4,10,18,1]{3,2,1,0:T(8,128)S(1)}, u32[]{:S(2)}, u32[]{:S(2)}) collective-permute-start(f32[4,10,18,1]{3,2,1,0:T(8,128)} %get-tuple-element.26), channel_id=1, source_target_pairs={{0,1},{2,3},{4,5},{6,7},{8,9},{10,11},{12,13},{14,15},{16,17},{18,... | collective-permute-start | bytes 8648 | tf_op jit(solution)/shard_map/ppermute | solution.py:23
  28.9 14.0 %collective-permute-start.4 = (f32[4,10,18,1]{3,2,1,0:T(8,128)S(1)}, f32[4,10,18,1]{3,2,1,0:T(8,128)S(1)}, u32[]{:S(2)}, u32[]{:S(2)}) collective-permute-start(f32[4,10,18,1]{3,2,1,0:T(8,128)S(1)} %get-tuple-element.25), channel_id=1, source_target_pairs={{1,0},{3,2},{5,4},{7,6},{9,8},{11,10},{13,12},{15,14},{17,16},{19,... | collective-permute-start | bytes 8648 | tf_op jit(solution)/shard_map/ppermute | solution.py:25
  60.3 5.6 %collective-permute-start.6 = (f32[4,1,16,256]{3,2,1,0:T(8,128)S(1)}, f32[4,1,16,256]{3,2,1,0:T(8,128)S(1)}, u32[]{:S(2)}, u32[]{:S(2)}) collective-permute-start(f32[4,1,16,256]{3,2,1,0:T(8,128)S(1)} %get-tuple-element.62), channel_id=1, source_target_pairs={{4,0},{8,4},{12,8},{16,12},{20,16},{24,20},{28,24},{5,1},{9,5},{13... | collective-permute-start | bytes 196616 | tf_op jit(solution)/shard_map/ppermute | solution.py:25
  62.8 6.8 %collective-permute-start.7 = (f32[4,1,16,256]{3,2,1,0:T(8,128)S(1)}, f32[4,1,16,256]{3,2,1,0:T(8,128)S(1)}, u32[]{:S(2)}, u32[]{:S(2)}) collective-permute-start(f32[4,1,16,256]{3,2,1,0:T(8,128)S(1)} %get-tuple-element.61), channel_id=1, source_target_pairs={{0,4},{4,8},{8,12},{12,16},{16,20},{20,24},{24,28},{1,5},{5,9},{9,... | collective-permute-start | bytes 196616 | tf_op jit(solution)/shard_map/ppermute | solution.py:23
  69.7 5.6 %collective-permute-start.8 = (f32[4,10,1,256]{3,2,1,0:T(1,128)S(1)}, f32[4,10,1,256]{3,2,1,0:T(1,128)S(1)}, u32[]{:S(2)}, u32[]{:S(2)}) collective-permute-start(f32[4,10,1,256]{3,2,1,0:T(1,128)S(1)} %get-tuple-element.52), channel_id=1, source_target_pairs={{2,0},{3,1},{6,4},{7,5},{10,8},{11,9},{14,12},{15,13},{18,16},{19,... | collective-permute-start | bytes 122888 | tf_op jit(solution)/shard_map/ppermute | solution.py:25
  71.0 5.3 %collective-permute-start.9 = (f32[4,10,1,256]{3,2,1,0:T(1,128)S(1)}, f32[4,10,1,256]{3,2,1,0:T(1,128)S(1)}, u32[]{:S(2)}, u32[]{:S(2)}) collective-permute-start(f32[4,10,1,256]{3,2,1,0:T(1,128)S(1)} %get-tuple-element.51), channel_id=1, source_target_pairs={{0,2},{1,3},{4,6},{5,7},{8,10},{9,11},{12,14},{13,15},{16,18},{17,... | collective-permute-start | bytes 122888 | tf_op jit(solution)/shard_map/ppermute | solution.py:23
  84.7 6.3 %collective-permute-start.12 = (f32[4,1,16,256]{3,2,1,0:T(8,128)S(1)}, f32[4,1,16,256]{3,2,1,0:T(8,128)S(1)}, u32[]{:S(2)}, u32[]{:S(2)}) collective-permute-start(f32[4,1,16,256]{3,2,1,0:T(8,128)S(1)} %get-tuple-element.60), channel_id=1, source_target_pairs={{4,0},{8,4},{12,8},{16,12},{20,16},{24,20},{28,24},{5,1},{9,5},{13... | collective-permute-start | bytes 196616 | tf_op jit(solution)/shard_map/ppermute | solution.py:25
  86.7 5.9 %collective-permute-start.13 = (f32[4,1,16,256]{3,2,1,0:T(8,128)S(1)}, f32[4,1,16,256]{3,2,1,0:T(8,128)S(1)}, u32[]{:S(2)}, u32[]{:S(2)}) collective-permute-start(f32[4,1,16,256]{3,2,1,0:T(8,128)S(1)} %get-tuple-element.59), channel_id=1, source_target_pairs={{0,4},{4,8},{8,12},{12,16},{16,20},{20,24},{24,28},{1,5},{5,9},{9,... | collective-permute-start | bytes 196616 | tf_op jit(solution)/shard_map/ppermute | solution.py:23
  92.6 5.5 %collective-permute-start.14 = (f32[4,10,1,256]{3,2,1,0:T(1,128)S(1)}, f32[4,10,1,256]{3,2,1,0:T(1,128)S(1)}, u32[]{:S(2)}, u32[]{:S(2)}) collective-permute-start(f32[4,10,1,256]{3,2,1,0:T(1,128)S(1)} %get-tuple-element.48), channel_id=1, source_target_pairs={{2,0},{3,1},{6,4},{7,5},{10,8},{11,9},{14,12},{15,13},{18,16},{19,... | collective-permute-start | bytes 122888 | tf_op jit(solution)/shard_map/ppermute | solution.py:25
  99.4 6.1 %collective-permute-start.17 = (f32[4,10,18,1]{3,2,1,0:T(8,128)S(1)}, f32[4,10,18,1]{3,2,1,0:T(8,128)S(1)}, u32[]{:S(2)}, u32[]{:S(2)}) collective-permute-start(f32[4,10,18,1]{3,2,1,0:T(8,128)S(1)} %get-tuple-element.22), channel_id=1, source_target_pairs={{0,1},{2,3},{4,5},{6,7},{8,9},{10,11},{12,13},{14,15},{16,17},{18,... | collective-permute-start | bytes 8648 | tf_op jit(solution)/shard_map/ppermute | solution.py:23
  100.7 6.1 %collective-permute-start.16 = (f32[4,10,18,1]{3,2,1,0:T(8,128)S(1)}, f32[4,10,18,1]{3,2,1,0:T(8,128)S(1)}, u32[]{:S(2)}, u32[]{:S(2)}) collective-permute-start(f32[4,10,18,1]{3,2,1,0:T(8,128)S(1)} %get-tuple-element.21), channel_id=1, source_target_pairs={{1,0},{3,2},{5,4},{7,6},{9,8},{11,10},{13,12},{15,14},{17,16},{19,... | collective-permute-start | bytes 8648 | tf_op jit(solution)/shard_map/ppermute | solution.py:25
  129.9 5.3 %collective-permute-start.18 = (f32[4,1,8,128]{3,2,1,0:T(8,128)S(1)}, f32[4,1,8,128]{3,2,1,0:T(8,128)S(1)}, u32[]{:S(2)}, u32[]{:S(2)}) collective-permute-start(f32[4,1,8,128]{3,2,1,0:T(8,128)S(1)} %get-tuple-element.124), channel_id=1, source_target_pairs={{4,0},{8,4},{12,8},{16,12},{20,16},{24,20},{28,24},{5,1},{9,5},{13... | collective-permute-start | bytes 49160 | tf_op jit(solution)/shard_map/ppermute | solution.py:25
  131.8 5.4 %collective-permute-start.19 = (f32[4,1,8,128]{3,2,1,0:T(8,128)S(1)}, f32[4,1,8,128]{3,2,1,0:T(8,128)S(1)}, u32[]{:S(2)}, u32[]{:S(2)}) collective-permute-start(f32[4,1,8,128]{3,2,1,0:T(8,128)S(1)} %get-tuple-element.123), channel_id=1, source_target_pairs={{0,4},{4,8},{8,12},{12,16},{16,20},{20,24},{24,28},{1,5},{5,9},{9,... | collective-permute-start | bytes 49160 | tf_op jit(solution)/shard_map/ppermute | solution.py:23
  145.8 6.2 %collective-permute-start.22 = (f32[4,6,10,1]{3,0,2,1:T(4,128)S(1)}, f32[4,6,10,1]{3,0,2,1:T(4,128)S(1)}, u32[]{:S(2)}, u32[]{:S(2)}) collective-permute-start(f32[4,6,10,1]{3,0,2,1:T(4,128)S(1)} %get-tuple-element.105), channel_id=1, source_target_pairs={{1,0},{3,2},{5,4},{7,6},{9,8},{11,10},{13,12},{15,14},{17,16},{19,... | collective-permute-start | bytes 2888 | tf_op jit(solution)/shard_map/ppermute | solution.py:25
  154.5 5.3 %collective-permute-start.24 = (f32[4,1,8,128]{3,2,1,0:T(8,128)S(1)}, f32[4,1,8,128]{3,2,1,0:T(8,128)S(1)}, u32[]{:S(2)}, u32[]{:S(2)}) collective-permute-start(f32[4,1,8,128]{3,2,1,0:T(8,128)S(1)} %get-tuple-element.122), channel_id=1, source_target_pairs={{4,0},{8,4},{12,8},{16,12},{20,16},{24,20},{28,24},{5,1},{9,5},{13... | collective-permute-start | bytes 49160 | tf_op jit(solution)/shard_map/ppermute | solution.py:25
  156.5 5.4 %collective-permute-start.25 = (f32[4,1,8,128]{3,2,1,0:T(8,128)S(1)}, f32[4,1,8,128]{3,2,1,0:T(8,128)S(1)}, u32[]{:S(2)}, u32[]{:S(2)}) collective-permute-start(f32[4,1,8,128]{3,2,1,0:T(8,128)S(1)} %get-tuple-element.121), channel_id=1, source_target_pairs={{0,4},{4,8},{8,12},{12,16},{16,20},{20,24},{24,28},{1,5},{5,9},{9,... | collective-permute-start | bytes 49160 | tf_op jit(solution)/shard_map/ppermute | solution.py:23
  167.8 6.0 %collective-permute-start.28 = (f32[4,6,10,1]{3,0,2,1:T(4,128)S(1)}, f32[4,6,10,1]{3,0,2,1:T(4,128)S(1)}, u32[]{:S(2)}, u32[]{:S(2)}) collective-permute-start(f32[4,6,10,1]{3,0,2,1:T(4,128)S(1)} %get-tuple-element.99), channel_id=1, source_target_pairs={{1,0},{3,2},{5,4},{7,6},{9,8},{11,10},{13,12},{15,14},{17,16},{19,... | collective-permute-start | bytes 2888 | tf_op jit(solution)/shard_map/ppermute | solution.py:25
  176.4 5.3 %collective-permute-start.30 = (f32[4,1,8,128]{3,2,1,0:T(8,128)S(1)}, f32[4,1,8,128]{3,2,1,0:T(8,128)S(1)}, u32[]{:S(2)}, u32[]{:S(2)}) collective-permute-start(f32[4,1,8,128]{3,2,1,0:T(8,128)S(1)} %get-tuple-element.120), channel_id=1, source_target_pairs={{4,0},{8,4},{12,8},{16,12},{20,16},{24,20},{28,24},{5,1},{9,5},{13... | collective-permute-start | bytes 49160 | tf_op jit(solution)/shard_map/ppermute | solution.py:25
  178.3 5.4 %collective-permute-start.31 = (f32[4,1,8,128]{3,2,1,0:T(8,128)S(1)}, f32[4,1,8,128]{3,2,1,0:T(8,128)S(1)}, u32[]{:S(2)}, u32[]{:S(2)}) collective-permute-start(f32[4,1,8,128]{3,2,1,0:T(8,128)S(1)} %get-tuple-element.119), channel_id=1, source_target_pairs={{0,4},{4,8},{8,12},{12,16},{16,20},{20,24},{24,28},{1,5},{5,9},{9,... | collective-permute-start | bytes 49160 | tf_op jit(solution)/shard_map/ppermute | solution.py:23
  189.7 6.0 %collective-permute-start.34 = (f32[4,6,10,1]{3,0,2,1:T(4,128)S(1)}, f32[4,6,10,1]{3,0,2,1:T(4,128)S(1)}, u32[]{:S(2)}, u32[]{:S(2)}) collective-permute-start(f32[4,6,10,1]{3,0,2,1:T(4,128)S(1)} %get-tuple-element.93), channel_id=1, source_target_pairs={{1,0},{3,2},{5,4},{7,6},{9,8},{11,10},{13,12},{15,14},{17,16},{19,... | collective-permute-start | bytes 2888 | tf_op jit(solution)/shard_map/ppermute | solution.py:25
  205.9 5.4 %collective-permute-start.36 = (f32[4,1,16,256]{3,2,1,0:T(8,128)S(1)}, f32[4,1,16,256]{3,2,1,0:T(8,128)S(1)}, u32[]{:S(2)}, u32[]{:S(2)}) collective-permute-start(f32[4,1,16,256]{3,2,1,0:T(8,128)S(1)} %get-tuple-element.58), channel_id=1, source_target_pairs={{4,0},{8,4},{12,8},{16,12},{20,16},{24,20},{28,24},{5,1},{9,5},{13... | collective-permute-start | bytes 196616 | tf_op jit(solution)/shard_map/ppermute | solution.py:25
  207.8 6.3 %collective-permute-start.37 = (f32[4,1,16,256]{3,2,1,0:T(8,128)S(1)}, f32[4,1,16,256]{3,2,1,0:T(8,128)S(1)}, u32[]{:S(2)}, u32[]{:S(2)}) collective-permute-start(f32[4,1,16,256]{3,2,1,0:T(8,128)S(1)} %get-tuple-element.57), channel_id=1, source_target_pairs={{0,4},{4,8},{8,12},{12,16},{16,20},{20,24},{24,28},{1,5},{5,9},{9,... | collective-permute-start | bytes 196616 | tf_op jit(solution)/shard_map/ppermute | solution.py:23
  220.9 5.8 %collective-permute-start.41 = (f32[4,10,18,1]{3,2,1,0:T(8,128)S(1)}, f32[4,10,18,1]{3,2,1,0:T(8,128)S(1)}, u32[]{:S(2)}, u32[]{:S(2)}) collective-permute-start(f32[4,10,18,1]{3,2,1,0:T(8,128)S(1)} %get-tuple-element.20), channel_id=1, source_target_pairs={{0,1},{2,3},{4,5},{6,7},{8,9},{10,11},{12,13},{14,15},{16,17},{18,... | collective-permute-start | bytes 8648 | tf_op jit(solution)/shard_map/ppermute | solution.py:23
  222.2 5.5 %collective-permute-start.40 = (f32[4,10,18,1]{3,2,1,0:T(8,128)S(1)}, f32[4,10,18,1]{3,2,1,0:T(8,128)S(1)}, u32[]{:S(2)}, u32[]{:S(2)}) collective-permute-start(f32[4,10,18,1]{3,2,1,0:T(8,128)S(1)} %get-tuple-element.19), channel_id=1, source_target_pairs={{1,0},{3,2},{5,4},{7,6},{9,8},{11,10},{13,12},{15,14},{17,16},{19,... | collective-permute-start | bytes 8648 | tf_op jit(solution)/shard_map/ppermute | solution.py:25
  230.0 5.3 %collective-permute-start.42 = (f32[4,1,16,256]{3,2,1,0:T(8,128)S(1)}, f32[4,1,16,256]{3,2,1,0:T(8,128)S(1)}, u32[]{:S(2)}, u32[]{:S(2)}) collective-permute-start(f32[4,1,16,256]{3,2,1,0:T(8,128)S(1)} %get-tuple-element.56), channel_id=1, source_target_pairs={{4,0},{8,4},{12,8},{16,12},{20,16},{24,20},{28,24},{5,1},{9,5},{13... | collective-permute-start | bytes 196616 | tf_op jit(solution)/shard_map/ppermute | solution.py:25
  231.9 5.9 %collective-permute-start.43 = (f32[4,1,16,256]{3,2,1,0:T(8,128)S(1)}, f32[4,1,16,256]{3,2,1,0:T(8,128)S(1)}, u32[]{:S(2)}, u32[]{:S(2)}) collective-permute-start(f32[4,1,16,256]{3,2,1,0:T(8,128)S(1)} %get-tuple-element.55), channel_id=1, source_target_pairs={{0,4},{4,8},{8,12},{12,16},{16,20},{20,24},{24,28},{1,5},{5,9},{9,... | collective-permute-start | bytes 196616 | tf_op jit(solution)/shard_map/ppermute | solution.py:23
  244.6 6.1 %collective-permute-start.47 = (f32[4,10,18,1]{3,2,1,0:T(8,128)S(1)}, f32[4,10,18,1]{3,2,1,0:T(8,128)S(1)}, u32[]{:S(2)}, u32[]{:S(2)}) collective-permute-start(f32[4,10,18,1]{3,2,1,0:T(8,128)S(1)} %get-tuple-element.18), channel_id=1, source_target_pairs={{0,1},{2,3},{4,5},{6,7},{8,9},{10,11},{12,13},{14,15},{16,17},{18,... | collective-permute-start | bytes 8648 | tf_op jit(solution)/shard_map/ppermute | solution.py:23
  245.9 6.1 %collective-permute-start.46 = (f32[4,10,18,1]{3,2,1,0:T(8,128)S(1)}, f32[4,10,18,1]{3,2,1,0:T(8,128)S(1)}, u32[]{:S(2)}, u32[]{:S(2)}) collective-permute-start(f32[4,10,18,1]{3,2,1,0:T(8,128)S(1)} %get-tuple-element.17), channel_id=1, source_target_pairs={{1,0},{3,2},{5,4},{7,6},{9,8},{11,10},{13,12},{15,14},{17,16},{19,... | collective-permute-start | bytes 8648 | tf_op jit(solution)/shard_map/ppermute | solution.py:25
  (28 other events, 106.2 us)
where the time goes:
time: 259 us; the launch traced here: 255 us
  starting transfers between devices  135 us (52%)
  waiting for transfers between devices  41.6 us (16%)
  local copies, waits for them, and re-layouts  41.4 us (16%)
  other arithmetic  35.5 us (14%)
    ppermute x24, starting transfers between devices, with_halo(): lax.ppermute(head, axis, [((i + 1) % count, i) for i in range(ends)])  65.6 us
    ppermute x24, starting transfers between devices, with_halo(): lax.ppermute(tail, axis, [(i, (i + 1) % count) for i in range(ends)])  63.4 us
    ppermute x24, waiting for transfers between devices, with_halo(): lax.ppermute(tail, axis, [(i, (i + 1) % count) for i in range(ends)])  27.2 us
    ppermute x24, waiting for transfers between devices, with_halo(): lax.ppermute(head, axis, [((i + 1) % count, i) for i in range(ends)])  14.5 us
    reduce_sum x3, other arithmetic, restrict(): return jnp.mean(shaped, axis=(2, 4, 6))  13.7 us
    sub x1, local copies, waits for them, and re-layouts, fine_residual(): return right_side - apply_operator(padded, chi, 1.0, 0.5)  8.8 us
    concatenate x24, other arithmetic, with_halo(): jnp.concatenate([lax.ppermute(tail, axis, [(i, (i + 1) % count) for i in...  6.24 us
    scatter x1, local copies, waits for them, and re-layouts, body(): slot_of = jnp.full((tiles * capacity,), slots, jnp.int32).at[target.resha...  6.16 us
  transfers between devices with their start and end apart: 49, of which 24 were waited for; matrix products, arithmetic and copies ran while one was open for 7% of the time, Pallas kernels for 0%

commit v1 on v0

v1 whole, which is shorter than its diff:
```python
import functools

import jax
import jax.numpy as jnp
from jax import lax
from jax.experimental import pallas as pl
from jax.experimental.pallas import tpu as pltpu
from jax.sharding import PartitionSpec as P

COARSE_SWEEPS = 4
SHIFT = 0.05
RELAX = 0.6
KEEP = 1.0 - RELAX
LANES = 128
FIRST_W = 2
FINE_W = 3
COARSE_W = 4
HIGHEST = lax.Precision.HIGHEST
VMEM = pl.BlockSpec(memory_space=pltpu.VMEM)
SMEM = pl.BlockSpec(memory_space=pltpu.SMEM)
PARAMS = pltpu.CompilerParams(vmem_limit_bytes=48 << 20)


def pairs(count, first):
    return [p for i in range(first, count - 1, 2) for p in ((i, i + 1), (i + 1, i))]


def cut(values, dim, width, to_next):
    size = values.shape[dim]
    if size == width:
        return values
    start = jnp.where(to_next, size - width, 0)
    return lax.dynamic_slice_in_dim(values, start, width, axis=dim)


def swap(axis, values, dim, width):
    count = lax.axis_size(axis)
    even = lax.axis_index(axis) % 2 == 0
    got = [lax.ppermute(cut(values, dim, width, even), axis, pairs(count, 0))]
    if count > 2:
        got.append(lax.ppermute(cut(values, dim, width, ~even), axis, pairs(count, 1)))
    return got


def halo(values, width):
    xs = swap("gx", values, 1, width)
    values = jnp.concatenate([values, *xs], axis=1)
    ys = swap("gy", values, 2, width)
    values = jnp.concatenate([values, *ys], axis=2)
    zs = swap("lvl", values, 3, LANES)
    return xs, ys, zs


def place_halo(dst, margin, own, xs, ys, zs, flags, width):
    fields, planes, rows, lanes = own.shape
    total = dst.shape[2]
    even_x, even_y, even_z = flags[0] == 1, flags[1] == 1, flags[2] == 1
    near = (lax.broadcasted_iota(jnp.int32, (1, LANES), 1) < LANES // 2) == even_z
    gap = total - rows - 2 * width

    def field(f, _):
        for k in range(planes + len(xs) * width):
            if k < planes:
                at, source, j = margin + k, own, k
            else:
                which, j = divmod(k - planes, width)
                up, down = margin + planes + j, margin - width + j
                at = jnp.where(even_x, up, down) if which == 0 else jnp.where(even_x, down, up)
                source = xs[which]
            dst[f, at, 0:rows, 0:lanes] = source[f, j]
            zv = jnp.where(near, zs[0][f, k], 0.0 if len(zs) == 1 else zs[1][f, k])
            dst[f, at, 0:rows, lanes:] = zv[0:rows]
            for src, z_at, to in ((0, 0, slice(0, lanes)), (1, 0, slice(lanes, lanes + LANES))):
                if src == 0:
                    first = ys[0][f, k]
                    second = ys[1][f, k] if len(ys) > 1 else jnp.zeros_like(first)
                else:
                    first = zv[rows:rows + width]
                    second = zv[rows + width:rows + 2 * width] if len(ys) > 1 else jnp.zeros_like(first)
                dst[f, at, rows:rows + width, to] = jnp.where(even_y, first, second)
                dst[f, at, total - width:total, to] = jnp.where(even_y, second, first)
            if gap:
                dst[f, at, rows + width:total - width, :] = jnp.zeros((gap, dst.shape[3]), jnp.float32)
        return 0

    lax.fori_loop(0, fields, field, 0)


def inside(flags, rows, lanes, total, depth):
    row = lax.broadcasted_iota(jnp.int32, (total, lanes + LANES), 0)
    lane = lax.broadcasted_iota(jnp.int32, (total, lanes + LANES), 1)
    end = lanes + LANES
    row_ok = (row < rows) | ((row < rows + depth) & (flags[5] == 1)) | ((row >= total - depth) & (flags[6] == 1))
    lane_ok = (lane < lanes) | ((lane < lanes + depth) & (flags[7] == 1)) | ((lane >= end - depth) & (flags[8] == 1))
    return jnp.where(row_ok & lane_ok, 1.0, 0.0)


def plane_inside(flags, p, margin, planes):
    return jnp.where(p < margin, flags[4], jnp.where(p >= margin + planes, flags[3], 1)).astype(jnp.float32)


def neighbours(ref, p):
    rows, lanes = ref.shape[2], ref.shape[3]
    sums, grads, spread = [], [], 0.0
    for f in range(4):
        c, xn, xp = ref[f, p], ref[f, p + 1], ref[f, p - 1]
        yn, yp = pltpu.roll(c, rows - 1, 0), pltpu.roll(c, 1, 0)
        zn, zp = pltpu.roll(c, lanes - 1, 1), pltpu.roll(c, 1, 1)
        sums.append((xn + xp) + (yn + yp) + (zn + zp))
        if f == 3:
            grads = [xn - xp, yn - yp, zn - zp]
        else:
            spread = spread + (xn - xp, yn - yp, zn - zp)[f]
    return sums, grads + [spread]


def pack_kernel(tile_ref, mask_ref, out_ref, used_ref, *, capacity):
    tiles = out_ref.shape[0]
    count = mask_ref.shape[0]
    out_ref[...] = jnp.zeros(out_ref.shape, jnp.float32)

    def clear(t, _):
        used_ref[t] = 0
        return 0

    lax.fori_loop(0, tiles, clear, 0)

    def row(r, _):
        t = tile_ref[r]
        n = used_ref[t]
        used_ref[t] = n + 1
        out_ref[t, jnp.minimum(n, capacity - 1)] = mask_ref[r]
        return 0

    lax.fori_loop(0, count, row, 0)


def first_kernel(flags, rhs, start, *refs, nxs, nys, nzs):
    halos, (rhs_out, part_out, both) = refs[:nxs + nys + nzs], refs[nxs + nys + nzs:]
    xs, ys, zs = halos[:nxs], halos[nxs:nxs + nys], halos[nxs + nys:]
    half = lambda refs_, lo: [r.at[lo:lo + 4] for r in refs_]
    planes, rows, lanes = rhs.shape[1:]
    place_halo(rhs_out, FIRST_W, rhs, half(xs, 0), half(ys, 0), half(zs, 0), flags, FIRST_W)
    place_halo(both, FIRST_W, start, half(xs, 4), half(ys, 4), half(zs, 4), flags, FIRST_W)

    def plane(k, _):
        p = k + FIRST_W
        sums, grads = neighbours(both, p)
        for f in range(4):
            part = rhs_out[f, p] + sums[f] - 0.5 * grads[f]
            part_out[f, k] = part[0:rows, 0:lanes]
        return 0

    lax.fori_loop(0, planes, plane, 0)


def chi_kernel(slot_ref, rows_ref, start, part, out, coarse_out, acc, pooled):
    planes, rows, lanes = start.shape[1:]
    acc[...] = jnp.zeros(acc.shape, jnp.float32)
    per = rows_ref.shape[1]

    def add(s, _):
        for c in range(per):
            at = pl.ds(pl.multiple_of(slot_ref[s * per + c] * 8, 8), 8)
            acc[at, :] = acc[at, :] + rows_ref[s, c]
        return 0

    lax.fori_loop(0, rows_ref.shape[0], add, 0)
    z_tiles = lanes // LANES
    across = rows // 2
    for qx in range(planes // 2):
        for zt in range(z_tiles):
            total = None
            for i in range(2):
                for j in range(2):
                    v = acc[pl.ds(qx * across * 8 + (2 * i + j) * z_tiles + zt, across, stride=8), :]
                    pooled[zt, pl.ds(j, across, stride=2), :] = v
                    total = v if total is None else total + v
                out[4, 2 * qx + i, :, zt * LANES:(zt + 1) * LANES] = pooled[zt]
            coarse_out[qx, :, zt * LANES:(zt + 1) * LANES] = total
    for f in range(4):
        for p in range(planes):
            weight = RELAX / (SHIFT + 6.0 + out[4, p]) if f < 3 else RELAX / (SHIFT + 6.0)
            out[f, p] = KEEP * start[f, p] + weight * part[f, p]


def second_kernel(flags, own, pooled_chi, rhs, *refs, nxs, nys, nzs):
    halos, (state_out, weight_out, coarse_out, ext, tmp, pooled) = refs[:nxs + nys + nzs], refs[nxs + nys + nzs:]
    xs, ys, zs = halos[:nxs], halos[nxs:nxs + nys], halos[nxs + nys:]
    planes, rows, lanes = own.shape[1:]
    total = ext.shape[2]
    place_halo(ext, FINE_W, own, xs, ys, zs, flags, FINE_W)
    mask = inside(flags, rows, lanes, total, 2)
    w_p = (RELAX / (SHIFT + 6.0)) * mask

    def sweep(k, _):
        p = k + FINE_W - 2
        here = plane_inside(flags, k, 2, planes)
        sums, grads = neighbours(ext, p)
        w_u = (RELAX / (SHIFT + 6.0 + ext[4, p])) * (mask * here)
        weight_out[k] = w_u
        for f in range(4):
            w = w_u if f < 3 else w_p * here
            state_out[f, k] = KEEP * ext[f, p] + w * (rhs[f, k] + sums[f] - 0.5 * grads[f])
        return 0

    lax.fori_loop(0, planes + 4, sweep, 0)

    def pool(cx, _):
        both = [None] * 4
        for i in range(2):
            k = 2 + 2 * cx + i
            sums, grads = neighbours(state_out, k)
            for f in range(4):
                diag = SHIFT + 6.0 + (ext[4, k + FINE_W - 2] if f < 3 else 0.0)
                r = rhs[f, k] + sums[f] - 0.5 * grads[f] - diag * state_out[f, k]
                both[f] = r if i == 0 else both[f] + r
        for f in range(4):
            for zt in range(lanes // LANES):
                tmp[f, zt] = both[f][0:rows, zt * LANES:(zt + 1) * LANES]
                v = tmp[f, zt, pl.ds(0, rows // 2, stride=2), :] + tmp[f, zt, pl.ds(1, rows // 2, stride=2), :]
                pooled[f, cx, :, zt * LANES:(zt + 1) * LANES] = v
        return 0

    lax.fori_loop(0, planes // 2, pool, 0)
    pooled[4] = pooled_chi[...]
    lane = lax.broadcasted_iota(jnp.int32, (lanes, lanes // 2), 0)
    cell = lax.broadcasted_iota(jnp.int32, (lanes, lanes // 2), 1)
    gather = jnp.where(lane // 2 == cell, 0.125, 0.0)
    flat = pooled[...].reshape(5 * planes // 2 * rows // 2, lanes)
    coarse = jnp.dot(flat, gather, precision=HIGHEST, preferred_element_type=jnp.float32)
    coarse_out[...] = coarse.reshape(coarse_out.shape)


def last_kernel(flags, own, state, weight, rhs, *refs, nxs, nys, nzs):
    halos = refs[:nxs + nys + nzs]
    out, ext, one, two, fine, mid, tmp = refs[nxs + nys + nzs:]
    xs, ys, zs = halos[:nxs], halos[nxs:nxs + nys], halos[nxs + nys:]
    planes, rows, lanes = own.shape[1:]
    total, wide = ext.shape[2], ext.shape[3]
    place_halo(ext, COARSE_W, own, xs, ys, zs, flags, COARSE_W)
    mask = inside(flags, rows, lanes, total, COARSE_W)
    w_p = (RELAX / (SHIFT + 1.5)) * mask

    def begin(p, _):
        here = plane_inside(flags, p, COARSE_W, planes)
        w_u = (RELAX / (SHIFT + 1.5 + ext[4, p])) * (mask * here)
        ext[4, p] = w_u
        for f in range(4):
            one[f, p] = (w_u if f < 3 else w_p * here) * ext[f, p]
        return 0

    lax.fori_loop(0, planes + 2 * COARSE_W, begin, 0)
    now, then = one, two
    for s in range(1, COARSE_SWEEPS):
        def sweep(k, _, now=now, then=then, s=s):
            p = k + s
            here = plane_inside(flags, p, COARSE_W, planes)
            sums, grads = neighbours(now, p)
            for f in range(4):
                w = ext[4, p] if f < 3 else w_p * here
                then[f, p] = KEEP * now[f, p] + w * (ext[f, p] + 0.25 * (sums[f] - grads[f]))
            return 0

        lax.fori_loop(0, planes + 2 * COARSE_W - 2 * s, sweep, 0)
        now, then = then, now

    f_total, f_wide = fine.shape[2], fine.shape[3]
    f_rows, f_lanes = 2 * rows, 2 * lanes
    cell = lax.broadcasted_iota(jnp.int32, (wide, f_wide), 0)
    lane = lax.broadcasted_iota(jnp.int32, (wide, f_wide), 1)
    from_cell = jnp.where(lane < f_lanes + LANES // 2, lane // 2, wide - 1 - (f_wide - 1 - lane) // 2)
    spread = jnp.where(cell == from_cell, 1.0, 0.0)
    c_planes = planes + 2
    flat = now[:, COARSE_W - 1:COARSE_W - 1 + c_planes].reshape(4 * c_planes * total, wide)
    grown = jnp.dot(flat, spread, precision=HIGHEST, preferred_element_type=jnp.float32)
    for f in range(4):
        for cp in range(c_planes):
            lo = (f * c_planes + cp) * total
            for zt in range(f_wide // LANES):
                v = grown[lo:lo + total, zt * LANES:(zt + 1) * LANES]
                at = f * c_planes + cp
                for j in range(2):
                    tmp[zt, pl.ds(j, rows, stride=2), :] = v[0:rows]
                    tmp[zt, pl.ds(f_rows + j, 2, stride=2), :] = v[rows:rows + 2]
                    tmp[zt, pl.ds(f_total - 4 + j, 2, stride=2), :] = v[total - 2:total]
                for i in range(2):
                    to = slice(zt * LANES, (zt + 1) * LANES)
                    fine[f, 2 * cp + i, :, to] = state[f, 2 * cp + i, :, to] + tmp[zt]
    f_planes = 2 * planes
    f_mask = inside(flags, f_rows, f_lanes, f_total, 2)
    w_q = (RELAX / (SHIFT + 6.0)) * f_mask

    def post(k, _):
        p = k + 1
        here = plane_inside(flags, p, 2, f_planes)
        sums, grads = neighbours(fine, p)
        for f in range(4):
            w = weight[p] if f < 3 else w_q * here
            mid[f, p] = KEEP * fine[f, p] + w * (rhs[f, p] + sums[f] - 0.5 * grads[f])
        return 0

    lax.fori_loop(0, f_planes + 2, post, 0)

    def final(k, _):
        p = k + 2
        sums, grads = neighbours(mid, p)
        for f in range(4):
            w = weight[p] if f < 3 else w_q
            v = KEEP * mid[f, p] + w * (rhs[f, p] + sums[f] - 0.5 * grads[f])
            out[f, k] = v[0:f_rows, 0:f_lanes]
        return 0

    lax.fori_loop(0, f_planes, final, 0)


def call(kernel, shapes, scratch, *args, smem=1):
    outs = [jax.ShapeDtypeStruct(s, jnp.float32) for s in shapes]
    return pl.pallas_call(
        kernel,
        out_shape=outs,
        in_specs=[SMEM] * smem + [VMEM] * (len(args) - smem),
        out_specs=[VMEM] * len(outs),
        scratch_shapes=scratch,
        compiler_params=PARAMS,
    )(*args)


def routes(block_tile, block_slot, tiles, count_l, per_device, capacity, slots):
    my_tile = lax.axis_index("gx") * lax.axis_size("gy") + lax.axis_index("gy")
    index_l = lax.axis_index("lvl")
    their_tiles = lax.dynamic_index_in_dim(block_tile.reshape(tiles, count_l, per_device), index_l, 1, keepdims=False)
    their_slots = lax.dynamic_index_in_dim(block_slot.reshape(tiles, count_l, per_device), index_l, 1, keepdims=False)
    arriving = their_tiles == my_tile
    counter = jnp.arange(per_device, dtype=jnp.int32)
    earlier = counter[None, :, None] < counter[None, None, :]
    order = jnp.sum(jnp.where(arriving[:, :, None] & earlier, 1, 0), axis=1)
    places = jnp.arange(capacity, dtype=jnp.int32)
    hit = arriving[:, None, :] & (order[:, None, :] == places[None, :, None])
    slot = jnp.sum(jnp.where(hit, their_slots[:, None, :] - slots, 0), axis=2) + slots
    return slot.reshape(-1)


def body(right_side, start_field, mask_blocks, block_tile, block_slot):
    axes = ("gx", "gy", "lvl")
    counts = [lax.axis_size(a) for a in axes]
    index = [lax.axis_index(a) for a in axes]
    tiles = counts[0] * counts[1]
    per_device, width = mask_blocks.shape
    capacity = max(2, 2 * per_device // tiles)
    _, planes, rows, lanes = right_side.shape
    slots = planes // 2 * (rows // 2)
    c_planes, c_rows, c_lanes = planes // 2, rows // 2, lanes // 2
    flags = [i % 2 == 0 for i in index]
    for i, n in zip(index, counts):
        flags += [i < n - 1, i > 0]
    flags = jnp.stack(flags).astype(jnp.int32)

    my_flat = (index[0] * counts[1] + index[1]) * counts[2] + index[2]
    tile_ids = block_tile[:, 0]
    my_tiles = lax.dynamic_slice_in_dim(tile_ids, my_flat * per_device, per_device)
    (outgoing,) = call(
        functools.partial(pack_kernel, capacity=capacity),
        [(tiles, capacity, width // LANES, LANES)],
        [pltpu.SMEM((tiles,), jnp.int32)],
        my_tiles, mask_blocks.reshape(per_device, width // LANES, LANES),
    )
    arrived = lax.all_to_all(outgoing, ("gx", "gy"), split_axis=0, concat_axis=0, tiled=True)
    slot_of = routes(tile_ids, block_slot, tiles, counts[2], per_device, capacity, slots)

    fields = jnp.concatenate([right_side, start_field], axis=0)
    xs, ys, zs = halo(fields, FIRST_W)
    num = dict(nxs=len(xs), nys=len(ys), nzs=len(zs))
    total, wide = rows + 8, lanes + LANES
    near = planes + 4
    rhs, part = call(
        functools.partial(first_kernel, **num),
        [(4, near, total, wide), (4, planes, rows, lanes)],
        [pltpu.VMEM((4, near, total, wide), jnp.float32)],
        flags, right_side, start_field, *xs, *ys, *zs,
    )
    state, pooled_chi = call(
        chi_kernel,
        [(5, planes, rows, lanes), (c_planes, c_rows, lanes)],
        [pltpu.VMEM(((slots + 1) * 8, LANES), jnp.float32), pltpu.VMEM((lanes // LANES, rows, LANES), jnp.float32)],
        slot_of, arrived, start_field, part,
    )
    xs, ys, zs = halo(state, FINE_W)
    state, weight, coarse = call(
        functools.partial(second_kernel, **num),
        [(4, near, total, wide), (near, total, wide), (5, c_planes, c_rows, c_lanes)],
        [
            pltpu.VMEM((5, planes + 2 * FINE_W, total, wide), jnp.float32),
            pltpu.VMEM((4, lanes // LANES, rows, LANES), jnp.float32),
            pltpu.VMEM((5, c_planes, c_rows, lanes), jnp.float32),
        ],
        flags, state, pooled_chi, rhs, *xs, *ys, *zs,
    )
    xs, ys, zs = halo(coarse, COARSE_W)
    c_ext = (c_planes + 2 * COARSE_W, c_rows + 8, c_lanes + LANES)
    (out,) = call(
        functools.partial(last_kernel, **num),
        [right_side.shape],
        [
            pltpu.VMEM((5, *c_ext), jnp.float32),
            pltpu.VMEM((4, *c_ext), jnp.float32),
            pltpu.VMEM((4, *c_ext), jnp.float32),
            pltpu.VMEM((4, near, total, wide), jnp.float32),
            pltpu.VMEM((4, near, total, wide), jnp.float32),
            pltpu.VMEM((wide // LANES, total, LANES), jnp.float32),
        ],
        flags, coarse, state, weight, rhs, *xs, *ys, *zs,
    )
    return out


def solution(mesh):
    in_specs = (
        P(None, "gx", "gy", "lvl"),
        P(None, "gx", "gy", "lvl"),
        P(("gx", "gy", "lvl"), None),
        P(),
        P(),
    )
    out_specs = P(None, "gx", "gy", "lvl")
    return jax.shard_map(body, mesh=mesh, in_specs=in_specs, out_specs=out_specs, check_vma=False)
```

time: 259 us -> 98.3 us (0.38); the launches traced: 255 us -> 97.2 us
  starting transfers between devices: 135 us -> 28.5 us
  other arithmetic: 35.5 us -> 1.63 us
  local copies, waits for them, and re-layouts: 41.4 us -> 8.02 us
  Pallas kernels: 0 us -> 19.5 us
    ppermute x48 -> x12, starting transfers between devices: 129 us -> 23 us  [the longest x9 14.2 us: swap(): got = [lax.ppermute(cut(values, dim, width, even), axis, pairs(count, 0))]]
    pallas_call x0 -> x5, Pallas kernels: none -> 19.5 us  [call(): pl.pallas_call(kernel, out_shape=outs, in_specs=[SMEM] * smem + [VMEM] *...]
    reduce_sum x4 -> x2, other arithmetic: 13.9 us -> 0.56 us  [the longest x1 0.29 us: routes(): order = jnp.sum(jnp.where(arriving[:, :, None] & earlier, 1, 0), axis=1)]
    sub x1 -> x0, local copies, waits for them, and re-layouts: 8.8 us -> none  [fine_residual(): return right_side - apply_operator(padded, chi, 1.0, 0.5)]
    scatter x2 -> x0, local copies, waits for them, and re-layouts: 7.73 us -> none  [the longest x1 6.16 us: body(): slot_of = jnp.full((tiles * capacity,), slots, jnp.int32).at[target.resha...]
    add x34 -> x1, other arithmetic: 6.93 us -> 0.01 us  [routes(): jnp.sum(jnp.where(hit, their_slots[:, None, :] - slots, 0), axis=2) + slots]
    concatenate x24 -> x4, other arithmetic: 6.24 us -> 0.32 us  [the longest x3 0.23 us: halo(): values = jnp.concatenate([values, *ys], axis=2)]
    reshape x4 -> x1, local copies, waits for them, and re-layouts: 4.57 us -> 0.08 us  [routes(): block_slot.reshape(tiles, count_l, per_device)]
  transfers between devices with their start and end apart: 49 -> 13, of which waited for: 24 -> 8; matrix products, arithmetic and copies ran while one was open for 7% -> 5% of each run, Pallas kernels for 0% -> 5%
where the time goes in v1:
time: 98.3 us; the launch traced here: 97.2 us
  waiting for transfers between devices  39.2 us (40%)
  starting transfers between devices  28.5 us (29%)
  Pallas kernels  19.5 us (20%)
  local copies, waits for them, and re-layouts  8.02 us (8%)
  other arithmetic  1.63 us (2%)
    ppermute x9, waiting for transfers between devices, swap(): got = [lax.ppermute(cut(values, dim, width, even), axis, pairs(count, 0))]  39.2 us
    pallas_call x5, Pallas kernels, call(): pl.pallas_call(kernel, out_shape=outs, in_specs=[SMEM] * smem + [VMEM] *...  19.5 us
    ppermute x9, starting transfers between devices, swap(): got = [lax.ppermute(cut(values, dim, width, even), axis, pairs(count, 0))]  14.2 us
    ppermute x3, starting transfers between devices, swap(): lax.ppermute(cut(values, dim, width, ~even), axis, pairs(count, 1))  8.8 us
    all_to_all x1, starting transfers between devices, body(): lax.all_to_all(outgoing, ('gx', 'gy'), split_axis=0, concat_axis=0, tiled...  5.54 us
    unnamed x22, local copies, waits for them, and re-layouts  3.14 us
    ppermute x2, local copies, waits for them, and re-layouts, swap(): got = [lax.ppermute(cut(values, dim, width, even), axis, pairs(count, 0))]  2.73 us
  transfers between devices with their start and end apart: 13, of which 8 were waited for; matrix products, arithmetic and copies ran while one was open for 5% of the time, Pallas kernels for 5%

profile of v1, /device:TPU:9, one launch (start us, length us, event | category | flops | bytes accessed | tf_op | source)
XLA Modules:
  0.0 97.2 jit_solution(1770054387210001490)
XLA Ops:
  0.0 1.1 %constant_dynamic-update-slice_fusion.1 = f32[8,8,16,256]{3,2,1,0:T(8,128)S(1)} fusion(f32[4,8,16,256]{3,2,1,0:T(8,128)} %rhs.5), kind=kLoop, calls=%fused_computation.22 | loop fusion | bytes 1048576
  1.3 0.7 constant_dynamic-slice_fusion.3
  2.0 3.0 %collective-permute-start.1 = (f32[8,2,16,256]{3,2,1,0:T(8,128)}, f32[8,2,16,256]{3,2,1,0:T(8,128)S(1)}, u32[]{:S(2)}, u32[]{:S(2)}) collective-permute-start(f32[8,2,16,256]{3,2,1,0:T(8,128)} %get-tuple-element.19), channel_id=1, source_target_pairs={{4,8},{8,4},{12,16},{16,12},{20,24},{24,20},{5,9},{9,5},{13,17},{1... | collective-permute-start | bytes 786440 | tf_op jit(solution)/shard_map/ppermute | solution.py:41
  5.0 1.4 %collective-permute-start = (f32[8,2,16,256]{3,2,1,0:T(8,128)S(1)}, f32[8,2,16,256]{3,2,1,0:T(8,128)S(1)}, u32[]{:S(2)}, u32[]{:S(2)}) collective-permute-start(f32[8,2,16,256]{3,2,1,0:T(8,128)S(1)} %get-tuple-element.20), channel_id=1, source_target_pairs={{0,4},{4,0},{8,12},{12,8},{16,20},{20,16},{24,28},{28,24},{1,5},{5... | collective-permute-start | bytes 786440 | tf_op jit(solution)/shard_map/ppermute | solution.py:39
  6.6 2.6 %shard_map.55 = f32[16,12,8,128]{3,2,1,0:T(8,128)} custom-call(s32[96]{0:T(128)S(1)} %fusion.7.tile_ref, f32[96,8,128]{2,1,0:T(8,128)S(1)} %bitcast.18), custom_call_target="tpu_custom_call" | custom-call | tf_op jit(solution)/shard_map/pallas_call | solution.py:319
  9.2 5.5 %all-to-all-start = ((f32[16,12,8,128]{3,2,1,0:T(8,128)}), f32[16,12,8,128]{3,2,1,0:T(8,128)S(1)}, u32[]{:S(2)}, u32[]{:S(2)}) async-start(f32[16,12,8,128]{3,2,1,0:T(8,128)} %shard_map.55), calls=%async_computation | async-start | bytes 1572864 | tf_op jit(solution)/shard_map/all_to_all | solution.py:368
  14.8 4.1 %collective-permute-done.refs_0_ = f32[8,2,16,256]{3,2,1,0:T(8,128)S(1)} collective-permute-done((f32[8,2,16,256]{3,2,1,0:T(8,128)S(1)}, f32[8,2,16,256]{3,2,1,0:T(8,128)S(1)}, u32[]{:S(2)}, u32[]{:S(2)}) %collective-permute-start) | collective-permute-done | bytes 262176 | tf_op jit(solution)/shard_map/ppermute | solution.py:39
  18.9 1.3 %collective-permute-start.2 = (f32[8,12,2,256]{3,2,1,0:T(2,128)S(1)}, f32[8,12,2,256]{3,2,1,0:T(2,128)S(1)}, u32[]{:S(2)}, u32[]{:S(2)}) collective-permute-start(f32[8,12,2,256]{3,2,1,0:T(2,128)S(1)} %fusion.5), channel_id=1, source_target_pairs={{0,2},{2,0},{1,3},{3,1},{4,6},{6,4},{5,7},{7,5},{8,10},{10,8},{9,1... | collective-permute-start | bytes 589832 | tf_op jit(solution)/shard_map/ppermute | solution.py:39
  20.2 9.5 %collective-permute-done.2.refs_2_ = f32[8,12,2,256]{3,2,1,0:T(2,128)S(1)} collective-permute-done((f32[8,12,2,256]{3,2,1,0:T(2,128)S(1)}, f32[8,12,2,256]{3,2,1,0:T(2,128)S(1)}, u32[]{:S(2)}, u32[]{:S(2)}) %collective-permute-start.2) | collective-permute-done | bytes 196640 | tf_op jit(solution)/shard_map/ppermute | solution.py:39
  29.9 0.5 copy.15
  30.4 1.5 %collective-permute-start.3 = (f32[8,12,18,128]{3,0,2,1:T(8,128)S(1)}, f32[8,12,18,128]{3,0,2,1:T(8,128)}, u32[]{:S(2)}, u32[]{:S(2)}) collective-permute-start(f32[8,12,18,128]{3,0,2,1:T(8,128)S(1)} %copy.15), channel_id=1, source_target_pairs={{0,1},{1,0},{2,3},{3,2},{4,5},{5,4},{6,7},{7,6},{8,9},{9,8},{10,11... | collective-permute-start | bytes 2654216 | tf_op jit(solution)/shard_map/ppermute | solution.py:39
  32.1 0.5 broadcast.31
  32.6 0.7 reduce.3
  34.3 1.4 %copy.16.refs_3_ = f32[8,12,18,128]{3,2,1,0:T(8,128)S(1)} copy(f32[8,12,18,128]{3,0,2,1:T(8,128)} %collective-permute-done.3) | data formatting | bytes 1769472 | tf_op jit(solution)/shard_map/ppermute | solution.py:39
  35.7 2.0 %shard_map.56 = (f32[4,12,24,384]{3,2,1,0:T(8,128)S(1)}, f32[4,8,16,256]{3,2,1,0:T(8,128)S(1)}) custom-call(s32[9]{0:T(128)S(1)} %convert_element_type.3.flags, f32[4,8,16,256]{3,2,1,0:T(8,128)S(1)} %copy-done.3, f32[4,8,16,256]{3,2,1,0:T(8,128)S(1)} %copy-done.2, f32[8,2,16,256]{3,2,1,0:T(8,128)S(1)} %collective-permute-done.refs_0_, ...), custom_call_target="tpu_custom_call" | custom-call | tf_op jit(solution)/shard_map/pallas_call | solution.py:319
  37.7 1.2 %copy-done = f32[4,12,24,384]{3,2,1,0:T(8,128)} copy-done((f32[4,12,24,384]{3,2,1,0:T(8,128)}, f32[4,12,24,384]{3,2,1,0:T(8,128)S(1)}, u32[]{:S(2)}) %copy-start) | copy-done | bytes 1769496
  39.0 1.8 %shard_map.57 = (f32[5,8,16,256]{3,2,1,0:T(8,128)S(1)}, f32[4,8,256]{2,1,0:T(8,128)S(1)}) custom-call(s32[192]{0:T(256)S(1)} %add.59.slot_ref, f32[16,12,8,128]{3,2,1,0:T(8,128)S(1)} %all-to-all-done.rows_ref, f32[4,8,16,256]{3,2,1,0:T(8,128)S(1)} %copy-done.2, f32[4,8,16,256]{3,2,1,0:T(8,128)S(1)} %get-tuple-element.12.part), custom_call_target="tpu_custom_call" | custom-call | tf_op jit(solution)/shard_map/pallas_call | solution.py:319
  41.1 2.8 %collective-permute-start.5 = (f32[5,3,16,256]{3,2,1,0:T(8,128)S(1)}, f32[5,3,16,256]{3,2,1,0:T(8,128)S(1)}, u32[]{:S(2)}, u32[]{:S(2)}) collective-permute-start(f32[5,3,16,256]{3,2,1,0:T(8,128)S(1)} %get-tuple-element.21), channel_id=1, source_target_pairs={{4,8},{8,4},{12,16},{16,12},{20,24},{24,20},{5,9},{9,5},{13,17},{1... | collective-permute-start | bytes 737288 | tf_op jit(solution)/shard_map/ppermute | solution.py:41
  43.9 9.5 %collective-permute-done.4.refs_0_ = f32[5,3,16,256]{3,2,1,0:T(8,128)S(1)} collective-permute-done((f32[5,3,16,256]{3,2,1,0:T(8,128)S(1)}, f32[5,3,16,256]{3,2,1,0:T(8,128)S(1)}, u32[]{:S(2)}, u32[]{:S(2)}) %collective-permute-start.4) | collective-permute-done | bytes 245792 | tf_op jit(solution)/shard_map/ppermute | solution.py:39
  53.7 7.3 %collective-permute-done.6.refs_2_ = f32[5,14,3,256]{3,2,1,0:T(4,128)S(1)} collective-permute-done((f32[5,14,3,256]{3,2,1,0:T(4,128)S(1)}, f32[5,14,3,256]{3,2,1,0:T(4,128)S(1)}, u32[]{:S(2)}, u32[]{:S(2)}) %collective-permute-start.6) | collective-permute-done | bytes 215072 | tf_op jit(solution)/shard_map/ppermute | solution.py:39
  61.2 2.0 %collective-permute-start.7 = (f32[5,14,19,128]{3,1,2,0:T(8,128)S(1)}, f32[5,14,19,128]{3,1,2,0:T(8,128)}, u32[]{:S(2)}, u32[]{:S(2)}) collective-permute-start(f32[5,14,19,128]{3,1,2,0:T(8,128)S(1)} %copy.17), channel_id=1, source_target_pairs={{0,1},{1,0},{2,3},{3,2},{4,5},{5,4},{6,7},{7,6},{8,9},{9,8},{10,11... | collective-permute-start | bytes 2042888 | tf_op jit(solution)/shard_map/ppermute | solution.py:39
  63.2 2.0 %collective-permute-done.7 = f32[5,14,19,128]{3,1,2,0:T(8,128)} collective-permute-done((f32[5,14,19,128]{3,1,2,0:T(8,128)S(1)}, f32[5,14,19,128]{3,1,2,0:T(8,128)}, u32[]{:S(2)}, u32[]{:S(2)}) %collective-permute-start.7) | collective-permute-done | bytes 680992 | tf_op jit(solution)/shard_map/ppermute | solution.py:39
  65.2 1.4 %copy.18.refs_3_ = f32[5,14,19,128]{3,2,1,0:T(8,128)S(1)} copy(f32[5,14,19,128]{3,1,2,0:T(8,128)} %collective-permute-done.7) | data formatting | bytes 1361920 | tf_op jit(solution)/shard_map/ppermute | solution.py:39
  66.6 5.1 %shard_map.58 = (f32[4,12,24,384]{3,2,1,0:T(8,128)S(1)}, f32[12,24,384]{2,1,0:T(8,128)S(1)}, f32[5,4,8,128]{3,2,1,0:T(8,128)S(1)}) custom-call(s32[9]{0:T(128)S(1)} %convert_element_type.3.flags, f32[5,8,16,256]{3,2,1,0:T(8,128)S(1)} %get-tuple-element.13.own, f32[4,8,256]{2,1,0:T(8,128)S(1)} %get-tuple-element.14.pooled_chi, f32[4,12,24,384]{3,2,1,0:T(8,128)} %copy-done, ...), custom_call_target="tpu_custom_call" | custom-call | tf_op jit(solution)/shard_map/pallas_call | solution.py:319
  71.7 3.0 %collective-permute-start.9 = (f32[5,4,8,128]{3,2,1,0:T(8,128)S(1)}, f32[5,4,8,128]{3,2,1,0:T(8,128)S(1)}, u32[]{:S(2)}, u32[]{:S(2)}) collective-permute-start(f32[5,4,8,128]{3,2,1,0:T(8,128)S(1)} %get-tuple-element.16.own), channel_id=1, source_target_pairs={{4,8},{8,4},{12,16},{16,12},{20,24},{24,20},{5,9},{9,5},{13,17},{1... | collective-permute-start | bytes 245768 | tf_op jit(solution)/shard_map/ppermute | solution.py:41
  74.8 4.4 %collective-permute-start.8 = (f32[5,4,8,128]{3,2,1,0:T(8,128)S(1)}, f32[5,4,8,128]{3,2,1,0:T(8,128)S(1)}, u32[]{:S(2)}, u32[]{:S(2)}) collective-permute-start(f32[5,4,8,128]{3,2,1,0:T(8,128)S(1)} %get-tuple-element.16.own), channel_id=1, source_target_pairs={{0,4},{4,0},{8,12},{12,8},{16,20},{20,16},{24,28},{28,24},{1,5},{5... | collective-permute-start | bytes 245768 | tf_op jit(solution)/shard_map/ppermute | solution.py:39
  79.2 2.2 %collective-permute-done.8.refs_0_ = f32[5,4,8,128]{3,2,1,0:T(8,128)S(1)} collective-permute-done((f32[5,4,8,128]{3,2,1,0:T(8,128)S(1)}, f32[5,4,8,128]{3,2,1,0:T(8,128)S(1)}, u32[]{:S(2)}, u32[]{:S(2)}) %collective-permute-start.8) | collective-permute-done | bytes 81952 | tf_op jit(solution)/shard_map/ppermute | solution.py:39
  81.4 0.7 collective-permute-start.10
  82.1 3.1 %collective-permute-done.10.refs_2_ = f32[5,12,4,128]{3,2,1,0:T(4,128)S(1)} collective-permute-done((f32[5,12,4,128]{3,2,1,0:T(4,128)S(1)}, f32[5,12,4,128]{3,2,1,0:T(4,128)S(1)}, u32[]{:S(2)}, u32[]{:S(2)}) %collective-permute-start.10) | collective-permute-done | bytes 122912 | tf_op jit(solution)/shard_map/ppermute | solution.py:39
  85.3 2.4 %collective-permute-start.11 = (f32[5,12,12,128]{3,2,1,0:T(8,128)S(1)}, f32[5,12,12,128]{3,2,1,0:T(8,128)S(1)}, u32[]{:S(2)}, u32[]{:S(2)}) collective-permute-start(f32[5,12,12,128]{3,2,1,0:T(8,128)S(1)} %pad_maximum_fusion), channel_id=1, source_target_pairs={{0,1},{1,0},{2,3},{3,2},{4,5},{5,4},{6,7},{7,6},{8,9},{9,8},{10,11... | collective-permute-start | bytes 1105928 | tf_op jit(solution)/shard_map/ppermute | solution.py:39
  87.7 1.5 %collective-permute-done.11.refs_3_ = f32[5,12,12,128]{3,2,1,0:T(8,128)S(1)} collective-permute-done((f32[5,12,12,128]{3,2,1,0:T(8,128)S(1)}, f32[5,12,12,128]{3,2,1,0:T(8,128)S(1)}, u32[]{:S(2)}, u32[]{:S(2)}) %collective-permute-start.11) | collective-permute-done | bytes 368672 | tf_op jit(solution)/shard_map/ppermute | solution.py:39
  89.2 8.0 %shard_map.59 = f32[4,8,16,256]{3,2,1,0:T(8,128)} custom-call(s32[9]{0:T(128)S(1)} %convert_element_type.3.flags, f32[5,4,8,128]{3,2,1,0:T(8,128)S(1)} %get-tuple-element.16.own, f32[4,12,24,384]{3,2,1,0:T(8,128)S(1)} %get-tuple-element.17.state, f32[12,24,384]{2,1,0:T(8,128)S(1)} %get-tuple-element.18.weight, f32[4,12,24,384]{3,2,1,0:T(8,128)S(1)} %copy-done.1, ...), custom_call_target="tpu_custom_call" | custom-call | tf_op jit(solution)/shard_map/pallas_call | solution.py:319
  (50 shorter events, 2.5 us)
Async XLA Ops:
  0.0 1.2 %copy-start.2 = (f32[4,8,16,256]{3,2,1,0:T(8,128)S(1)}, f32[4,8,16,256]{3,2,1,0:T(8,128)}, u32[]{:S(2)}) copy-start(f32[4,8,16,256]{3,2,1,0:T(8,128)} %start.3) | copy-start | bytes 1572868
  1.2 5.3 %copy-start.4 = (f32[96,1024]{1,0:T(8,128)S(1)}, f32[96,1024]{1,0:T(8,128)}, u32[]{:S(2)}) copy-start(f32[96,1024]{1,0:T(8,128)} %param.7) | copy-start | bytes 1179652
  1.2 5.3 %copy-start.6 = (s32[3072,1]{0,1:T(1,128)S(1)}, s32[3072,1]{0,1:T(1,128)}, u32[]{:S(2)}) copy-start(s32[3072,1]{0,1:T(1,128)} %param.8) | copy-start | bytes 36868
  2.0 12.8 %collective-permute-start.1 = (f32[8,2,16,256]{3,2,1,0:T(8,128)}, f32[8,2,16,256]{3,2,1,0:T(8,128)S(1)}, u32[]{:S(2)}, u32[]{:S(2)}) collective-permute-start(f32[8,2,16,256]{3,2,1,0:T(8,128)} %get-tuple-element.19), channel_id=1, source_target_pairs={{4,8},{8,4},{12,16},{16,12},{20,24},{24,20},{5,9},{9,5},{13,17},{1... | collective-permute-start | bytes 786440 | tf_op jit(solution)/shard_map/ppermute | solution.py:41
  5.0 13.8 %collective-permute-start = (f32[8,2,16,256]{3,2,1,0:T(8,128)S(1)}, f32[8,2,16,256]{3,2,1,0:T(8,128)S(1)}, u32[]{:S(2)}, u32[]{:S(2)}) collective-permute-start(f32[8,2,16,256]{3,2,1,0:T(8,128)S(1)} %get-tuple-element.20), channel_id=1, source_target_pairs={{0,4},{4,0},{8,12},{12,8},{16,20},{20,16},{24,28},{28,24},{1,5},{5... | collective-permute-start | bytes 786440 | tf_op jit(solution)/shard_map/ppermute | solution.py:39
  9.2 29.7 %all-to-all-start = ((f32[16,12,8,128]{3,2,1,0:T(8,128)}), f32[16,12,8,128]{3,2,1,0:T(8,128)S(1)}, u32[]{:S(2)}, u32[]{:S(2)}) async-start(f32[16,12,8,128]{3,2,1,0:T(8,128)} %shard_map.55), calls=%async_computation | async-start | bytes 1572864 | tf_op jit(solution)/shard_map/all_to_all | solution.py:368
  18.9 10.8 %collective-permute-start.2 = (f32[8,12,2,256]{3,2,1,0:T(2,128)S(1)}, f32[8,12,2,256]{3,2,1,0:T(2,128)S(1)}, u32[]{:S(2)}, u32[]{:S(2)}) collective-permute-start(f32[8,12,2,256]{3,2,1,0:T(2,128)S(1)} %fusion.5), channel_id=1, source_target_pairs={{0,2},{2,0},{1,3},{3,1},{4,6},{6,4},{5,7},{7,5},{8,10},{10,8},{9,1... | collective-permute-start | bytes 589832 | tf_op jit(solution)/shard_map/ppermute | solution.py:39
  29.9 3.5 %copy-start.5 = (s32[3072]{0:T(1024)S(1)}, s32[3072]{0:T(1024)}, u32[]{:S(2)}) copy-start(s32[3072]{0:T(1024)} %param.9) | copy-start | bytes 36868
  30.4 5.3 %copy-start.3 = (f32[4,8,16,256]{3,2,1,0:T(8,128)S(1)}, f32[4,8,16,256]{3,2,1,0:T(8,128)}, u32[]{:S(2)}) copy-start(f32[4,8,16,256]{3,2,1,0:T(8,128)} %rhs.5) | copy-start | bytes 1572868
  30.4 3.9 %collective-permute-start.3 = (f32[8,12,18,128]{3,0,2,1:T(8,128)S(1)}, f32[8,12,18,128]{3,0,2,1:T(8,128)}, u32[]{:S(2)}, u32[]{:S(2)}) collective-permute-start(f32[8,12,18,128]{3,0,2,1:T(8,128)S(1)} %copy.15), channel_id=1, source_target_pairs={{0,1},{1,0},{2,3},{3,2},{4,5},{5,4},{6,7},{7,6},{8,9},{9,8},{10,11... | collective-permute-start | bytes 2654216 | tf_op jit(solution)/shard_map/ppermute | solution.py:39
  37.7 1.2 %copy-start = (f32[4,12,24,384]{3,2,1,0:T(8,128)}, f32[4,12,24,384]{3,2,1,0:T(8,128)S(1)}, u32[]{:S(2)}) copy-start(f32[4,12,24,384]{3,2,1,0:T(8,128)S(1)} %get-tuple-element.15.rhs) | copy-start | bytes 5308420
  40.8 12.6 %collective-permute-start.4 = (f32[5,3,16,256]{3,2,1,0:T(8,128)S(1)}, f32[5,3,16,256]{3,2,1,0:T(8,128)S(1)}, u32[]{:S(2)}, u32[]{:S(2)}) collective-permute-start(f32[5,3,16,256]{3,2,1,0:T(8,128)S(1)} %get-tuple-element.22), channel_id=1, source_target_pairs={{0,4},{4,0},{8,12},{12,8},{16,20},{20,16},{24,28},{28,24},{1,5},{5... | collective-permute-start | bytes 737288 | tf_op jit(solution)/shard_map/ppermute | solution.py:39
  41.1 12.4 %collective-permute-start.5 = (f32[5,3,16,256]{3,2,1,0:T(8,128)S(1)}, f32[5,3,16,256]{3,2,1,0:T(8,128)S(1)}, u32[]{:S(2)}, u32[]{:S(2)}) collective-permute-start(f32[5,3,16,256]{3,2,1,0:T(8,128)S(1)} %get-tuple-element.21), channel_id=1, source_target_pairs={{4,8},{8,4},{12,16},{16,12},{20,24},{24,20},{5,9},{9,5},{13,17},{1... | collective-permute-start | bytes 737288 | tf_op jit(solution)/shard_map/ppermute | solution.py:41
  53.6 7.3 %collective-permute-start.6 = (f32[5,14,3,256]{3,2,1,0:T(4,128)S(1)}, f32[5,14,3,256]{3,2,1,0:T(4,128)S(1)}, u32[]{:S(2)}, u32[]{:S(2)}) collective-permute-start(f32[5,14,3,256]{3,2,1,0:T(4,128)S(1)} %constant_dynamic-slice_fusion), channel_id=1, source_target_pairs={{0,2},{2,0},{1,3},{3,1},{4,6},{6,4},{5,7},{7,5},{8,10},{10,8},{9,1... | collective-permute-start | bytes 645128 | tf_op jit(solution)/shard_map/ppermute | solution.py:39
  61.2 4.1 %collective-permute-start.7 = (f32[5,14,19,128]{3,1,2,0:T(8,128)S(1)}, f32[5,14,19,128]{3,1,2,0:T(8,128)}, u32[]{:S(2)}, u32[]{:S(2)}) collective-permute-start(f32[5,14,19,128]{3,1,2,0:T(8,128)S(1)} %copy.17), channel_id=1, source_target_pairs={{0,1},{1,0},{2,3},{3,2},{4,5},{5,4},{6,7},{7,6},{8,9},{9,8},{10,11... | collective-permute-start | bytes 2042888 | tf_op jit(solution)/shard_map/ppermute | solution.py:39
  66.6 22.6 %copy-start.1 = (f32[4,12,24,384]{3,2,1,0:T(8,128)S(1)}, f32[4,12,24,384]{3,2,1,0:T(8,128)}, u32[]{:S(2)}) copy-start(f32[4,12,24,384]{3,2,1,0:T(8,128)} %copy-done) | copy-start | bytes 5308420
  71.7 9.6 %collective-permute-start.9 = (f32[5,4,8,128]{3,2,1,0:T(8,128)S(1)}, f32[5,4,8,128]{3,2,1,0:T(8,128)S(1)}, u32[]{:S(2)}, u32[]{:S(2)}) collective-permute-start(f32[5,4,8,128]{3,2,1,0:T(8,128)S(1)} %get-tuple-element.16.own), channel_id=1, source_target_pairs={{4,8},{8,4},{12,16},{16,12},{20,24},{24,20},{5,9},{9,5},{13,17},{1... | collective-permute-start | bytes 245768 | tf_op jit(solution)/shard_map/ppermute | solution.py:41
  74.8 6.6 %collective-permute-start.8 = (f32[5,4,8,128]{3,2,1,0:T(8,128)S(1)}, f32[5,4,8,128]{3,2,1,0:T(8,128)S(1)}, u32[]{:S(2)}, u32[]{:S(2)}) collective-permute-start(f32[5,4,8,128]{3,2,1,0:T(8,128)S(1)} %get-tuple-element.16.own), channel_id=1, source_target_pairs={{0,4},{4,0},{8,12},{12,8},{16,20},{20,16},{24,28},{28,24},{1,5},{5... | collective-permute-start | bytes 245768 | tf_op jit(solution)/shard_map/ppermute | solution.py:39
  81.4 3.8 %collective-permute-start.10 = (f32[5,12,4,128]{3,2,1,0:T(4,128)S(1)}, f32[5,12,4,128]{3,2,1,0:T(4,128)S(1)}, u32[]{:S(2)}, u32[]{:S(2)}) collective-permute-start(f32[5,12,4,128]{3,2,1,0:T(4,128)S(1)} %constant_dynamic-slice_fusion.6), channel_id=1, source_target_pairs={{0,2},{2,0},{1,3},{3,1},{4,6},{6,4},{5,7},{7,5},{8,10},{10,8},{9,1... | collective-permute-start | bytes 368648 | tf_op jit(solution)/shard_map/ppermute | solution.py:39
  85.3 3.9 %collective-permute-start.11 = (f32[5,12,12,128]{3,2,1,0:T(8,128)S(1)}, f32[5,12,12,128]{3,2,1,0:T(8,128)S(1)}, u32[]{:S(2)}, u32[]{:S(2)}) collective-permute-start(f32[5,12,12,128]{3,2,1,0:T(8,128)S(1)} %pad_maximum_fusion), channel_id=1, source_target_pairs={{0,1},{1,0},{2,3},{3,2},{4,5},{5,4},{6,7},{7,6},{8,9},{9,8},{10,11... | collective-permute-start | bytes 1105928 | tf_op jit(solution)/shard_map/ppermute | solution.py:39

commit v2 on v1

--- a/solution.py
+++ b/solution.py
@@ -12,9 +12,11 @@
 RELAX = 0.6
 KEEP = 1.0 - RELAX
 LANES = 128
-FIRST_W = 2
+START_W = 4
 FINE_W = 3
+STATE_W = 2
 COARSE_W = 4
+PAD = 4
 HIGHEST = lax.Precision.HIGHEST
 VMEM = pl.BlockSpec(memory_space=pltpu.VMEM)
 SMEM = pl.BlockSpec(memory_space=pltpu.SMEM)
@@ -33,57 +35,83 @@
     return lax.dynamic_slice_in_dim(values, start, width, axis=dim)
 
 
-def swap(axis, values, dim, width):
+def flat(parts):
+    return jnp.concatenate([p.reshape(-1, *p.shape[-2:]) for p in parts], axis=0)
+
+
+def swap(axis, message):
     count = lax.axis_size(axis)
     even = lax.axis_index(axis) % 2 == 0
-    got = [lax.ppermute(cut(values, dim, width, even), axis, pairs(count, 0))]
+    got = [lax.ppermute(message(even), axis, pairs(count, 0))]
     if count > 2:
-        got.append(lax.ppermute(cut(values, dim, width, ~even), axis, pairs(count, 1)))
+        got.append(lax.ppermute(message(~even), axis, pairs(count, 1)))
     return got
 
 
-def halo(values, width):
-    xs = swap("gx", values, 1, width)
-    values = jnp.concatenate([values, *xs], axis=1)
-    ys = swap("gy", values, 2, width)
-    values = jnp.concatenate([values, *ys], axis=2)
-    zs = swap("lvl", values, 3, LANES)
-    return xs, ys, zs
-
-
-def place_halo(dst, margin, own, xs, ys, zs, flags, width):
+def halo(groups, depth):
+    xs = swap("gx", lambda up: flat([cut(v, 1, w, up) for v, w in groups]))
+    whole, at = [], 0
+    for v, w in groups:
+        got = [x[at:at + v.shape[0] * w].reshape(v.shape[0], w, *v.shape[2:]) for x in xs]
+        whole.append((v, *got))
+        at += v.shape[0] * w
+
+    def slabs(dim, width, up):
+        return flat([jnp.concatenate([cut(p, dim, width, up) for p in parts], axis=1) for parts in whole])
+
+    ys = swap("gy", lambda up: slabs(2, depth, up))
+    rows = groups[0][0].shape[2]
+
+    def last(up):
+        sent = [slabs(3, LANES, up)]
+        for y in ys:
+            edge = cut(y, 2, LANES, up)
+            short = -edge.shape[0] % (rows // PAD)
+            edge = jnp.pad(edge, ((0, short), (0, PAD - depth), (0, 0)))
+            sent.append(edge.reshape(-1, rows, LANES))
+        return jnp.concatenate(sent, axis=0)
+
+    return xs, ys, swap("lvl", last)
+
+
+def place_halo(dst, margin, own, got, flags, width, depth, before=(0, 0), slab_count=None):
+    xs, ys, zs = got
     fields, planes, rows, lanes = own.shape
     total = dst.shape[2]
+    count = planes + len(xs) * width
+    slab_count = slab_count or fields * count
+    per = rows // PAD
     even_x, even_y, even_z = flags[0] == 1, flags[1] == 1, flags[2] == 1
     near = (lax.broadcasted_iota(jnp.int32, (1, LANES), 1) < LANES // 2) == even_z
-    gap = total - rows - 2 * width
-
-    def field(f, _):
-        for k in range(planes + len(xs) * width):
+    gap = total - rows - 2 * depth
+
+    def edge(at, row, size):
+        part = slice(row, row + size)
+        return jnp.where(near, zs[0][at, part], 0.0 if len(zs) == 1 else zs[1][at, part])
+
+    for f in range(fields):
+        for k in range(count):
             if k < planes:
-                at, source, j = margin + k, own, k
+                at, plane = margin + k, own[f, k]
             else:
                 which, j = divmod(k - planes, width)
                 up, down = margin + planes + j, margin - width + j
                 at = jnp.where(even_x, up, down) if which == 0 else jnp.where(even_x, down, up)
-                source = xs[which]
-            dst[f, at, 0:rows, 0:lanes] = source[f, j]
-            zv = jnp.where(near, zs[0][f, k], 0.0 if len(zs) == 1 else zs[1][f, k])
-            dst[f, at, 0:rows, lanes:] = zv[0:rows]
-            for src, z_at, to in ((0, 0, slice(0, lanes)), (1, 0, slice(lanes, lanes + LANES))):
-                if src == 0:
-                    first = ys[0][f, k]
-                    second = ys[1][f, k] if len(ys) > 1 else jnp.zeros_like(first)
-                else:
-                    first = zv[rows:rows + width]
-                    second = zv[rows + width:rows + 2 * width] if len(ys) > 1 else jnp.zeros_like(first)
-                dst[f, at, rows:rows + width, to] = jnp.where(even_y, first, second)
-                dst[f, at, total - width:total, to] = jnp.where(even_y, second, first)
+                plane = xs[which][before[0] + f * width + j]
+            slab = before[1] + f * count + k
+            dst[f, at, 0:rows, 0:lanes] = plane
+            dst[f, at, 0:rows, lanes:] = edge(slab, 0, rows)
+            sides = []
+            for n, y in enumerate(ys):
+                at_z = slab_count + n * (-(-slab_count // per)) + slab // per
+                sides.append((y[slab], edge(at_z, slab % per * PAD, depth)))
+            if len(sides) == 1:
+                sides.append([jnp.zeros_like(v) for v in sides[0]])
+            for to, first, second in zip((slice(0, lanes), slice(lanes, lanes + LANES)), *sides):
+                dst[f, at, rows:rows + depth, to] = jnp.where(even_y, first, second)
+                dst[f, at, total - depth:total, to] = jnp.where(even_y, second, first)
             if gap:
-                dst[f, at, rows + width:total - width, :] = jnp.zeros((gap, dst.shape[3]), jnp.float32)
-        return 0
-
-    lax.fori_loop(0, fields, field, 0)
+                dst[f, at, rows + depth:total - depth, :] = jnp.zeros((gap, dst.shape[3]), jnp.float32)
 
 
 def inside(flags, rows, lanes, total, depth):
@@ -135,27 +163,32 @@
     lax.fori_loop(0, count, row, 0)
 
 
-def first_kernel(flags, rhs, start, *refs, nxs, nys, nzs):
-    halos, (rhs_out, part_out, both) = refs[:nxs + nys + nzs], refs[nxs + nys + nzs:]
-    xs, ys, zs = halos[:nxs], halos[nxs:nxs + nys], halos[nxs + nys:]
-    half = lambda refs_, lo: [r.at[lo:lo + 4] for r in refs_]
-    planes, rows, lanes = rhs.shape[1:]
-    place_halo(rhs_out, FIRST_W, rhs, half(xs, 0), half(ys, 0), half(zs, 0), flags, FIRST_W)
-    place_halo(both, FIRST_W, start, half(xs, 4), half(ys, 4), half(zs, 4), flags, FIRST_W)
+def split(refs, nums):
+    at, got = 0, []
+    for n in nums:
+        got.append(refs[at:at + n])
+        at += n
+    return got, refs[at:]
+
+
+def first_kernel(flags, rhs, start, *refs, nums):
+    got, (rhs_out, start_out, part_out) = split(refs, nums)
+    planes = rhs.shape[1]
+    many = [4 * (planes + len(got[0]) * w) for w in (START_W, FINE_W)]
+    place_halo(start_out, START_W, start, got, flags, START_W, START_W, slab_count=sum(many))
+    place_halo(rhs_out, FINE_W, rhs, got, flags, FINE_W, START_W, (4 * START_W, many[0]), sum(many))
 
     def plane(k, _):
-        p = k + FIRST_W
-        sums, grads = neighbours(both, p)
-        for f in range(4):
-            part = rhs_out[f, p] + sums[f] - 0.5 * grads[f]
-            part_out[f, k] = part[0:rows, 0:lanes]
-        return 0
-
-    lax.fori_loop(0, planes, plane, 0)
-
-
-def chi_kernel(slot_ref, rows_ref, start, part, out, coarse_out, acc, pooled):
-    planes, rows, lanes = start.shape[1:]
+        sums, grads = neighbours(start_out, k + START_W - FINE_W)
+        for f in range(4):
+            part_out[f, k] = rhs_out[f, k] + sums[f] - 0.5 * grads[f]
+        return 0
+
+    lax.fori_loop(0, planes + 2 * FINE_W, plane, 0)
+
+
+def chi_kernel(slot_ref, rows_ref, out, coarse_out, acc, pooled):
+    _, planes, rows, lanes = out.shape
     acc[...] = jnp.zeros(acc.shape, jnp.float32)
     per = rows_ref.shape[1]
 
@@ -176,44 +209,50 @@
                     v = acc[pl.ds(qx * across * 8 + (2 * i + j) * z_tiles + zt, across, stride=8), :]
                     pooled[zt, pl.ds(j, across, stride=2), :] = v
                     total = v if total is None else total + v
-                out[4, 2 * qx + i, :, zt * LANES:(zt + 1) * LANES] = pooled[zt]
+                out[0, 2 * qx + i, :, zt * LANES:(zt + 1) * LANES] = pooled[zt]
             coarse_out[qx, :, zt * LANES:(zt + 1) * LANES] = total
-    for f in range(4):
-        for p in range(planes):
-            weight = RELAX / (SHIFT + 6.0 + out[4, p]) if f < 3 else RELAX / (SHIFT + 6.0)
-            out[f, p] = KEEP * start[f, p] + weight * part[f, p]
-
-
-def second_kernel(flags, own, pooled_chi, rhs, *refs, nxs, nys, nzs):
-    halos, (state_out, weight_out, coarse_out, ext, tmp, pooled) = refs[:nxs + nys + nzs], refs[nxs + nys + nzs:]
-    xs, ys, zs = halos[:nxs], halos[nxs:nxs + nys], halos[nxs + nys:]
-    planes, rows, lanes = own.shape[1:]
+
+
+def second_kernel(flags, own, pooled_chi, rhs, start, part, *refs, nums):
+    got, (state_out, weight_out, coarse_out, chi, ext, tmp, pooled) = split(refs, nums)
+    _, planes, rows, lanes = own.shape
     total = ext.shape[2]
-    place_halo(ext, FINE_W, own, xs, ys, zs, flags, FINE_W)
-    mask = inside(flags, rows, lanes, total, 2)
+    place_halo(chi, FINE_W, own, got, flags, FINE_W, FINE_W)
+    mask = inside(flags, rows, lanes, total, FINE_W)
     w_p = (RELAX / (SHIFT + 6.0)) * mask
 
+    def begin(k, _):
+        here = plane_inside(flags, k, FINE_W, planes)
+        w_u = (RELAX / (SHIFT + 6.0 + chi[0, k])) * (mask * here)
+        weight_out[k] = w_u
+        for f in range(4):
+            w = w_u if f < 3 else w_p * here
+            ext[f, k] = KEEP * start[f, k + START_W - FINE_W] + w * part[f, k]
+        return 0
+
+    lax.fori_loop(0, planes + 2 * FINE_W, begin, 0)
+
     def sweep(k, _):
-        p = k + FINE_W - 2
-        here = plane_inside(flags, k, 2, planes)
+        p = k + FINE_W - STATE_W
+        here = plane_inside(flags, k, STATE_W, planes)
         sums, grads = neighbours(ext, p)
-        w_u = (RELAX / (SHIFT + 6.0 + ext[4, p])) * (mask * here)
-        weight_out[k] = w_u
+        w_u = weight_out[p]
         for f in range(4):
             w = w_u if f < 3 else w_p * here
-            state_out[f, k] = KEEP * ext[f, p] + w * (rhs[f, k] + sums[f] - 0.5 * grads[f])
-        return 0
-
-    lax.fori_loop(0, planes + 4, sweep, 0)
+            state_out[f, k] = KEEP * ext[f, p] + w * (rhs[f, p] + sums[f] - 0.5 * grads[f])
+        return 0
+
+    lax.fori_loop(0, planes + 2 * STATE_W, sweep, 0)
 
     def pool(cx, _):
         both = [None] * 4
         for i in range(2):
-            k = 2 + 2 * cx + i
+            k = STATE_W + 2 * cx + i
+            p = FINE_W + 2 * cx + i
             sums, grads = neighbours(state_out, k)
             for f in range(4):
-                diag = SHIFT + 6.0 + (ext[4, k + FINE_W - 2] if f < 3 else 0.0)
-                r = rhs[f, k] + sums[f] - 0.5 * grads[f] - diag * state_out[f, k]
+                diag = SHIFT + 6.0 + (chi[0, p] if f < 3 else 0.0)
+                r = rhs[f, p] + sums[f] - 0.5 * grads[f] - diag * state_out[f, k]
                 both[f] = r if i == 0 else both[f] + r
         for f in range(4):
             for zt in range(lanes // LANES):
@@ -227,18 +266,16 @@
     lane = lax.broadcasted_iota(jnp.int32, (lanes, lanes // 2), 0)
     cell = lax.broadcasted_iota(jnp.int32, (lanes, lanes // 2), 1)
     gather = jnp.where(lane // 2 == cell, 0.125, 0.0)
-    flat = pooled[...].reshape(5 * planes // 2 * rows // 2, lanes)
-    coarse = jnp.dot(flat, gather, precision=HIGHEST, preferred_element_type=jnp.float32)
+    flat_rows = pooled[...].reshape(5 * planes // 2 * rows // 2, lanes)
+    coarse = jnp.dot(flat_rows, gather, precision=HIGHEST, preferred_element_type=jnp.float32)
     coarse_out[...] = coarse.reshape(coarse_out.shape)
 
 
-def last_kernel(flags, own, state, weight, rhs, *refs, nxs, nys, nzs):
-    halos = refs[:nxs + nys + nzs]
-    out, ext, one, two, fine, mid, tmp = refs[nxs + nys + nzs:]
-    xs, ys, zs = halos[:nxs], halos[nxs:nxs + nys], halos[nxs + nys:]
+def last_kernel(flags, own, state, weight, rhs, *refs, nums):
+    got, (out, ext, one, two, fine, mid, tmp) = split(refs, nums)
     planes, rows, lanes = own.shape[1:]
     total, wide = ext.shape[2], ext.shape[3]
-    place_halo(ext, COARSE_W, own, xs, ys, zs, flags, COARSE_W)
+    place_halo(ext, COARSE_W, own, got, flags, COARSE_W, COARSE_W)
     mask = inside(flags, rows, lanes, total, COARSE_W)
     w_p = (RELAX / (SHIFT + 1.5)) * mask
 
@@ -288,16 +325,17 @@
                     to = slice(zt * LANES, (zt + 1) * LANES)
                     fine[f, 2 * cp + i, :, to] = state[f, 2 * cp + i, :, to] + tmp[zt]
     f_planes = 2 * planes
-    f_mask = inside(flags, f_rows, f_lanes, f_total, 2)
+    f_mask = inside(flags, f_rows, f_lanes, f_total, STATE_W)
+    off = FINE_W - STATE_W
     w_q = (RELAX / (SHIFT + 6.0)) * f_mask
 
     def post(k, _):
         p = k + 1
-        here = plane_inside(flags, p, 2, f_planes)
+        here = plane_inside(flags, p, STATE_W, f_planes)
         sums, grads = neighbours(fine, p)
         for f in range(4):
-            w = weight[p] if f < 3 else w_q * here
-            mid[f, p] = KEEP * fine[f, p] + w * (rhs[f, p] + sums[f] - 0.5 * grads[f])
+            w = weight[p + off] if f < 3 else w_q * here
+            mid[f, p] = KEEP * fine[f, p] + w * (rhs[f, p + off] + sums[f] - 0.5 * grads[f])
         return 0
 
     lax.fori_loop(0, f_planes + 2, post, 0)
@@ -306,8 +344,8 @@
         p = k + 2
         sums, grads = neighbours(mid, p)
         for f in range(4):
-            w = weight[p] if f < 3 else w_q
-            v = KEEP * mid[f, p] + w * (rhs[f, p] + sums[f] - 0.5 * grads[f])
+            w = weight[p + off] if f < 3 else w_q
+            v = KEEP * mid[f, p] + w * (rhs[f, p + off] + sums[f] - 0.5 * grads[f])
             out[f, k] = v[0:f_rows, 0:f_lanes]
         return 0
 
@@ -365,41 +403,42 @@
         [pltpu.SMEM((tiles,), jnp.int32)],
         my_tiles, mask_blocks.reshape(per_device, width // LANES, LANES),
     )
+    outgoing, right_side, start_field = lax.optimization_barrier((outgoing, right_side, start_field))
     arrived = lax.all_to_all(outgoing, ("gx", "gy"), split_axis=0, concat_axis=0, tiled=True)
     slot_of = routes(tile_ids, block_slot, tiles, counts[2], per_device, capacity, slots)
 
-    fields = jnp.concatenate([right_side, start_field], axis=0)
-    xs, ys, zs = halo(fields, FIRST_W)
-    num = dict(nxs=len(xs), nys=len(ys), nzs=len(zs))
     total, wide = rows + 8, lanes + LANES
-    near = planes + 4
-    rhs, part = call(
-        functools.partial(first_kernel, **num),
-        [(4, near, total, wide), (4, planes, rows, lanes)],
-        [pltpu.VMEM((4, near, total, wide), jnp.float32)],
-        flags, right_side, start_field, *xs, *ys, *zs,
-    )
-    state, pooled_chi = call(
+    near, far = planes + 2 * STATE_W, planes + 2 * FINE_W
+    got = halo([(start_field, START_W), (right_side, FINE_W)], START_W)
+    nums = [len(g) for g in got]
+    rhs, start, part = call(
+        functools.partial(first_kernel, nums=nums),
+        [(4, far, total, wide), (4, planes + 2 * START_W, total, wide), (4, far, total, wide)],
+        [],
+        flags, right_side, start_field, *sum(got, []),
+    )
+    chi, pooled_chi = call(
         chi_kernel,
-        [(5, planes, rows, lanes), (c_planes, c_rows, lanes)],
+        [(1, planes, rows, lanes), (c_planes, c_rows, lanes)],
         [pltpu.VMEM(((slots + 1) * 8, LANES), jnp.float32), pltpu.VMEM((lanes // LANES, rows, LANES), jnp.float32)],
-        slot_of, arrived, start_field, part,
-    )
-    xs, ys, zs = halo(state, FINE_W)
+        slot_of, arrived,
+    )
+    got = halo([(chi, FINE_W)], FINE_W)
     state, weight, coarse = call(
-        functools.partial(second_kernel, **num),
-        [(4, near, total, wide), (near, total, wide), (5, c_planes, c_rows, c_lanes)],
+        functools.partial(second_kernel, nums=nums),
+        [(4, near, total, wide), (far, total, wide), (5, c_planes, c_rows, c_lanes)],
         [
-            pltpu.VMEM((5, planes + 2 * FINE_W, total, wide), jnp.float32),
+            pltpu.VMEM((1, far, total, wide), jnp.float32),
+            pltpu.VMEM((4, far, total, wide), jnp.float32),
             pltpu.VMEM((4, lanes // LANES, rows, LANES), jnp.float32),
             pltpu.VMEM((5, c_planes, c_rows, lanes), jnp.float32),
         ],
-        flags, state, pooled_chi, rhs, *xs, *ys, *zs,
-    )
-    xs, ys, zs = halo(coarse, COARSE_W)
+        flags, chi, pooled_chi, rhs, start, part, *sum(got, []),
+    )
+    got = halo([(coarse, COARSE_W)], COARSE_W)
     c_ext = (c_planes + 2 * COARSE_W, c_rows + 8, c_lanes + LANES)
     (out,) = call(
-        functools.partial(last_kernel, **num),
+        functools.partial(last_kernel, nums=nums),
         [right_side.shape],
         [
             pltpu.VMEM((5, *c_ext), jnp.float32),
@@ -409,7 +448,7 @@
             pltpu.VMEM((4, near, total, wide), jnp.float32),
             pltpu.VMEM((wide // LANES, total, LANES), jnp.float32),
         ],
-        flags, coarse, state, weight, rhs, *xs, *ys, *zs,
+        flags, coarse, state, weight, rhs, *sum(got, []),
     )
     return out
 

time: 98.3 us -> 107 us (1.089)
  Pallas kernels: 19.5 us -> 23.9 us
  other arithmetic: 1.63 us -> 5.38 us
  waiting for transfers between devices: 39.2 us -> 42.4 us
  starting transfers between devices: 28.5 us -> 27 us
  local copies, waits for them, and re-layouts: 8.02 us -> 6.79 us
    pallas_call x5, Pallas kernels: 19.5 us -> 23.9 us  [call(): pl.pallas_call(kernel, out_shape=outs, in_specs=[SMEM] * smem + [VMEM] *...]
    concatenate x4 -> x12, other arithmetic: 0.32 us -> 4.07 us  [the longest x3 1.72 us: flat(): jnp.concatenate([p.reshape(-1, *p.shape[-2:]) for p in parts], axis=0)]
    ppermute x12, waiting for transfers between devices: 39.2 us -> 42.4 us  [the longest x3 26.2 us: swap(): got.append(lax.ppermute(message(~even), axis, pairs(count, 1)))]
    ppermute x12, starting transfers between devices: 23 us -> 20.2 us  [the longest x9 14.1 us: swap(): got = [lax.ppermute(message(even), axis, pairs(count, 0))]]
    ppermute x2 -> x0, local copies, waits for them, and re-layouts: 2.73 us -> none  [swap(): got = [lax.ppermute(cut(values, dim, width, even), axis, pairs(count, 0))]]
    dynamic_slice x6 -> x19, local copies, waits for them, and re-layouts: 1.56 us -> 3.18 us  [cut(): return lax.dynamic_slice_in_dim(values, start, width, axis=dim)]
    all_to_all x1, starting transfers between devices: 5.54 us -> 6.77 us  [body(): lax.all_to_all(outgoing, ('gx', 'gy'), split_axis=0, concat_axis=0, tiled...]
    unnamed x22 -> x21, local copies, waits for them, and re-layouts: 3.14 us -> 2.33 us
  transfers between devices with their start and end apart: 13 -> 13, of which waited for: 8 -> 8; matrix products, arithmetic and copies ran while one was open for 5% -> 9% of each run, Pallas kernels for 5% -> 7%
where the time goes in v2:
time: 107 us; the launch traced here: 106 us
  waiting for transfers between devices  42.4 us (40%)
  starting transfers between devices  27 us (25%)
  Pallas kernels  23.9 us (22%)
  local copies, waits for them, and re-layouts  6.79 us (6%)
  other arithmetic  5.38 us (5%)
    ppermute x3, waiting for transfers between devices, swap(): got.append(lax.ppermute(message(~even), axis, pairs(count, 1)))  26.2 us
    pallas_call x5, Pallas kernels, call(): pl.pallas_call(kernel, out_shape=outs, in_specs=[SMEM] * smem + [VMEM] *...  23.9 us
    ppermute x9, waiting for transfers between devices, swap(): got = [lax.ppermute(message(even), axis, pairs(count, 0))]  16.2 us
    ppermute x9, starting transfers between devices, swap(): got = [lax.ppermute(message(even), axis, pairs(count, 0))]  14.1 us
    all_to_all x1, starting transfers between devices, body(): lax.all_to_all(outgoing, ('gx', 'gy'), split_axis=0, concat_axis=0, tiled...  6.77 us
    ppermute x3, starting transfers between devices, swap(): got.append(lax.ppermute(message(~even), axis, pairs(count, 1)))  6.15 us
    dynamic_slice x19, local copies, waits for them, and re-layouts, cut(): return lax.dynamic_slice_in_dim(values, start, width, axis=dim)  3.18 us
    unnamed x21, local copies, waits for them, and re-layouts  2.33 us
  transfers between devices with their start and end apart: 13, of which 8 were waited for; matrix products, arithmetic and copies ran while one was open for 9% of the time, Pallas kernels for 7%

profile of v2, /device:TPU:9, one launch (start us, length us, event | category | flops | bytes accessed | tf_op | source)
XLA Modules:
  0.0 105.9 jit_solution(5674086487629112510)
XLA Ops:
  0.0 1.1 %copy.8 = f32[12,8,8,128]{3,2,1,0:T(8,128)S(1)} copy(f32[12,8,8,128]{3,1,2,0:T(8,128)} %bitcast.80) | data formatting | bytes 786432
  1.8 2.6 %shard_map.55 = f32[16,12,8,128]{3,2,1,0:T(8,128)} custom-call(s32[96]{0:T(128)S(1)} %fusion.1.tile_ref, f32[96,8,128]{2,1,0:T(8,128)S(1)} %bitcast.54), custom_call_target="tpu_custom_call" | custom-call | tf_op jit(solution)/shard_map/pallas_call | solution.py:357
  4.4 6.8 %all-to-all-start = ((f32[16,12,8,128]{3,2,1,0:T(8,128)}), f32[16,12,8,128]{3,2,1,0:T(8,128)S(1)}, u32[]{:S(2)}, u32[]{:S(2)}) async-start(f32[16,12,8,128]{3,2,1,0:T(8,128)} %shard_map.55), calls=%async_computation | async-start | bytes 1572864 | tf_op jit(solution)/shard_map/all_to_all | solution.py:407
  11.4 1.2 %collective-permute-start = (f32[28,16,256]{2,1,0:T(8,128)S(1)}, f32[28,16,256]{2,1,0:T(8,128)S(1)}, u32[]{:S(2)}, u32[]{:S(2)}) collective-permute-start(f32[28,16,256]{2,1,0:T(8,128)S(1)} %pad_maximum_fusion.3), channel_id=1, source_target_pairs={{0,4},{4,0},{8,12},{12,8},{16,20},{20,16},{24,28},{28,24},{1,5},{5... | collective-permute-start | bytes 1376264 | tf_op jit(solution)/shard_map/ppermute | solution.py:45
  13.4 2.0 %collective-permute-start.1 = (f32[28,16,256]{2,1,0:T(8,128)}, f32[28,16,256]{2,1,0:T(8,128)S(1)}, u32[]{:S(2)}, u32[]{:S(2)}) collective-permute-start(f32[28,16,256]{2,1,0:T(8,128)} %pad_maximum_fusion.4), channel_id=1, source_target_pairs={{4,8},{8,4},{12,16},{16,12},{20,24},{24,20},{5,9},{9,5},{13,17},{1... | collective-permute-start | bytes 1376264 | tf_op jit(solution)/shard_map/ppermute | solution.py:47
  17.7 18.2 %collective-permute-done.1.refs_1_ = f32[28,16,256]{2,1,0:T(8,128)S(1)} collective-permute-done((f32[28,16,256]{2,1,0:T(8,128)}, f32[28,16,256]{2,1,0:T(8,128)S(1)}, u32[]{:S(2)}, u32[]{:S(2)}) %collective-permute-start.1) | collective-permute-done | bytes 458784 | tf_op jit(solution)/shard_map/ppermute | solution.py:47
  36.0 4.5 %collective-permute-done.refs_0_ = f32[28,16,256]{2,1,0:T(8,128)S(1)} collective-permute-done((f32[28,16,256]{2,1,0:T(8,128)S(1)}, f32[28,16,256]{2,1,0:T(8,128)S(1)}, u32[]{:S(2)}, u32[]{:S(2)}) %collective-permute-start) | collective-permute-done | bytes 458784 | tf_op jit(solution)/shard_map/ppermute | solution.py:45
  41.4 0.9 pad_maximum_fusion.2
  42.2 1.2 %collective-permute-start.2 = (f32[120,4,256]{2,1,0:T(4,128)}, f32[120,4,256]{2,1,0:T(4,128)S(1)}, u32[]{:S(2)}, u32[]{:S(2)}) collective-permute-start(f32[120,4,256]{2,1,0:T(4,128)} %pad_maximum_fusion.2), channel_id=1, source_target_pairs={{0,2},{2,0},{1,3},{3,1},{4,6},{6,4},{5,7},{7,5},{8,10},{10,8},{9,1... | collective-permute-start | bytes 1474568 | tf_op jit(solution)/shard_map/ppermute | solution.py:45
  43.4 0.8 constant_dynamic-slice_fusion.8
  44.4 1.0 constant_dynamic-slice_fusion.6
  45.4 1.0 constant_dynamic-slice_fusion.9
  46.4 1.0 pad_maximum_fusion.5
  47.5 5.8 %collective-permute-done.2.refs_2_ = f32[120,4,256]{2,1,0:T(4,128)S(1)} collective-permute-done((f32[120,4,256]{2,1,0:T(4,128)}, f32[120,4,256]{2,1,0:T(4,128)S(1)}, u32[]{:S(2)}, u32[]{:S(2)}) %collective-permute-start.2) | collective-permute-done | bytes 491552 | tf_op jit(solution)/shard_map/ppermute | solution.py:45
  53.3 1.1 %pad_maximum_fusion = f32[150,16,128]{2,1,0:T(8,128)} fusion(f32[30,16,128]{2,1,0:T(8,128)S(1)} %bitcast.67, f32[56,16,128]{2,1,0:T(8,128)S(1)} %bitcast.63, f32[64,16,128]{2,1,0:T(8,128)S(1)} %bitcast.62), kind=kLoop, calls=%fused_computation | loop fusion | flops 614400 | bytes 2457600 | tf_op jit(solution)/shard_map/concatenate | solution.py:72
  54.5 2.8 %collective-permute-start.3 = (f32[150,16,128]{2,1,0:T(8,128)}, f32[150,16,128]{2,1,0:T(8,128)}, u32[]{:S(2)}, u32[]{:S(2)}) collective-permute-start(f32[150,16,128]{2,1,0:T(8,128)} %pad_maximum_fusion), channel_id=1, source_target_pairs={{0,1},{1,0},{2,3},{3,2},{4,5},{5,4},{6,7},{7,6},{8,9},{9,8},{10,11... | collective-permute-start | bytes 3686408 | tf_op jit(solution)/shard_map/ppermute | solution.py:45
  57.3 1.6 %shard_map.56 = (f32[1,8,16,256]{3,2,1,0:T(8,128)S(1)}, f32[4,8,256]{2,1,0:T(8,128)S(1)}) custom-call(s32[192]{0:T(256)S(1)} %add.81.slot_ref, f32[16,12,8,128]{3,2,1,0:T(8,128)S(1)} %all-to-all-done.rows_ref), custom_call_target="tpu_custom_call" | custom-call | tf_op jit(solution)/shard_map/pallas_call | solution.py:357
  59.4 2.2 %collective-permute-start.5 = (f32[3,16,256]{2,1,0:T(8,128)S(1)}, f32[3,16,256]{2,1,0:T(8,128)S(1)}, u32[]{:S(2)}, u32[]{:S(2)}) collective-permute-start(f32[3,16,256]{2,1,0:T(8,128)S(1)} %get-tuple-element.31), channel_id=1, source_target_pairs={{4,8},{8,4},{12,16},{16,12},{20,24},{24,20},{5,9},{9,5},{13,17},{1... | collective-permute-start | bytes 147464 | tf_op jit(solution)/shard_map/ppermute | solution.py:47
  61.7 3.4 %collective-permute-done.5.refs_1_ = f32[3,16,256]{2,1,0:T(8,128)S(1)} collective-permute-done((f32[3,16,256]{2,1,0:T(8,128)S(1)}, f32[3,16,256]{2,1,0:T(8,128)S(1)}, u32[]{:S(2)}, u32[]{:S(2)}) %collective-permute-start.5) | collective-permute-done | bytes 49184 | tf_op jit(solution)/shard_map/ppermute | solution.py:47
  65.2 1.0 collective-permute-start.6
  66.1 2.1 %collective-permute-done.6.refs_2_ = f32[14,3,256]{2,1,0:T(4,128)S(1)} collective-permute-done((f32[14,3,256]{2,1,0:T(4,128)S(1)}, f32[14,3,256]{2,1,0:T(4,128)S(1)}, u32[]{:S(2)}, u32[]{:S(2)}) %collective-permute-start.6) | collective-permute-done | bytes 43040 | tf_op jit(solution)/shard_map/ppermute | solution.py:45
  68.3 2.7 %collective-permute-start.7 = (f32[18,16,128]{2,1,0:T(8,128)S(1)}, f32[18,16,128]{2,1,0:T(8,128)S(1)}, u32[]{:S(2)}, u32[]{:S(2)}) collective-permute-start(f32[18,16,128]{2,1,0:T(8,128)S(1)} %pad_maximum_fusion.10), channel_id=1, source_target_pairs={{0,1},{1,0},{2,3},{3,2},{4,5},{5,4},{6,7},{7,6},{8,9},{9,8},{10,11... | collective-permute-start | bytes 442376 | tf_op jit(solution)/shard_map/ppermute | solution.py:45
  71.1 5.8 %shard_map.57 = (f32[4,14,24,384]{3,2,1,0:T(8,128)S(1)}, f32[4,16,24,384]{3,2,1,0:T(8,128)}, f32[4,14,24,384]{3,2,1,0:T(8,128)}) custom-call(s32[9]{0:T(128)S(1)} %convert_element_type.5.flags, f32[4,8,16,256]{3,2,1,0:T(8,128)S(1)} %copy-done.1, f32[4,8,16,256]{3,2,1,0:T(8,128)S(1)} %copy-done, f32[28,16,256]{2,1,0:T(8,128)S(1)} %collective-permute-done.refs_0_, ...), custom_call_target="tpu_custom_call" | custom-call | tf_op jit(solution)/shard_map/pallas_call | solution.py:357
  76.9 5.9 %shard_map.58 = (f32[4,12,24,384]{3,2,1,0:T(8,128)S(1)}, f32[14,24,384]{2,1,0:T(8,128)S(1)}, f32[5,4,8,128]{3,2,1,0:T(8,128)S(1)}) custom-call(s32[9]{0:T(128)S(1)} %convert_element_type.5.flags, f32[1,8,16,256]{3,2,1,0:T(8,128)S(1)} %get-tuple-element.17.own, f32[4,8,256]{2,1,0:T(8,128)S(1)} %get-tuple-element.18.pooled_chi, ...), custom_call_target="tpu_custom_call" | custom-call | tf_op jit(solution)/shard_map/pallas_call | solution.py:357
  82.8 1.0 collective-permute-start.8
  83.8 1.9 %collective-permute-start.9 = (f32[20,8,128]{2,1,0:T(8,128)S(1)}, f32[20,8,128]{2,1,0:T(8,128)S(1)}, u32[]{:S(2)}, u32[]{:S(2)}) collective-permute-start(f32[20,8,128]{2,1,0:T(8,128)S(1)} %bitcast.56), channel_id=1, source_target_pairs={{4,8},{8,4},{12,16},{16,12},{20,24},{24,20},{5,9},{9,5},{13,17},{1... | collective-permute-start | bytes 245768 | tf_op jit(solution)/shard_map/ppermute | solution.py:47
  85.8 4.6 %collective-permute-done.9.refs_1_ = f32[20,8,128]{2,1,0:T(8,128)S(1)} collective-permute-done((f32[20,8,128]{2,1,0:T(8,128)S(1)}, f32[20,8,128]{2,1,0:T(8,128)S(1)}, u32[]{:S(2)}, u32[]{:S(2)}) %collective-permute-start.9) | collective-permute-done | bytes 81952 | tf_op jit(solution)/shard_map/ppermute | solution.py:47
  90.4 1.3 %collective-permute-start.10 = (f32[60,4,128]{2,1,0:T(4,128)S(1)}, f32[60,4,128]{2,1,0:T(4,128)S(1)}, u32[]{:S(2)}, u32[]{:S(2)}) collective-permute-start(f32[60,4,128]{2,1,0:T(4,128)S(1)} %bitcast.82), channel_id=1, source_target_pairs={{0,2},{2,0},{1,3},{3,1},{4,6},{6,4},{5,7},{7,5},{8,10},{10,8},{9,1... | collective-permute-start | bytes 368648 | tf_op jit(solution)/shard_map/ppermute | solution.py:45
  91.7 2.5 %collective-permute-done.10.refs_2_ = f32[60,4,128]{2,1,0:T(4,128)S(1)} collective-permute-done((f32[60,4,128]{2,1,0:T(4,128)S(1)}, f32[60,4,128]{2,1,0:T(4,128)S(1)}, u32[]{:S(2)}, u32[]{:S(2)}) %collective-permute-start.10) | collective-permute-done | bytes 122912 | tf_op jit(solution)/shard_map/ppermute | solution.py:45
  94.2 2.4 %collective-permute-start.11 = (f32[90,8,128]{2,1,0:T(8,128)S(1)}, f32[90,8,128]{2,1,0:T(8,128)S(1)}, u32[]{:S(2)}, u32[]{:S(2)}) collective-permute-start(f32[90,8,128]{2,1,0:T(8,128)S(1)} %pad_maximum_fusion.6), channel_id=1, source_target_pairs={{0,1},{1,0},{2,3},{3,2},{4,5},{5,4},{6,7},{7,6},{8,9},{9,8},{10,11... | collective-permute-start | bytes 1105928 | tf_op jit(solution)/shard_map/ppermute | solution.py:45
  96.6 1.3 %collective-permute-done.11.refs_3_ = f32[90,8,128]{2,1,0:T(8,128)S(1)} collective-permute-done((f32[90,8,128]{2,1,0:T(8,128)S(1)}, f32[90,8,128]{2,1,0:T(8,128)S(1)}, u32[]{:S(2)}, u32[]{:S(2)}) %collective-permute-start.11) | collective-permute-done | bytes 368672 | tf_op jit(solution)/shard_map/ppermute | solution.py:45
  97.9 8.0 %shard_map.59 = f32[4,8,16,256]{3,2,1,0:T(8,128)} custom-call(s32[9]{0:T(128)S(1)} %convert_element_type.5.flags, f32[5,4,8,128]{3,2,1,0:T(8,128)S(1)} %get-tuple-element.24.own, f32[4,12,24,384]{3,2,1,0:T(8,128)S(1)} %get-tuple-element.25.state, f32[14,24,384]{2,1,0:T(8,128)S(1)} %get-tuple-element.26.weight, f32[4,14,24,384]{3,2,1,0:T(8,128)S(1)} %get-tuple-element.21.rhs, ...), custom_call_target="tpu_custom_call" | custom-call | tf_op jit(solution)/shard_map/pallas_call | solution.py:357
  (73 shorter events, 5.8 us)
Async XLA Ops:
  1.8 9.4 %copy-start.1 = (f32[4,8,16,256]{3,2,1,0:T(8,128)S(1)}, f32[4,8,16,256]{3,2,1,0:T(8,128)}, u32[]{:S(2)}) copy-start(f32[4,8,16,256]{3,2,1,0:T(8,128)} %rhs.4) | copy-start | bytes 1572868
  4.4 6.8 %copy-start = (f32[4,8,16,256]{3,2,1,0:T(8,128)S(1)}, f32[4,8,16,256]{3,2,1,0:T(8,128)}, u32[]{:S(2)}) copy-start(f32[4,8,16,256]{3,2,1,0:T(8,128)} %start) | copy-start | bytes 1572868
  4.4 52.8 %all-to-all-start = ((f32[16,12,8,128]{3,2,1,0:T(8,128)}), f32[16,12,8,128]{3,2,1,0:T(8,128)S(1)}, u32[]{:S(2)}, u32[]{:S(2)}) async-start(f32[16,12,8,128]{3,2,1,0:T(8,128)} %shard_map.55), calls=%async_computation | async-start | bytes 1572864 | tf_op jit(solution)/shard_map/all_to_all | solution.py:407
  11.3 4.2 %copy-start.7 = (s32[3072]{0:T(1024)S(1)}, s32[3072]{0:T(1024)}, u32[]{:S(2)}) copy-start(s32[3072]{0:T(1024)} %param.9) | copy-start | bytes 36868
  11.3 4.9 %copy-start.8 = (s32[3072,1]{0,1:T(1,128)S(1)}, s32[3072,1]{0,1:T(1,128)}, u32[]{:S(2)}) copy-start(s32[3072,1]{0,1:T(1,128)} %param.8) | copy-start | bytes 36868
  11.4 29.0 %collective-permute-start = (f32[28,16,256]{2,1,0:T(8,128)S(1)}, f32[28,16,256]{2,1,0:T(8,128)S(1)}, u32[]{:S(2)}, u32[]{:S(2)}) collective-permute-start(f32[28,16,256]{2,1,0:T(8,128)S(1)} %pad_maximum_fusion.3), channel_id=1, source_target_pairs={{0,4},{4,0},{8,12},{12,8},{16,20},{20,16},{24,28},{28,24},{1,5},{5... | collective-permute-start | bytes 1376264 | tf_op jit(solution)/shard_map/ppermute | solution.py:45
  13.4 22.5 %collective-permute-start.1 = (f32[28,16,256]{2,1,0:T(8,128)}, f32[28,16,256]{2,1,0:T(8,128)S(1)}, u32[]{:S(2)}, u32[]{:S(2)}) collective-permute-start(f32[28,16,256]{2,1,0:T(8,128)} %pad_maximum_fusion.4), channel_id=1, source_target_pairs={{4,8},{8,4},{12,16},{16,12},{20,24},{24,20},{5,9},{9,5},{13,17},{1... | collective-permute-start | bytes 1376264 | tf_op jit(solution)/shard_map/ppermute | solution.py:47
  35.9 4.7 %copy-start.5 = (f32[12,16,256]{2,1,0:T(8,128)}, f32[12,16,256]{2,1,0:T(8,128)S(1)}, u32[]{:S(2)}) copy-start(f32[12,16,256]{2,1,0:T(8,128)S(1)} %slice.19) | copy-start | bytes 589828
  35.9 4.6 %copy-start.3 = (f32[16,16,256]{2,1,0:T(8,128)}, f32[16,16,256]{2,1,0:T(8,128)S(1)}, u32[]{:S(2)}) copy-start(f32[16,16,256]{2,1,0:T(8,128)S(1)} %slice.17) | copy-start | bytes 786436
  40.4 0.7 copy-start.6
  40.5 0.8 copy-start.4
  42.2 11.0 %collective-permute-start.2 = (f32[120,4,256]{2,1,0:T(4,128)}, f32[120,4,256]{2,1,0:T(4,128)S(1)}, u32[]{:S(2)}, u32[]{:S(2)}) collective-permute-start(f32[120,4,256]{2,1,0:T(4,128)} %pad_maximum_fusion.2), channel_id=1, source_target_pairs={{0,2},{2,0},{1,3},{3,1},{4,6},{6,4},{5,7},{7,5},{8,10},{10,8},{9,1... | collective-permute-start | bytes 1474568 | tf_op jit(solution)/shard_map/ppermute | solution.py:45
  44.4 3.0 %copy-start.2 = (f32[4,8,16,128]{3,2,1,0:T(8,128)S(1)}, f32[4,8,16,128]{3,2,1,0:T(8,128)}, u32[]{:S(2)}) copy-start(f32[4,8,16,128]{3,2,1,0:T(8,128)} %get-tuple-element.34) | copy-start | bytes 786436
  54.5 16.6 %collective-permute-start.3 = (f32[150,16,128]{2,1,0:T(8,128)}, f32[150,16,128]{2,1,0:T(8,128)}, u32[]{:S(2)}, u32[]{:S(2)}) collective-permute-start(f32[150,16,128]{2,1,0:T(8,128)} %pad_maximum_fusion), channel_id=1, source_target_pairs={{0,1},{1,0},{2,3},{3,2},{4,5},{5,4},{6,7},{7,6},{8,9},{9,8},{10,11... | collective-permute-start | bytes 3686408 | tf_op jit(solution)/shard_map/ppermute | solution.py:45
  58.9 6.2 %collective-permute-start.4 = (f32[3,16,256]{2,1,0:T(8,128)S(1)}, f32[3,16,256]{2,1,0:T(8,128)S(1)}, u32[]{:S(2)}, u32[]{:S(2)}) collective-permute-start(f32[3,16,256]{2,1,0:T(8,128)S(1)} %get-tuple-element.32), channel_id=1, source_target_pairs={{0,4},{4,0},{8,12},{12,8},{16,20},{20,16},{24,28},{28,24},{1,5},{5... | collective-permute-start | bytes 147464 | tf_op jit(solution)/shard_map/ppermute | solution.py:45
  59.4 5.7 %collective-permute-start.5 = (f32[3,16,256]{2,1,0:T(8,128)S(1)}, f32[3,16,256]{2,1,0:T(8,128)S(1)}, u32[]{:S(2)}, u32[]{:S(2)}) collective-permute-start(f32[3,16,256]{2,1,0:T(8,128)S(1)} %get-tuple-element.31), channel_id=1, source_target_pairs={{4,8},{8,4},{12,16},{16,12},{20,24},{24,20},{5,9},{9,5},{13,17},{1... | collective-permute-start | bytes 147464 | tf_op jit(solution)/shard_map/ppermute | solution.py:47
  65.2 3.1 %collective-permute-start.6 = (f32[14,3,256]{2,1,0:T(4,128)S(1)}, f32[14,3,256]{2,1,0:T(4,128)S(1)}, u32[]{:S(2)}, u32[]{:S(2)}) collective-permute-start(f32[14,3,256]{2,1,0:T(4,128)S(1)} %maximum_bitcast_fusion.1), channel_id=1, source_target_pairs={{0,2},{2,0},{1,3},{3,1},{4,6},{6,4},{5,7},{7,5},{8,10},{10,8},{9,1... | collective-permute-start | bytes 129032 | tf_op jit(solution)/shard_map/ppermute | solution.py:45
  68.3 8.6 %collective-permute-start.7 = (f32[18,16,128]{2,1,0:T(8,128)S(1)}, f32[18,16,128]{2,1,0:T(8,128)S(1)}, u32[]{:S(2)}, u32[]{:S(2)}) collective-permute-start(f32[18,16,128]{2,1,0:T(8,128)S(1)} %pad_maximum_fusion.10), channel_id=1, source_target_pairs={{0,1},{1,0},{2,3},{3,2},{4,5},{5,4},{6,7},{7,6},{8,9},{9,8},{10,11... | collective-permute-start | bytes 442376 | tf_op jit(solution)/shard_map/ppermute | solution.py:45
  82.8 7.6 %collective-permute-start.8 = (f32[20,8,128]{2,1,0:T(8,128)S(1)}, f32[20,8,128]{2,1,0:T(8,128)S(1)}, u32[]{:S(2)}, u32[]{:S(2)}) collective-permute-start(f32[20,8,128]{2,1,0:T(8,128)S(1)} %bitcast.55), channel_id=1, source_target_pairs={{0,4},{4,0},{8,12},{12,8},{16,20},{20,16},{24,28},{28,24},{1,5},{5... | collective-permute-start | bytes 245768 | tf_op jit(solution)/shard_map/ppermute | solution.py:45
  83.8 6.5 %collective-permute-start.9 = (f32[20,8,128]{2,1,0:T(8,128)S(1)}, f32[20,8,128]{2,1,0:T(8,128)S(1)}, u32[]{:S(2)}, u32[]{:S(2)}) collective-permute-start(f32[20,8,128]{2,1,0:T(8,128)S(1)} %bitcast.56), channel_id=1, source_target_pairs={{4,8},{8,4},{12,16},{16,12},{20,24},{24,20},{5,9},{9,5},{13,17},{1... | collective-permute-start | bytes 245768 | tf_op jit(solution)/shard_map/ppermute | solution.py:47
  90.4 3.8 %collective-permute-start.10 = (f32[60,4,128]{2,1,0:T(4,128)S(1)}, f32[60,4,128]{2,1,0:T(4,128)S(1)}, u32[]{:S(2)}, u32[]{:S(2)}) collective-permute-start(f32[60,4,128]{2,1,0:T(4,128)S(1)} %bitcast.82), channel_id=1, source_target_pairs={{0,2},{2,0},{1,3},{3,1},{4,6},{6,4},{5,7},{7,5},{8,10},{10,8},{9,1... | collective-permute-start | bytes 368648 | tf_op jit(solution)/shard_map/ppermute | solution.py:45
  94.2 3.7 %collective-permute-start.11 = (f32[90,8,128]{2,1,0:T(8,128)S(1)}, f32[90,8,128]{2,1,0:T(8,128)S(1)}, u32[]{:S(2)}, u32[]{:S(2)}) collective-permute-start(f32[90,8,128]{2,1,0:T(8,128)S(1)} %pad_maximum_fusion.6), channel_id=1, source_target_pairs={{0,1},{1,0},{2,3},{3,2},{4,5},{5,4},{6,7},{7,6},{8,9},{9,8},{10,11... | collective-permute-start | bytes 1105928 | tf_op jit(solution)/shard_map/ppermute | solution.py:45

commit v3 on v2

--- a/solution.py
+++ b/solution.py
@@ -12,8 +12,9 @@
 RELAX = 0.6
 KEEP = 1.0 - RELAX
 LANES = 128
-START_W = 4
-FINE_W = 3
+START_W = 3
+FINE_W = 2
+CORNER = 2
 STATE_W = 2
 COARSE_W = 4
 PAD = 4
@@ -48,70 +49,116 @@
     return got
 
 
-def halo(groups, depth):
+def halo(groups, depth, corner=0):
     xs = swap("gx", lambda up: flat([cut(v, 1, w, up) for v, w in groups]))
-    whole, at = [], 0
-    for v, w in groups:
-        got = [x[at:at + v.shape[0] * w].reshape(v.shape[0], w, *v.shape[2:]) for x in xs]
-        whole.append((v, *got))
-        at += v.shape[0] * w
-
-    def slabs(dim, width, up):
-        return flat([jnp.concatenate([cut(p, dim, width, up) for p in parts], axis=1) for parts in whole])
-
-    ys = swap("gy", lambda up: slabs(2, depth, up))
+    own_y = lambda up: flat([cut(v, 2, depth, up) for v, _ in groups])
+    far_y = lambda up: jnp.concatenate([cut(x, 1, corner or depth, up) for x in xs], axis=0)
+    if corner:
+        ys = swap("gy", own_y) + swap("gy", far_y)
+        pad = lambda v: jnp.pad(v, ((0, 0), (0, PAD - v.shape[1]), (0, 0)))
+        half = len(ys) // 2
+        joined = [jnp.concatenate([pad(o), pad(c)], axis=0) for o, c in zip(ys[:half], ys[half:])]
+    else:
+        ys = swap("gy", lambda up: jnp.concatenate([own_y(up), far_y(up)], axis=0))
+        joined = ys
     rows = groups[0][0].shape[2]
 
     def last(up):
-        sent = [slabs(3, LANES, up)]
-        for y in ys:
+        sent = [flat([cut(v, 3, LANES, up) for v, _ in groups]), *[cut(x, 2, LANES, up) for x in xs]]
+        for y in joined:
             edge = cut(y, 2, LANES, up)
             short = -edge.shape[0] % (rows // PAD)
-            edge = jnp.pad(edge, ((0, short), (0, PAD - depth), (0, 0)))
+            edge = jnp.pad(edge, ((0, short), (0, PAD - edge.shape[1]), (0, 0)))
             sent.append(edge.reshape(-1, rows, LANES))
         return jnp.concatenate(sent, axis=0)
 
     return xs, ys, swap("lvl", last)
 
 
-def place_halo(dst, margin, own, got, flags, width, depth, before=(0, 0), slab_count=None):
+def place_halo(dst, margin, own, got, flags, width, depth, group=(0, 0), corner=0):
     xs, ys, zs = got
     fields, planes, rows, lanes = own.shape
     total = dst.shape[2]
-    count = planes + len(xs) * width
-    slab_count = slab_count or fields * count
+    x_slabs = xs[0].shape[0]
+    pairs_y = len(ys) // 2 if corner else len(ys)
+    if corner:
+        own_slabs = ys[0].shape[0]
+    else:
+        own_slabs = ys[0].shape[0] - len(xs) * x_slabs
+    slab_count = own_slabs + len(xs) * x_slabs
     per = rows // PAD
     even_x, even_y, even_z = flags[0] == 1, flags[1] == 1, flags[2] == 1
     near = (lax.broadcasted_iota(jnp.int32, (1, LANES), 1) < LANES // 2) == even_z
-    gap = total - rows - 2 * depth
 
     def edge(at, row, size):
         part = slice(row, row + size)
         return jnp.where(near, zs[0][at, part], 0.0 if len(zs) == 1 else zs[1][at, part])
 
     for f in range(fields):
-        for k in range(count):
+        for k in range(planes + len(xs) * width):
+            deep = depth
             if k < planes:
-                at, plane = margin + k, own[f, k]
+                at, plane, slab = margin + k, own[f, k], group[0] + f * planes + k
             else:
                 which, j = divmod(k - planes, width)
                 up, down = margin + planes + j, margin - width + j
                 at = jnp.where(even_x, up, down) if which == 0 else jnp.where(even_x, down, up)
-                plane = xs[which][before[0] + f * width + j]
-            slab = before[1] + f * count + k
+                plane = xs[which][group[1] + f * width + j]
+                slab = own_slabs + which * x_slabs + group[1] + f * width + j
+                deep = corner or depth
             dst[f, at, 0:rows, 0:lanes] = plane
             dst[f, at, 0:rows, lanes:] = edge(slab, 0, rows)
             sides = []
-            for n, y in enumerate(ys):
+            for n in range(pairs_y):
                 at_z = slab_count + n * (-(-slab_count // per)) + slab // per
-                sides.append((y[slab], edge(at_z, slab % per * PAD, depth)))
+                if corner and k >= planes:
+                    y = ys[pairs_y + n][slab - own_slabs]
+                else:
+                    y = ys[n][slab]
+                sides.append((y, edge(at_z, slab % per * PAD, deep)))
             if len(sides) == 1:
                 sides.append([jnp.zeros_like(v) for v in sides[0]])
             for to, first, second in zip((slice(0, lanes), slice(lanes, lanes + LANES)), *sides):
-                dst[f, at, rows:rows + depth, to] = jnp.where(even_y, first, second)
-                dst[f, at, total - depth:total, to] = jnp.where(even_y, second, first)
+                dst[f, at, rows:rows + deep, to] = jnp.where(even_y, first, second)
+                dst[f, at, total - deep:total, to] = jnp.where(even_y, second, first)
+            gap = total - rows - 2 * deep
             if gap:
-                dst[f, at, rows + depth:total - depth, :] = jnp.zeros((gap, dst.shape[3]), jnp.float32)
+                dst[f, at, rows + deep:total - deep, :] = jnp.zeros((gap, dst.shape[3]), jnp.float32)
+
+
+def state_halo(state):
+    first, rows, lanes = STATE_W, state.shape[2] - 8, state.shape[3] - LANES
+    planes = state.shape[1] - 2 * STATE_W
+    own = state[:, first:first + planes, :rows, :lanes]
+    xs = swap("gx", lambda up: lax.dynamic_index_in_dim(own, jnp.where(up, planes - 2, 1), 1, keepdims=False))
+    near = state[:, first - 1:first + planes + 1]
+    ys = swap("gy", lambda up: cut(near[:, :, :rows, :lanes], 2, STATE_W, up).reshape(-1, STATE_W, lanes))
+    zs = swap("lvl", lambda up: cut(near[..., :lanes], 3, LANES, up).reshape(-1, rows + 8, LANES))
+    return xs, ys, zs
+
+
+def outer_kernel(flags, state, *refs, nums):
+    got, (out,) = split(refs, nums)
+    xs, ys, zs = got
+    fields, near, total, wide = state.shape
+    planes, rows, lanes = near - 2 * STATE_W, total - 8, wide - LANES
+    even_x, even_y, even_z = flags[0] == 1, flags[1] == 1, flags[2] == 1
+    side = (lax.broadcasted_iota(jnp.int32, (1, LANES), 1) < LANES // 2) == even_z
+    for f in range(fields):
+        for k in range(planes + 2):
+            p, slab = STATE_W - 1 + k, f * (planes + 2) + k
+            out[f, p, :, 0:lanes] = state[f, p, :, 0:lanes]
+            out[f, p, :, lanes:] = jnp.where(side, zs[0][slab], 0.0 if len(zs) == 1 else zs[1][slab])
+            first = ys[0][slab]
+            second = ys[1][slab] if len(ys) > 1 else jnp.zeros_like(first)
+            out[f, p, rows:rows + STATE_W, 0:lanes] = jnp.where(even_y, first, second)
+            out[f, p, total - STATE_W:total, 0:lanes] = jnp.where(even_y, second, first)
+        first = xs[0][f]
+        second = xs[1][f] if len(xs) > 1 else jnp.zeros_like(first)
+        for p in (0, near - 1):
+            out[f, p] = jnp.zeros((total, wide), jnp.float32)
+            is_first = even_x if p else ~even_x
+            out[f, p, 0:rows, 0:lanes] = jnp.where(is_first, first, second)
 
 
 def inside(flags, rows, lanes, total, depth):
@@ -174,9 +221,8 @@
 def first_kernel(flags, rhs, start, *refs, nums):
     got, (rhs_out, start_out, part_out) = split(refs, nums)
     planes = rhs.shape[1]
-    many = [4 * (planes + len(got[0]) * w) for w in (START_W, FINE_W)]
-    place_halo(start_out, START_W, start, got, flags, START_W, START_W, slab_count=sum(many))
-    place_halo(rhs_out, FINE_W, rhs, got, flags, FINE_W, START_W, (4 * START_W, many[0]), sum(many))
+    place_halo(start_out, START_W, start, got, flags, START_W, START_W, corner=CORNER)
+    place_halo(rhs_out, FINE_W, rhs, got, flags, FINE_W, START_W, (4 * planes, 4 * START_W), CORNER)
 
     def plane(k, _):
         sums, grads = neighbours(start_out, k + START_W - FINE_W)
@@ -233,26 +279,25 @@
     lax.fori_loop(0, planes + 2 * FINE_W, begin, 0)
 
     def sweep(k, _):
-        p = k + FINE_W - STATE_W
-        here = plane_inside(flags, k, STATE_W, planes)
+        p = k + 1
+        here = plane_inside(flags, p, FINE_W, planes)
         sums, grads = neighbours(ext, p)
         w_u = weight_out[p]
         for f in range(4):
             w = w_u if f < 3 else w_p * here
-            state_out[f, k] = KEEP * ext[f, p] + w * (rhs[f, p] + sums[f] - 0.5 * grads[f])
-        return 0
-
-    lax.fori_loop(0, planes + 2 * STATE_W, sweep, 0)
+            state_out[f, p] = KEEP * ext[f, p] + w * (rhs[f, p] + sums[f] - 0.5 * grads[f])
+        return 0
+
+    lax.fori_loop(0, planes + 2 * (FINE_W - 1), sweep, 0)
 
     def pool(cx, _):
         both = [None] * 4
         for i in range(2):
-            k = STATE_W + 2 * cx + i
             p = FINE_W + 2 * cx + i
-            sums, grads = neighbours(state_out, k)
+            sums, grads = neighbours(state_out, p)
             for f in range(4):
                 diag = SHIFT + 6.0 + (chi[0, p] if f < 3 else 0.0)
-                r = rhs[f, p] + sums[f] - 0.5 * grads[f] - diag * state_out[f, k]
+                r = rhs[f, p] + sums[f] - 0.5 * grads[f] - diag * state_out[f, p]
                 both[f] = r if i == 0 else both[f] + r
         for f in range(4):
             for zt in range(lanes // LANES):
@@ -409,7 +454,7 @@
 
     total, wide = rows + 8, lanes + LANES
     near, far = planes + 2 * STATE_W, planes + 2 * FINE_W
-    got = halo([(start_field, START_W), (right_side, FINE_W)], START_W)
+    got = halo([(start_field, START_W), (right_side, FINE_W)], START_W, CORNER)
     nums = [len(g) for g in got]
     rhs, start, part = call(
         functools.partial(first_kernel, nums=nums),
@@ -424,6 +469,7 @@
         slot_of, arrived,
     )
     got = halo([(chi, FINE_W)], FINE_W)
+    nums = [len(g) for g in got]
     state, weight, coarse = call(
         functools.partial(second_kernel, nums=nums),
         [(4, near, total, wide), (far, total, wide), (5, c_planes, c_rows, c_lanes)],
@@ -436,6 +482,13 @@
         flags, chi, pooled_chi, rhs, start, part, *sum(got, []),
     )
     got = halo([(coarse, COARSE_W)], COARSE_W)
+    outer = state_halo(state)
+    (state,) = call(
+        functools.partial(outer_kernel, nums=[len(g) for g in outer]),
+        [state.shape],
+        [],
+        flags, state, *sum(outer, []),
+    )
     c_ext = (c_planes + 2 * COARSE_W, c_rows + 8, c_lanes + LANES)
     (out,) = call(
         functools.partial(last_kernel, nums=nums),

time: 107 us -> 111 us (1.037); the launches traced: 106 us -> 109 us
  waiting for transfers between devices: 42.4 us -> 26.6 us
  local copies, waits for them, and re-layouts: 6.79 us -> 17.6 us
  starting transfers between devices: 27 us -> 37.3 us
  other arithmetic: 5.38 us -> 3.71 us
    unnamed x21 -> x79, local copies, waits for them, and re-layouts: 2.33 us -> 14.3 us
    ppermute x9 -> x13, waiting for transfers between devices: 16.2 us -> 6.75 us  [swap(): got = [lax.ppermute(message(even), axis, pairs(count, 0))]]
    ppermute x9 -> x13, starting transfers between devices: 14.1 us -> 22.1 us  [swap(): got = [lax.ppermute(message(even), axis, pairs(count, 0))]]
    ppermute x3 -> x4, waiting for transfers between devices: 26.2 us -> 19.8 us  [swap(): got.append(lax.ppermute(message(~even), axis, pairs(count, 1)))]
    ppermute x3 -> x4, starting transfers between devices: 6.15 us -> 8.43 us  [swap(): got.append(lax.ppermute(message(~even), axis, pairs(count, 1)))]
    dynamic_slice x19 -> x16, local copies, waits for them, and re-layouts: 3.18 us -> 1.13 us  [cut(): return lax.dynamic_slice_in_dim(values, start, width, axis=dim)]
    pallas_call x5 -> x6, Pallas kernels: 23.9 us -> 22.9 us  [call(): pl.pallas_call(kernel, out_shape=outs, in_specs=[SMEM] * smem + [VMEM] *...]
  transfers between devices with their start and end apart: 13 -> 18, of which waited for: 8 -> 9; matrix products, arithmetic and copies ran while one was open for 9% -> 9% of each run, Pallas kernels for 7% -> 6%
where the time goes in v3:
time: 111 us; the launch traced here: 109 us
  starting transfers between devices  37.3 us (34%)
  waiting for transfers between devices  26.6 us (24%)
  Pallas kernels  22.9 us (21%)
  local copies, waits for them, and re-layouts  17.6 us (16%)
  other arithmetic  3.71 us (3%)
    pallas_call x6, Pallas kernels, call(): pl.pallas_call(kernel, out_shape=outs, in_specs=[SMEM] * smem + [VMEM] *...  22.9 us
    ppermute x13, starting transfers between devices, swap(): got = [lax.ppermute(message(even), axis, pairs(count, 0))]  22.1 us
    ppermute x4, waiting for transfers between devices, swap(): got.append(lax.ppermute(message(~even), axis, pairs(count, 1)))  19.8 us
    unnamed x79, local copies, waits for them, and re-layouts  14.3 us
    ppermute x4, starting transfers between devices, swap(): got.append(lax.ppermute(message(~even), axis, pairs(count, 1)))  8.43 us
    all_to_all x1, starting transfers between devices, body(): lax.all_to_all(outgoing, ('gx', 'gy'), split_axis=0, concat_axis=0, tiled...  6.77 us
    ppermute x13, waiting for transfers between devices, swap(): got = [lax.ppermute(message(even), axis, pairs(count, 0))]  6.75 us
  transfers between devices with their start and end apart: 18, of which 9 were waited for; matrix products, arithmetic and copies ran while one was open for 9% of the time, Pallas kernels for 6%

profile of v3, /device:TPU:9, one launch (start us, length us, event | category | flops | bytes accessed | tf_op | source)
XLA Modules:
  0.0 108.7 jit_solution(13385116305095941589)
XLA Ops:
  1.8 2.6 %shard_map.55 = f32[16,12,8,128]{3,2,1,0:T(8,128)} custom-call(s32[96]{0:T(128)S(1)} %fusion.6.tile_ref, f32[96,8,128]{2,1,0:T(8,128)S(1)} %bitcast.47), custom_call_target="tpu_custom_call" | custom-call | tf_op jit(solution)/shard_map/pallas_call | solution.py:402
  4.4 6.8 %all-to-all-start = ((f32[16,12,8,128]{3,2,1,0:T(8,128)}), f32[16,12,8,128]{3,2,1,0:T(8,128)S(1)}, u32[]{:S(2)}, u32[]{:S(2)}) async-start(f32[16,12,8,128]{3,2,1,0:T(8,128)} %shard_map.55), calls=%async_computation | async-start | bytes 1572864 | tf_op jit(solution)/shard_map/all_to_all | solution.py:452
  11.3 1.2 %collective-permute-start = (f32[20,16,256]{2,1,0:T(8,128)S(1)}, f32[20,16,256]{2,1,0:T(8,128)S(1)}, u32[]{:S(2)}, u32[]{:S(2)}) collective-permute-start(f32[20,16,256]{2,1,0:T(8,128)S(1)} %pad_maximum_fusion.1), channel_id=1, source_target_pairs={{0,4},{4,0},{8,12},{12,8},{16,20},{20,16},{24,28},{28,24},{1,5},{5... | collective-permute-start | bytes 983048 | tf_op jit(solution)/shard_map/ppermute | solution.py:46
  12.6 2.0 %collective-permute-start.1 = (f32[20,16,256]{2,1,0:T(8,128)S(1)}, f32[20,16,256]{2,1,0:T(8,128)S(1)}, u32[]{:S(2)}, u32[]{:S(2)}) collective-permute-start(f32[20,16,256]{2,1,0:T(8,128)S(1)} %pad_maximum_fusion.2), channel_id=1, source_target_pairs={{4,8},{8,4},{12,16},{16,12},{20,24},{24,20},{5,9},{9,5},{13,17},{1... | collective-permute-start | bytes 983048 | tf_op jit(solution)/shard_map/ppermute | solution.py:48
  15.5 1.3 %collective-permute-start.2 = (f32[64,3,256]{2,1,0:T(4,128)}, f32[64,3,256]{2,1,0:T(4,128)S(1)}, u32[]{:S(2)}, u32[]{:S(2)}) collective-permute-start(f32[64,3,256]{2,1,0:T(4,128)} %pad_maximum_fusion.3), channel_id=1, source_target_pairs={{0,2},{2,0},{1,3},{3,1},{4,6},{6,4},{5,7},{7,5},{8,10},{10,8},{9,1... | collective-permute-start | bytes 589832 | tf_op jit(solution)/shard_map/ppermute | solution.py:46
  20.6 12.5 %collective-permute-done.1.refs_1_ = f32[20,16,256]{2,1,0:T(8,128)S(1)} collective-permute-done((f32[20,16,256]{2,1,0:T(8,128)S(1)}, f32[20,16,256]{2,1,0:T(8,128)S(1)}, u32[]{:S(2)}, u32[]{:S(2)}) %collective-permute-start.1) | collective-permute-done | bytes 327712 | tf_op jit(solution)/shard_map/ppermute | solution.py:48
  33.1 1.7 %collective-permute-done.refs_0_ = f32[20,16,256]{2,1,0:T(8,128)S(1)} collective-permute-done((f32[20,16,256]{2,1,0:T(8,128)S(1)}, f32[20,16,256]{2,1,0:T(8,128)S(1)}, u32[]{:S(2)}, u32[]{:S(2)}) %collective-permute-start) | collective-permute-done | bytes 327712 | tf_op jit(solution)/shard_map/ppermute | solution.py:46
  34.9 1.2 %collective-permute-start.3 = (f32[40,2,256]{2,1,0:T(2,128)S(1)}, f32[40,2,256]{2,1,0:T(2,128)S(1)}, u32[]{:S(2)}, u32[]{:S(2)}) collective-permute-start(f32[40,2,256]{2,1,0:T(2,128)S(1)} %pad_maximum_fusion.6), channel_id=1, source_target_pairs={{0,2},{2,0},{1,3},{3,1},{4,6},{6,4},{5,7},{7,5},{8,10},{10,8},{9,1... | collective-permute-start | bytes 245768 | tf_op jit(solution)/shard_map/ppermute | solution.py:46
  39.5 3.0 %collective-permute-start.4 = (f32[130,16,128]{2,1,0:T(8,128)}, f32[130,16,128]{2,1,0:T(8,128)S(1)}, u32[]{:S(2)}, u32[]{:S(2)}) collective-permute-start(f32[130,16,128]{2,1,0:T(8,128)} %bitcast_dynamic-update-slice_fusion), channel_id=1, source_target_pairs={{0,1},{1,0},{2,3},{3,2},{4,5},{5,4},{6,7},{7,6},{8,9},{9,8},{10,11... | collective-permute-start | bytes 3194888 | tf_op jit(solution)/shard_map/ppermute | solution.py:46
  42.6 1.3 %shard_map.56 = (f32[1,8,16,256]{3,2,1,0:T(8,128)S(1)}, f32[4,8,256]{2,1,0:T(8,128)S(1)}) custom-call(s32[192]{0:T(256)S(1)} %add.90.slot_ref, f32[16,12,8,128]{3,2,1,0:T(8,128)S(1)} %all-to-all-done.rows_ref), custom_call_target="tpu_custom_call" | custom-call | tf_op jit(solution)/shard_map/pallas_call | solution.py:402
  43.9 2.4 %collective-permute-start.6 = (f32[2,16,256]{2,1,0:T(8,128)S(1)}, f32[2,16,256]{2,1,0:T(8,128)S(1)}, u32[]{:S(2)}, u32[]{:S(2)}) collective-permute-start(f32[2,16,256]{2,1,0:T(8,128)S(1)} %get-tuple-element.33), channel_id=1, source_target_pairs={{4,8},{8,4},{12,16},{16,12},{20,24},{24,20},{5,9},{9,5},{13,17},{1... | collective-permute-start | bytes 98312 | tf_op jit(solution)/shard_map/ppermute | solution.py:48
  46.4 3.7 %collective-permute-start.5 = (f32[2,16,256]{2,1,0:T(8,128)S(1)}, f32[2,16,256]{2,1,0:T(8,128)S(1)}, u32[]{:S(2)}, u32[]{:S(2)}) collective-permute-start(f32[2,16,256]{2,1,0:T(8,128)S(1)} %get-tuple-element.34), channel_id=1, source_target_pairs={{0,4},{4,0},{8,12},{12,8},{16,20},{20,16},{24,28},{28,24},{1,5},{5... | collective-permute-start | bytes 98312 | tf_op jit(solution)/shard_map/ppermute | solution.py:46
  50.1 1.3 %collective-permute-done.5.refs_0_ = f32[2,16,256]{2,1,0:T(8,128)S(1)} collective-permute-done((f32[2,16,256]{2,1,0:T(8,128)S(1)}, f32[2,16,256]{2,1,0:T(8,128)S(1)}, u32[]{:S(2)}, u32[]{:S(2)}) %collective-permute-start.5) | collective-permute-done | bytes 32800 | tf_op jit(solution)/shard_map/ppermute | solution.py:46
  51.4 1.2 %collective-permute-start.7 = (f32[12,2,256]{2,1,0:T(2,128)S(1)}, f32[12,2,256]{2,1,0:T(2,128)S(1)}, u32[]{:S(2)}, u32[]{:S(2)}) collective-permute-start(f32[12,2,256]{2,1,0:T(2,128)S(1)} %pad_maximum_fusion.7), channel_id=1, source_target_pairs={{0,2},{2,0},{1,3},{3,1},{4,6},{6,4},{5,7},{7,5},{8,10},{10,8},{9,1... | collective-permute-start | bytes 73736 | tf_op jit(solution)/shard_map/ppermute | solution.py:46
  52.7 1.5 %collective-permute-done.7.refs_2_ = f32[12,2,256]{2,1,0:T(2,128)S(1)} collective-permute-done((f32[12,2,256]{2,1,0:T(2,128)S(1)}, f32[12,2,256]{2,1,0:T(2,128)S(1)}, u32[]{:S(2)}, u32[]{:S(2)}) %collective-permute-start.7) | collective-permute-done | bytes 24608 | tf_op jit(solution)/shard_map/ppermute | solution.py:46
  54.8 2.3 %collective-permute-start.8 = (f32[15,16,128]{2,1,0:T(8,128)}, f32[15,16,128]{2,1,0:T(8,128)}, u32[]{:S(2)}, u32[]{:S(2)}) collective-permute-start(f32[15,16,128]{2,1,0:T(8,128)} %pad_maximum_fusion.4), channel_id=1, source_target_pairs={{0,1},{1,0},{2,3},{3,2},{4,5},{5,4},{6,7},{7,6},{8,9},{9,8},{10,11... | collective-permute-start | bytes 368648 | tf_op jit(solution)/shard_map/ppermute | solution.py:46
  59.4 1.2 %copy-done.5 = f32[130,16,128]{2,1,0:T(8,128)S(1)} copy-done((f32[130,16,128]{2,1,0:T(8,128)S(1)}, f32[130,16,128]{2,1,0:T(8,128)}, u32[]{:S(2)}) %copy-start.5) | copy-done | bytes 1064984
  64.4 4.6 %shard_map.57 = (f32[4,12,24,384]{3,2,1,0:T(8,128)S(1)}, f32[4,14,24,384]{3,2,1,0:T(8,128)}, f32[4,12,24,384]{3,2,1,0:T(8,128)}) custom-call(s32[9]{0:T(128)S(1)} %convert_element_type.9.flags, f32[4,8,16,256]{3,2,1,0:T(8,128)S(1)} %copy-done.2, f32[4,8,16,256]{3,2,1,0:T(8,128)S(1)} %copy-done, f32[20,16,256]{2,1,0:T(8,128)S(1)} %copy-done.9, ...), custom_call_target="tpu_custom_call" | custom-call | tf_op jit(solution)/shard_map/pallas_call | solution.py:402
  69.0 1.5 %copy-done.3 = f32[4,12,24,384]{3,2,1,0:T(8,128)S(1)} copy-done((f32[4,12,24,384]{3,2,1,0:T(8,128)S(1)}, f32[4,12,24,384]{3,2,1,0:T(8,128)}, u32[]{:S(2)}) %copy-start.3) | copy-done | bytes 1769496
  70.5 4.8 %shard_map.58 = (f32[4,12,24,384]{3,2,1,0:T(8,128)S(1)}, f32[12,24,384]{2,1,0:T(8,128)S(1)}, f32[5,4,8,128]{3,2,1,0:T(8,128)S(1)}) custom-call(s32[9]{0:T(128)S(1)} %convert_element_type.9.flags, f32[1,8,16,256]{3,2,1,0:T(8,128)S(1)} %copy-done.13, f32[4,8,256]{2,1,0:T(8,128)S(1)} %copy-done.33, f32[4,12,24,384]{3,2,1,0:T(8,128)S(1)} %get-tuple-element.21.rhs, ...), custom_call_target="tpu_custom_call" | custom-call | tf_op jit(solution)/shard_map/pallas_call | solution.py:402
  76.1 1.7 %collective-permute-start.13 = (f32[20,8,128]{2,1,0:T(8,128)S(1)}, f32[20,8,128]{2,1,0:T(8,128)S(1)}, u32[]{:S(2)}, u32[]{:S(2)}) collective-permute-start(f32[20,8,128]{2,1,0:T(8,128)S(1)} %bitcast.48), channel_id=1, source_target_pairs={{0,4},{4,0},{8,12},{12,8},{16,20},{20,16},{24,28},{28,24},{1,5},{5... | collective-permute-start | bytes 245768 | tf_op jit(solution)/shard_map/ppermute | solution.py:46
  77.8 1.9 %collective-permute-start.14 = (f32[20,8,128]{2,1,0:T(8,128)S(1)}, f32[20,8,128]{2,1,0:T(8,128)S(1)}, u32[]{:S(2)}, u32[]{:S(2)}) collective-permute-start(f32[20,8,128]{2,1,0:T(8,128)S(1)} %bitcast.49), channel_id=1, source_target_pairs={{4,8},{8,4},{12,16},{16,12},{20,24},{24,20},{5,9},{9,5},{13,17},{1... | collective-permute-start | bytes 245768 | tf_op jit(solution)/shard_map/ppermute | solution.py:48
  79.9 4.5 %collective-permute-done.14.refs_1_ = f32[20,8,128]{2,1,0:T(8,128)S(1)} collective-permute-done((f32[20,8,128]{2,1,0:T(8,128)S(1)}, f32[20,8,128]{2,1,0:T(8,128)S(1)}, u32[]{:S(2)}, u32[]{:S(2)}) %collective-permute-start.14) | collective-permute-done | bytes 81952 | tf_op jit(solution)/shard_map/ppermute | solution.py:48
  84.5 1.2 %collective-permute-start.15 = (f32[60,4,128]{2,1,0:T(4,128)S(1)}, f32[60,4,128]{2,1,0:T(4,128)S(1)}, u32[]{:S(2)}, u32[]{:S(2)}) collective-permute-start(f32[60,4,128]{2,1,0:T(4,128)S(1)} %pad_maximum_fusion.5), channel_id=1, source_target_pairs={{0,2},{2,0},{1,3},{3,1},{4,6},{6,4},{5,7},{7,5},{8,10},{10,8},{9,1... | collective-permute-start | bytes 368648 | tf_op jit(solution)/shard_map/ppermute | solution.py:46
  86.5 1.4 %collective-permute-start.12 = (f32[40,24,128]{2,1,0:T(8,128)}, f32[40,24,128]{2,1,0:T(8,128)}, u32[]{:S(2)}, u32[]{:S(2)}) collective-permute-start(f32[40,24,128]{2,1,0:T(8,128)} %bitcast.28), channel_id=1, source_target_pairs={{0,1},{1,0},{2,3},{3,2},{4,5},{5,4},{6,7},{7,6},{8,9},{9,8},{10,11... | collective-permute-start | bytes 1474568 | tf_op jit(solution)/shard_map/ppermute | solution.py:46
  89.1 2.3 %collective-permute-start.16 = (f32[90,8,128]{2,1,0:T(8,128)}, f32[90,8,128]{2,1,0:T(8,128)}, u32[]{:S(2)}, u32[]{:S(2)}) collective-permute-start(f32[90,8,128]{2,1,0:T(8,128)} %pad_maximum_fusion), channel_id=1, source_target_pairs={{0,1},{1,0},{2,3},{3,2},{4,5},{5,4},{6,7},{7,6},{8,9},{9,8},{10,11... | collective-permute-start | bytes 1105928 | tf_op jit(solution)/shard_map/ppermute | solution.py:46
  91.6 1.2 %collective-permute-start.11 = (f32[40,2,256]{2,1,0:T(2,128)S(1)}, f32[40,2,256]{2,1,0:T(2,128)S(1)}, u32[]{:S(2)}, u32[]{:S(2)}) collective-permute-start(f32[40,2,256]{2,1,0:T(2,128)S(1)} %bitcast.64), channel_id=1, source_target_pairs={{0,2},{2,0},{1,3},{3,1},{4,6},{6,4},{5,7},{7,5},{8,10},{10,8},{9,1... | collective-permute-start | bytes 245768 | tf_op jit(solution)/shard_map/ppermute | solution.py:46
  92.9 2.1 %collective-permute-start.10 = (f32[4,16,256]{2,1,0:T(8,128)S(1)}, f32[4,16,256]{2,1,0:T(8,128)S(1)}, u32[]{:S(2)}, u32[]{:S(2)}) collective-permute-start(f32[4,16,256]{2,1,0:T(8,128)S(1)} %get-tuple-element.27), channel_id=1, source_target_pairs={{4,8},{8,4},{12,16},{16,12},{20,24},{24,20},{5,9},{9,5},{13,17},{1... | collective-permute-start | bytes 196616 | tf_op jit(solution)/shard_map/ppermute | solution.py:48
  95.0 1.1 collective-permute-done.9.refs_0_
  96.1 2.9 %collective-permute-done.10.refs_1_ = f32[4,16,256]{2,1,0:T(8,128)S(1)} collective-permute-done((f32[4,16,256]{2,1,0:T(8,128)S(1)}, f32[4,16,256]{2,1,0:T(8,128)S(1)}, u32[]{:S(2)}, u32[]{:S(2)}) %collective-permute-start.10) | collective-permute-done | bytes 65568 | tf_op jit(solution)/shard_map/ppermute | solution.py:48
  99.0 1.2 %shard_map.59.state = f32[4,12,24,384]{3,2,1,0:T(8,128)S(1)} custom-call(s32[9]{0:T(128)S(1)} %convert_element_type.9.flags, f32[4,12,24,384]{3,2,1,0:T(8,128)S(1)} %get-tuple-element.25.state, f32[4,16,256]{2,1,0:T(8,128)S(1)} %collective-permute-done.9.refs_0_, f32[4,16,256]{2,1,0:T(8,128)S(1)} %collective-permute-done.10.refs_1_, ...), custom_call_target="tpu_custom_call" | custom-call | tf_op jit(solution)/shard_map/pallas_call | solution.py:402
  100.2 8.5 %shard_map.60 = f32[4,8,16,256]{3,2,1,0:T(8,128)} custom-call(s32[9]{0:T(128)S(1)} %convert_element_type.9.flags, f32[5,4,8,128]{3,2,1,0:T(8,128)S(1)} %copy-done.15, f32[4,12,24,384]{3,2,1,0:T(8,128)S(1)} %shard_map.59.state, f32[12,24,384]{2,1,0:T(8,128)S(1)} %copy-done.23, f32[4,12,24,384]{3,2,1,0:T(8,128)S(1)} %get-tuple-element.21.rhs, ...), custom_call_target="tpu_custom_call" | custom-call | tf_op jit(solution)/shard_map/pallas_call | solution.py:402
  (137 shorter events, 20.0 us)
Async XLA Ops:
  4.4 6.8 %copy-start.1 = (f32[4,8,16,256]{3,2,1,0:T(8,128)S(1)}, f32[4,8,16,256]{3,2,1,0:T(8,128)}, u32[]{:S(2)}) copy-start(f32[4,8,16,256]{3,2,1,0:T(8,128)} %rhs.4) | copy-start | bytes 1572868
  4.4 6.8 %copy-start = (f32[4,8,16,256]{3,2,1,0:T(8,128)S(1)}, f32[4,8,16,256]{3,2,1,0:T(8,128)}, u32[]{:S(2)}) copy-start(f32[4,8,16,256]{3,2,1,0:T(8,128)} %start) | copy-start | bytes 1572868
  4.4 38.2 %all-to-all-start = ((f32[16,12,8,128]{3,2,1,0:T(8,128)}), f32[16,12,8,128]{3,2,1,0:T(8,128)S(1)}, u32[]{:S(2)}, u32[]{:S(2)}) async-start(f32[16,12,8,128]{3,2,1,0:T(8,128)} %shard_map.55), calls=%async_computation | async-start | bytes 1572864 | tf_op jit(solution)/shard_map/all_to_all | solution.py:452
  11.3 5.6 %copy-start.34 = (s32[3072]{0:T(1024)S(1)}, s32[3072]{0:T(1024)}, u32[]{:S(2)}) copy-start(s32[3072]{0:T(1024)} %param.9) | copy-start | bytes 36868
  11.3 6.2 %copy-start.35 = (s32[3072,1]{0,1:T(1,128)S(1)}, s32[3072,1]{0,1:T(1,128)}, u32[]{:S(2)}) copy-start(s32[3072,1]{0,1:T(1,128)} %param.8) | copy-start | bytes 36868
  11.3 23.4 %collective-permute-start = (f32[20,16,256]{2,1,0:T(8,128)S(1)}, f32[20,16,256]{2,1,0:T(8,128)S(1)}, u32[]{:S(2)}, u32[]{:S(2)}) collective-permute-start(f32[20,16,256]{2,1,0:T(8,128)S(1)} %pad_maximum_fusion.1), channel_id=1, source_target_pairs={{0,4},{4,0},{8,12},{12,8},{16,20},{20,16},{24,28},{28,24},{1,5},{5... | collective-permute-start | bytes 983048 | tf_op jit(solution)/shard_map/ppermute | solution.py:46
  12.6 20.5 %collective-permute-start.1 = (f32[20,16,256]{2,1,0:T(8,128)S(1)}, f32[20,16,256]{2,1,0:T(8,128)S(1)}, u32[]{:S(2)}, u32[]{:S(2)}) collective-permute-start(f32[20,16,256]{2,1,0:T(8,128)S(1)} %pad_maximum_fusion.2), channel_id=1, source_target_pairs={{4,8},{8,4},{12,16},{16,12},{20,24},{24,20},{5,9},{9,5},{13,17},{1... | collective-permute-start | bytes 983048 | tf_op jit(solution)/shard_map/ppermute | solution.py:48
  15.5 21.9 %collective-permute-start.2 = (f32[64,3,256]{2,1,0:T(4,128)}, f32[64,3,256]{2,1,0:T(4,128)S(1)}, u32[]{:S(2)}, u32[]{:S(2)}) collective-permute-start(f32[64,3,256]{2,1,0:T(4,128)} %pad_maximum_fusion.3), channel_id=1, source_target_pairs={{0,2},{2,0},{1,3},{3,1},{4,6},{6,4},{5,7},{7,5},{8,10},{10,8},{9,1... | collective-permute-start | bytes 589832 | tf_op jit(solution)/shard_map/ppermute | solution.py:46
  33.1 10.8 %copy-start.10 = (f32[20,16,256]{2,1,0:T(8,128)}, f32[20,16,256]{2,1,0:T(8,128)S(1)}, u32[]{:S(2)}) copy-start(f32[20,16,256]{2,1,0:T(8,128)S(1)} %collective-permute-done.1.refs_1_) | copy-start | bytes 983044
  34.9 3.4 %collective-permute-start.3 = (f32[40,2,256]{2,1,0:T(2,128)S(1)}, f32[40,2,256]{2,1,0:T(2,128)S(1)}, u32[]{:S(2)}, u32[]{:S(2)}) collective-permute-start(f32[40,2,256]{2,1,0:T(2,128)S(1)} %pad_maximum_fusion.6), channel_id=1, source_target_pairs={{0,2},{2,0},{1,3},{3,1},{4,6},{6,4},{5,7},{7,5},{8,10},{10,8},{9,1... | collective-permute-start | bytes 245768 | tf_op jit(solution)/shard_map/ppermute | solution.py:46
  39.5 17.8 %collective-permute-start.4 = (f32[130,16,128]{2,1,0:T(8,128)}, f32[130,16,128]{2,1,0:T(8,128)S(1)}, u32[]{:S(2)}, u32[]{:S(2)}) collective-permute-start(f32[130,16,128]{2,1,0:T(8,128)} %bitcast_dynamic-update-slice_fusion), channel_id=1, source_target_pairs={{0,1},{1,0},{2,3},{3,2},{4,5},{5,4},{6,7},{7,6},{8,9},{9,8},{10,11... | collective-permute-start | bytes 3194888 | tf_op jit(solution)/shard_map/ppermute | solution.py:46
  43.9 13.4 %copy-start.32 = (f32[4,8,256]{2,1,0:T(8,128)}, f32[4,8,256]{2,1,0:T(8,128)S(1)}, u32[]{:S(2)}) copy-start(f32[4,8,256]{2,1,0:T(8,128)S(1)} %get-tuple-element.18.pooled_chi) | copy-start | bytes 98308
  43.9 6.1 %collective-permute-start.6 = (f32[2,16,256]{2,1,0:T(8,128)S(1)}, f32[2,16,256]{2,1,0:T(8,128)S(1)}, u32[]{:S(2)}, u32[]{:S(2)}) collective-permute-start(f32[2,16,256]{2,1,0:T(8,128)S(1)} %get-tuple-element.33), channel_id=1, source_target_pairs={{4,8},{8,4},{12,16},{16,12},{20,24},{24,20},{5,9},{9,5},{13,17},{1... | collective-permute-start | bytes 98312 | tf_op jit(solution)/shard_map/ppermute | solution.py:48
  46.4 5.0 %collective-permute-start.5 = (f32[2,16,256]{2,1,0:T(8,128)S(1)}, f32[2,16,256]{2,1,0:T(8,128)S(1)}, u32[]{:S(2)}, u32[]{:S(2)}) collective-permute-start(f32[2,16,256]{2,1,0:T(8,128)S(1)} %get-tuple-element.34), channel_id=1, source_target_pairs={{0,4},{4,0},{8,12},{12,8},{16,20},{20,16},{24,28},{28,24},{1,5},{5... | collective-permute-start | bytes 98312 | tf_op jit(solution)/shard_map/ppermute | solution.py:46
  50.1 7.2 %copy-start.26 = (f32[2,16,256]{2,1,0:T(8,128)}, f32[2,16,256]{2,1,0:T(8,128)S(1)}, u32[]{:S(2)}) copy-start(f32[2,16,256]{2,1,0:T(8,128)S(1)} %collective-permute-done.6.refs_1_) | copy-start | bytes 98308
  51.4 5.9 %copy-start.28 = (f32[2,16,256]{2,1,0:T(8,128)}, f32[2,16,256]{2,1,0:T(8,128)S(1)}, u32[]{:S(2)}) copy-start(f32[2,16,256]{2,1,0:T(8,128)S(1)} %collective-permute-done.5.refs_0_) | copy-start | bytes 98308
  51.4 2.7 %collective-permute-start.7 = (f32[12,2,256]{2,1,0:T(2,128)S(1)}, f32[12,2,256]{2,1,0:T(2,128)S(1)}, u32[]{:S(2)}, u32[]{:S(2)}) collective-permute-start(f32[12,2,256]{2,1,0:T(2,128)S(1)} %pad_maximum_fusion.7), channel_id=1, source_target_pairs={{0,2},{2,0},{1,3},{3,1},{4,6},{6,4},{5,7},{7,5},{8,10},{10,8},{9,1... | collective-permute-start | bytes 73736 | tf_op jit(solution)/shard_map/ppermute | solution.py:46
  54.8 14.1 %collective-permute-start.8 = (f32[15,16,128]{2,1,0:T(8,128)}, f32[15,16,128]{2,1,0:T(8,128)}, u32[]{:S(2)}, u32[]{:S(2)}) collective-permute-start(f32[15,16,128]{2,1,0:T(8,128)} %pad_maximum_fusion.4), channel_id=1, source_target_pairs={{0,1},{1,0},{2,3},{3,2},{4,5},{5,4},{6,7},{7,6},{8,9},{9,8},{10,11... | collective-permute-start | bytes 368648 | tf_op jit(solution)/shard_map/ppermute | solution.py:46
  76.1 12.2 %copy-start.14 = (f32[5,4,8,128]{3,2,1,0:T(8,128)}, f32[5,4,8,128]{3,2,1,0:T(8,128)S(1)}, u32[]{:S(2)}) copy-start(f32[5,4,8,128]{3,2,1,0:T(8,128)S(1)} %get-tuple-element.24.own) | copy-start | bytes 245764
  76.1 8.3 %collective-permute-start.13 = (f32[20,8,128]{2,1,0:T(8,128)S(1)}, f32[20,8,128]{2,1,0:T(8,128)S(1)}, u32[]{:S(2)}, u32[]{:S(2)}) collective-permute-start(f32[20,8,128]{2,1,0:T(8,128)S(1)} %bitcast.48), channel_id=1, source_target_pairs={{0,4},{4,0},{8,12},{12,8},{16,20},{20,16},{24,28},{28,24},{1,5},{5... | collective-permute-start | bytes 245768 | tf_op jit(solution)/shard_map/ppermute | solution.py:46
  77.8 6.5 %collective-permute-start.14 = (f32[20,8,128]{2,1,0:T(8,128)S(1)}, f32[20,8,128]{2,1,0:T(8,128)S(1)}, u32[]{:S(2)}, u32[]{:S(2)}) collective-permute-start(f32[20,8,128]{2,1,0:T(8,128)S(1)} %bitcast.49), channel_id=1, source_target_pairs={{4,8},{8,4},{12,16},{16,12},{20,24},{24,20},{5,9},{9,5},{13,17},{1... | collective-permute-start | bytes 245768 | tf_op jit(solution)/shard_map/ppermute | solution.py:48
  84.5 3.8 %collective-permute-start.15 = (f32[60,4,128]{2,1,0:T(4,128)S(1)}, f32[60,4,128]{2,1,0:T(4,128)S(1)}, u32[]{:S(2)}, u32[]{:S(2)}) collective-permute-start(f32[60,4,128]{2,1,0:T(4,128)S(1)} %pad_maximum_fusion.5), channel_id=1, source_target_pairs={{0,2},{2,0},{1,3},{3,1},{4,6},{6,4},{5,7},{7,5},{8,10},{10,8},{9,1... | collective-permute-start | bytes 368648 | tf_op jit(solution)/shard_map/ppermute | solution.py:46
  86.5 12.5 %collective-permute-start.12 = (f32[40,24,128]{2,1,0:T(8,128)}, f32[40,24,128]{2,1,0:T(8,128)}, u32[]{:S(2)}, u32[]{:S(2)}) collective-permute-start(f32[40,24,128]{2,1,0:T(8,128)} %bitcast.28), channel_id=1, source_target_pairs={{0,1},{1,0},{2,3},{3,2},{4,5},{5,4},{6,7},{7,6},{8,9},{9,8},{10,11... | collective-permute-start | bytes 1474568 | tf_op jit(solution)/shard_map/ppermute | solution.py:46
  89.1 11.1 %collective-permute-start.16 = (f32[90,8,128]{2,1,0:T(8,128)}, f32[90,8,128]{2,1,0:T(8,128)}, u32[]{:S(2)}, u32[]{:S(2)}) collective-permute-start(f32[90,8,128]{2,1,0:T(8,128)} %pad_maximum_fusion), channel_id=1, source_target_pairs={{0,1},{1,0},{2,3},{3,2},{4,5},{5,4},{6,7},{7,6},{8,9},{9,8},{10,11... | collective-permute-start | bytes 1105928 | tf_op jit(solution)/shard_map/ppermute | solution.py:46
  91.6 7.4 %collective-permute-start.11 = (f32[40,2,256]{2,1,0:T(2,128)S(1)}, f32[40,2,256]{2,1,0:T(2,128)S(1)}, u32[]{:S(2)}, u32[]{:S(2)}) collective-permute-start(f32[40,2,256]{2,1,0:T(2,128)S(1)} %bitcast.64), channel_id=1, source_target_pairs={{0,2},{2,0},{1,3},{3,1},{4,6},{6,4},{5,7},{7,5},{8,10},{10,8},{9,1... | collective-permute-start | bytes 245768 | tf_op jit(solution)/shard_map/ppermute | solution.py:46
  92.8 3.3 %collective-permute-start.9 = (f32[4,16,256]{2,1,0:T(8,128)S(1)}, f32[4,16,256]{2,1,0:T(8,128)S(1)}, u32[]{:S(2)}, u32[]{:S(2)}) collective-permute-start(f32[4,16,256]{2,1,0:T(8,128)S(1)} %get-tuple-element.28), channel_id=1, source_target_pairs={{0,4},{4,0},{8,12},{12,8},{16,20},{20,16},{24,28},{28,24},{1,5},{5... | collective-permute-start | bytes 196616 | tf_op jit(solution)/shard_map/ppermute | solution.py:46
  92.9 7.3 %copy-start.15 = (f32[5,4,8,128]{3,2,1,0:T(8,128)S(1)}, f32[5,4,8,128]{3,2,1,0:T(8,128)}, u32[]{:S(2)}) copy-start(f32[5,4,8,128]{3,2,1,0:T(8,128)} %copy-done.14) | copy-start | bytes 245764
  92.9 7.3 %copy-start.17 = (f32[20,8,128]{2,1,0:T(8,128)S(1)}, f32[20,8,128]{2,1,0:T(8,128)}, u32[]{:S(2)}) copy-start(f32[20,8,128]{2,1,0:T(8,128)} %copy-done.16) | copy-start | bytes 245764
  92.9 7.3 %copy-start.19 = (f32[20,8,128]{2,1,0:T(8,128)S(1)}, f32[20,8,128]{2,1,0:T(8,128)}, u32[]{:S(2)}) copy-start(f32[20,8,128]{2,1,0:T(8,128)} %copy-done.18) | copy-start | bytes 245764
  92.9 7.3 %copy-start.21 = (f32[60,4,128]{2,1,0:T(4,128)S(1)}, f32[60,4,128]{2,1,0:T(4,128)}, u32[]{:S(2)}) copy-start(f32[60,4,128]{2,1,0:T(4,128)} %copy-done.20) | copy-start | bytes 368644
  92.9 7.3 %copy-start.23 = (f32[12,24,384]{2,1,0:T(8,128)S(1)}, f32[12,24,384]{2,1,0:T(8,128)}, u32[]{:S(2)}) copy-start(f32[12,24,384]{2,1,0:T(8,128)} %copy-done.22) | copy-start | bytes 1327108
  92.9 6.0 %collective-permute-start.10 = (f32[4,16,256]{2,1,0:T(8,128)S(1)}, f32[4,16,256]{2,1,0:T(8,128)S(1)}, u32[]{:S(2)}, u32[]{:S(2)}) collective-permute-start(f32[4,16,256]{2,1,0:T(8,128)S(1)} %get-tuple-element.27), channel_id=1, source_target_pairs={{4,8},{8,4},{12,16},{16,12},{20,24},{24,20},{5,9},{9,5},{13,17},{1... | collective-permute-start | bytes 196616 | tf_op jit(solution)/shard_map/ppermute | solution.py:48
  (22 other events, 52.9 us)

commit v4 on v3

--- a/solution.py
+++ b/solution.py
@@ -21,7 +21,7 @@
 HIGHEST = lax.Precision.HIGHEST
 VMEM = pl.BlockSpec(memory_space=pltpu.VMEM)
 SMEM = pl.BlockSpec(memory_space=pltpu.SMEM)
-PARAMS = pltpu.CompilerParams(vmem_limit_bytes=48 << 20)
+PARAMS = pltpu.CompilerParams(vmem_limit_bytes=24 << 20)
 
 
 def pairs(count, first):
@@ -43,48 +43,46 @@
 def swap(axis, message):
     count = lax.axis_size(axis)
     even = lax.axis_index(axis) % 2 == 0
-    got = [lax.ppermute(message(even), axis, pairs(count, 0))]
+    got = [lax.ppermute(message(even, 0), axis, pairs(count, 0))]
     if count > 2:
-        got.append(lax.ppermute(message(~even), axis, pairs(count, 1)))
+        got.append(lax.ppermute(message(~even, 1), axis, pairs(count, 1)))
     return got
 
 
-def halo(groups, depth, corner=0):
-    xs = swap("gx", lambda up: flat([cut(v, 1, w, up) for v, w in groups]))
-    own_y = lambda up: flat([cut(v, 2, depth, up) for v, _ in groups])
-    far_y = lambda up: jnp.concatenate([cut(x, 1, corner or depth, up) for x in xs], axis=0)
-    if corner:
-        ys = swap("gy", own_y) + swap("gy", far_y)
-        pad = lambda v: jnp.pad(v, ((0, 0), (0, PAD - v.shape[1]), (0, 0)))
-        half = len(ys) // 2
-        joined = [jnp.concatenate([pad(o), pad(c)], axis=0) for o, c in zip(ys[:half], ys[half:])]
-    else:
-        ys = swap("gy", lambda up: jnp.concatenate([own_y(up), far_y(up)], axis=0))
-        joined = ys
+def ride(messages, n, extra):
+    return jnp.concatenate([*messages, *([extra[n]] if extra else [])], axis=0)
+
+
+def halo_x(groups):
+    return swap("gx", lambda up, n: flat([cut(v, 1, w, up) for v, w in groups]))
+
+
+def halo_y(groups, depth, xs=(), extra=()):
+    own = lambda up: [cut(v.reshape(-1, *v.shape[2:]), 1, depth, up) for v, _ in groups]
+    return swap("gy", lambda up, n: ride([*own(up), *[cut(x, 1, depth, up) for x in xs]], n, extra))
+
+
+def halo_z(groups, xs, ys, extra=()):
     rows = groups[0][0].shape[2]
 
-    def last(up):
+    def last(up, n):
         sent = [flat([cut(v, 3, LANES, up) for v, _ in groups]), *[cut(x, 2, LANES, up) for x in xs]]
-        for y in joined:
-            edge = cut(y, 2, LANES, up)
-            short = -edge.shape[0] % (rows // PAD)
-            edge = jnp.pad(edge, ((0, short), (0, PAD - edge.shape[1]), (0, 0)))
+        for parts in ys:
+            edge = [jnp.pad(cut(y, 2, LANES, up), ((0, 0), (0, PAD - y.shape[1]), (0, 0))) for y in parts]
+            edge = jnp.concatenate(edge, axis=0)
+            edge = jnp.pad(edge, ((0, -edge.shape[0] % (rows // PAD)), (0, 0), (0, 0)))
             sent.append(edge.reshape(-1, rows, LANES))
-        return jnp.concatenate(sent, axis=0)
-
-    return xs, ys, swap("lvl", last)
-
-
-def place_halo(dst, margin, own, got, flags, width, depth, group=(0, 0), corner=0):
+        return ride(sent, n, extra)
+
+    return swap("lvl", last)
+
+
+def place_halo(dst, margin, own, got, flags, width, depth, group=(0, 0), slabs=None, corner=0):
     xs, ys, zs = got
-    fields, planes, rows, lanes = own.shape
-    total = dst.shape[2]
-    x_slabs = xs[0].shape[0]
+    rows, lanes = own.shape[-2:]
+    fields, planes, total = dst.shape[0], dst.shape[1] - 2 * margin, dst.shape[2]
+    own_slabs, x_slabs = slabs or (fields * planes, fields * width)
     pairs_y = len(ys) // 2 if corner else len(ys)
-    if corner:
-        own_slabs = ys[0].shape[0]
-    else:
-        own_slabs = ys[0].shape[0] - len(xs) * x_slabs
     slab_count = own_slabs + len(xs) * x_slabs
     per = rows // PAD
     even_x, even_y, even_z = flags[0] == 1, flags[1] == 1, flags[2] == 1
@@ -98,7 +96,7 @@
         for k in range(planes + len(xs) * width):
             deep = depth
             if k < planes:
-                at, plane, slab = margin + k, own[f, k], group[0] + f * planes + k
+                at, plane, slab = margin + k, own[f, k] if len(own.shape) == 4 else own[f * planes + k], group[0] + f * planes + k
             else:
                 which, j = divmod(k - planes, width)
                 up, down = margin + planes + j, margin - width + j
@@ -126,39 +124,60 @@
                 dst[f, at, rows + deep:total - deep, :] = jnp.zeros((gap, dst.shape[3]), jnp.float32)
 
 
-def state_halo(state):
-    first, rows, lanes = STATE_W, state.shape[2] - 8, state.shape[3] - LANES
-    planes = state.shape[1] - 2 * STATE_W
-    own = state[:, first:first + planes, :rows, :lanes]
-    xs = swap("gx", lambda up: lax.dynamic_index_in_dim(own, jnp.where(up, planes - 2, 1), 1, keepdims=False))
-    near = state[:, first - 1:first + planes + 1]
-    ys = swap("gy", lambda up: cut(near[:, :, :rows, :lanes], 2, STATE_W, up).reshape(-1, STATE_W, lanes))
-    zs = swap("lvl", lambda up: cut(near[..., :lanes], 3, LANES, up).reshape(-1, rows + 8, LANES))
-    return xs, ys, zs
-
-
-def outer_kernel(flags, state, *refs, nums):
-    got, (out,) = split(refs, nums)
+def place_outer(out, state, got, flags, before):
     xs, ys, zs = got
     fields, near, total, wide = state.shape
     planes, rows, lanes = near - 2 * STATE_W, total - 8, wide - LANES
     even_x, even_y, even_z = flags[0] == 1, flags[1] == 1, flags[2] == 1
     side = (lax.broadcasted_iota(jnp.int32, (1, LANES), 1) < LANES // 2) == even_z
+    tiles = [(r, z) for r in range(rows // 8) for z in range(lanes // LANES)]
     for f in range(fields):
         for k in range(planes + 2):
             p, slab = STATE_W - 1 + k, f * (planes + 2) + k
             out[f, p, :, 0:lanes] = state[f, p, :, 0:lanes]
-            out[f, p, :, lanes:] = jnp.where(side, zs[0][slab], 0.0 if len(zs) == 1 else zs[1][slab])
-            first = ys[0][slab]
-            second = ys[1][slab] if len(ys) > 1 else jnp.zeros_like(first)
-            out[f, p, rows:rows + STATE_W, 0:lanes] = jnp.where(even_y, first, second)
-            out[f, p, total - STATE_W:total, 0:lanes] = jnp.where(even_y, second, first)
-        first = xs[0][f]
-        second = xs[1][f] if len(xs) > 1 else jnp.zeros_like(first)
+            for r in range(total // 8):
+                at = before[2] + slab * (total // 8) + r
+                z = jnp.where(side, zs[0][at], 0.0 if len(zs) == 1 else zs[1][at])
+                out[f, p, r * 8:(r + 1) * 8, lanes:] = z
+            for z in range(lanes // LANES):
+                part = slice(z * STATE_W, (z + 1) * STATE_W)
+                first = ys[0][before[1] + slab, part]
+                second = ys[1][before[1] + slab, part] if len(ys) > 1 else jnp.zeros_like(first)
+                to = slice(z * LANES, (z + 1) * LANES)
+                out[f, p, rows:rows + STATE_W, to] = jnp.where(even_y, first, second)
+                out[f, p, total - STATE_W:total, to] = jnp.where(even_y, second, first)
         for p in (0, near - 1):
             out[f, p] = jnp.zeros((total, wide), jnp.float32)
             is_first = even_x if p else ~even_x
-            out[f, p, 0:rows, 0:lanes] = jnp.where(is_first, first, second)
+            for t, (r, z) in enumerate(tiles):
+                at = before[0] + f * len(tiles) + t
+                first = xs[0][at]
+                second = xs[1][at] if len(xs) > 1 else jnp.zeros_like(first)
+                out[f, p, r * 8:(r + 1) * 8, z * LANES:(z + 1) * LANES] = jnp.where(is_first, first, second)
+
+
+def send_outer(state, flags, x_out, y_out, z_out, before):
+    fields, near, total, wide = state.shape
+    planes, rows, lanes = near - 2 * STATE_W, total - 8, wide - LANES
+    up = [[(flags[a] == 1) == (n == 0) for n in range(2)] for a in range(3)]
+    tiles = [(r, z) for r in range(rows // 8) for z in range(lanes // LANES)]
+    for n, ref in enumerate(x_out):
+        p = jnp.where(up[0][n], STATE_W + planes - 2, STATE_W + 1)
+        for f in range(fields):
+            for t, (r, z) in enumerate(tiles):
+                ref[before + f * len(tiles) + t] = state[f, p, r * 8:(r + 1) * 8, z * LANES:(z + 1) * LANES]
+    for f in range(fields):
+        for k in range(planes + 2):
+            p, slab = STATE_W - 1 + k, f * (planes + 2) + k
+            for n, ref in enumerate(y_out):
+                v = jnp.where(up[1][n], state[f, p, rows - STATE_W:rows, 0:lanes], state[f, p, 0:STATE_W, 0:lanes])
+                for z in range(lanes // LANES):
+                    ref[slab, z * STATE_W:(z + 1) * STATE_W] = v[:, z * LANES:(z + 1) * LANES]
+            for n, ref in enumerate(z_out):
+                for r in range(total // 8):
+                    part = slice(r * 8, (r + 1) * 8)
+                    v = jnp.where(up[2][n], state[f, p, part, lanes - LANES:lanes], state[f, p, part, 0:LANES])
+                    ref[slab * (total // 8) + r] = v
 
 
 def inside(flags, rows, lanes, total, depth):
@@ -218,21 +237,6 @@
     return got, refs[at:]
 
 
-def first_kernel(flags, rhs, start, *refs, nums):
-    got, (rhs_out, start_out, part_out) = split(refs, nums)
-    planes = rhs.shape[1]
-    place_halo(start_out, START_W, start, got, flags, START_W, START_W, corner=CORNER)
-    place_halo(rhs_out, FINE_W, rhs, got, flags, FINE_W, START_W, (4 * planes, 4 * START_W), CORNER)
-
-    def plane(k, _):
-        sums, grads = neighbours(start_out, k + START_W - FINE_W)
-        for f in range(4):
-            part_out[f, k] = rhs_out[f, k] + sums[f] - 0.5 * grads[f]
-        return 0
-
-    lax.fori_loop(0, planes + 2 * FINE_W, plane, 0)
-
-
 def chi_kernel(slot_ref, rows_ref, out, coarse_out, acc, pooled):
     _, planes, rows, lanes = out.shape
     acc[...] = jnp.zeros(acc.shape, jnp.float32)
@@ -259,38 +263,37 @@
             coarse_out[qx, :, zt * LANES:(zt + 1) * LANES] = total
 
 
-def second_kernel(flags, own, pooled_chi, rhs, start, part, *refs, nums):
-    got, (state_out, weight_out, coarse_out, chi, ext, tmp, pooled) = split(refs, nums)
+def second_kernel(flags, own, pooled_chi, right_side, start_field, *refs, nums):
+    (got, refs), (fields_got, refs) = split(refs, nums[:3]), split(refs[sum(nums[:3]):], nums[3:6])
+    rhs, state_out, weight_out = refs[:3]
+    (x_out, y_out, z_out), (chi, start, ext, tmp, pooled) = split(refs[3:], nums[6:])
     _, planes, rows, lanes = own.shape
     total = ext.shape[2]
+    slabs = (8 * planes, 4 * (START_W + FINE_W))
+    place_halo(start, START_W, start_field, fields_got, flags, START_W, START_W, (0, 0), slabs, CORNER)
+    place_halo(rhs, FINE_W, right_side, fields_got, flags, FINE_W, START_W, (4 * planes, 4 * START_W), slabs, CORNER)
     place_halo(chi, FINE_W, own, got, flags, FINE_W, FINE_W)
     mask = inside(flags, rows, lanes, total, FINE_W)
     w_p = (RELAX / (SHIFT + 6.0)) * mask
 
-    def begin(k, _):
+    for k in range(planes + 2 * FINE_W):
         here = plane_inside(flags, k, FINE_W, planes)
         w_u = (RELAX / (SHIFT + 6.0 + chi[0, k])) * (mask * here)
         weight_out[k] = w_u
+        sums, grads = neighbours(start, k + START_W - FINE_W)
         for f in range(4):
             w = w_u if f < 3 else w_p * here
-            ext[f, k] = KEEP * start[f, k + START_W - FINE_W] + w * part[f, k]
-        return 0
-
-    lax.fori_loop(0, planes + 2 * FINE_W, begin, 0)
-
-    def sweep(k, _):
-        p = k + 1
+            ext[f, k] = KEEP * start[f, k + START_W - FINE_W] + w * (rhs[f, k] + sums[f] - 0.5 * grads[f])
+
+    for p in range(1, planes + 2 * FINE_W - 1):
         here = plane_inside(flags, p, FINE_W, planes)
         sums, grads = neighbours(ext, p)
         w_u = weight_out[p]
         for f in range(4):
             w = w_u if f < 3 else w_p * here
             state_out[f, p] = KEEP * ext[f, p] + w * (rhs[f, p] + sums[f] - 0.5 * grads[f])
-        return 0
-
-    lax.fori_loop(0, planes + 2 * (FINE_W - 1), sweep, 0)
-
-    def pool(cx, _):
+
+    for cx in range(planes // 2):
         both = [None] * 4
         for i in range(2):
             p = FINE_W + 2 * cx + i
@@ -304,47 +307,46 @@
                 tmp[f, zt] = both[f][0:rows, zt * LANES:(zt + 1) * LANES]
                 v = tmp[f, zt, pl.ds(0, rows // 2, stride=2), :] + tmp[f, zt, pl.ds(1, rows // 2, stride=2), :]
                 pooled[f, cx, :, zt * LANES:(zt + 1) * LANES] = v
-        return 0
-
-    lax.fori_loop(0, planes // 2, pool, 0)
     pooled[4] = pooled_chi[...]
     lane = lax.broadcasted_iota(jnp.int32, (lanes, lanes // 2), 0)
     cell = lax.broadcasted_iota(jnp.int32, (lanes, lanes // 2), 1)
     gather = jnp.where(lane // 2 == cell, 0.125, 0.0)
     flat_rows = pooled[...].reshape(5 * planes // 2 * rows // 2, lanes)
     coarse = jnp.dot(flat_rows, gather, precision=HIGHEST, preferred_element_type=jnp.float32)
-    coarse_out[...] = coarse.reshape(coarse_out.shape)
+    coarse = coarse.reshape(5 * planes // 2, rows // 2, lanes // 2)
+    for ref in x_out:
+        ref[0:coarse.shape[0]] = coarse
+    send_outer(state_out, flags, x_out, y_out, z_out, coarse.shape[0])
 
 
 def last_kernel(flags, own, state, weight, rhs, *refs, nums):
     got, (out, ext, one, two, fine, mid, tmp) = split(refs, nums)
-    planes, rows, lanes = own.shape[1:]
+    planes = ext.shape[1] - 2 * COARSE_W
+    rows, lanes = own.shape[1:]
     total, wide = ext.shape[2], ext.shape[3]
+    own = own.at[0:5 * planes]
     place_halo(ext, COARSE_W, own, got, flags, COARSE_W, COARSE_W)
+    x_slabs = 5 * COARSE_W
+    slabs = 5 * planes + len(got[0]) * x_slabs
+    z_slabs = slabs + len(got[1]) * -(-slabs // (rows // PAD))
+    place_outer(fine, state, got, flags, (x_slabs, slabs, z_slabs))
     mask = inside(flags, rows, lanes, total, COARSE_W)
     w_p = (RELAX / (SHIFT + 1.5)) * mask
 
-    def begin(p, _):
+    for p in range(planes + 2 * COARSE_W):
         here = plane_inside(flags, p, COARSE_W, planes)
         w_u = (RELAX / (SHIFT + 1.5 + ext[4, p])) * (mask * here)
         ext[4, p] = w_u
         for f in range(4):
             one[f, p] = (w_u if f < 3 else w_p * here) * ext[f, p]
-        return 0
-
-    lax.fori_loop(0, planes + 2 * COARSE_W, begin, 0)
     now, then = one, two
     for s in range(1, COARSE_SWEEPS):
-        def sweep(k, _, now=now, then=then, s=s):
-            p = k + s
+        for p in range(s, planes + 2 * COARSE_W - s):
             here = plane_inside(flags, p, COARSE_W, planes)
             sums, grads = neighbours(now, p)
             for f in range(4):
                 w = ext[4, p] if f < 3 else w_p * here
                 then[f, p] = KEEP * now[f, p] + w * (ext[f, p] + 0.25 * (sums[f] - grads[f]))
-            return 0
-
-        lax.fori_loop(0, planes + 2 * COARSE_W - 2 * s, sweep, 0)
         now, then = then, now
 
     f_total, f_wide = fine.shape[2], fine.shape[3]
@@ -368,33 +370,26 @@
                     tmp[zt, pl.ds(f_total - 4 + j, 2, stride=2), :] = v[total - 2:total]
                 for i in range(2):
                     to = slice(zt * LANES, (zt + 1) * LANES)
-                    fine[f, 2 * cp + i, :, to] = state[f, 2 * cp + i, :, to] + tmp[zt]
+                    fine[f, 2 * cp + i, :, to] = fine[f, 2 * cp + i, :, to] + tmp[zt]
     f_planes = 2 * planes
     f_mask = inside(flags, f_rows, f_lanes, f_total, STATE_W)
     off = FINE_W - STATE_W
     w_q = (RELAX / (SHIFT + 6.0)) * f_mask
 
-    def post(k, _):
-        p = k + 1
+    for p in range(1, f_planes + 3):
         here = plane_inside(flags, p, STATE_W, f_planes)
         sums, grads = neighbours(fine, p)
         for f in range(4):
             w = weight[p + off] if f < 3 else w_q * here
             mid[f, p] = KEEP * fine[f, p] + w * (rhs[f, p + off] + sums[f] - 0.5 * grads[f])
-        return 0
-
-    lax.fori_loop(0, f_planes + 2, post, 0)
-
-    def final(k, _):
+
+    for k in range(f_planes):
         p = k + 2
         sums, grads = neighbours(mid, p)
         for f in range(4):
             w = weight[p + off] if f < 3 else w_q
             v = KEEP * mid[f, p] + w * (rhs[f, p + off] + sums[f] - 0.5 * grads[f])
             out[f, k] = v[0:f_rows, 0:f_lanes]
-        return 0
-
-    lax.fori_loop(0, f_planes, final, 0)
 
 
 def call(kernel, shapes, scratch, *args, smem=1):
@@ -454,44 +449,49 @@
 
     total, wide = rows + 8, lanes + LANES
     near, far = planes + 2 * STATE_W, planes + 2 * FINE_W
-    got = halo([(start_field, START_W), (right_side, FINE_W)], START_W, CORNER)
-    nums = [len(g) for g in got]
-    rhs, start, part = call(
-        functools.partial(first_kernel, nums=nums),
-        [(4, far, total, wide), (4, planes + 2 * START_W, total, wide), (4, far, total, wide)],
-        [],
-        flags, right_side, start_field, *sum(got, []),
-    )
+    pair_counts = [1 + (n > 2) for n in counts]
+    groups = [(start_field, START_W), (right_side, FINE_W)]
+    first_x = halo_x(groups)
+    first_y = halo_y(groups, START_W)
     chi, pooled_chi = call(
         chi_kernel,
         [(1, planes, rows, lanes), (c_planes, c_rows, lanes)],
         [pltpu.VMEM(((slots + 1) * 8, LANES), jnp.float32), pltpu.VMEM((lanes // LANES, rows, LANES), jnp.float32)],
         slot_of, arrived,
     )
-    got = halo([(chi, FINE_W)], FINE_W)
-    nums = [len(g) for g in got]
-    state, weight, coarse = call(
-        functools.partial(second_kernel, nums=nums),
-        [(4, near, total, wide), (far, total, wide), (5, c_planes, c_rows, c_lanes)],
+    first_x, chi = lax.optimization_barrier((first_x, chi))
+    group = [(chi, FINE_W)]
+    chi_x = halo_x(group)
+    corners = swap("gy", lambda up, n: jnp.concatenate([cut(x, 1, CORNER, up) for x in first_x], axis=0))
+    chi_y = halo_y(group, FINE_W, chi_x)
+    chi_y, corners = lax.optimization_barrier((chi_y, corners))
+    chi_z = halo_z(group, chi_x, [[y] for y in chi_y])
+    first_z = halo_z(groups, first_x, list(zip(first_y, corners)))
+    c_slabs, s_slabs = 5 * c_planes, 4 * (rows // 8) * (lanes // LANES)
+    outers = [[(c_slabs + s_slabs, 8, LANES)], [(4 * (planes + 2), PAD, LANES)], [(4 * (planes + 2) * total // 8, 8, LANES)]]
+    outers = [shape * n for shape, n in zip(outers, pair_counts)]
+    rhs, state, weight, *sent = call(
+        functools.partial(second_kernel, nums=[*pair_counts, pair_counts[0], 2 * pair_counts[1], pair_counts[2], *pair_counts]),
+        [(4, far, total, wide), (4, near, total, wide), (far, total, wide), *sum(outers, [])],
         [
             pltpu.VMEM((1, far, total, wide), jnp.float32),
+            pltpu.VMEM((4, planes + 2 * START_W, total, wide), jnp.float32),
             pltpu.VMEM((4, far, total, wide), jnp.float32),
             pltpu.VMEM((4, lanes // LANES, rows, LANES), jnp.float32),
             pltpu.VMEM((5, c_planes, c_rows, lanes), jnp.float32),
         ],
-        flags, chi, pooled_chi, rhs, start, part, *sum(got, []),
+        flags, chi, pooled_chi, right_side, start_field, *chi_x, *chi_y, *chi_z, *first_x, *first_y, *corners, *first_z,
     )
-    got = halo([(coarse, COARSE_W)], COARSE_W)
-    outer = state_halo(state)
-    (state,) = call(
-        functools.partial(outer_kernel, nums=[len(g) for g in outer]),
-        [state.shape],
-        [],
-        flags, state, *sum(outer, []),
-    )
+    (x_out, y_out, z_out), _ = split(sent, pair_counts)
+    group = [(x_out[0][:c_slabs].reshape(5, c_planes, c_rows, c_lanes), COARSE_W)]
+    last_x = swap("gx", lambda up, n: x_out[n])
+    halo_slabs = [x[:5 * COARSE_W] for x in last_x]
+    last_y = halo_y(group, COARSE_W, halo_slabs, y_out)
+    slabs = c_slabs + len(last_x) * 5 * COARSE_W
+    last_z = halo_z(group, halo_slabs, [[y[:slabs]] for y in last_y], z_out)
     c_ext = (c_planes + 2 * COARSE_W, c_rows + 8, c_lanes + LANES)
     (out,) = call(
-        functools.partial(last_kernel, nums=nums),
+        functools.partial(last_kernel, nums=pair_counts),
         [right_side.shape],
         [
             pltpu.VMEM((5, *c_ext), jnp.float32),
@@ -501,7 +501,7 @@
             pltpu.VMEM((4, near, total, wide), jnp.float32),
             pltpu.VMEM((wide // LANES, total, LANES), jnp.float32),
         ],
-        flags, coarse, state, weight, rhs, *sum(got, []),
+        flags, x_out[0], state, weight, rhs, *last_x, *last_y, *last_z,
     )
     return out
 

time: 111 us -> 89.5 us (0.81); the launches traced: 109 us -> 88.9 us
  Pallas kernels: 22.9 us -> 13.7 us
  starting transfers between devices: 37.3 us -> 28.6 us
  local copies, waits for them, and re-layouts: 17.6 us -> 12.2 us
  waiting for transfers between devices: 26.6 us -> 30.3 us
    pallas_call x6 -> x4, Pallas kernels: 22.9 us -> 13.7 us  [call(): pl.pallas_call(kernel, out_shape=outs, in_specs=[SMEM] * smem + [VMEM] *...]
    ppermute x17 -> x13, starting transfers between devices: 30.5 us -> 21.9 us  [the longest x10 15.8 us: swap(): got = [lax.ppermute(message(even, 0), axis, pairs(count, 0))]]
    all_to_all x1, waiting for transfers between devices: 0.01 us -> 6.13 us  [body(): lax.all_to_all(outgoing, ('gx', 'gy'), split_axis=0, concat_axis=0, tiled...]
    unnamed x79 -> x47, local copies, waits for them, and re-layouts: 14.3 us -> 9.9 us
    ppermute x17 -> x13, waiting for transfers between devices: 26.6 us -> 24.1 us  [the longest x10 20.5 us: swap(): got = [lax.ppermute(message(even, 0), axis, pairs(count, 0))]]
  transfers between devices with their start and end apart: 18 -> 14, of which waited for: 9 -> 10; matrix products, arithmetic and copies ran while one was open for 9% -> 9% of each run, Pallas kernels for 6% -> 1%
where the time goes in v4:
time: 89.5 us; the launch traced here: 88.9 us
  waiting for transfers between devices  30.3 us (34%)
  starting transfers between devices  28.6 us (32%)
  Pallas kernels  13.7 us (15%)
  local copies, waits for them, and re-layouts  12.2 us (14%)
  other arithmetic  3.62 us (4%)
    ppermute x10, waiting for transfers between devices, swap(): got = [lax.ppermute(message(even, 0), axis, pairs(count, 0))]  20.5 us
    ppermute x10, starting transfers between devices, swap(): got = [lax.ppermute(message(even, 0), axis, pairs(count, 0))]  15.8 us
    pallas_call x4, Pallas kernels, call(): pl.pallas_call(kernel, out_shape=outs, in_specs=[SMEM] * smem + [VMEM] *...  13.7 us
    unnamed x47, local copies, waits for them, and re-layouts  9.9 us
    all_to_all x1, starting transfers between devices, body(): lax.all_to_all(outgoing, ('gx', 'gy'), split_axis=0, concat_axis=0, tiled...  6.77 us
    all_to_all x1, waiting for transfers between devices, body(): lax.all_to_all(outgoing, ('gx', 'gy'), split_axis=0, concat_axis=0, tiled...  6.13 us
    ppermute x3, starting transfers between devices, swap(): got.append(lax.ppermute(message(~even, 1), axis, pairs(count, 1)))  6.02 us
    ppermute x3, waiting for transfers between devices, swap(): got.append(lax.ppermute(message(~even, 1), axis, pairs(count, 1)))  3.61 us
  transfers between devices with their start and end apart: 14, of which 10 were waited for; matrix products, arithmetic and copies ran while one was open for 9% of the time, Pallas kernels for 1%

profile of v4, /device:TPU:9, one launch (start us, length us, event | category | flops | bytes accessed | tf_op | source)
XLA Modules:
  0.0 88.9 jit_solution(11724577654848621511)
XLA Ops:
  0.0 1.1 %copy.8 = f32[12,8,8,128]{3,2,1,0:T(8,128)S(1)} copy(f32[12,8,8,128]{3,1,2,0:T(8,128)} %bitcast.52) | data formatting | bytes 786432
  1.1 0.8 fusion.1.tile_ref
  1.8 2.6 %shard_map.55 = f32[16,12,8,128]{3,2,1,0:T(8,128)} custom-call(s32[96]{0:T(128)S(1)} %fusion.1.tile_ref, f32[96,8,128]{2,1,0:T(8,128)S(1)} %bitcast.43), custom_call_target="tpu_custom_call" | custom-call | tf_op jit(solution)/shard_map/pallas_call | solution.py:397
  4.4 6.8 %all-to-all-start = ((f32[16,12,8,128]{3,2,1,0:T(8,128)}), f32[16,12,8,128]{3,2,1,0:T(8,128)S(1)}, u32[]{:S(2)}, u32[]{:S(2)}) async-start(f32[16,12,8,128]{3,2,1,0:T(8,128)} %shard_map.55), calls=%async_computation | async-start | bytes 1572864 | tf_op jit(solution)/shard_map/all_to_all | solution.py:447
  11.3 0.8 pad_maximum_fusion.2
  12.1 1.2 %collective-permute-start.7 = (f32[64,3,256]{2,1,0:T(4,128)}, f32[64,3,256]{2,1,0:T(4,128)S(1)}, u32[]{:S(2)}, u32[]{:S(2)}) collective-permute-start(f32[64,3,256]{2,1,0:T(4,128)} %pad_maximum_fusion.2), channel_id=1, source_target_pairs={{0,2},{2,0},{1,3},{3,1},{4,6},{6,4},{5,7},{7,5},{8,10},{10,8},{9,1... | collective-permute-start | bytes 589832 | tf_op jit(solution)/shard_map/ppermute | solution.py:46
  14.1 1.2 %collective-permute-start = (f32[20,16,256]{2,1,0:T(8,128)}, f32[20,16,256]{2,1,0:T(8,128)S(1)}, u32[]{:S(2)}, u32[]{:S(2)}) collective-permute-start(f32[20,16,256]{2,1,0:T(8,128)} %pad_maximum_fusion), channel_id=1, source_target_pairs={{0,4},{4,0},{8,12},{12,8},{16,20},{20,16},{24,28},{28,24},{1,5},{5... | collective-permute-start | bytes 983048 | tf_op jit(solution)/shard_map/ppermute | solution.py:46
  16.0 2.2 %collective-permute-start.1 = (f32[20,16,256]{2,1,0:T(8,128)}, f32[20,16,256]{2,1,0:T(8,128)S(1)}, u32[]{:S(2)}, u32[]{:S(2)}) collective-permute-start(f32[20,16,256]{2,1,0:T(8,128)} %pad_maximum_fusion.1), channel_id=1, source_target_pairs={{4,8},{8,4},{12,16},{16,12},{20,24},{24,20},{5,9},{9,5},{13,17},{1... | collective-permute-start | bytes 983048 | tf_op jit(solution)/shard_map/ppermute | solution.py:48
  21.8 2.7 %collective-permute-done.7.refs_6_ = f32[64,3,256]{2,1,0:T(4,128)S(1)} collective-permute-done((f32[64,3,256]{2,1,0:T(4,128)}, f32[64,3,256]{2,1,0:T(4,128)S(1)}, u32[]{:S(2)}, u32[]{:S(2)}) %collective-permute-start.7) | collective-permute-done | bytes 196640 | tf_op jit(solution)/shard_map/ppermute | solution.py:46
  24.5 6.1 %all-to-all-done.rows_ref = f32[16,12,8,128]{3,2,1,0:T(8,128)S(1)} async-done(((f32[16,12,8,128]{3,2,1,0:T(8,128)}), f32[16,12,8,128]{3,2,1,0:T(8,128)S(1)}, u32[]{:S(2)}, u32[]{:S(2)}) %all-to-all-start) | async-done | bytes 786464 | tf_op jit(solution)/shard_map/all_to_all | solution.py:447
  30.7 1.3 %shard_map.56 = (f32[1,8,16,256]{3,2,1,0:T(8,128)S(1)}, f32[4,8,256]{2,1,0:T(8,128)S(1)}) custom-call(s32[192]{0:T(256)S(1)} %add.85.slot_ref, f32[16,12,8,128]{3,2,1,0:T(8,128)S(1)} %all-to-all-done.rows_ref), custom_call_target="tpu_custom_call" | custom-call | tf_op jit(solution)/shard_map/pallas_call | solution.py:397
  32.0 4.0 %collective-permute-done.refs_4_ = f32[20,16,256]{2,1,0:T(8,128)S(1)} collective-permute-done((f32[20,16,256]{2,1,0:T(8,128)}, f32[20,16,256]{2,1,0:T(8,128)S(1)}, u32[]{:S(2)}, u32[]{:S(2)}) %collective-permute-start) | collective-permute-done | bytes 327712 | tf_op jit(solution)/shard_map/ppermute | solution.py:46
  36.0 1.9 %collective-permute-start.3 = (f32[2,16,256]{2,1,0:T(8,128)S(1)}, f32[2,16,256]{2,1,0:T(8,128)S(1)}, u32[]{:S(2)}, u32[]{:S(2)}) collective-permute-start(f32[2,16,256]{2,1,0:T(8,128)S(1)} %get-tuple-element.49), channel_id=1, source_target_pairs={{4,8},{8,4},{12,16},{16,12},{20,24},{24,20},{5,9},{9,5},{13,17},{1... | collective-permute-start | bytes 98312 | tf_op jit(solution)/shard_map/ppermute | solution.py:48
  38.0 1.0 %collective-permute-start.5 = (f32[40,2,256]{2,1,0:T(2,128)S(1)}, f32[40,2,256]{2,1,0:T(2,128)S(1)}, u32[]{:S(2)}, u32[]{:S(2)}) collective-permute-start(f32[40,2,256]{2,1,0:T(2,128)S(1)} %pad_maximum_fusion.5), channel_id=1, source_target_pairs={{0,2},{2,0},{1,3},{3,1},{4,6},{6,4},{5,7},{7,5},{8,10},{10,8},{9,1... | collective-permute-start | bytes 245768 | tf_op jit(solution)/shard_map/ppermute | solution.py:46
  39.7 3.7 %collective-permute-start.2 = (f32[2,16,256]{2,1,0:T(8,128)S(1)}, f32[2,16,256]{2,1,0:T(8,128)S(1)}, u32[]{:S(2)}, u32[]{:S(2)}) collective-permute-start(f32[2,16,256]{2,1,0:T(8,128)S(1)} %get-tuple-element.50), channel_id=1, source_target_pairs={{0,4},{4,0},{8,12},{12,8},{16,20},{20,16},{24,28},{28,24},{1,5},{5... | collective-permute-start | bytes 98312 | tf_op jit(solution)/shard_map/ppermute | solution.py:46
  43.4 1.3 %collective-permute-done.2.refs_0_ = f32[2,16,256]{2,1,0:T(8,128)S(1)} collective-permute-done((f32[2,16,256]{2,1,0:T(8,128)S(1)}, f32[2,16,256]{2,1,0:T(8,128)S(1)}, u32[]{:S(2)}, u32[]{:S(2)}) %collective-permute-start.2) | collective-permute-done | bytes 32800 | tf_op jit(solution)/shard_map/ppermute | solution.py:46
  45.8 1.7 %collective-permute-done.4.refs_2_ = f32[12,2,256]{2,1,0:T(2,128)S(1)} collective-permute-done((f32[12,2,256]{2,1,0:T(2,128)S(1)}, f32[12,2,256]{2,1,0:T(2,128)S(1)}, u32[]{:S(2)}, u32[]{:S(2)}) %collective-permute-start.4) | collective-permute-done | bytes 24608 | tf_op jit(solution)/shard_map/ppermute | solution.py:46
  48.3 3.7 %collective-permute-start.8 = (f32[130,16,128]{2,1,0:T(8,128)}, f32[130,16,128]{2,1,0:T(8,128)S(1)}, u32[]{:S(2)}, u32[]{:S(2)}) collective-permute-start(f32[130,16,128]{2,1,0:T(8,128)} %bitcast_dynamic-update-slice_fusion), channel_id=1, source_target_pairs={{0,1},{1,0},{2,3},{3,2},{4,5},{5,4},{6,7},{7,6},{8,9},{9,8},{10,11... | collective-permute-start | bytes 3194888 | tf_op jit(solution)/shard_map/ppermute | solution.py:46
  52.3 2.1 %collective-permute-done.6.refs_3_ = f32[15,16,128]{2,1,0:T(8,128)S(1)} collective-permute-done((f32[15,16,128]{2,1,0:T(8,128)S(1)}, f32[15,16,128]{2,1,0:T(8,128)S(1)}, u32[]{:S(2)}, u32[]{:S(2)}) %collective-permute-start.6) | collective-permute-done | bytes 122912 | tf_op jit(solution)/shard_map/ppermute | solution.py:46
  55.1 0.9 %copy-done.3 = f32[1,8,16,256]{3,2,1,0:T(8,128)S(1)} copy-done((f32[1,8,16,256]{3,2,1,0:T(8,128)S(1)}, f32[1,8,16,256]{3,2,1,0:T(8,128)}, u32[]{:S(2)}) %copy-start.3) | copy-done | bytes 131096
  56.0 0.9 %copy-done.7 = f32[15,16,128]{2,1,0:T(8,128)S(1)} copy-done((f32[15,16,128]{2,1,0:T(8,128)S(1)}, f32[15,16,128]{2,1,0:T(8,128)}, u32[]{:S(2)}) %copy-start.7) | copy-done | bytes 122904
  56.9 0.8 copy-done.9
  57.6 0.8 copy-done.11
  59.9 4.6 %shard_map.57 = (f32[4,12,24,384]{3,2,1,0:T(8,128)S(1)}, f32[4,12,24,384]{3,2,1,0:T(8,128)S(1)}, f32[12,24,384]{2,1,0:T(8,128)S(1)}, f32[36,8,128]{2,1,0:T(8,128...) custom-call(s32[9]{0:T(128)S(1)} %convert_element_type.9.flags, ...), custom_call_target="tpu_custom_call" | custom-call | tf_op jit(solution)/shard_map/pallas_call | solution.py:397
  64.5 1.8 %collective-permute-start.9 = (f32[36,8,128]{2,1,0:T(8,128)S(1)}, f32[36,8,128]{2,1,0:T(8,128)S(1)}, u32[]{:S(2)}, u32[]{:S(2)}) collective-permute-start(f32[36,8,128]{2,1,0:T(8,128)S(1)} %get-tuple-element.32.own), channel_id=1, source_target_pairs={{0,4},{4,0},{8,12},{12,8},{16,20},{20,16},{24,28},{28,24},{1,5},{5... | collective-permute-start | bytes 442376 | tf_op jit(solution)/shard_map/ppermute | solution.py:46
  66.4 1.9 %collective-permute-start.10 = (f32[36,8,128]{2,1,0:T(8,128)S(1)}, f32[36,8,128]{2,1,0:T(8,128)S(1)}, u32[]{:S(2)}, u32[]{:S(2)}) collective-permute-start(f32[36,8,128]{2,1,0:T(8,128)S(1)} %get-tuple-element.36), channel_id=1, source_target_pairs={{4,8},{8,4},{12,16},{16,12},{20,24},{24,20},{5,9},{9,5},{13,17},{1... | collective-permute-start | bytes 442376 | tf_op jit(solution)/shard_map/ppermute | solution.py:48
  68.3 1.9 %collective-permute-done.9.refs_0_ = f32[36,8,128]{2,1,0:T(8,128)S(1)} collective-permute-done((f32[36,8,128]{2,1,0:T(8,128)S(1)}, f32[36,8,128]{2,1,0:T(8,128)S(1)}, u32[]{:S(2)}, u32[]{:S(2)}) %collective-permute-start.9) | collective-permute-done | bytes 147488 | tf_op jit(solution)/shard_map/ppermute | solution.py:46
  70.3 3.6 %collective-permute-done.10.refs_1_ = f32[36,8,128]{2,1,0:T(8,128)S(1)} collective-permute-done((f32[36,8,128]{2,1,0:T(8,128)S(1)}, f32[36,8,128]{2,1,0:T(8,128)S(1)}, u32[]{:S(2)}, u32[]{:S(2)}) %collective-permute-start.10) | collective-permute-done | bytes 147488 | tf_op jit(solution)/shard_map/ppermute | solution.py:48
  74.3 4.7 %collective-permute-done.11.refs_2_ = f32[100,4,128]{2,1,0:T(4,128)S(1)} collective-permute-done((f32[100,4,128]{2,1,0:T(4,128)S(1)}, f32[100,4,128]{2,1,0:T(4,128)S(1)}, u32[]{:S(2)}, u32[]{:S(2)}) %collective-permute-start.11) | collective-permute-done | bytes 204832 | tf_op jit(solution)/shard_map/ppermute | solution.py:46
  79.1 2.5 %collective-permute-start.12 = (f32[210,8,128]{2,1,0:T(8,128)S(1)}, f32[210,8,128]{2,1,0:T(8,128)S(1)}, u32[]{:S(2)}, u32[]{:S(2)}) collective-permute-start(f32[210,8,128]{2,1,0:T(8,128)S(1)} %constant_dynamic-update-slice_fusion.2), channel_id=1, source_target_pairs={{0,1},{1,0},{2,3},{3,2},{4,5},{5,4},{6,7},{7,6},{8,9},{9,8},{10,11... | collective-permute-start | bytes 2580488 | tf_op jit(solution)/shard_map/ppermute | solution.py:46
  81.7 2.0 %collective-permute-done.12.refs_3_ = f32[210,8,128]{2,1,0:T(8,128)S(1)} collective-permute-done((f32[210,8,128]{2,1,0:T(8,128)S(1)}, f32[210,8,128]{2,1,0:T(8,128)S(1)}, u32[]{:S(2)}, u32[]{:S(2)}) %collective-permute-start.12) | collective-permute-done | bytes 860192 | tf_op jit(solution)/shard_map/ppermute | solution.py:46
  83.7 5.2 %shard_map.58 = f32[4,8,16,256]{3,2,1,0:T(8,128)} custom-call(s32[9]{0:T(128)S(1)} %convert_element_type.9.flags, f32[36,8,128]{2,1,0:T(8,128)S(1)} %get-tuple-element.32.own, f32[4,12,24,384]{3,2,1,0:T(8,128)S(1)} %get-tuple-element.33.state, f32[12,24,384]{2,1,0:T(8,128)S(1)} %get-tuple-element.34.weight, f32[4,12,24,384]{3,2,1,0:T(8,128)S(1)} %get-tuple-element.35.rhs, ...), custom_call_target="tpu_custom_call" | custom-call | tf_op jit(solution)/shard_map/pallas_call | solution.py:397
  (91 shorter events, 10.7 us)
Async XLA Ops:
  4.4 6.8 %copy-start = (f32[4,8,16,256]{3,2,1,0:T(8,128)S(1)}, f32[4,8,16,256]{3,2,1,0:T(8,128)}, u32[]{:S(2)}) copy-start(f32[4,8,16,256]{3,2,1,0:T(8,128)} %start_field) | copy-start | bytes 1572868
  4.4 6.8 %copy-start.1 = (f32[4,8,16,256]{3,2,1,0:T(8,128)S(1)}, f32[4,8,16,256]{3,2,1,0:T(8,128)}, u32[]{:S(2)}) copy-start(f32[4,8,16,256]{3,2,1,0:T(8,128)} %right_side) | copy-start | bytes 1572868
  4.4 26.2 %all-to-all-start = ((f32[16,12,8,128]{3,2,1,0:T(8,128)}), f32[16,12,8,128]{3,2,1,0:T(8,128)S(1)}, u32[]{:S(2)}, u32[]{:S(2)}) async-start(f32[16,12,8,128]{3,2,1,0:T(8,128)} %shard_map.55), calls=%async_computation | async-start | bytes 1572864 | tf_op jit(solution)/shard_map/all_to_all | solution.py:447
  12.1 12.5 %collective-permute-start.7 = (f32[64,3,256]{2,1,0:T(4,128)}, f32[64,3,256]{2,1,0:T(4,128)S(1)}, u32[]{:S(2)}, u32[]{:S(2)}) collective-permute-start(f32[64,3,256]{2,1,0:T(4,128)} %pad_maximum_fusion.2), channel_id=1, source_target_pairs={{0,2},{2,0},{1,3},{3,1},{4,6},{6,4},{5,7},{7,5},{8,10},{10,8},{9,1... | collective-permute-start | bytes 589832 | tf_op jit(solution)/shard_map/ppermute | solution.py:46
  13.3 5.5 %copy-start.17 = (s32[3072,1]{0,1:T(1,128)S(1)}, s32[3072,1]{0,1:T(1,128)}, u32[]{:S(2)}) copy-start(s32[3072,1]{0,1:T(1,128)} %param.8) | copy-start | bytes 36868
  13.3 6.2 %copy-start.16 = (s32[3072]{0:T(1024)S(1)}, s32[3072]{0:T(1024)}, u32[]{:S(2)}) copy-start(s32[3072]{0:T(1024)} %param.9) | copy-start | bytes 36868
  14.1 21.9 %collective-permute-start = (f32[20,16,256]{2,1,0:T(8,128)}, f32[20,16,256]{2,1,0:T(8,128)S(1)}, u32[]{:S(2)}, u32[]{:S(2)}) collective-permute-start(f32[20,16,256]{2,1,0:T(8,128)} %pad_maximum_fusion), channel_id=1, source_target_pairs={{0,4},{4,0},{8,12},{12,8},{16,20},{20,16},{24,28},{28,24},{1,5},{5... | collective-permute-start | bytes 983048 | tf_op jit(solution)/shard_map/ppermute | solution.py:46
  16.0 20.0 %collective-permute-start.1 = (f32[20,16,256]{2,1,0:T(8,128)}, f32[20,16,256]{2,1,0:T(8,128)S(1)}, u32[]{:S(2)}, u32[]{:S(2)}) collective-permute-start(f32[20,16,256]{2,1,0:T(8,128)} %pad_maximum_fusion.1), channel_id=1, source_target_pairs={{4,8},{8,4},{12,16},{16,12},{20,24},{24,20},{5,9},{9,5},{13,17},{1... | collective-permute-start | bytes 983048 | tf_op jit(solution)/shard_map/ppermute | solution.py:48
  24.5 21.3 %copy-start.4 = (f32[64,3,256]{2,1,0:T(4,128)}, f32[64,3,256]{2,1,0:T(4,128)S(1)}, u32[]{:S(2)}) copy-start(f32[64,3,256]{2,1,0:T(4,128)S(1)} %collective-permute-done.7.refs_6_) | copy-start | bytes 589828
  31.9 15.6 %copy-start.14 = (f32[4,8,256]{2,1,0:T(8,128)}, f32[4,8,256]{2,1,0:T(8,128)S(1)}, u32[]{:S(2)}) copy-start(f32[4,8,256]{2,1,0:T(8,128)S(1)} %get-tuple-element.27.pooled_chi) | copy-start | bytes 98308
  31.9 20.0 %copy-start.2 = (f32[1,8,16,256]{3,2,1,0:T(8,128)}, f32[1,8,16,256]{3,2,1,0:T(8,128)S(1)}, u32[]{:S(2)}) copy-start(f32[1,8,16,256]{3,2,1,0:T(8,128)S(1)} %get-tuple-element.26.own) | copy-start | bytes 393220
  36.0 7.4 %collective-permute-start.3 = (f32[2,16,256]{2,1,0:T(8,128)S(1)}, f32[2,16,256]{2,1,0:T(8,128)S(1)}, u32[]{:S(2)}, u32[]{:S(2)}) collective-permute-start(f32[2,16,256]{2,1,0:T(8,128)S(1)} %get-tuple-element.49), channel_id=1, source_target_pairs={{4,8},{8,4},{12,16},{16,12},{20,24},{24,20},{5,9},{9,5},{13,17},{1... | collective-permute-start | bytes 98312 | tf_op jit(solution)/shard_map/ppermute | solution.py:48
  38.0 9.5 %collective-permute-start.5 = (f32[40,2,256]{2,1,0:T(2,128)S(1)}, f32[40,2,256]{2,1,0:T(2,128)S(1)}, u32[]{:S(2)}, u32[]{:S(2)}) collective-permute-start(f32[40,2,256]{2,1,0:T(2,128)S(1)} %pad_maximum_fusion.5), channel_id=1, source_target_pairs={{0,2},{2,0},{1,3},{3,1},{4,6},{6,4},{5,7},{7,5},{8,10},{10,8},{9,1... | collective-permute-start | bytes 245768 | tf_op jit(solution)/shard_map/ppermute | solution.py:46
  39.7 5.0 %collective-permute-start.2 = (f32[2,16,256]{2,1,0:T(8,128)S(1)}, f32[2,16,256]{2,1,0:T(8,128)S(1)}, u32[]{:S(2)}, u32[]{:S(2)}) collective-permute-start(f32[2,16,256]{2,1,0:T(8,128)S(1)} %get-tuple-element.50), channel_id=1, source_target_pairs={{0,4},{4,0},{8,12},{12,8},{16,20},{20,16},{24,28},{28,24},{1,5},{5... | collective-permute-start | bytes 98312 | tf_op jit(solution)/shard_map/ppermute | solution.py:46
  43.4 8.6 %copy-start.8 = (f32[2,16,256]{2,1,0:T(8,128)}, f32[2,16,256]{2,1,0:T(8,128)S(1)}, u32[]{:S(2)}) copy-start(f32[2,16,256]{2,1,0:T(8,128)S(1)} %collective-permute-done.3.refs_1_) | copy-start | bytes 98308
  44.7 7.3 %copy-start.10 = (f32[2,16,256]{2,1,0:T(8,128)}, f32[2,16,256]{2,1,0:T(8,128)S(1)}, u32[]{:S(2)}) copy-start(f32[2,16,256]{2,1,0:T(8,128)S(1)} %collective-permute-done.2.refs_0_) | copy-start | bytes 98308
  44.7 2.7 %collective-permute-start.4 = (f32[12,2,256]{2,1,0:T(2,128)S(1)}, f32[12,2,256]{2,1,0:T(2,128)S(1)}, u32[]{:S(2)}, u32[]{:S(2)}) collective-permute-start(f32[12,2,256]{2,1,0:T(2,128)S(1)} %pad_maximum_fusion.6), channel_id=1, source_target_pairs={{0,2},{2,0},{1,3},{3,1},{4,6},{6,4},{5,7},{7,5},{8,10},{10,8},{9,1... | collective-permute-start | bytes 73736 | tf_op jit(solution)/shard_map/ppermute | solution.py:46
  47.5 4.6 %copy-start.12 = (f32[12,2,256]{2,1,0:T(2,128)}, f32[12,2,256]{2,1,0:T(2,128)S(1)}, u32[]{:S(2)}) copy-start(f32[12,2,256]{2,1,0:T(2,128)S(1)} %collective-permute-done.4.refs_2_) | copy-start | bytes 73732
  47.5 7.6 %copy-start.5 = (f32[64,3,256]{2,1,0:T(4,128)S(1)}, f32[64,3,256]{2,1,0:T(4,128)}, u32[]{:S(2)}) copy-start(f32[64,3,256]{2,1,0:T(4,128)} %copy-done.4) | copy-start | bytes 589828
  48.3 6.8 %collective-permute-start.8 = (f32[130,16,128]{2,1,0:T(8,128)}, f32[130,16,128]{2,1,0:T(8,128)S(1)}, u32[]{:S(2)}, u32[]{:S(2)}) collective-permute-start(f32[130,16,128]{2,1,0:T(8,128)} %bitcast_dynamic-update-slice_fusion), channel_id=1, source_target_pairs={{0,1},{1,0},{2,3},{3,2},{4,5},{5,4},{6,7},{7,6},{8,9},{9,8},{10,11... | collective-permute-start | bytes 3194888 | tf_op jit(solution)/shard_map/ppermute | solution.py:46
  52.1 2.4 %collective-permute-start.6 = (f32[15,16,128]{2,1,0:T(8,128)S(1)}, f32[15,16,128]{2,1,0:T(8,128)S(1)}, u32[]{:S(2)}, u32[]{:S(2)}) collective-permute-start(f32[15,16,128]{2,1,0:T(8,128)S(1)} %pad_maximum_fusion.4), channel_id=1, source_target_pairs={{0,1},{1,0},{2,3},{3,2},{4,5},{5,4},{6,7},{7,6},{8,9},{9,8},{10,11... | collective-permute-start | bytes 368648 | tf_op jit(solution)/shard_map/ppermute | solution.py:46
  54.4 0.6 copy-start.6
  55.1 0.9 %copy-start.3 = (f32[1,8,16,256]{3,2,1,0:T(8,128)S(1)}, f32[1,8,16,256]{3,2,1,0:T(8,128)}, u32[]{:S(2)}) copy-start(f32[1,8,16,256]{3,2,1,0:T(8,128)} %copy-done.2) | copy-start | bytes 393220
  56.0 0.9 %copy-start.7 = (f32[15,16,128]{2,1,0:T(8,128)S(1)}, f32[15,16,128]{2,1,0:T(8,128)}, u32[]{:S(2)}) copy-start(f32[15,16,128]{2,1,0:T(8,128)} %copy-done.6) | copy-start | bytes 368644
  56.9 0.8 copy-start.9
  57.6 0.8 copy-start.11
  58.4 0.7 copy-start.13
  59.1 0.8 copy-start.15
  64.5 5.7 %collective-permute-start.9 = (f32[36,8,128]{2,1,0:T(8,128)S(1)}, f32[36,8,128]{2,1,0:T(8,128)S(1)}, u32[]{:S(2)}, u32[]{:S(2)}) collective-permute-start(f32[36,8,128]{2,1,0:T(8,128)S(1)} %get-tuple-element.32.own), channel_id=1, source_target_pairs={{0,4},{4,0},{8,12},{12,8},{16,20},{20,16},{24,28},{28,24},{1,5},{5... | collective-permute-start | bytes 442376 | tf_op jit(solution)/shard_map/ppermute | solution.py:46
  66.4 7.5 %collective-permute-start.10 = (f32[36,8,128]{2,1,0:T(8,128)S(1)}, f32[36,8,128]{2,1,0:T(8,128)S(1)}, u32[]{:S(2)}, u32[]{:S(2)}) collective-permute-start(f32[36,8,128]{2,1,0:T(8,128)S(1)} %get-tuple-element.36), channel_id=1, source_target_pairs={{4,8},{8,4},{12,16},{16,12},{20,24},{24,20},{5,9},{9,5},{13,17},{1... | collective-permute-start | bytes 442376 | tf_op jit(solution)/shard_map/ppermute | solution.py:48
  74.0 5.1 %collective-permute-start.11 = (f32[100,4,128]{2,1,0:T(4,128)S(1)}, f32[100,4,128]{2,1,0:T(4,128)S(1)}, u32[]{:S(2)}, u32[]{:S(2)}) collective-permute-start(f32[100,4,128]{2,1,0:T(4,128)S(1)} %pad_maximum_fusion.3), channel_id=1, source_target_pairs={{0,2},{2,0},{1,3},{3,1},{4,6},{6,4},{5,7},{7,5},{8,10},{10,8},{9,1... | collective-permute-start | bytes 614408 | tf_op jit(solution)/shard_map/ppermute | solution.py:46
  79.1 4.5 %collective-permute-start.12 = (f32[210,8,128]{2,1,0:T(8,128)S(1)}, f32[210,8,128]{2,1,0:T(8,128)S(1)}, u32[]{:S(2)}, u32[]{:S(2)}) collective-permute-start(f32[210,8,128]{2,1,0:T(8,128)S(1)} %constant_dynamic-update-slice_fusion.2), channel_id=1, source_target_pairs={{0,1},{1,0},{2,3},{3,2},{4,5},{5,4},{6,7},{7,6},{8,9},{9,8},{10,11... | collective-permute-start | bytes 2580488 | tf_op jit(solution)/shard_map/ppermute | solution.py:46

commit v5 on v4

--- a/solution.py
+++ b/solution.py
@@ -77,7 +77,7 @@
     return swap("lvl", last)
 
 
-def place_halo(dst, margin, own, got, flags, width, depth, group=(0, 0), slabs=None, corner=0):
+def place_halo(dst, margin, own, got, flags, width, depth, group=(0, 0), slabs=None, corner=0, base=(0, 0)):
     xs, ys, zs = got
     rows, lanes = own.shape[-2:]
     fields, planes, total = dst.shape[0], dst.shape[1] - 2 * margin, dst.shape[2]
@@ -89,7 +89,7 @@
     near = (lax.broadcasted_iota(jnp.int32, (1, LANES), 1) < LANES // 2) == even_z
 
     def edge(at, row, size):
-        part = slice(row, row + size)
+        at, part = base[1] + at, slice(row, row + size)
         return jnp.where(near, zs[0][at, part], 0.0 if len(zs) == 1 else zs[1][at, part])
 
     for f in range(fields):
@@ -110,7 +110,7 @@
             for n in range(pairs_y):
                 at_z = slab_count + n * (-(-slab_count // per)) + slab // per
                 if corner and k >= planes:
-                    y = ys[pairs_y + n][slab - own_slabs]
+                    y = ys[pairs_y + n][base[0] + slab - own_slabs]
                 else:
                     y = ys[n][slab]
                 sides.append((y, edge(at_z, slab % per * PAD, deep)))
@@ -263,16 +263,70 @@
             coarse_out[qx, :, zt * LANES:(zt + 1) * LANES] = total
 
 
+def side(up, v, dim, width):
+    size = v.shape[dim]
+    low = v[..., 0:width] if dim == 1 else v[0:width]
+    high = v[..., size - width:] if dim == 1 else v[size - width:]
+    return jnp.where(up, high, low)
+
+
+def y_kernel(flags, *refs, nums):
+    (chi_x, first_x), outs = split(refs[1:], [nums[0]] * 2)
+    for n, out in enumerate(outs):
+        up = (flags[1] == 1) == (n == 0)
+        at = 0
+        for ref in (refs[0], *chi_x, *first_x):
+            for s in range(ref.shape[0]):
+                out[at] = side(up, ref[s], 0, out.shape[1])
+                at += 1
+
+
+def z_kernel(flags, *refs, nums):
+    (chi, chi_x, start, rhs, first_x, first_y, corners), outs = split(refs, [1, nums[0], 1, 1, nums[0], nums[1], nums[1]])
+    rows = chi[0].shape[1]
+    per = rows // PAD
+    chi_slabs = chi[0].shape[0] + sum(x.shape[0] for x in chi_x)
+    for n, out in enumerate(outs):
+        up = (flags[2] == 1) == (n == 0)
+        at = 0
+        for slabs, edges in (
+            ((*chi, *chi_x), [[(c, 0, chi_slabs)] for c in corners]),
+            ((*start, *rhs, *first_x), [[(y, 0, y.shape[0]), (c, chi_slabs, c.shape[0])] for y, c in zip(first_y, corners)]),
+        ):
+            for ref in slabs:
+                for s in range(ref.shape[0]):
+                    out[at] = side(up, ref[s], 1, LANES)
+                    at += 1
+            for parts in edges:
+                k = 0
+                for ref, low, high in parts:
+                    for s in range(low, high):
+                        depth = ref.shape[1]
+                        row = k % per * PAD
+                        out[at + k // per, row:row + depth] = side(up, ref[s], 1, LANES)
+                        out[at + k // per, row + depth:row + PAD] = jnp.zeros((PAD - depth, LANES), jnp.float32)
+                        k += 1
+                while k % per:
+                    row = k % per * PAD
+                    out[at + k // per, row:row + PAD] = jnp.zeros((PAD, LANES), jnp.float32)
+                    k += 1
+                at += k // per
+
+
 def second_kernel(flags, own, pooled_chi, right_side, start_field, *refs, nums):
-    (got, refs), (fields_got, refs) = split(refs, nums[:3]), split(refs[sum(nums[:3]):], nums[3:6])
+    n_x, n_y, n_z = nums
+    (chi_x, first_x, first_y, far_y, far_z), refs = split(refs, [n_x, n_x, n_y, n_y, n_z])
     rhs, state_out, weight_out = refs[:3]
-    (x_out, y_out, z_out), (chi, start, ext, tmp, pooled) = split(refs[3:], nums[6:])
+    (x_out, y_out, z_out), (chi, start, ext, tmp, pooled) = split(refs[3:], nums)
     _, planes, rows, lanes = own.shape
     total = ext.shape[2]
+    chi_slabs = planes + n_x * FINE_W
+    base = (chi_slabs, chi_slabs + n_y * -(-chi_slabs // (rows // PAD)))
     slabs = (8 * planes, 4 * (START_W + FINE_W))
-    place_halo(start, START_W, start_field, fields_got, flags, START_W, START_W, (0, 0), slabs, CORNER)
-    place_halo(rhs, FINE_W, right_side, fields_got, flags, FINE_W, START_W, (4 * planes, 4 * START_W), slabs, CORNER)
-    place_halo(chi, FINE_W, own, got, flags, FINE_W, FINE_W)
+    fields_got = (first_x, (*first_y, *far_y), far_z)
+    place_halo(chi, FINE_W, own, (chi_x, far_y, far_z), flags, FINE_W, FINE_W)
+    place_halo(start, START_W, start_field, fields_got, flags, START_W, START_W, (0, 0), slabs, CORNER, base)
+    place_halo(rhs, FINE_W, right_side, fields_got, flags, FINE_W, START_W, (4 * planes, 4 * START_W), slabs, CORNER, base)
     mask = inside(flags, rows, lanes, total, FINE_W)
     w_p = (RELAX / (SHIFT + 6.0)) * mask
 
@@ -459,19 +513,33 @@
         [pltpu.VMEM(((slots + 1) * 8, LANES), jnp.float32), pltpu.VMEM((lanes // LANES, rows, LANES), jnp.float32)],
         slot_of, arrived,
     )
-    first_x, chi = lax.optimization_barrier((first_x, chi))
     group = [(chi, FINE_W)]
     chi_x = halo_x(group)
-    corners = swap("gy", lambda up, n: jnp.concatenate([cut(x, 1, CORNER, up) for x in first_x], axis=0))
-    chi_y = halo_y(group, FINE_W, chi_x)
-    chi_y, corners = lax.optimization_barrier((chi_y, corners))
-    chi_z = halo_z(group, chi_x, [[y] for y in chi_y])
-    first_z = halo_z(groups, first_x, list(zip(first_y, corners)))
+    first_x, chi_x = lax.optimization_barrier((first_x, chi_x))
+    slabs = lambda v: v.reshape(-1, rows, lanes)
+    far_x = len(first_x) * 4 * (START_W + FINE_W)
+    chi_slabs = planes + len(chi_x) * FINE_W
+    y_sent = call(
+        functools.partial(y_kernel, nums=pair_counts),
+        [(chi_slabs + far_x, CORNER, lanes)] * pair_counts[1],
+        [],
+        flags, slabs(chi), *chi_x, *first_x,
+    )
+    far_y = swap("gy", lambda up, n: y_sent[n])
+    per = rows // PAD
+    edges = -(-chi_slabs // per) + -(-(8 * planes + far_x) // per)
+    z_sent = call(
+        functools.partial(z_kernel, nums=pair_counts),
+        [(chi_slabs + 8 * planes + far_x + pair_counts[1] * edges, rows, LANES)] * pair_counts[2],
+        [],
+        flags, slabs(chi), *chi_x, slabs(start_field), slabs(right_side), *first_x, *first_y, *far_y,
+    )
+    far_z = swap("lvl", lambda up, n: z_sent[n])
     c_slabs, s_slabs = 5 * c_planes, 4 * (rows // 8) * (lanes // LANES)
     outers = [[(c_slabs + s_slabs, 8, LANES)], [(4 * (planes + 2), PAD, LANES)], [(4 * (planes + 2) * total // 8, 8, LANES)]]
     outers = [shape * n for shape, n in zip(outers, pair_counts)]
     rhs, state, weight, *sent = call(
-        functools.partial(second_kernel, nums=[*pair_counts, pair_counts[0], 2 * pair_counts[1], pair_counts[2], *pair_counts]),
+        functools.partial(second_kernel, nums=pair_counts),
         [(4, far, total, wide), (4, near, total, wide), (far, total, wide), *sum(outers, [])],
         [
             pltpu.VMEM((1, far, total, wide), jnp.float32),
@@ -480,7 +548,7 @@
             pltpu.VMEM((4, lanes // LANES, rows, LANES), jnp.float32),
             pltpu.VMEM((5, c_planes, c_rows, lanes), jnp.float32),
         ],
-        flags, chi, pooled_chi, right_side, start_field, *chi_x, *chi_y, *chi_z, *first_x, *first_y, *corners, *first_z,
+        flags, chi, pooled_chi, right_side, start_field, *chi_x, *first_x, *first_y, *far_y, *far_z,
     )
     (x_out, y_out, z_out), _ = split(sent, pair_counts)
     group = [(x_out[0][:c_slabs].reshape(5, c_planes, c_rows, c_lanes), COARSE_W)]

time: 89.5 us -> 80.9 us (0.904)
  local copies, waits for them, and re-layouts: 12.2 us -> 3.22 us
  Pallas kernels: 13.7 us -> 16.9 us
  other arithmetic: 3.62 us -> 2.17 us
  starting transfers between devices: 28.6 us -> 27.6 us
    unnamed x47 -> x15, local copies, waits for them, and re-layouts: 9.9 us -> 1.8 us
    ppermute x10 -> x8, waiting for transfers between devices: 20.5 us -> 13.6 us  [swap(): got = [lax.ppermute(message(even, 0), axis, pairs(count, 0))]]
    all_to_all x1, waiting for transfers between devices: 6.13 us -> 11.5 us  [body(): lax.all_to_all(outgoing, ('gx', 'gy'), split_axis=0, concat_axis=0, tiled...]
    pallas_call x4 -> x6, Pallas kernels: 13.7 us -> 16.9 us  [call(): pl.pallas_call(kernel, out_shape=outs, in_specs=[SMEM] * smem + [VMEM] *...]
    ppermute x3, waiting for transfers between devices: 3.61 us -> 5.48 us  [swap(): got.append(lax.ppermute(message(~even, 1), axis, pairs(count, 1)))]
    ppermute x10 -> x8, starting transfers between devices: 15.8 us -> 14.8 us  [swap(): got = [lax.ppermute(message(even, 0), axis, pairs(count, 0))]]
  transfers between devices with their start and end apart: 14 -> 12, of which waited for: 10 -> 9; matrix products, arithmetic and copies ran while one was open for 9% -> 4% of each run, Pallas kernels for 1% -> 2%
where the time goes in v5:
time: 80.9 us; the launch traced here: 80.7 us
  waiting for transfers between devices  30.6 us (38%)
  starting transfers between devices  27.6 us (34%)
  Pallas kernels  16.9 us (21%)
  local copies, waits for them, and re-layouts  3.22 us (4%)
  other arithmetic  2.17 us (3%)
    pallas_call x6, Pallas kernels, call(): pl.pallas_call(kernel, out_shape=outs, in_specs=[SMEM] * smem + [VMEM] *...  16.9 us
    ppermute x8, starting transfers between devices, swap(): got = [lax.ppermute(message(even, 0), axis, pairs(count, 0))]  14.8 us
    ppermute x8, waiting for transfers between devices, swap(): got = [lax.ppermute(message(even, 0), axis, pairs(count, 0))]  13.6 us
    all_to_all x1, waiting for transfers between devices, body(): lax.all_to_all(outgoing, ('gx', 'gy'), split_axis=0, concat_axis=0, tiled...  11.5 us
    all_to_all x1, starting transfers between devices, body(): lax.all_to_all(outgoing, ('gx', 'gy'), split_axis=0, concat_axis=0, tiled...  6.64 us
    ppermute x3, starting transfers between devices, swap(): got.append(lax.ppermute(message(~even, 1), axis, pairs(count, 1)))  6.11 us
    ppermute x3, waiting for transfers between devices, swap(): got.append(lax.ppermute(message(~even, 1), axis, pairs(count, 1)))  5.48 us
    unnamed x15, local copies, waits for them, and re-layouts  1.8 us
  transfers between devices with their start and end apart: 12, of which 9 were waited for; matrix products, arithmetic and copies ran while one was open for 4% of the time, Pallas kernels for 2%

profile of v5, /device:TPU:9, one launch (start us, length us, event | category | flops | bytes accessed | tf_op | source)
XLA Modules:
  0.0 80.7 jit_solution(533879234892404004)
XLA Ops:
  0.0 1.2 %copy.8 = f32[12,8,8,128]{3,2,1,0:T(8,128)S(1)} copy(f32[12,8,8,128]{3,1,2,0:T(8,128)} %bitcast.44) | data formatting | bytes 786432
  1.2 0.8 fusion.1.tile_ref
  1.9 2.6 %shard_map.55 = f32[16,12,8,128]{3,2,1,0:T(8,128)} custom-call(s32[96]{0:T(128)S(1)} %fusion.1.tile_ref, f32[96,8,128]{2,1,0:T(8,128)S(1)} %bitcast.38), custom_call_target="tpu_custom_call" | custom-call | tf_op jit(solution)/shard_map/pallas_call | solution.py:451
  4.5 6.6 %all-to-all-start = ((f32[16,12,8,128]{3,2,1,0:T(8,128)}), f32[16,12,8,128]{3,2,1,0:T(8,128)S(1)}, u32[]{:S(2)}, u32[]{:S(2)}) async-start(f32[16,12,8,128]{3,2,1,0:T(8,128)} %shard_map.55), calls=%async_computation | async-start | bytes 1572864 | tf_op jit(solution)/shard_map/all_to_all | solution.py:501
  11.3 1.2 %collective-permute-start.4 = (f32[64,3,256]{2,1,0:T(4,128)S(1)}, f32[64,3,256]{2,1,0:T(4,128)S(1)}, u32[]{:S(2)}, u32[]{:S(2)}) collective-permute-start(f32[64,3,256]{2,1,0:T(4,128)S(1)} %pad_maximum_fusion.2), channel_id=1, source_target_pairs={{0,2},{2,0},{1,3},{3,1},{4,6},{6,4},{5,7},{7,5},{8,10},{10,8},{9,1... | collective-permute-start | bytes 589832 | tf_op jit(solution)/shard_map/ppermute | solution.py:46
  12.7 1.2 %collective-permute-start = (f32[20,16,256]{2,1,0:T(8,128)S(1)}, f32[20,16,256]{2,1,0:T(8,128)S(1)}, u32[]{:S(2)}, u32[]{:S(2)}) collective-permute-start(f32[20,16,256]{2,1,0:T(8,128)S(1)} %pad_maximum_fusion), channel_id=1, source_target_pairs={{0,4},{4,0},{8,12},{12,8},{16,20},{20,16},{24,28},{28,24},{1,5},{5... | collective-permute-start | bytes 983048 | tf_op jit(solution)/shard_map/ppermute | solution.py:46
  13.9 0.7 pad_maximum_fusion.1
  14.7 2.2 %collective-permute-start.1 = (f32[20,16,256]{2,1,0:T(8,128)}, f32[20,16,256]{2,1,0:T(8,128)S(1)}, u32[]{:S(2)}, u32[]{:S(2)}) collective-permute-start(f32[20,16,256]{2,1,0:T(8,128)} %pad_maximum_fusion.1), channel_id=1, source_target_pairs={{4,8},{8,4},{12,16},{16,12},{20,24},{24,20},{5,9},{9,5},{13,17},{1... | collective-permute-start | bytes 983048 | tf_op jit(solution)/shard_map/ppermute | solution.py:48
  16.9 0.6 broadcast.31
  17.4 0.7 reduce.3
  18.4 0.3 select_reduce_fusion
  19.1 11.5 %all-to-all-done.rows_ref = f32[16,12,8,128]{3,2,1,0:T(8,128)S(1)} async-done(((f32[16,12,8,128]{3,2,1,0:T(8,128)}), f32[16,12,8,128]{3,2,1,0:T(8,128)S(1)}, u32[]{:S(2)}, u32[]{:S(2)}) %all-to-all-start) | async-done | bytes 786464 | tf_op jit(solution)/shard_map/all_to_all | solution.py:501
  30.6 1.3 %shard_map.56 = (f32[1,8,16,256]{3,2,1,0:T(8,128)S(1)}, f32[4,8,256]{2,1,0:T(8,128)S(1)}) custom-call(s32[192]{0:T(256)S(1)} %add.58.slot_ref, f32[16,12,8,128]{3,2,1,0:T(8,128)S(1)} %all-to-all-done.rows_ref), custom_call_target="tpu_custom_call" | custom-call | tf_op jit(solution)/shard_map/pallas_call | solution.py:451
  31.9 1.9 %collective-permute-start.3 = (f32[2,16,256]{2,1,0:T(8,128)S(1)}, f32[2,16,256]{2,1,0:T(8,128)S(1)}, u32[]{:S(2)}, u32[]{:S(2)}) collective-permute-start(f32[2,16,256]{2,1,0:T(8,128)S(1)} %get-tuple-element.47), channel_id=1, source_target_pairs={{4,8},{8,4},{12,16},{16,12},{20,24},{24,20},{5,9},{9,5},{13,17},{1... | collective-permute-start | bytes 98312 | tf_op jit(solution)/shard_map/ppermute | solution.py:48
  33.8 1.7 %collective-permute-start.2 = (f32[2,16,256]{2,1,0:T(8,128)S(1)}, f32[2,16,256]{2,1,0:T(8,128)S(1)}, u32[]{:S(2)}, u32[]{:S(2)}) collective-permute-start(f32[2,16,256]{2,1,0:T(8,128)S(1)} %get-tuple-element.48), channel_id=1, source_target_pairs={{0,4},{4,0},{8,12},{12,8},{16,20},{20,16},{24,28},{28,24},{1,5},{5... | collective-permute-start | bytes 98312 | tf_op jit(solution)/shard_map/ppermute | solution.py:46
  35.8 1.6 %collective-permute-done.3.refs_2_.refs_1_ = f32[2,16,256]{2,1,0:T(8,128)S(1)} collective-permute-done((f32[2,16,256]{2,1,0:T(8,128)S(1)}, f32[2,16,256]{2,1,0:T(8,128)S(1)}, u32[]{:S(2)}, u32[]{:S(2)}) %collective-permute-start.3) | collective-permute-done | bytes 32800 | tf_op jit(solution)/shard_map/ppermute | solution.py:48
  37.5 0.6 shard_map.57
  38.1 1.2 %collective-permute-start.5 = (f32[52,2,256]{2,1,0:T(2,128)S(1)}, f32[52,2,256]{2,1,0:T(2,128)S(1)}, u32[]{:S(2)}, u32[]{:S(2)}) collective-permute-start(f32[52,2,256]{2,1,0:T(2,128)S(1)} %shard_map.57), channel_id=1, source_target_pairs={{0,2},{2,0},{1,3},{3,1},{4,6},{6,4},{5,7},{7,5},{8,10},{10,8},{9,1... | collective-permute-start | bytes 319496 | tf_op jit(solution)/shard_map/ppermute | solution.py:46
  39.3 2.4 %collective-permute-done.5.refs_8_.refs_5_ = f32[52,2,256]{2,1,0:T(2,128)S(1)} collective-permute-done((f32[52,2,256]{2,1,0:T(2,128)S(1)}, f32[52,2,256]{2,1,0:T(2,128)S(1)}, u32[]{:S(2)}, u32[]{:S(2)}) %collective-permute-start.5) | collective-permute-done | bytes 106528 | tf_op jit(solution)/shard_map/ppermute | solution.py:46
  41.7 1.8 %shard_map.58 = f32[145,16,128]{2,1,0:T(8,128)} custom-call(s32[9]{0:T(128)S(1)} %convert_element_type.3.flags, f32[8,16,256]{2,1,0:T(8,128)S(1)} %bitcast.37, f32[2,16,256]{2,1,0:T(8,128)S(1)} %collective-permute-done.2.refs_1_.refs_0_, f32[2,16,256]{2,1,0:T(8,128)S(1)} %collective-permute-done.3.refs_2_.refs_1_, f32[32,16,256]{2,1,0:T(8,128)S(1)} %bitcast.33, ...), custom_call_target="tpu_custom_call" | custom-call | tf_op jit(solution)/shard_map/pallas_call | solution.py:451
  43.5 4.9 %collective-permute-start.6 = (f32[145,16,128]{2,1,0:T(8,128)}, f32[145,16,128]{2,1,0:T(8,128)}, u32[]{:S(2)}, u32[]{:S(2)}) collective-permute-start(f32[145,16,128]{2,1,0:T(8,128)} %shard_map.58), channel_id=1, source_target_pairs={{0,1},{1,0},{2,3},{3,2},{4,5},{5,4},{6,7},{7,6},{8,9},{9,8},{10,11... | collective-permute-start | bytes 3563528 | tf_op jit(solution)/shard_map/ppermute | solution.py:46
  48.4 2.8 %collective-permute-done.6.refs_6_ = f32[145,16,128]{2,1,0:T(8,128)} collective-permute-done((f32[145,16,128]{2,1,0:T(8,128)}, f32[145,16,128]{2,1,0:T(8,128)}, u32[]{:S(2)}, u32[]{:S(2)}) %collective-permute-start.6) | collective-permute-done | bytes 1187872 | tf_op jit(solution)/shard_map/ppermute | solution.py:46
  51.2 5.4 %shard_map.59 = (f32[4,12,24,384]{3,2,1,0:T(8,128)S(1)}, f32[4,12,24,384]{3,2,1,0:T(8,128)S(1)}, f32[12,24,384]{2,1,0:T(8,128)S(1)}, f32[36,8,128]{2,1,0:T(8,128...) custom-call(s32[9]{0:T(128)S(1)} %convert_element_type.3.flags, ...), custom_call_target="tpu_custom_call" | custom-call | tf_op jit(solution)/shard_map/pallas_call | solution.py:451
  56.6 1.5 %collective-permute-start.7 = (f32[36,8,128]{2,1,0:T(8,128)S(1)}, f32[36,8,128]{2,1,0:T(8,128)S(1)}, u32[]{:S(2)}, u32[]{:S(2)}) collective-permute-start(f32[36,8,128]{2,1,0:T(8,128)S(1)} %get-tuple-element.30.own), channel_id=1, source_target_pairs={{0,4},{4,0},{8,12},{12,8},{16,20},{20,16},{24,28},{28,24},{1,5},{5... | collective-permute-start | bytes 442376 | tf_op jit(solution)/shard_map/ppermute | solution.py:46
  58.1 2.0 %collective-permute-start.8 = (f32[36,8,128]{2,1,0:T(8,128)S(1)}, f32[36,8,128]{2,1,0:T(8,128)S(1)}, u32[]{:S(2)}, u32[]{:S(2)}) collective-permute-start(f32[36,8,128]{2,1,0:T(8,128)S(1)} %get-tuple-element.34), channel_id=1, source_target_pairs={{4,8},{8,4},{12,16},{16,12},{20,24},{24,20},{5,9},{9,5},{13,17},{1... | collective-permute-start | bytes 442376 | tf_op jit(solution)/shard_map/ppermute | solution.py:48
  60.2 1.6 %collective-permute-done.7.refs_0_ = f32[36,8,128]{2,1,0:T(8,128)S(1)} collective-permute-done((f32[36,8,128]{2,1,0:T(8,128)S(1)}, f32[36,8,128]{2,1,0:T(8,128)S(1)}, u32[]{:S(2)}, u32[]{:S(2)}) %collective-permute-start.7) | collective-permute-done | bytes 147488 | tf_op jit(solution)/shard_map/ppermute | solution.py:46
  61.8 3.8 %collective-permute-done.8.refs_1_ = f32[36,8,128]{2,1,0:T(8,128)S(1)} collective-permute-done((f32[36,8,128]{2,1,0:T(8,128)S(1)}, f32[36,8,128]{2,1,0:T(8,128)S(1)}, u32[]{:S(2)}, u32[]{:S(2)}) %collective-permute-start.8) | collective-permute-done | bytes 147488 | tf_op jit(solution)/shard_map/ppermute | solution.py:48
  65.7 0.5 collective-permute-start.9
  66.3 4.6 %collective-permute-done.9.refs_2_ = f32[100,4,128]{2,1,0:T(4,128)S(1)} collective-permute-done((f32[100,4,128]{2,1,0:T(4,128)S(1)}, f32[100,4,128]{2,1,0:T(4,128)S(1)}, u32[]{:S(2)}, u32[]{:S(2)}) %collective-permute-start.9) | collective-permute-done | bytes 204832 | tf_op jit(solution)/shard_map/ppermute | solution.py:46
  70.9 2.5 %collective-permute-start.10 = (f32[210,8,128]{2,1,0:T(8,128)S(1)}, f32[210,8,128]{2,1,0:T(8,128)S(1)}, u32[]{:S(2)}, u32[]{:S(2)}) collective-permute-start(f32[210,8,128]{2,1,0:T(8,128)S(1)} %constant_dynamic-update-slice_fusion), channel_id=1, source_target_pairs={{0,1},{1,0},{2,3},{3,2},{4,5},{5,4},{6,7},{7,6},{8,9},{9,8},{10,11... | collective-permute-start | bytes 2580488 | tf_op jit(solution)/shard_map/ppermute | solution.py:46
  73.4 2.0 %collective-permute-done.10.refs_3_ = f32[210,8,128]{2,1,0:T(8,128)S(1)} collective-permute-done((f32[210,8,128]{2,1,0:T(8,128)S(1)}, f32[210,8,128]{2,1,0:T(8,128)S(1)}, u32[]{:S(2)}, u32[]{:S(2)}) %collective-permute-start.10) | collective-permute-done | bytes 860192 | tf_op jit(solution)/shard_map/ppermute | solution.py:46
  75.5 5.2 %shard_map.60 = f32[4,8,16,256]{3,2,1,0:T(8,128)} custom-call(s32[9]{0:T(128)S(1)} %convert_element_type.3.flags, f32[36,8,128]{2,1,0:T(8,128)S(1)} %get-tuple-element.30.own, f32[4,12,24,384]{3,2,1,0:T(8,128)S(1)} %get-tuple-element.31.state, f32[12,24,384]{2,1,0:T(8,128)S(1)} %get-tuple-element.32.weight, f32[4,12,24,384]{3,2,1,0:T(8,128)S(1)} %get-tuple-element.33.rhs, ...), custom_call_target="tpu_custom_call" | custom-call | tf_op jit(solution)/shard_map/pallas_call | solution.py:451
  (40 shorter events, 1.4 us)
Async XLA Ops:
  0.0 11.2 %copy-start = (f32[4,8,16,256]{3,2,1,0:T(8,128)S(1)}, f32[4,8,16,256]{3,2,1,0:T(8,128)}, u32[]{:S(2)}) copy-start(f32[4,8,16,256]{3,2,1,0:T(8,128)} %start_field) | copy-start | bytes 1572868
  0.0 11.2 %copy-start.1 = (f32[4,8,16,256]{3,2,1,0:T(8,128)S(1)}, f32[4,8,16,256]{3,2,1,0:T(8,128)}, u32[]{:S(2)}) copy-start(f32[4,8,16,256]{3,2,1,0:T(8,128)} %right_side) | copy-start | bytes 1572868
  4.5 26.1 %all-to-all-start = ((f32[16,12,8,128]{3,2,1,0:T(8,128)}), f32[16,12,8,128]{3,2,1,0:T(8,128)S(1)}, u32[]{:S(2)}, u32[]{:S(2)}) async-start(f32[16,12,8,128]{3,2,1,0:T(8,128)} %shard_map.55), calls=%async_computation | async-start | bytes 1572864 | tf_op jit(solution)/shard_map/all_to_all | solution.py:501
  11.2 6.3 %copy-start.3 = (s32[3072,1]{0,1:T(1,128)S(1)}, s32[3072,1]{0,1:T(1,128)}, u32[]{:S(2)}) copy-start(s32[3072,1]{0,1:T(1,128)} %param.8) | copy-start | bytes 36868
  11.3 7.0 %copy-start.2 = (s32[3072]{0:T(1024)S(1)}, s32[3072]{0:T(1024)}, u32[]{:S(2)}) copy-start(s32[3072]{0:T(1024)} %param.9) | copy-start | bytes 36868
  11.3 27.9 %collective-permute-start.4 = (f32[64,3,256]{2,1,0:T(4,128)S(1)}, f32[64,3,256]{2,1,0:T(4,128)S(1)}, u32[]{:S(2)}, u32[]{:S(2)}) collective-permute-start(f32[64,3,256]{2,1,0:T(4,128)S(1)} %pad_maximum_fusion.2), channel_id=1, source_target_pairs={{0,2},{2,0},{1,3},{3,1},{4,6},{6,4},{5,7},{7,5},{8,10},{10,8},{9,1... | collective-permute-start | bytes 589832 | tf_op jit(solution)/shard_map/ppermute | solution.py:46
  12.7 23.1 %collective-permute-start = (f32[20,16,256]{2,1,0:T(8,128)S(1)}, f32[20,16,256]{2,1,0:T(8,128)S(1)}, u32[]{:S(2)}, u32[]{:S(2)}) collective-permute-start(f32[20,16,256]{2,1,0:T(8,128)S(1)} %pad_maximum_fusion), channel_id=1, source_target_pairs={{0,4},{4,0},{8,12},{12,8},{16,20},{20,16},{24,28},{28,24},{1,5},{5... | collective-permute-start | bytes 983048 | tf_op jit(solution)/shard_map/ppermute | solution.py:46
  14.7 21.1 %collective-permute-start.1 = (f32[20,16,256]{2,1,0:T(8,128)}, f32[20,16,256]{2,1,0:T(8,128)S(1)}, u32[]{:S(2)}, u32[]{:S(2)}) collective-permute-start(f32[20,16,256]{2,1,0:T(8,128)} %pad_maximum_fusion.1), channel_id=1, source_target_pairs={{4,8},{8,4},{12,16},{16,12},{20,24},{24,20},{5,9},{9,5},{13,17},{1... | collective-permute-start | bytes 983048 | tf_op jit(solution)/shard_map/ppermute | solution.py:48
  31.9 5.6 %collective-permute-start.3 = (f32[2,16,256]{2,1,0:T(8,128)S(1)}, f32[2,16,256]{2,1,0:T(8,128)S(1)}, u32[]{:S(2)}, u32[]{:S(2)}) collective-permute-start(f32[2,16,256]{2,1,0:T(8,128)S(1)} %get-tuple-element.47), channel_id=1, source_target_pairs={{4,8},{8,4},{12,16},{16,12},{20,24},{24,20},{5,9},{9,5},{13,17},{1... | collective-permute-start | bytes 98312 | tf_op jit(solution)/shard_map/ppermute | solution.py:48
  33.8 3.6 %collective-permute-start.2 = (f32[2,16,256]{2,1,0:T(8,128)S(1)}, f32[2,16,256]{2,1,0:T(8,128)S(1)}, u32[]{:S(2)}, u32[]{:S(2)}) collective-permute-start(f32[2,16,256]{2,1,0:T(8,128)S(1)} %get-tuple-element.48), channel_id=1, source_target_pairs={{0,4},{4,0},{8,12},{12,8},{16,20},{20,16},{24,28},{28,24},{1,5},{5... | collective-permute-start | bytes 98312 | tf_op jit(solution)/shard_map/ppermute | solution.py:46
  38.1 3.6 %collective-permute-start.5 = (f32[52,2,256]{2,1,0:T(2,128)S(1)}, f32[52,2,256]{2,1,0:T(2,128)S(1)}, u32[]{:S(2)}, u32[]{:S(2)}) collective-permute-start(f32[52,2,256]{2,1,0:T(2,128)S(1)} %shard_map.57), channel_id=1, source_target_pairs={{0,2},{2,0},{1,3},{3,1},{4,6},{6,4},{5,7},{7,5},{8,10},{10,8},{9,1... | collective-permute-start | bytes 319496 | tf_op jit(solution)/shard_map/ppermute | solution.py:46
  43.5 7.8 %collective-permute-start.6 = (f32[145,16,128]{2,1,0:T(8,128)}, f32[145,16,128]{2,1,0:T(8,128)}, u32[]{:S(2)}, u32[]{:S(2)}) collective-permute-start(f32[145,16,128]{2,1,0:T(8,128)} %shard_map.58), channel_id=1, source_target_pairs={{0,1},{1,0},{2,3},{3,2},{4,5},{5,4},{6,7},{7,6},{8,9},{9,8},{10,11... | collective-permute-start | bytes 3563528 | tf_op jit(solution)/shard_map/ppermute | solution.py:46
  56.6 5.1 %collective-permute-start.7 = (f32[36,8,128]{2,1,0:T(8,128)S(1)}, f32[36,8,128]{2,1,0:T(8,128)S(1)}, u32[]{:S(2)}, u32[]{:S(2)}) collective-permute-start(f32[36,8,128]{2,1,0:T(8,128)S(1)} %get-tuple-element.30.own), channel_id=1, source_target_pairs={{0,4},{4,0},{8,12},{12,8},{16,20},{20,16},{24,28},{28,24},{1,5},{5... | collective-permute-start | bytes 442376 | tf_op jit(solution)/shard_map/ppermute | solution.py:46
  58.1 7.5 %collective-permute-start.8 = (f32[36,8,128]{2,1,0:T(8,128)S(1)}, f32[36,8,128]{2,1,0:T(8,128)S(1)}, u32[]{:S(2)}, u32[]{:S(2)}) collective-permute-start(f32[36,8,128]{2,1,0:T(8,128)S(1)} %get-tuple-element.34), channel_id=1, source_target_pairs={{4,8},{8,4},{12,16},{16,12},{20,24},{24,20},{5,9},{9,5},{13,17},{1... | collective-permute-start | bytes 442376 | tf_op jit(solution)/shard_map/ppermute | solution.py:48
  65.7 5.1 %collective-permute-start.9 = (f32[100,4,128]{2,1,0:T(4,128)S(1)}, f32[100,4,128]{2,1,0:T(4,128)S(1)}, u32[]{:S(2)}, u32[]{:S(2)}) collective-permute-start(f32[100,4,128]{2,1,0:T(4,128)S(1)} %pad_maximum_fusion.3), channel_id=1, source_target_pairs={{0,2},{2,0},{1,3},{3,1},{4,6},{6,4},{5,7},{7,5},{8,10},{10,8},{9,1... | collective-permute-start | bytes 614408 | tf_op jit(solution)/shard_map/ppermute | solution.py:46
  70.9 4.5 %collective-permute-start.10 = (f32[210,8,128]{2,1,0:T(8,128)S(1)}, f32[210,8,128]{2,1,0:T(8,128)S(1)}, u32[]{:S(2)}, u32[]{:S(2)}) collective-permute-start(f32[210,8,128]{2,1,0:T(8,128)S(1)} %constant_dynamic-update-slice_fusion), channel_id=1, source_target_pairs={{0,1},{1,0},{2,3},{3,2},{4,5},{5,4},{6,7},{7,6},{8,9},{9,8},{10,11... | collective-permute-start | bytes 2580488 | tf_op jit(solution)/shard_map/ppermute | solution.py:46

commit v6 on v5

--- a/solution.py
+++ b/solution.py
@@ -43,41 +43,16 @@
 def swap(axis, message):
     count = lax.axis_size(axis)
     even = lax.axis_index(axis) % 2 == 0
-    got = [lax.ppermute(message(even, 0), axis, pairs(count, 0))]
-    if count > 2:
-        got.append(lax.ppermute(message(~even, 1), axis, pairs(count, 1)))
+    got = [lax.ppermute(message(~even, 1), axis, pairs(count, 1))] if count > 2 else []
+    got.insert(0, lax.ppermute(message(even, 0), axis, pairs(count, 0)))
     return got
-
-
-def ride(messages, n, extra):
-    return jnp.concatenate([*messages, *([extra[n]] if extra else [])], axis=0)
 
 
 def halo_x(groups):
     return swap("gx", lambda up, n: flat([cut(v, 1, w, up) for v, w in groups]))
 
 
-def halo_y(groups, depth, xs=(), extra=()):
-    own = lambda up: [cut(v.reshape(-1, *v.shape[2:]), 1, depth, up) for v, _ in groups]
-    return swap("gy", lambda up, n: ride([*own(up), *[cut(x, 1, depth, up) for x in xs]], n, extra))
-
-
-def halo_z(groups, xs, ys, extra=()):
-    rows = groups[0][0].shape[2]
-
-    def last(up, n):
-        sent = [flat([cut(v, 3, LANES, up) for v, _ in groups]), *[cut(x, 2, LANES, up) for x in xs]]
-        for parts in ys:
-            edge = [jnp.pad(cut(y, 2, LANES, up), ((0, 0), (0, PAD - y.shape[1]), (0, 0))) for y in parts]
-            edge = jnp.concatenate(edge, axis=0)
-            edge = jnp.pad(edge, ((0, -edge.shape[0] % (rows // PAD)), (0, 0), (0, 0)))
-            sent.append(edge.reshape(-1, rows, LANES))
-        return ride(sent, n, extra)
-
-    return swap("lvl", last)
-
-
-def place_halo(dst, margin, own, got, flags, width, depth, group=(0, 0), slabs=None, corner=0, base=(0, 0)):
+def place_halo(dst, margin, own, got, flags, width, depth, group=(0, 0), slabs=None, corner=0, base=(0, 0), early=()):
     xs, ys, zs = got
     rows, lanes = own.shape[-2:]
     fields, planes, total = dst.shape[0], dst.shape[1] - 2 * margin, dst.shape[2]
@@ -89,7 +64,10 @@
     near = (lax.broadcasted_iota(jnp.int32, (1, LANES), 1) < LANES // 2) == even_z
 
     def edge(at, row, size):
-        at, part = base[1] + at, slice(row, row + size)
+        part = slice(row, row + size)
+        if early and at < own_slabs:
+            return jnp.where(near, early[0][at, part], 0.0 if len(zs) == 1 else early[1][at, part])
+        at = base[1] + at - (own_slabs if early else 0)
         return jnp.where(near, zs[0][at, part], 0.0 if len(zs) == 1 else zs[1][at, part])
 
     for f in range(fields):
@@ -208,25 +186,27 @@
     return sums, grads + [spread]
 
 
-def pack_kernel(tile_ref, mask_ref, out_ref, used_ref, *, capacity):
+def pack_kernel(tile_ref, mask_ref, out_ref, used_ref, rows_ref, *, capacity):
     tiles = out_ref.shape[0]
-    count = mask_ref.shape[0]
+    count, width = mask_ref.shape
     out_ref[...] = jnp.zeros(out_ref.shape, jnp.float32)
+    for r in range(0, count, 8):
+        rows_ref[r:r + 8] = mask_ref[r:r + 8].reshape(8, width // LANES, LANES)
 
     def clear(t, _):
         used_ref[t] = 0
         return 0
 
-    lax.fori_loop(0, tiles, clear, 0)
+    lax.fori_loop(0, tiles, clear, 0, unroll=8)
 
     def row(r, _):
         t = tile_ref[r]
         n = used_ref[t]
         used_ref[t] = n + 1
-        out_ref[t, jnp.minimum(n, capacity - 1)] = mask_ref[r]
+        out_ref[t, jnp.minimum(n, capacity - 1)] = rows_ref[r]
         return 0
 
-    lax.fori_loop(0, count, row, 0)
+    lax.fori_loop(0, count, row, 0, unroll=8)
 
 
 def split(refs, nums):
@@ -270,52 +250,53 @@
     return jnp.where(up, high, low)
 
 
-def y_kernel(flags, *refs, nums):
-    (chi_x, first_x), outs = split(refs[1:], [nums[0]] * 2)
+def y_kernel(flags, *refs, take, order, added):
+    ready, (_, *outs) = split(refs[len(take):], [added])
     for n, out in enumerate(outs):
         up = (flags[1] == 1) == (n == 0)
         at = 0
-        for ref in (refs[0], *chi_x, *first_x):
-            for s in range(ref.shape[0]):
+        for i in order:
+            ref, count = refs[i], take[i]
+            for s in range(count):
                 out[at] = side(up, ref[s], 0, out.shape[1])
                 at += 1
-
-
-def z_kernel(flags, *refs, nums):
-    (chi, chi_x, start, rhs, first_x, first_y, corners), outs = split(refs, [1, nums[0], 1, 1, nums[0], nums[1], nums[1]])
-    rows = chi[0].shape[1]
-    per = rows // PAD
-    chi_slabs = chi[0].shape[0] + sum(x.shape[0] for x in chi_x)
+        if added:
+            out[at:] = ready[0][n][...]
+
+
+def z_kernel(flags, *refs, plan, count, added):
+    ready, outs = split(refs[count:], [added])
     for n, out in enumerate(outs):
         up = (flags[2] == 1) == (n == 0)
+        per = out.shape[1] // PAD
         at = 0
-        for slabs, edges in (
-            ((*chi, *chi_x), [[(c, 0, chi_slabs)] for c in corners]),
-            ((*start, *rhs, *first_x), [[(y, 0, y.shape[0]), (c, chi_slabs, c.shape[0])] for y, c in zip(first_y, corners)]),
-        ):
-            for ref in slabs:
-                for s in range(ref.shape[0]):
-                    out[at] = side(up, ref[s], 1, LANES)
+        for slabs, edges in plan:
+            for i, low, high in slabs:
+                for s in range(low, high):
+                    out[at] = side(up, refs[i][s], 1, LANES)
                     at += 1
             for parts in edges:
                 k = 0
-                for ref, low, high in parts:
+                for i, low, high in parts:
                     for s in range(low, high):
-                        depth = ref.shape[1]
+                        depth = refs[i].shape[1]
                         row = k % per * PAD
-                        out[at + k // per, row:row + depth] = side(up, ref[s], 1, LANES)
-                        out[at + k // per, row + depth:row + PAD] = jnp.zeros((PAD - depth, LANES), jnp.float32)
+                        out[at + k // per, row:row + depth] = side(up, refs[i][s], 1, LANES)
+                        if depth < PAD:
+                            out[at + k // per, row + depth:row + PAD] = jnp.zeros((PAD - depth, LANES), jnp.float32)
                         k += 1
                 while k % per:
                     row = k % per * PAD
                     out[at + k // per, row:row + PAD] = jnp.zeros((PAD, LANES), jnp.float32)
                     k += 1
                 at += k // per
+        if added:
+            out[at:] = ready[0][n][...]
 
 
 def second_kernel(flags, own, pooled_chi, right_side, start_field, *refs, nums):
     n_x, n_y, n_z = nums
-    (chi_x, first_x, first_y, far_y, far_z), refs = split(refs, [n_x, n_x, n_y, n_y, n_z])
+    (chi_x, first_x, first_y, first_z, far_y, far_z), refs = split(refs, [n_x, n_x, n_y, n_z, n_y, n_z])
     rhs, state_out, weight_out = refs[:3]
     (x_out, y_out, z_out), (chi, start, ext, tmp, pooled) = split(refs[3:], nums)
     _, planes, rows, lanes = own.shape
@@ -325,8 +306,8 @@
     slabs = (8 * planes, 4 * (START_W + FINE_W))
     fields_got = (first_x, (*first_y, *far_y), far_z)
     place_halo(chi, FINE_W, own, (chi_x, far_y, far_z), flags, FINE_W, FINE_W)
-    place_halo(start, START_W, start_field, fields_got, flags, START_W, START_W, (0, 0), slabs, CORNER, base)
-    place_halo(rhs, FINE_W, right_side, fields_got, flags, FINE_W, START_W, (4 * planes, 4 * START_W), slabs, CORNER, base)
+    place_halo(start, START_W, start_field, fields_got, flags, START_W, START_W, (0, 0), slabs, CORNER, base, first_z)
+    place_halo(rhs, FINE_W, right_side, fields_got, flags, FINE_W, START_W, (4 * planes, 4 * START_W), slabs, CORNER, base, first_z)
     mask = inside(flags, rows, lanes, total, FINE_W)
     w_p = (RELAX / (SHIFT + 6.0)) * mask
 
@@ -379,7 +360,7 @@
     rows, lanes = own.shape[1:]
     total, wide = ext.shape[2], ext.shape[3]
     own = own.at[0:5 * planes]
-    place_halo(ext, COARSE_W, own, got, flags, COARSE_W, COARSE_W)
+    place_halo(ext, COARSE_W, own, got[:3], flags, COARSE_W, COARSE_W)
     x_slabs = 5 * COARSE_W
     slabs = 5 * planes + len(got[0]) * x_slabs
     z_slabs = slabs + len(got[1]) * -(-slabs // (rows // PAD))
@@ -494,8 +475,8 @@
     (outgoing,) = call(
         functools.partial(pack_kernel, capacity=capacity),
         [(tiles, capacity, width // LANES, LANES)],
-        [pltpu.SMEM((tiles,), jnp.int32)],
-        my_tiles, mask_blocks.reshape(per_device, width // LANES, LANES),
+        [pltpu.SMEM((tiles,), jnp.int32), pltpu.VMEM((per_device, width // LANES, LANES), jnp.float32)],
+        my_tiles, mask_blocks,
     )
     outgoing, right_side, start_field = lax.optimization_barrier((outgoing, right_side, start_field))
     arrived = lax.all_to_all(outgoing, ("gx", "gy"), split_axis=0, concat_axis=0, tiled=True)
@@ -506,7 +487,9 @@
     pair_counts = [1 + (n > 2) for n in counts]
     groups = [(start_field, START_W), (right_side, FINE_W)]
     first_x = halo_x(groups)
-    first_y = halo_y(groups, START_W)
+    first_y = swap("gy", lambda up, n: flat([cut(v, 2, START_W, up) for v, _ in groups]))
+    first_z = swap("lvl", lambda up, n: flat([cut(v, 3, LANES, up) for v, _ in groups]))
+    first_y, first_z, slot_of = lax.optimization_barrier((first_y, first_z, slot_of))
     chi, pooled_chi = call(
         chi_kernel,
         [(1, planes, rows, lanes), (c_planes, c_rows, lanes)],
@@ -519,20 +502,35 @@
     slabs = lambda v: v.reshape(-1, rows, lanes)
     far_x = len(first_x) * 4 * (START_W + FINE_W)
     chi_slabs = planes + len(chi_x) * FINE_W
+    n_x, n_y, n_z = pair_counts
     y_sent = call(
-        functools.partial(y_kernel, nums=pair_counts),
-        [(chi_slabs + far_x, CORNER, lanes)] * pair_counts[1],
+        functools.partial(
+            y_kernel,
+            take=[planes, *[x.shape[0] for x in (*chi_x[::-1], *first_x[::-1])]],
+            order=[0, *range(n_x, 0, -1), *range(2 * n_x, n_x, -1)],
+            added=0,
+        ),
+        [(chi_slabs + far_x, CORNER, lanes)] * n_y,
         [],
-        flags, slabs(chi), *chi_x, *first_x,
+        flags, slabs(chi), *chi_x[::-1], *first_x[::-1], chi_x[0][0, :1, :LANES],
     )
     far_y = swap("gy", lambda up, n: y_sent[n])
     per = rows // PAD
     edges = -(-chi_slabs // per) + -(-(8 * planes + far_x) // per)
+    whole = lambda first, refs: [(first + i, 0, r.shape[0]) for i, r in enumerate(refs)]
+    far_at = 1 + 2 * n_x + n_y
+    plan = [
+        ([(0, 0, planes), *whole(1, chi_x)], [[(far_at + n, 0, chi_slabs)] for n in range(n_y)]),
+        (
+            whole(1 + n_x, first_x),
+            [[(1 + 2 * n_x + n, 0, 8 * planes), (far_at + n, chi_slabs, chi_slabs + far_x)] for n in range(n_y)],
+        ),
+    ]
     z_sent = call(
-        functools.partial(z_kernel, nums=pair_counts),
-        [(chi_slabs + 8 * planes + far_x + pair_counts[1] * edges, rows, LANES)] * pair_counts[2],
+        functools.partial(z_kernel, plan=plan, count=far_at + n_y, added=0),
+        [(chi_slabs + far_x + n_y * edges, rows, LANES)] * n_z,
         [],
-        flags, slabs(chi), *chi_x, slabs(start_field), slabs(right_side), *first_x, *first_y, *far_y,
+        flags, slabs(chi), *chi_x, *first_x, *first_y, *far_y,
     )
     far_z = swap("lvl", lambda up, n: z_sent[n])
     c_slabs, s_slabs = 5 * c_planes, 4 * (rows // 8) * (lanes // LANES)
@@ -548,15 +546,27 @@
             pltpu.VMEM((4, lanes // LANES, rows, LANES), jnp.float32),
             pltpu.VMEM((5, c_planes, c_rows, lanes), jnp.float32),
         ],
-        flags, chi, pooled_chi, right_side, start_field, *chi_x, *first_x, *first_y, *far_y, *far_z,
+        flags, chi, pooled_chi, right_side, start_field, *chi_x, *first_x, *first_y, *first_z, *far_y, *far_z,
     )
     (x_out, y_out, z_out), _ = split(sent, pair_counts)
-    group = [(x_out[0][:c_slabs].reshape(5, c_planes, c_rows, c_lanes), COARSE_W)]
     last_x = swap("gx", lambda up, n: x_out[n])
-    halo_slabs = [x[:5 * COARSE_W] for x in last_x]
-    last_y = halo_y(group, COARSE_W, halo_slabs, y_out)
-    slabs = c_slabs + len(last_x) * 5 * COARSE_W
-    last_z = halo_z(group, halo_slabs, [[y[:slabs]] for y in last_y], z_out)
+    take = [c_slabs, *[5 * COARSE_W] * n_x]
+    y_sent = call(
+        functools.partial(y_kernel, take=take, order=[0, *range(n_x, 0, -1)], added=n_y),
+        [(sum(take) + y_out[0].shape[0], COARSE_W, c_lanes)] * n_y,
+        [],
+        flags, x_out[0], *last_x[::-1], *y_out, last_x[0][0, :1, :LANES],
+    )
+    last_y = swap("gy", lambda up, n: y_sent[n])
+    plan = [([(i, 0, t) for i, t in enumerate(take)], [[(1 + n_x + n, 0, sum(take))] for n in range(n_y)])]
+    z_slabs = sum(take) + n_y * -(-sum(take) // (c_rows // PAD))
+    z_sent = call(
+        functools.partial(z_kernel, plan=plan, count=1 + n_x + n_y, added=n_z),
+        [(z_slabs + z_out[0].shape[0], c_rows, LANES)] * n_z,
+        [],
+        flags, x_out[0], *last_x, *last_y, *z_out,
+    )
+    last_z = swap("lvl", lambda up, n: z_sent[n])
     c_ext = (c_planes + 2 * COARSE_W, c_rows + 8, c_lanes + LANES)
     (out,) = call(
         functools.partial(last_kernel, nums=pair_counts),

time: 80.9 us -> 78.4 us (0.969)
  waiting for transfers between devices: 30.6 us -> 26.1 us
  other arithmetic: 2.17 us -> 4.27 us
  starting transfers between devices: 27.6 us -> 28.9 us
  Pallas kernels: 16.9 us -> 15.7 us
    all_to_all x1, waiting for transfers between devices: 11.5 us -> 6.17 us  [body(): lax.all_to_all(outgoing, ('gx', 'gy'), split_axis=0, concat_axis=0, tiled...]
    concatenate x2 -> x4, other arithmetic: 0.77 us -> 3.07 us  [flat(): jnp.concatenate([p.reshape(-1, *p.shape[-2:]) for p in parts], axis=0)]
    ppermute x11 -> x12, starting transfers between devices: 20.9 us -> 22.3 us  [the longest x9 16 us: swap(): got.insert(0, lax.ppermute(message(even, 0), axis, pairs(count, 0)))]
    pallas_call x6 -> x8, Pallas kernels: 16.9 us -> 15.7 us  [call(): pl.pallas_call(kernel, out_shape=outs, in_specs=[SMEM] * smem + [VMEM] *...]
    ppermute x11 -> x12, waiting for transfers between devices: 19.1 us -> 19.9 us  [the longest x9 14.4 us: swap(): got.insert(0, lax.ppermute(message(even, 0), axis, pairs(count, 0)))]
    unnamed x15 -> x12, local copies, waits for them, and re-layouts: 1.8 us -> 1.5 us
  transfers between devices with their start and end apart: 12 -> 13, of which waited for: 9 -> 10; matrix products, arithmetic and copies ran while one was open for 4% -> 7% of each run, Pallas kernels for 2% -> 2%
where the time goes in v6:
time: 78.4 us; the launch traced here: 78.2 us
  starting transfers between devices  28.9 us (37%)
  waiting for transfers between devices  26.1 us (33%)
  Pallas kernels  15.7 us (20%)
  other arithmetic  4.27 us (5%)
  local copies, waits for them, and re-layouts  2.95 us (4%)
    ppermute x9, starting transfers between devices, swap(): got.insert(0, lax.ppermute(message(even, 0), axis, pairs(count, 0)))  16 us
    pallas_call x8, Pallas kernels, call(): pl.pallas_call(kernel, out_shape=outs, in_specs=[SMEM] * smem + [VMEM] *...  15.7 us
    ppermute x9, waiting for transfers between devices, swap(): got.insert(0, lax.ppermute(message(even, 0), axis, pairs(count, 0)))  14.4 us
    all_to_all x1, starting transfers between devices, body(): lax.all_to_all(outgoing, ('gx', 'gy'), split_axis=0, concat_axis=0, tiled...  6.64 us
    ppermute x3, starting transfers between devices, swap(): lax.ppermute(message(~even, 1), axis, pairs(count, 1))  6.21 us
    all_to_all x1, waiting for transfers between devices, body(): lax.all_to_all(outgoing, ('gx', 'gy'), split_axis=0, concat_axis=0, tiled...  6.17 us
    ppermute x3, waiting for transfers between devices, swap(): lax.ppermute(message(~even, 1), axis, pairs(count, 1))  5.5 us
    concatenate x4, other arithmetic, flat(): jnp.concatenate([p.reshape(-1, *p.shape[-2:]) for p in parts], axis=0)  3.07 us
  transfers between devices with their start and end apart: 13, of which 10 were waited for; matrix products, arithmetic and copies ran while one was open for 7% of the time, Pallas kernels for 2%

profile of v6, /device:TPU:9, one launch (start us, length us, event | category | flops | bytes accessed | tf_op | source)
XLA Modules:
  0.0 78.2 jit_solution(11394124463548751028)
XLA Ops:
  0.0 0.8 %fusion.1.tile_ref = s32[96]{0:T(128)S(1)} fusion(s32[3072,1]{0,1:T(1,128)} %param.8, s32[]{:T(128)S(6)} %select_n.75), kind=kLoop, calls=%fused_computation.24 | loop fusion | bytes 772 | tf_op jit(solution)/shard_map/dynamic_slice | solution.py:474
  0.8 1.0 %copy-done.2 = f32[96,1024]{1,0:T(8,128)S(1)} copy-done((f32[96,1024]{1,0:T(8,128)S(1)}, f32[96,1024]{1,0:T(8,128)}, u32[]{:S(2)}) %copy-start.2) | copy-done | bytes 393240
  1.8 2.0 %shard_map.55 = f32[16,12,8,128]{3,2,1,0:T(8,128)} custom-call(s32[96]{0:T(128)S(1)} %fusion.1.tile_ref, f32[96,1024]{1,0:T(8,128)S(1)} %copy-done.2), custom_call_target="tpu_custom_call" | custom-call | tf_op jit(solution)/shard_map/pallas_call | solution.py:432
  3.9 6.6 %all-to-all-start = ((f32[16,12,8,128]{3,2,1,0:T(8,128)}), f32[16,12,8,128]{3,2,1,0:T(8,128)S(1)}, u32[]{:S(2)}, u32[]{:S(2)}) async-start(f32[16,12,8,128]{3,2,1,0:T(8,128)} %shard_map.55), calls=%async_computation | async-start | bytes 1572864 | tf_op jit(solution)/shard_map/all_to_all | solution.py:482
  10.6 0.8 pad_maximum_fusion.3
  11.4 1.2 %collective-permute-start = (f32[64,3,256]{2,1,0:T(4,128)}, f32[64,3,256]{2,1,0:T(4,128)S(1)}, u32[]{:S(2)}, u32[]{:S(2)}) collective-permute-start(f32[64,3,256]{2,1,0:T(4,128)} %pad_maximum_fusion.3), channel_id=1, source_target_pairs={{0,2},{2,0},{1,3},{3,1},{4,6},{6,4},{5,7},{7,5},{8,10},{10,8},{9,1... | collective-permute-start | bytes 589832 | tf_op jit(solution)/shard_map/ppermute | solution.py:47
  12.6 0.7 pad_maximum_fusion.1
  13.4 1.2 %collective-permute-start.2 = (f32[20,16,256]{2,1,0:T(8,128)}, f32[20,16,256]{2,1,0:T(8,128)S(1)}, u32[]{:S(2)}, u32[]{:S(2)}) collective-permute-start(f32[20,16,256]{2,1,0:T(8,128)} %pad_maximum_fusion.1), channel_id=1, source_target_pairs={{0,4},{4,0},{8,12},{12,8},{16,20},{20,16},{24,28},{28,24},{1,5},{5... | collective-permute-start | bytes 983048 | tf_op jit(solution)/shard_map/ppermute | solution.py:47
  14.6 0.7 pad_maximum_fusion.2
  15.3 2.2 %collective-permute-start.3 = (f32[20,16,256]{2,1,0:T(8,128)}, f32[20,16,256]{2,1,0:T(8,128)S(1)}, u32[]{:S(2)}, u32[]{:S(2)}) collective-permute-start(f32[20,16,256]{2,1,0:T(8,128)} %pad_maximum_fusion.2), channel_id=1, source_target_pairs={{4,8},{8,4},{12,16},{16,12},{20,24},{24,20},{5,9},{9,5},{13,17},{1... | collective-permute-start | bytes 983048 | tf_op jit(solution)/shard_map/ppermute | solution.py:46
  17.6 0.8 %pad_maximum_fusion = f32[64,16,128]{2,1,0:T(8,128)} fusion(f32[32,16,128]{2,1,0:T(8,128)S(1)} %bitcast.35, f32[32,16,128]{2,1,0:T(8,128)S(1)} %bitcast.36), kind=kLoop, calls=%fused_computation.1 | loop fusion | flops 131072 | bytes 1048576 | tf_op jit(solution)/shard_map/concatenate | solution.py:40
  18.4 2.1 %collective-permute-start.1 = (f32[64,16,128]{2,1,0:T(8,128)}, f32[64,16,128]{2,1,0:T(8,128)S(1)}, u32[]{:S(2)}, u32[]{:S(2)}) collective-permute-start(f32[64,16,128]{2,1,0:T(8,128)} %pad_maximum_fusion), channel_id=1, source_target_pairs={{0,1},{1,0},{2,3},{3,2},{4,5},{5,4},{6,7},{7,6},{8,9},{9,8},{10,11... | collective-permute-start | bytes 1572872 | tf_op jit(solution)/shard_map/ppermute | solution.py:47
  22.6 1.2 %collective-permute-done.refs_5_.refs_4_ = f32[64,3,256]{2,1,0:T(4,128)S(1)} collective-permute-done((f32[64,3,256]{2,1,0:T(4,128)}, f32[64,3,256]{2,1,0:T(4,128)S(1)}, u32[]{:S(2)}, u32[]{:S(2)}) %collective-permute-start) | collective-permute-done | bytes 196640 | tf_op jit(solution)/shard_map/ppermute | solution.py:47
  23.8 6.2 %all-to-all-done.rows_ref = f32[16,12,8,128]{3,2,1,0:T(8,128)S(1)} async-done(((f32[16,12,8,128]{3,2,1,0:T(8,128)}), f32[16,12,8,128]{3,2,1,0:T(8,128)S(1)}, u32[]{:S(2)}, u32[]{:S(2)}) %all-to-all-start) | async-done | bytes 786464 | tf_op jit(solution)/shard_map/all_to_all | solution.py:482
  30.0 1.4 %shard_map.56 = (f32[1,8,16,256]{3,2,1,0:T(8,128)S(1)}, f32[4,8,256]{2,1,0:T(8,128)S(1)}) custom-call(s32[192]{0:T(256)S(1)} %add.59.slot_ref, f32[16,12,8,128]{3,2,1,0:T(8,128)S(1)} %all-to-all-done.rows_ref), custom_call_target="tpu_custom_call" | custom-call | tf_op jit(solution)/shard_map/pallas_call | solution.py:432
  31.4 1.9 %collective-permute-start.5 = (f32[2,16,256]{2,1,0:T(8,128)S(1)}, f32[2,16,256]{2,1,0:T(8,128)S(1)}, u32[]{:S(2)}, u32[]{:S(2)}) collective-permute-start(f32[2,16,256]{2,1,0:T(8,128)S(1)} %get-tuple-element.47), channel_id=1, source_target_pairs={{4,8},{8,4},{12,16},{16,12},{20,24},{24,20},{5,9},{9,5},{13,17},{1... | collective-permute-start | bytes 98312 | tf_op jit(solution)/shard_map/ppermute | solution.py:46
  33.4 1.3 %collective-permute-start.4 = (f32[2,16,256]{2,1,0:T(8,128)S(1)}, f32[2,16,256]{2,1,0:T(8,128)S(1)}, u32[]{:S(2)}, u32[]{:S(2)}) collective-permute-start(f32[2,16,256]{2,1,0:T(8,128)S(1)} %get-tuple-element.48), channel_id=1, source_target_pairs={{0,4},{4,0},{8,12},{12,8},{16,20},{20,16},{24,28},{28,24},{1,5},{5... | collective-permute-start | bytes 98312 | tf_op jit(solution)/shard_map/ppermute | solution.py:47
  35.3 1.7 %collective-permute-done.5.refs_1_.refs_2_ = f32[2,16,256]{2,1,0:T(8,128)S(1)} collective-permute-done((f32[2,16,256]{2,1,0:T(8,128)S(1)}, f32[2,16,256]{2,1,0:T(8,128)S(1)}, u32[]{:S(2)}, u32[]{:S(2)}) %collective-permute-start.5) | collective-permute-done | bytes 32800 | tf_op jit(solution)/shard_map/ppermute | solution.py:46
  37.6 1.0 %collective-permute-start.6 = (f32[52,2,256]{2,1,0:T(2,128)S(1)}, f32[52,2,256]{2,1,0:T(2,128)S(1)}, u32[]{:S(2)}, u32[]{:S(2)}) collective-permute-start(f32[52,2,256]{2,1,0:T(2,128)S(1)} %shard_map.57), channel_id=1, source_target_pairs={{0,2},{2,0},{1,3},{3,1},{4,6},{6,4},{5,7},{7,5},{8,10},{10,8},{9,1... | collective-permute-start | bytes 319496 | tf_op jit(solution)/shard_map/ppermute | solution.py:47
  38.6 2.6 %collective-permute-done.6.refs_6_ = f32[52,2,256]{2,1,0:T(2,128)S(1)} collective-permute-done((f32[52,2,256]{2,1,0:T(2,128)S(1)}, f32[52,2,256]{2,1,0:T(2,128)S(1)}, u32[]{:S(2)}, u32[]{:S(2)}) %collective-permute-start.6) | collective-permute-done | bytes 106528 | tf_op jit(solution)/shard_map/ppermute | solution.py:47
  41.2 0.7 shard_map.58
  41.9 4.7 %collective-permute-start.7 = (f32[81,16,128]{2,1,0:T(8,128)S(1)}, f32[81,16,128]{2,1,0:T(8,128)S(1)}, u32[]{:S(2)}, u32[]{:S(2)}) collective-permute-start(f32[81,16,128]{2,1,0:T(8,128)S(1)} %shard_map.58), channel_id=1, source_target_pairs={{0,1},{1,0},{2,3},{3,2},{4,5},{5,4},{6,7},{7,6},{8,9},{9,8},{10,11... | collective-permute-start | bytes 1990664 | tf_op jit(solution)/shard_map/ppermute | solution.py:47
  46.5 1.7 %collective-permute-done.7.refs_7_ = f32[81,16,128]{2,1,0:T(8,128)S(1)} collective-permute-done((f32[81,16,128]{2,1,0:T(8,128)S(1)}, f32[81,16,128]{2,1,0:T(8,128)S(1)}, u32[]{:S(2)}, u32[]{:S(2)}) %collective-permute-start.7) | collective-permute-done | bytes 663584 | tf_op jit(solution)/shard_map/ppermute | solution.py:47
  48.3 4.7 %shard_map.59 = (f32[4,12,24,384]{3,2,1,0:T(8,128)S(1)}, f32[4,12,24,384]{3,2,1,0:T(8,128)S(1)}, f32[12,24,384]{2,1,0:T(8,128)S(1)}, f32[36,8,128]{2,1,0:T(8,128...) custom-call(s32[9]{0:T(128)S(1)} %convert_element_type.3.flags, ...), custom_call_target="tpu_custom_call" | custom-call | tf_op jit(solution)/shard_map/pallas_call | solution.py:432
  52.9 1.7 %collective-permute-start.8 = (f32[36,8,128]{2,1,0:T(8,128)S(1)}, f32[36,8,128]{2,1,0:T(8,128)S(1)}, u32[]{:S(2)}, u32[]{:S(2)}) collective-permute-start(f32[36,8,128]{2,1,0:T(8,128)S(1)} %get-tuple-element.36.refs_0_.own), channel_id=1, source_target_pairs={{0,4},{4,0},{8,12},{12,8},{16,20},{20,16},{24,28},{28,24},{1,5},{5... | collective-permute-start | bytes 442376 | tf_op jit(solution)/shard_map/ppermute | solution.py:47
  54.6 2.1 %collective-permute-start.9 = (f32[36,8,128]{2,1,0:T(8,128)S(1)}, f32[36,8,128]{2,1,0:T(8,128)S(1)}, u32[]{:S(2)}, u32[]{:S(2)}) collective-permute-start(f32[36,8,128]{2,1,0:T(8,128)S(1)} %get-tuple-element.40), channel_id=1, source_target_pairs={{4,8},{8,4},{12,16},{16,12},{20,24},{24,20},{5,9},{9,5},{13,17},{1... | collective-permute-start | bytes 442376 | tf_op jit(solution)/shard_map/ppermute | solution.py:46
  56.7 1.6 %collective-permute-done.8.refs_2_.refs_1_.refs_0_ = f32[36,8,128]{2,1,0:T(8,128)S(1)} collective-permute-done((f32[36,8,128]{2,1,0:T(8,128)S(1)}, f32[36,8,128]{2,1,0:T(8,128)S(1)}, u32[]{:S(2)}, u32[]{:S(2)}) %collective-permute-start.8) | collective-permute-done | bytes 147488 | tf_op jit(solution)/shard_map/ppermute | solution.py:47
  58.4 3.8 %collective-permute-done.9.refs_1_.refs_2_ = f32[36,8,128]{2,1,0:T(8,128)S(1)} collective-permute-done((f32[36,8,128]{2,1,0:T(8,128)S(1)}, f32[36,8,128]{2,1,0:T(8,128)S(1)}, u32[]{:S(2)}, u32[]{:S(2)}) %collective-permute-start.9) | collective-permute-done | bytes 147488 | tf_op jit(solution)/shard_map/ppermute | solution.py:46
  63.2 4.6 %collective-permute-done.10.refs_3_.refs_2_ = f32[100,4,128]{2,1,0:T(4,128)S(1)} collective-permute-done((f32[100,4,128]{2,1,0:T(4,128)S(1)}, f32[100,4,128]{2,1,0:T(4,128)S(1)}, u32[]{:S(2)}, u32[]{:S(2)}) %collective-permute-start.10) | collective-permute-done | bytes 204832 | tf_op jit(solution)/shard_map/ppermute | solution.py:47
  68.4 2.5 %collective-permute-start.11 = (f32[210,8,128]{2,1,0:T(8,128)S(1)}, f32[210,8,128]{2,1,0:T(8,128)S(1)}, u32[]{:S(2)}, u32[]{:S(2)}) collective-permute-start(f32[210,8,128]{2,1,0:T(8,128)S(1)} %shard_map.61), channel_id=1, source_target_pairs={{0,1},{1,0},{2,3},{3,2},{4,5},{5,4},{6,7},{7,6},{8,9},{9,8},{10,11... | collective-permute-start | bytes 2580488 | tf_op jit(solution)/shard_map/ppermute | solution.py:47
  70.9 2.0 %collective-permute-done.11.refs_3_ = f32[210,8,128]{2,1,0:T(8,128)S(1)} collective-permute-done((f32[210,8,128]{2,1,0:T(8,128)S(1)}, f32[210,8,128]{2,1,0:T(8,128)S(1)}, u32[]{:S(2)}, u32[]{:S(2)}) %collective-permute-start.11) | collective-permute-done | bytes 860192 | tf_op jit(solution)/shard_map/ppermute | solution.py:47
  72.9 5.2 %shard_map.62 = f32[4,8,16,256]{3,2,1,0:T(8,128)} custom-call(s32[9]{0:T(128)S(1)} %convert_element_type.3.flags, f32[36,8,128]{2,1,0:T(8,128)S(1)} %get-tuple-element.36.refs_0_.own, f32[4,12,24,384]{3,2,1,0:T(8,128)S(1)} %get-tuple-element.37.state, f32[12,24,384]{2,1,0:T(8,128)S(1)} %get-tuple-element.38.weight, ...), custom_call_target="tpu_custom_call" | custom-call | tf_op jit(solution)/shard_map/pallas_call | solution.py:432
  (39 shorter events, 5.1 us)
Async XLA Ops:
  0.0 10.5 %copy-start = (f32[4,8,16,256]{3,2,1,0:T(8,128)S(1)}, f32[4,8,16,256]{3,2,1,0:T(8,128)}, u32[]{:S(2)}) copy-start(f32[4,8,16,256]{3,2,1,0:T(8,128)} %start_field) | copy-start | bytes 1572868
  0.0 10.5 %copy-start.1 = (f32[4,8,16,256]{3,2,1,0:T(8,128)S(1)}, f32[4,8,16,256]{3,2,1,0:T(8,128)}, u32[]{:S(2)}) copy-start(f32[4,8,16,256]{3,2,1,0:T(8,128)} %right_side) | copy-start | bytes 1572868
  0.8 1.0 %copy-start.2 = (f32[96,1024]{1,0:T(8,128)S(1)}, f32[96,1024]{1,0:T(8,128)}, u32[]{:S(2)}) copy-start(f32[96,1024]{1,0:T(8,128)} %mask_ref.1) | copy-start | bytes 1179652
  3.9 26.1 %all-to-all-start = ((f32[16,12,8,128]{3,2,1,0:T(8,128)}), f32[16,12,8,128]{3,2,1,0:T(8,128)S(1)}, u32[]{:S(2)}, u32[]{:S(2)}) async-start(f32[16,12,8,128]{3,2,1,0:T(8,128)} %shard_map.55), calls=%async_computation | async-start | bytes 1572864 | tf_op jit(solution)/shard_map/all_to_all | solution.py:482
  11.4 12.4 %collective-permute-start = (f32[64,3,256]{2,1,0:T(4,128)}, f32[64,3,256]{2,1,0:T(4,128)S(1)}, u32[]{:S(2)}, u32[]{:S(2)}) collective-permute-start(f32[64,3,256]{2,1,0:T(4,128)} %pad_maximum_fusion.3), channel_id=1, source_target_pairs={{0,2},{2,0},{1,3},{3,1},{4,6},{6,4},{5,7},{7,5},{8,10},{10,8},{9,1... | collective-permute-start | bytes 589832 | tf_op jit(solution)/shard_map/ppermute | solution.py:47
  12.6 8.4 %copy-start.4 = (s32[3072,1]{0,1:T(1,128)S(1)}, s32[3072,1]{0,1:T(1,128)}, u32[]{:S(2)}) copy-start(s32[3072,1]{0,1:T(1,128)} %param.8) | copy-start | bytes 36868
  12.6 9.0 %copy-start.3 = (s32[3072]{0:T(1024)S(1)}, s32[3072]{0:T(1024)}, u32[]{:S(2)}) copy-start(s32[3072]{0:T(1024)} %param.9) | copy-start | bytes 36868
  13.4 21.9 %collective-permute-start.2 = (f32[20,16,256]{2,1,0:T(8,128)}, f32[20,16,256]{2,1,0:T(8,128)S(1)}, u32[]{:S(2)}, u32[]{:S(2)}) collective-permute-start(f32[20,16,256]{2,1,0:T(8,128)} %pad_maximum_fusion.1), channel_id=1, source_target_pairs={{0,4},{4,0},{8,12},{12,8},{16,20},{20,16},{24,28},{28,24},{1,5},{5... | collective-permute-start | bytes 983048 | tf_op jit(solution)/shard_map/ppermute | solution.py:47
  15.3 19.9 %collective-permute-start.3 = (f32[20,16,256]{2,1,0:T(8,128)}, f32[20,16,256]{2,1,0:T(8,128)S(1)}, u32[]{:S(2)}, u32[]{:S(2)}) collective-permute-start(f32[20,16,256]{2,1,0:T(8,128)} %pad_maximum_fusion.2), channel_id=1, source_target_pairs={{4,8},{8,4},{12,16},{16,12},{20,24},{24,20},{5,9},{9,5},{13,17},{1... | collective-permute-start | bytes 983048 | tf_op jit(solution)/shard_map/ppermute | solution.py:46
  18.4 5.4 %collective-permute-start.1 = (f32[64,16,128]{2,1,0:T(8,128)}, f32[64,16,128]{2,1,0:T(8,128)S(1)}, u32[]{:S(2)}, u32[]{:S(2)}) collective-permute-start(f32[64,16,128]{2,1,0:T(8,128)} %pad_maximum_fusion), channel_id=1, source_target_pairs={{0,1},{1,0},{2,3},{3,2},{4,5},{5,4},{6,7},{7,6},{8,9},{9,8},{10,11... | collective-permute-start | bytes 1572872 | tf_op jit(solution)/shard_map/ppermute | solution.py:47
  31.4 5.6 %collective-permute-start.5 = (f32[2,16,256]{2,1,0:T(8,128)S(1)}, f32[2,16,256]{2,1,0:T(8,128)S(1)}, u32[]{:S(2)}, u32[]{:S(2)}) collective-permute-start(f32[2,16,256]{2,1,0:T(8,128)S(1)} %get-tuple-element.47), channel_id=1, source_target_pairs={{4,8},{8,4},{12,16},{16,12},{20,24},{24,20},{5,9},{9,5},{13,17},{1... | collective-permute-start | bytes 98312 | tf_op jit(solution)/shard_map/ppermute | solution.py:46
  33.4 3.6 %collective-permute-start.4 = (f32[2,16,256]{2,1,0:T(8,128)S(1)}, f32[2,16,256]{2,1,0:T(8,128)S(1)}, u32[]{:S(2)}, u32[]{:S(2)}) collective-permute-start(f32[2,16,256]{2,1,0:T(8,128)S(1)} %get-tuple-element.48), channel_id=1, source_target_pairs={{0,4},{4,0},{8,12},{12,8},{16,20},{20,16},{24,28},{28,24},{1,5},{5... | collective-permute-start | bytes 98312 | tf_op jit(solution)/shard_map/ppermute | solution.py:47
  37.6 3.6 %collective-permute-start.6 = (f32[52,2,256]{2,1,0:T(2,128)S(1)}, f32[52,2,256]{2,1,0:T(2,128)S(1)}, u32[]{:S(2)}, u32[]{:S(2)}) collective-permute-start(f32[52,2,256]{2,1,0:T(2,128)S(1)} %shard_map.57), channel_id=1, source_target_pairs={{0,2},{2,0},{1,3},{3,1},{4,6},{6,4},{5,7},{7,5},{8,10},{10,8},{9,1... | collective-permute-start | bytes 319496 | tf_op jit(solution)/shard_map/ppermute | solution.py:47
  41.9 6.4 %collective-permute-start.7 = (f32[81,16,128]{2,1,0:T(8,128)S(1)}, f32[81,16,128]{2,1,0:T(8,128)S(1)}, u32[]{:S(2)}, u32[]{:S(2)}) collective-permute-start(f32[81,16,128]{2,1,0:T(8,128)S(1)} %shard_map.58), channel_id=1, source_target_pairs={{0,1},{1,0},{2,3},{3,2},{4,5},{5,4},{6,7},{7,6},{8,9},{9,8},{10,11... | collective-permute-start | bytes 1990664 | tf_op jit(solution)/shard_map/ppermute | solution.py:47
  52.9 5.4 %collective-permute-start.8 = (f32[36,8,128]{2,1,0:T(8,128)S(1)}, f32[36,8,128]{2,1,0:T(8,128)S(1)}, u32[]{:S(2)}, u32[]{:S(2)}) collective-permute-start(f32[36,8,128]{2,1,0:T(8,128)S(1)} %get-tuple-element.36.refs_0_.own), channel_id=1, source_target_pairs={{0,4},{4,0},{8,12},{12,8},{16,20},{20,16},{24,28},{28,24},{1,5},{5... | collective-permute-start | bytes 442376 | tf_op jit(solution)/shard_map/ppermute | solution.py:47
  54.6 7.5 %collective-permute-start.9 = (f32[36,8,128]{2,1,0:T(8,128)S(1)}, f32[36,8,128]{2,1,0:T(8,128)S(1)}, u32[]{:S(2)}, u32[]{:S(2)}) collective-permute-start(f32[36,8,128]{2,1,0:T(8,128)S(1)} %get-tuple-element.40), channel_id=1, source_target_pairs={{4,8},{8,4},{12,16},{16,12},{20,24},{24,20},{5,9},{9,5},{13,17},{1... | collective-permute-start | bytes 442376 | tf_op jit(solution)/shard_map/ppermute | solution.py:46
  62.7 5.1 %collective-permute-start.10 = (f32[100,4,128]{2,1,0:T(4,128)S(1)}, f32[100,4,128]{2,1,0:T(4,128)S(1)}, u32[]{:S(2)}, u32[]{:S(2)}) collective-permute-start(f32[100,4,128]{2,1,0:T(4,128)S(1)} %shard_map.60), channel_id=1, source_target_pairs={{0,2},{2,0},{1,3},{3,1},{4,6},{6,4},{5,7},{7,5},{8,10},{10,8},{9,1... | collective-permute-start | bytes 614408 | tf_op jit(solution)/shard_map/ppermute | solution.py:47
  68.4 4.5 %collective-permute-start.11 = (f32[210,8,128]{2,1,0:T(8,128)S(1)}, f32[210,8,128]{2,1,0:T(8,128)S(1)}, u32[]{:S(2)}, u32[]{:S(2)}) collective-permute-start(f32[210,8,128]{2,1,0:T(8,128)S(1)} %shard_map.61), channel_id=1, source_target_pairs={{0,1},{1,0},{2,3},{3,2},{4,5},{5,4},{6,7},{7,6},{8,9},{9,8},{10,11... | collective-permute-start | bytes 2580488 | tf_op jit(solution)/shard_map/ppermute | solution.py:47

commit v7 on v6

--- a/solution.py
+++ b/solution.py
@@ -171,6 +171,19 @@
     return jnp.where(p < margin, flags[4], jnp.where(p >= margin + planes, flags[3], 1)).astype(jnp.float32)
 
 
+def put(ref, at, v, margin, planes, rows, lanes, reach):
+    p = at[-1]
+    reach = reach - max(margin - p, p - margin - planes + 1, 0)
+    if reach >= 2:
+        ref[at] = v
+        return
+    ends = v.shape
+    ref[(*at, slice(0, rows), slice(0, lanes))] = v[0:rows, 0:lanes]
+    for r, z in ((slice(0, rows), slice(lanes, ends[1])), (slice(rows, ends[0]), slice(0, lanes))):
+        ref[(*at, r, z)] = v[r, z] if reach == 1 else jnp.zeros((r.stop - r.start, z.stop - z.start), jnp.float32)
+    ref[(*at, slice(rows, ends[0]), slice(lanes, ends[1]))] = jnp.zeros((ends[0] - rows, ends[1] - lanes), jnp.float32)
+
+
 def neighbours(ref, p):
     rows, lanes = ref.shape[2], ref.shape[3]
     sums, grads, spread = [], [], 0.0
@@ -217,7 +230,8 @@
     return got, refs[at:]
 
 
-def chi_kernel(slot_ref, rows_ref, out, coarse_out, acc, pooled):
+def chi_kernel(flags, slot_ref, rows_ref, out, coarse_out, *refs):
+    *x_out, acc, pooled = refs
     _, planes, rows, lanes = out.shape
     acc[...] = jnp.zeros(acc.shape, jnp.float32)
     per = rows_ref.shape[1]
@@ -241,6 +255,10 @@
                     total = v if total is None else total + v
                 out[0, 2 * qx + i, :, zt * LANES:(zt + 1) * LANES] = pooled[zt]
             coarse_out[qx, :, zt * LANES:(zt + 1) * LANES] = total
+    for n, ref in enumerate(x_out):
+        start = jnp.where((flags[0] == 1) == (n == 0), planes - FINE_W, 0)
+        for j in range(FINE_W):
+            ref[j] = out[0, start + j]
 
 
 def side(up, v, dim, width):
@@ -314,11 +332,12 @@
     for k in range(planes + 2 * FINE_W):
         here = plane_inside(flags, k, FINE_W, planes)
         w_u = (RELAX / (SHIFT + 6.0 + chi[0, k])) * (mask * here)
-        weight_out[k] = w_u
+        put(weight_out, (k,), w_u, FINE_W, planes, rows, lanes, FINE_W)
         sums, grads = neighbours(start, k + START_W - FINE_W)
         for f in range(4):
             w = w_u if f < 3 else w_p * here
-            ext[f, k] = KEEP * start[f, k + START_W - FINE_W] + w * (rhs[f, k] + sums[f] - 0.5 * grads[f])
+            v = KEEP * start[f, k + START_W - FINE_W] + w * (rhs[f, k] + sums[f] - 0.5 * grads[f])
+            put(ext, (f, k), v, FINE_W, planes, rows, lanes, FINE_W)
 
     for p in range(1, planes + 2 * FINE_W - 1):
         here = plane_inside(flags, p, FINE_W, planes)
@@ -326,7 +345,8 @@
         w_u = weight_out[p]
         for f in range(4):
             w = w_u if f < 3 else w_p * here
-            state_out[f, p] = KEEP * ext[f, p] + w * (rhs[f, p] + sums[f] - 0.5 * grads[f])
+            v = KEEP * ext[f, p] + w * (rhs[f, p] + sums[f] - 0.5 * grads[f])
+            put(state_out, (f, p), v, FINE_W, planes, rows, lanes, FINE_W - 1)
 
     for cx in range(planes // 2):
         both = [None] * 4
@@ -381,7 +401,8 @@
             sums, grads = neighbours(now, p)
             for f in range(4):
                 w = ext[4, p] if f < 3 else w_p * here
-                then[f, p] = KEEP * now[f, p] + w * (ext[f, p] + 0.25 * (sums[f] - grads[f]))
+                v = KEEP * now[f, p] + w * (ext[f, p] + 0.25 * (sums[f] - grads[f]))
+                put(then, (f, p), v, COARSE_W, planes, rows, lanes, COARSE_W + 1 - s)
         now, then = then, now
 
     f_total, f_wide = fine.shape[2], fine.shape[3]
@@ -416,7 +437,8 @@
         sums, grads = neighbours(fine, p)
         for f in range(4):
             w = weight[p + off] if f < 3 else w_q * here
-            mid[f, p] = KEEP * fine[f, p] + w * (rhs[f, p + off] + sums[f] - 0.5 * grads[f])
+            v = KEEP * fine[f, p] + w * (rhs[f, p + off] + sums[f] - 0.5 * grads[f])
+            put(mid, (f, p), v, STATE_W, f_planes, f_rows, f_lanes, 1)
 
     for k in range(f_planes):
         p = k + 2
@@ -485,20 +507,20 @@
     total, wide = rows + 8, lanes + LANES
     near, far = planes + 2 * STATE_W, planes + 2 * FINE_W
     pair_counts = [1 + (n > 2) for n in counts]
-    groups = [(start_field, START_W), (right_side, FINE_W)]
+    flags, slot_of, start_late, right_late = lax.optimization_barrier((flags, slot_of, start_field, right_side))
+    groups = [(start_late, START_W), (right_late, FINE_W)]
     first_x = halo_x(groups)
     first_y = swap("gy", lambda up, n: flat([cut(v, 2, START_W, up) for v, _ in groups]))
     first_z = swap("lvl", lambda up, n: flat([cut(v, 3, LANES, up) for v, _ in groups]))
-    first_y, first_z, slot_of = lax.optimization_barrier((first_y, first_z, slot_of))
-    chi, pooled_chi = call(
+    first_z, slot_of = lax.optimization_barrier((first_z, slot_of))
+    chi, pooled_chi, *chi_out = call(
         chi_kernel,
-        [(1, planes, rows, lanes), (c_planes, c_rows, lanes)],
+        [(1, planes, rows, lanes), (c_planes, c_rows, lanes), *[(FINE_W, rows, lanes)] * pair_counts[0]],
         [pltpu.VMEM(((slots + 1) * 8, LANES), jnp.float32), pltpu.VMEM((lanes // LANES, rows, LANES), jnp.float32)],
-        slot_of, arrived,
-    )
-    group = [(chi, FINE_W)]
-    chi_x = halo_x(group)
-    first_x, chi_x = lax.optimization_barrier((first_x, chi_x))
+        flags, slot_of, arrived, smem=2,
+    )
+    chi_x = swap("gx", lambda up, n: chi_out[n])
+    first_x, first_y, chi_x = lax.optimization_barrier((first_x, first_y, chi_x))
     slabs = lambda v: v.reshape(-1, rows, lanes)
     far_x = len(first_x) * 4 * (START_W + FINE_W)
     chi_slabs = planes + len(chi_x) * FINE_W

time: 78.4 us -> 78.4 us (level)
  waiting for transfers between devices: 26.1 us -> 28 us
  starting transfers between devices: 28.9 us -> 27.7 us
    ppermute x3, waiting for transfers between devices: 5.5 us -> 3.06 us  [swap(): lax.ppermute(message(~even, 1), axis, pairs(count, 1))]
    all_to_all x1, waiting for transfers between devices: 6.17 us -> 8.59 us  [body(): lax.all_to_all(outgoing, ('gx', 'gy'), split_axis=0, concat_axis=0, tiled...]
    ppermute x9, waiting for transfers between devices: 14.4 us -> 16.4 us  [swap(): got.insert(0, lax.ppermute(message(even, 0), axis, pairs(count, 0)))]
  transfers between devices with their start and end apart: 13 -> 13, of which waited for: 10 -> 10; matrix products, arithmetic and copies ran while one was open for 7% -> 6% of each run, Pallas kernels for 2% -> 2%
where the time goes in v7:
time: 78.4 us; the launch traced here: 78 us
  waiting for transfers between devices  28 us (36%)
  starting transfers between devices  27.7 us (35%)
  Pallas kernels  15.3 us (20%)
  other arithmetic  3.7 us (5%)
  local copies, waits for them, and re-layouts  2.99 us (4%)
    ppermute x9, waiting for transfers between devices, swap(): got.insert(0, lax.ppermute(message(even, 0), axis, pairs(count, 0)))  16.4 us
    ppermute x9, starting transfers between devices, swap(): got.insert(0, lax.ppermute(message(even, 0), axis, pairs(count, 0)))  15.4 us
    pallas_call x8, Pallas kernels, call(): pl.pallas_call(kernel, out_shape=outs, in_specs=[SMEM] * smem + [VMEM] *...  15.3 us
    all_to_all x1, waiting for transfers between devices, body(): lax.all_to_all(outgoing, ('gx', 'gy'), split_axis=0, concat_axis=0, tiled...  8.59 us
    all_to_all x1, starting transfers between devices, body(): lax.all_to_all(outgoing, ('gx', 'gy'), split_axis=0, concat_axis=0, tiled...  6.64 us
    ppermute x3, starting transfers between devices, swap(): lax.ppermute(message(~even, 1), axis, pairs(count, 1))  5.72 us
    ppermute x3, waiting for transfers between devices, swap(): lax.ppermute(message(~even, 1), axis, pairs(count, 1))  3.06 us
    concatenate x4, other arithmetic, flat(): jnp.concatenate([p.reshape(-1, *p.shape[-2:]) for p in parts], axis=0)  2.39 us
  transfers between devices with their start and end apart: 13, of which 10 were waited for; matrix products, arithmetic and copies ran while one was open for 6% of the time, Pallas kernels for 2%

profile of v7, /device:TPU:9, one launch (start us, length us, event | category | flops | bytes accessed | tf_op | source)
XLA Modules:
  0.0 78.0 jit_solution(7617155342252320679)
XLA Ops:
  0.0 0.8 %fusion.1.tile_ref = s32[96]{0:T(128)S(1)} fusion(s32[3072,1]{0,1:T(1,128)} %param.8, s32[]{:T(128)S(6)} %select_n.72), kind=kLoop, calls=%fused_computation.22 | loop fusion | bytes 772 | tf_op jit(solution)/shard_map/dynamic_slice | solution.py:496
  0.8 1.0 %copy-done.2 = f32[96,1024]{1,0:T(8,128)S(1)} copy-done((f32[96,1024]{1,0:T(8,128)S(1)}, f32[96,1024]{1,0:T(8,128)}, u32[]{:S(2)}) %copy-start.2) | copy-done | bytes 393240
  1.8 2.0 %shard_map.55 = f32[16,12,8,128]{3,2,1,0:T(8,128)} custom-call(s32[96]{0:T(128)S(1)} %fusion.1.tile_ref, f32[96,1024]{1,0:T(8,128)S(1)} %copy-done.2), custom_call_target="tpu_custom_call" | custom-call | tf_op jit(solution)/shard_map/pallas_call | solution.py:454
  3.9 6.6 %all-to-all-start = ((f32[16,12,8,128]{3,2,1,0:T(8,128)}), f32[16,12,8,128]{3,2,1,0:T(8,128)S(1)}, u32[]{:S(2)}, u32[]{:S(2)}) async-start(f32[16,12,8,128]{3,2,1,0:T(8,128)} %shard_map.55), calls=%async_computation | async-start | bytes 1572864 | tf_op jit(solution)/shard_map/all_to_all | solution.py:504
  11.2 0.7 reduce.3
  13.0 0.8 %pad_maximum_fusion = f32[64,16,128]{2,1,0:T(8,128)} fusion(f32[32,16,128]{2,1,0:T(8,128)S(1)} %bitcast.31, f32[32,16,128]{2,1,0:T(8,128)S(1)} %bitcast.32), kind=kLoop, calls=%fused_computation.1 | loop fusion | flops 131072 | bytes 1048576 | tf_op jit(solution)/shard_map/concatenate | solution.py:40
  13.8 1.3 %collective-permute-start = (f32[64,16,128]{2,1,0:T(8,128)}, f32[64,16,128]{2,1,0:T(8,128)S(1)}, u32[]{:S(2)}, u32[]{:S(2)}) collective-permute-start(f32[64,16,128]{2,1,0:T(8,128)} %pad_maximum_fusion), channel_id=1, source_target_pairs={{0,1},{1,0},{2,3},{3,2},{4,5},{5,4},{6,7},{7,6},{8,9},{9,8},{10,11... | collective-permute-start | bytes 1572872 | tf_op jit(solution)/shard_map/ppermute | solution.py:47
  15.1 0.7 pad_maximum_fusion.1
  15.9 1.2 %collective-permute-start.1 = (f32[20,16,256]{2,1,0:T(8,128)}, f32[20,16,256]{2,1,0:T(8,128)S(1)}, u32[]{:S(2)}, u32[]{:S(2)}) collective-permute-start(f32[20,16,256]{2,1,0:T(8,128)} %pad_maximum_fusion.1), channel_id=1, source_target_pairs={{0,4},{4,0},{8,12},{12,8},{16,20},{20,16},{24,28},{28,24},{1,5},{5... | collective-permute-start | bytes 983048 | tf_op jit(solution)/shard_map/ppermute | solution.py:47
  17.1 0.8 pad_maximum_fusion.2
  17.8 1.9 %collective-permute-start.2 = (f32[20,16,256]{2,1,0:T(8,128)}, f32[20,16,256]{2,1,0:T(8,128)S(1)}, u32[]{:S(2)}, u32[]{:S(2)}) collective-permute-start(f32[20,16,256]{2,1,0:T(8,128)} %pad_maximum_fusion.2), channel_id=1, source_target_pairs={{4,8},{8,4},{12,16},{16,12},{20,24},{24,20},{5,9},{9,5},{13,17},{1... | collective-permute-start | bytes 983048 | tf_op jit(solution)/shard_map/ppermute | solution.py:46
  19.9 1.5 %collective-permute-start.3 = (f32[64,3,256]{2,1,0:T(4,128)S(1)}, f32[64,3,256]{2,1,0:T(4,128)S(1)}, u32[]{:S(2)}, u32[]{:S(2)}) collective-permute-start(f32[64,3,256]{2,1,0:T(4,128)S(1)} %pad_maximum_fusion.3), channel_id=1, source_target_pairs={{0,2},{2,0},{1,3},{3,1},{4,6},{6,4},{5,7},{7,5},{8,10},{10,8},{9,1... | collective-permute-start | bytes 589832 | tf_op jit(solution)/shard_map/ppermute | solution.py:47
  21.4 8.6 %all-to-all-done.rows_ref = f32[16,12,8,128]{3,2,1,0:T(8,128)S(1)} async-done(((f32[16,12,8,128]{3,2,1,0:T(8,128)}), f32[16,12,8,128]{3,2,1,0:T(8,128)S(1)}, u32[]{:S(2)}, u32[]{:S(2)}) %all-to-all-start) | async-done | bytes 786464 | tf_op jit(solution)/shard_map/all_to_all | solution.py:504
  30.0 1.3 %shard_map.56 = (f32[1,8,16,256]{3,2,1,0:T(8,128)S(1)}, f32[4,8,256]{2,1,0:T(8,128)S(1)}, f32[2,16,256]{2,1,0:T(8,128)S(1)}, f32[2,16,256]{2,1,0:T(8,128)S(1)}) custom-call(s32[9]{0:T(128)S(1)} %convert_element_type.3.flags, s32[192]{0:T(256)S(1)} %add.54.slot_ref, f32[16,12,8,128]{3,2,1,0:T(8,128)S(1)} %all-to-all-done.rows_ref), custom_call_target="tpu_custom_call" | custom-call | tf_op jit(solution)/shard_map/pallas_call | solution.py:454
  31.3 1.0 %collective-permute-start.4 = (f32[2,16,256]{2,1,0:T(8,128)S(1)}, f32[2,16,256]{2,1,0:T(8,128)S(1)}, u32[]{:S(2)}, u32[]{:S(2)}) collective-permute-start(f32[2,16,256]{2,1,0:T(8,128)S(1)} %get-tuple-element.40), channel_id=1, source_target_pairs={{0,4},{4,0},{8,12},{12,8},{16,20},{20,16},{24,28},{28,24},{1,5},{5... | collective-permute-start | bytes 98312 | tf_op jit(solution)/shard_map/ppermute | solution.py:47
  32.3 1.9 %collective-permute-start.5 = (f32[2,16,256]{2,1,0:T(8,128)S(1)}, f32[2,16,256]{2,1,0:T(8,128)S(1)}, u32[]{:S(2)}, u32[]{:S(2)}) collective-permute-start(f32[2,16,256]{2,1,0:T(8,128)S(1)} %get-tuple-element.41), channel_id=1, source_target_pairs={{4,8},{8,4},{12,16},{16,12},{20,24},{24,20},{5,9},{9,5},{13,17},{1... | collective-permute-start | bytes 98312 | tf_op jit(solution)/shard_map/ppermute | solution.py:46
  34.2 2.5 %collective-permute-done.1.refs_4_.refs_3_.refs_2_ = f32[20,16,256]{2,1,0:T(8,128)S(1)} collective-permute-done((f32[20,16,256]{2,1,0:T(8,128)}, f32[20,16,256]{2,1,0:T(8,128)S(1)}, u32[]{:S(2)}, u32[]{:S(2)}) %collective-permute-start.1) | collective-permute-done | bytes 327712 | tf_op jit(solution)/shard_map/ppermute | solution.py:47
  36.8 0.7 collective-permute-done.4.refs_2_.refs_1_.refs_0_
  38.5 1.2 %collective-permute-start.6 = (f32[52,2,256]{2,1,0:T(2,128)S(1)}, f32[52,2,256]{2,1,0:T(2,128)S(1)}, u32[]{:S(2)}, u32[]{:S(2)}) collective-permute-start(f32[52,2,256]{2,1,0:T(2,128)S(1)} %shard_map.57), channel_id=1, source_target_pairs={{0,2},{2,0},{1,3},{3,1},{4,6},{6,4},{5,7},{7,5},{8,10},{10,8},{9,1... | collective-permute-start | bytes 319496 | tf_op jit(solution)/shard_map/ppermute | solution.py:47
  39.7 2.4 %collective-permute-done.6.refs_6_ = f32[52,2,256]{2,1,0:T(2,128)S(1)} collective-permute-done((f32[52,2,256]{2,1,0:T(2,128)S(1)}, f32[52,2,256]{2,1,0:T(2,128)S(1)}, u32[]{:S(2)}, u32[]{:S(2)}) %collective-permute-start.6) | collective-permute-done | bytes 106528 | tf_op jit(solution)/shard_map/ppermute | solution.py:47
  42.1 0.7 shard_map.58
  42.8 5.4 %collective-permute-start.7 = (f32[81,16,128]{2,1,0:T(8,128)S(1)}, f32[81,16,128]{2,1,0:T(8,128)S(1)}, u32[]{:S(2)}, u32[]{:S(2)}) collective-permute-start(f32[81,16,128]{2,1,0:T(8,128)S(1)} %shard_map.58), channel_id=1, source_target_pairs={{0,1},{1,0},{2,3},{3,2},{4,5},{5,4},{6,7},{7,6},{8,9},{9,8},{10,11... | collective-permute-start | bytes 1990664 | tf_op jit(solution)/shard_map/ppermute | solution.py:47
  48.2 1.7 %collective-permute-done.7.refs_7_ = f32[81,16,128]{2,1,0:T(8,128)S(1)} collective-permute-done((f32[81,16,128]{2,1,0:T(8,128)S(1)}, f32[81,16,128]{2,1,0:T(8,128)S(1)}, u32[]{:S(2)}, u32[]{:S(2)}) %collective-permute-start.7) | collective-permute-done | bytes 663584 | tf_op jit(solution)/shard_map/ppermute | solution.py:47
  49.9 4.3 %shard_map.59 = (f32[4,12,24,384]{3,2,1,0:T(8,128)S(1)}, f32[4,12,24,384]{3,2,1,0:T(8,128)S(1)}, f32[12,24,384]{2,1,0:T(8,128)S(1)}, f32[36,8,128]{2,1,0:T(8,128...) custom-call(s32[9]{0:T(128)S(1)} %convert_element_type.3.flags, ...), custom_call_target="tpu_custom_call" | custom-call | tf_op jit(solution)/shard_map/pallas_call | solution.py:454
  54.3 1.9 %collective-permute-start.9 = (f32[36,8,128]{2,1,0:T(8,128)S(1)}, f32[36,8,128]{2,1,0:T(8,128)S(1)}, u32[]{:S(2)}, u32[]{:S(2)}) collective-permute-start(f32[36,8,128]{2,1,0:T(8,128)S(1)} %get-tuple-element.52), channel_id=1, source_target_pairs={{4,8},{8,4},{12,16},{16,12},{20,24},{24,20},{5,9},{9,5},{13,17},{1... | collective-permute-start | bytes 442376 | tf_op jit(solution)/shard_map/ppermute | solution.py:46
  56.2 3.1 %collective-permute-done.8.refs_2_.refs_1_.refs_0_ = f32[36,8,128]{2,1,0:T(8,128)S(1)} collective-permute-done((f32[36,8,128]{2,1,0:T(8,128)S(1)}, f32[36,8,128]{2,1,0:T(8,128)S(1)}, u32[]{:S(2)}, u32[]{:S(2)}) %collective-permute-start.8) | collective-permute-done | bytes 147488 | tf_op jit(solution)/shard_map/ppermute | solution.py:47
  59.3 2.6 %collective-permute-done.9.refs_1_.refs_2_ = f32[36,8,128]{2,1,0:T(8,128)S(1)} collective-permute-done((f32[36,8,128]{2,1,0:T(8,128)S(1)}, f32[36,8,128]{2,1,0:T(8,128)S(1)}, u32[]{:S(2)}, u32[]{:S(2)}) %collective-permute-start.9) | collective-permute-done | bytes 147488 | tf_op jit(solution)/shard_map/ppermute | solution.py:46
  62.5 0.8 collective-permute-start.10
  63.3 3.9 %collective-permute-done.10.refs_3_.refs_2_ = f32[100,4,128]{2,1,0:T(4,128)S(1)} collective-permute-done((f32[100,4,128]{2,1,0:T(4,128)S(1)}, f32[100,4,128]{2,1,0:T(4,128)S(1)}, u32[]{:S(2)}, u32[]{:S(2)}) %collective-permute-start.10) | collective-permute-done | bytes 204832 | tf_op jit(solution)/shard_map/ppermute | solution.py:47
  67.8 2.9 %collective-permute-start.11 = (f32[210,8,128]{2,1,0:T(8,128)S(1)}, f32[210,8,128]{2,1,0:T(8,128)S(1)}, u32[]{:S(2)}, u32[]{:S(2)}) collective-permute-start(f32[210,8,128]{2,1,0:T(8,128)S(1)} %shard_map.61), channel_id=1, source_target_pairs={{0,1},{1,0},{2,3},{3,2},{4,5},{5,4},{6,7},{7,6},{8,9},{9,8},{10,11... | collective-permute-start | bytes 2580488 | tf_op jit(solution)/shard_map/ppermute | solution.py:47
  70.7 2.0 %collective-permute-done.11.refs_3_ = f32[210,8,128]{2,1,0:T(8,128)S(1)} collective-permute-done((f32[210,8,128]{2,1,0:T(8,128)S(1)}, f32[210,8,128]{2,1,0:T(8,128)S(1)}, u32[]{:S(2)}, u32[]{:S(2)}) %collective-permute-start.11) | collective-permute-done | bytes 860192 | tf_op jit(solution)/shard_map/ppermute | solution.py:47
  72.8 5.2 %shard_map.62 = f32[4,8,16,256]{3,2,1,0:T(8,128)} custom-call(s32[9]{0:T(128)S(1)} %convert_element_type.3.flags, f32[36,8,128]{2,1,0:T(8,128)S(1)} %get-tuple-element.48.refs_0_.own, f32[4,12,24,384]{3,2,1,0:T(8,128)S(1)} %get-tuple-element.49.state, f32[12,24,384]{2,1,0:T(8,128)S(1)} %get-tuple-element.50.weight, ...), custom_call_target="tpu_custom_call" | custom-call | tf_op jit(solution)/shard_map/pallas_call | solution.py:454
  (38 shorter events, 4.2 us)
Async XLA Ops:
  0.0 12.9 %copy-start = (f32[4,8,16,256]{3,2,1,0:T(8,128)S(1)}, f32[4,8,16,256]{3,2,1,0:T(8,128)}, u32[]{:S(2)}) copy-start(f32[4,8,16,256]{3,2,1,0:T(8,128)} %start_field) | copy-start | bytes 1572868
  0.0 12.9 %copy-start.1 = (f32[4,8,16,256]{3,2,1,0:T(8,128)S(1)}, f32[4,8,16,256]{3,2,1,0:T(8,128)}, u32[]{:S(2)}) copy-start(f32[4,8,16,256]{3,2,1,0:T(8,128)} %right_side) | copy-start | bytes 1572868
  0.8 1.0 %copy-start.2 = (f32[96,1024]{1,0:T(8,128)S(1)}, f32[96,1024]{1,0:T(8,128)}, u32[]{:S(2)}) copy-start(f32[96,1024]{1,0:T(8,128)} %mask_ref.1) | copy-start | bytes 1179652
  1.8 9.4 %copy-start.4 = (s32[3072,1]{0,1:T(1,128)S(1)}, s32[3072,1]{0,1:T(1,128)}, u32[]{:S(2)}) copy-start(s32[3072,1]{0,1:T(1,128)} %param.8) | copy-start | bytes 36868
  1.8 10.2 %copy-start.3 = (s32[3072]{0:T(1024)S(1)}, s32[3072]{0:T(1024)}, u32[]{:S(2)}) copy-start(s32[3072]{0:T(1024)} %param.9) | copy-start | bytes 36868
  3.9 26.1 %all-to-all-start = ((f32[16,12,8,128]{3,2,1,0:T(8,128)}), f32[16,12,8,128]{3,2,1,0:T(8,128)S(1)}, u32[]{:S(2)}, u32[]{:S(2)}) async-start(f32[16,12,8,128]{3,2,1,0:T(8,128)} %shard_map.55), calls=%async_computation | async-start | bytes 1572864 | tf_op jit(solution)/shard_map/all_to_all | solution.py:504
  13.8 7.6 %collective-permute-start = (f32[64,16,128]{2,1,0:T(8,128)}, f32[64,16,128]{2,1,0:T(8,128)S(1)}, u32[]{:S(2)}, u32[]{:S(2)}) collective-permute-start(f32[64,16,128]{2,1,0:T(8,128)} %pad_maximum_fusion), channel_id=1, source_target_pairs={{0,1},{1,0},{2,3},{3,2},{4,5},{5,4},{6,7},{7,6},{8,9},{9,8},{10,11... | collective-permute-start | bytes 1572872 | tf_op jit(solution)/shard_map/ppermute | solution.py:47
  15.9 20.9 %collective-permute-start.1 = (f32[20,16,256]{2,1,0:T(8,128)}, f32[20,16,256]{2,1,0:T(8,128)S(1)}, u32[]{:S(2)}, u32[]{:S(2)}) collective-permute-start(f32[20,16,256]{2,1,0:T(8,128)} %pad_maximum_fusion.1), channel_id=1, source_target_pairs={{0,4},{4,0},{8,12},{12,8},{16,20},{20,16},{24,28},{28,24},{1,5},{5... | collective-permute-start | bytes 983048 | tf_op jit(solution)/shard_map/ppermute | solution.py:47
  17.8 19.0 %collective-permute-start.2 = (f32[20,16,256]{2,1,0:T(8,128)}, f32[20,16,256]{2,1,0:T(8,128)S(1)}, u32[]{:S(2)}, u32[]{:S(2)}) collective-permute-start(f32[20,16,256]{2,1,0:T(8,128)} %pad_maximum_fusion.2), channel_id=1, source_target_pairs={{4,8},{8,4},{12,16},{16,12},{20,24},{24,20},{5,9},{9,5},{13,17},{1... | collective-permute-start | bytes 983048 | tf_op jit(solution)/shard_map/ppermute | solution.py:46
  19.9 14.3 %collective-permute-start.3 = (f32[64,3,256]{2,1,0:T(4,128)S(1)}, f32[64,3,256]{2,1,0:T(4,128)S(1)}, u32[]{:S(2)}, u32[]{:S(2)}) collective-permute-start(f32[64,3,256]{2,1,0:T(4,128)S(1)} %pad_maximum_fusion.3), channel_id=1, source_target_pairs={{0,2},{2,0},{1,3},{3,1},{4,6},{6,4},{5,7},{7,5},{8,10},{10,8},{9,1... | collective-permute-start | bytes 589832 | tf_op jit(solution)/shard_map/ppermute | solution.py:47
  31.3 6.1 %collective-permute-start.4 = (f32[2,16,256]{2,1,0:T(8,128)S(1)}, f32[2,16,256]{2,1,0:T(8,128)S(1)}, u32[]{:S(2)}, u32[]{:S(2)}) collective-permute-start(f32[2,16,256]{2,1,0:T(8,128)S(1)} %get-tuple-element.40), channel_id=1, source_target_pairs={{0,4},{4,0},{8,12},{12,8},{16,20},{20,16},{24,28},{28,24},{1,5},{5... | collective-permute-start | bytes 98312 | tf_op jit(solution)/shard_map/ppermute | solution.py:47
  32.3 5.6 %collective-permute-start.5 = (f32[2,16,256]{2,1,0:T(8,128)S(1)}, f32[2,16,256]{2,1,0:T(8,128)S(1)}, u32[]{:S(2)}, u32[]{:S(2)}) collective-permute-start(f32[2,16,256]{2,1,0:T(8,128)S(1)} %get-tuple-element.41), channel_id=1, source_target_pairs={{4,8},{8,4},{12,16},{16,12},{20,24},{24,20},{5,9},{9,5},{13,17},{1... | collective-permute-start | bytes 98312 | tf_op jit(solution)/shard_map/ppermute | solution.py:46
  38.5 3.6 %collective-permute-start.6 = (f32[52,2,256]{2,1,0:T(2,128)S(1)}, f32[52,2,256]{2,1,0:T(2,128)S(1)}, u32[]{:S(2)}, u32[]{:S(2)}) collective-permute-start(f32[52,2,256]{2,1,0:T(2,128)S(1)} %shard_map.57), channel_id=1, source_target_pairs={{0,2},{2,0},{1,3},{3,1},{4,6},{6,4},{5,7},{7,5},{8,10},{10,8},{9,1... | collective-permute-start | bytes 319496 | tf_op jit(solution)/shard_map/ppermute | solution.py:47
  42.8 7.1 %collective-permute-start.7 = (f32[81,16,128]{2,1,0:T(8,128)S(1)}, f32[81,16,128]{2,1,0:T(8,128)S(1)}, u32[]{:S(2)}, u32[]{:S(2)}) collective-permute-start(f32[81,16,128]{2,1,0:T(8,128)S(1)} %shard_map.58), channel_id=1, source_target_pairs={{0,1},{1,0},{2,3},{3,2},{4,5},{5,4},{6,7},{7,6},{8,9},{9,8},{10,11... | collective-permute-start | bytes 1990664 | tf_op jit(solution)/shard_map/ppermute | solution.py:47
  54.2 5.1 %collective-permute-start.8 = (f32[36,8,128]{2,1,0:T(8,128)S(1)}, f32[36,8,128]{2,1,0:T(8,128)S(1)}, u32[]{:S(2)}, u32[]{:S(2)}) collective-permute-start(f32[36,8,128]{2,1,0:T(8,128)S(1)} %get-tuple-element.48.refs_0_.own), channel_id=1, source_target_pairs={{0,4},{4,0},{8,12},{12,8},{16,20},{20,16},{24,28},{28,24},{1,5},{5... | collective-permute-start | bytes 442376 | tf_op jit(solution)/shard_map/ppermute | solution.py:47
  54.3 7.6 %collective-permute-start.9 = (f32[36,8,128]{2,1,0:T(8,128)S(1)}, f32[36,8,128]{2,1,0:T(8,128)S(1)}, u32[]{:S(2)}, u32[]{:S(2)}) collective-permute-start(f32[36,8,128]{2,1,0:T(8,128)S(1)} %get-tuple-element.52), channel_id=1, source_target_pairs={{4,8},{8,4},{12,16},{16,12},{20,24},{24,20},{5,9},{9,5},{13,17},{1... | collective-permute-start | bytes 442376 | tf_op jit(solution)/shard_map/ppermute | solution.py:46
  62.5 4.7 %collective-permute-start.10 = (f32[100,4,128]{2,1,0:T(4,128)S(1)}, f32[100,4,128]{2,1,0:T(4,128)S(1)}, u32[]{:S(2)}, u32[]{:S(2)}) collective-permute-start(f32[100,4,128]{2,1,0:T(4,128)S(1)} %shard_map.60), channel_id=1, source_target_pairs={{0,2},{2,0},{1,3},{3,1},{4,6},{6,4},{5,7},{7,5},{8,10},{10,8},{9,1... | collective-permute-start | bytes 614408 | tf_op jit(solution)/shard_map/ppermute | solution.py:47
  67.8 5.0 %collective-permute-start.11 = (f32[210,8,128]{2,1,0:T(8,128)S(1)}, f32[210,8,128]{2,1,0:T(8,128)S(1)}, u32[]{:S(2)}, u32[]{:S(2)}) collective-permute-start(f32[210,8,128]{2,1,0:T(8,128)S(1)} %shard_map.61), channel_id=1, source_target_pairs={{0,1},{1,0},{2,3},{3,2},{4,5},{5,4},{6,7},{7,6},{8,9},{9,8},{10,11... | collective-permute-start | bytes 2580488 | tf_op jit(solution)/shard_map/ppermute | solution.py:47

commit v8 on v7

--- a/solution.py
+++ b/solution.py
@@ -117,13 +117,14 @@
                 at = before[2] + slab * (total // 8) + r
                 z = jnp.where(side, zs[0][at], 0.0 if len(zs) == 1 else zs[1][at])
                 out[f, p, r * 8:(r + 1) * 8, lanes:] = z
+            out_by = 1 if 0 < k <= planes else 0
             for z in range(lanes // LANES):
-                part = slice(z * STATE_W, (z + 1) * STATE_W)
-                first = ys[0][before[1] + slab, part]
-                second = ys[1][before[1] + slab, part] if len(ys) > 1 else jnp.zeros_like(first)
+                at, row = before[1] + slab // 2, slab % 2 * 2 + z
+                first = ys[0][at, row:row + 1]
+                second = ys[1][at, row:row + 1] if len(ys) > 1 else jnp.zeros_like(first)
                 to = slice(z * LANES, (z + 1) * LANES)
-                out[f, p, rows:rows + STATE_W, to] = jnp.where(even_y, first, second)
-                out[f, p, total - STATE_W:total, to] = jnp.where(even_y, second, first)
+                out[f, p, rows + out_by:rows + out_by + 1, to] = jnp.where(even_y, first, second)
+                out[f, p, total - 1 - out_by:total - out_by, to] = jnp.where(even_y, second, first)
         for p in (0, near - 1):
             out[f, p] = jnp.zeros((total, wide), jnp.float32)
             is_first = even_x if p else ~even_x
@@ -147,10 +148,13 @@
     for f in range(fields):
         for k in range(planes + 2):
             p, slab = STATE_W - 1 + k, f * (planes + 2) + k
+            out_by = 1 if 0 < k <= planes else 0
             for n, ref in enumerate(y_out):
-                v = jnp.where(up[1][n], state[f, p, rows - STATE_W:rows, 0:lanes], state[f, p, 0:STATE_W, 0:lanes])
+                high = state[f, p, rows - 1 - out_by:rows - out_by, 0:lanes]
+                v = jnp.where(up[1][n], high, state[f, p, out_by:out_by + 1, 0:lanes])
                 for z in range(lanes // LANES):
-                    ref[slab, z * STATE_W:(z + 1) * STATE_W] = v[:, z * LANES:(z + 1) * LANES]
+                    row = slab % 2 * 2 + z
+                    ref[slab // 2, row:row + 1] = v[:, z * LANES:(z + 1) * LANES]
             for n, ref in enumerate(z_out):
                 for r in range(total // 8):
                     part = slice(r * 8, (r + 1) * 8)
@@ -507,8 +511,7 @@
     total, wide = rows + 8, lanes + LANES
     near, far = planes + 2 * STATE_W, planes + 2 * FINE_W
     pair_counts = [1 + (n > 2) for n in counts]
-    flags, slot_of, start_late, right_late = lax.optimization_barrier((flags, slot_of, start_field, right_side))
-    groups = [(start_late, START_W), (right_late, FINE_W)]
+    groups = [(start_field, START_W), (right_side, FINE_W)]
     first_x = halo_x(groups)
     first_y = swap("gy", lambda up, n: flat([cut(v, 2, START_W, up) for v, _ in groups]))
     first_z = swap("lvl", lambda up, n: flat([cut(v, 3, LANES, up) for v, _ in groups]))
@@ -556,7 +559,7 @@
     )
     far_z = swap("lvl", lambda up, n: z_sent[n])
     c_slabs, s_slabs = 5 * c_planes, 4 * (rows // 8) * (lanes // LANES)
-    outers = [[(c_slabs + s_slabs, 8, LANES)], [(4 * (planes + 2), PAD, LANES)], [(4 * (planes + 2) * total // 8, 8, LANES)]]
+    outers = [[(c_slabs + s_slabs, 8, LANES)], [(4 * (planes + 2) // 2, PAD, LANES)], [(4 * (planes + 2) * total // 8, 8, LANES)]]
     outers = [shape * n for shape, n in zip(outers, pair_counts)]
     rhs, state, weight, *sent = call(
         functools.partial(second_kernel, nums=pair_counts),

time: 78.4 us -> 78 us (level)
  waiting for transfers between devices: 28 us -> 19.2 us
  other arithmetic: 3.7 us -> 8.39 us
  local copies, waits for them, and re-layouts: 2.99 us -> 7.5 us
  starting transfers between devices: 27.7 us -> 26.7 us
    all_to_all x1, waiting for transfers between devices: 8.59 us -> 0.01 us  [body(): lax.all_to_all(outgoing, ('gx', 'gy'), split_axis=0, concat_axis=0, tiled...]
    ppermute x9, waiting for transfers between devices: 16.4 us -> 13.1 us  [swap(): got.insert(0, lax.ppermute(message(even, 0), axis, pairs(count, 0)))]
    ppermute x3, waiting for transfers between devices: 3.06 us -> 6.16 us  [swap(): lax.ppermute(message(~even, 1), axis, pairs(count, 1))]
    ppermute x9, starting transfers between devices: 15.4 us -> 13.7 us  [swap(): got.insert(0, lax.ppermute(message(even, 0), axis, pairs(count, 0)))]
    sub x1, other arithmetic: 0.02 us -> 1.33 us  [routes(): their_slots[:, None, :] - slots]
    eq x1, other arithmetic: 0.02 us -> 1.33 us  [routes(): arriving = their_tiles == my_tile]
    reshape x1, local copies, waits for them, and re-layouts: 0.08 us -> 1.39 us  [routes(): block_slot.reshape(tiles, count_l, per_device)]
    add x2, local copies, waits for them, and re-layouts: 0.17 us -> 1.46 us  [routes(): jnp.sum(jnp.where(hit, their_slots[:, None, :] - slots, 0), axis=2) + slots]
  transfers between devices with their start and end apart: 13 -> 13, of which waited for: 10 -> 7; matrix products, arithmetic and copies ran while one was open for 6% -> 18% of each run, Pallas kernels for 2% -> 2%
where the time goes in v8:
time: 78 us; the launch traced here: 77.2 us
  starting transfers between devices  26.7 us (34%)
  waiting for transfers between devices  19.2 us (25%)
  Pallas kernels  15.2 us (19%)
  other arithmetic  8.39 us (11%)
  local copies, waits for them, and re-layouts  7.5 us (10%)
    pallas_call x8, Pallas kernels, call(): pl.pallas_call(kernel, out_shape=outs, in_specs=[SMEM] * smem + [VMEM] *...  15.2 us
    ppermute x9, starting transfers between devices, swap(): got.insert(0, lax.ppermute(message(even, 0), axis, pairs(count, 0)))  13.7 us
    ppermute x9, waiting for transfers between devices, swap(): got.insert(0, lax.ppermute(message(even, 0), axis, pairs(count, 0)))  13.1 us
    all_to_all x1, starting transfers between devices, body(): lax.all_to_all(outgoing, ('gx', 'gy'), split_axis=0, concat_axis=0, tiled...  6.64 us
    ppermute x3, starting transfers between devices, swap(): lax.ppermute(message(~even, 1), axis, pairs(count, 1))  6.36 us
    ppermute x3, waiting for transfers between devices, swap(): lax.ppermute(message(~even, 1), axis, pairs(count, 1))  6.16 us
    concatenate x4, other arithmetic, flat(): jnp.concatenate([p.reshape(-1, *p.shape[-2:]) for p in parts], axis=0)  2.4 us
    unnamed x8, local copies, waits for them, and re-layouts  2.28 us
  transfers between devices with their start and end apart: 13, of which 7 were waited for; matrix products, arithmetic and copies ran while one was open for 18% of the time, Pallas kernels for 2%

profile of v8, /device:TPU:9, one launch (start us, length us, event | category | flops | bytes accessed | tf_op | source)
XLA Modules:
  0.0 77.2 jit_solution(10038296351913790820)
XLA Ops:
  0.0 0.8 %fusion.1.tile_ref = s32[96]{0:T(128)S(1)} fusion(s32[3072,1]{0,1:T(1,128)} %param.8, s32[]{:T(128)S(6)} %select_n.69), kind=kLoop, calls=%fused_computation.22 | loop fusion | bytes 772 | tf_op jit(solution)/shard_map/dynamic_slice | solution.py:500
  0.8 1.0 %copy-done.2 = f32[96,1024]{1,0:T(8,128)S(1)} copy-done((f32[96,1024]{1,0:T(8,128)S(1)}, f32[96,1024]{1,0:T(8,128)}, u32[]{:S(2)}) %copy-start.2) | copy-done | bytes 393240
  1.8 2.1 %shard_map.55 = f32[16,12,8,128]{3,2,1,0:T(8,128)} custom-call(s32[96]{0:T(128)S(1)} %fusion.1.tile_ref, f32[96,1024]{1,0:T(8,128)S(1)} %copy-done.2), custom_call_target="tpu_custom_call" | custom-call | tf_op jit(solution)/shard_map/pallas_call | solution.py:458
  3.9 6.6 %all-to-all-start = ((f32[16,12,8,128]{3,2,1,0:T(8,128)}), f32[16,12,8,128]{3,2,1,0:T(8,128)S(1)}, u32[]{:S(2)}, u32[]{:S(2)}) async-start(f32[16,12,8,128]{3,2,1,0:T(8,128)} %shard_map.55), calls=%async_computation | async-start | bytes 1572864 | tf_op jit(solution)/shard_map/all_to_all | solution.py:508
  10.7 1.2 %collective-permute-start.3 = (f32[64,3,256]{2,1,0:T(4,128)S(1)}, f32[64,3,256]{2,1,0:T(4,128)S(1)}, u32[]{:S(2)}, u32[]{:S(2)}) collective-permute-start(f32[64,3,256]{2,1,0:T(4,128)S(1)} %pad_maximum_fusion.3), channel_id=1, source_target_pairs={{0,2},{2,0},{1,3},{3,1},{4,6},{6,4},{5,7},{7,5},{8,10},{10,8},{9,1... | collective-permute-start | bytes 589832 | tf_op jit(solution)/shard_map/ppermute | solution.py:47
  12.0 0.8 pad_maximum_fusion.1
  12.8 1.2 %collective-permute-start.1 = (f32[20,16,256]{2,1,0:T(8,128)}, f32[20,16,256]{2,1,0:T(8,128)S(1)}, u32[]{:S(2)}, u32[]{:S(2)}) collective-permute-start(f32[20,16,256]{2,1,0:T(8,128)} %pad_maximum_fusion.1), channel_id=1, source_target_pairs={{0,4},{4,0},{8,12},{12,8},{16,20},{20,16},{24,28},{28,24},{1,5},{5... | collective-permute-start | bytes 983048 | tf_op jit(solution)/shard_map/ppermute | solution.py:47
  14.0 0.7 pad_maximum_fusion.2
  14.7 2.2 %collective-permute-start.2 = (f32[20,16,256]{2,1,0:T(8,128)}, f32[20,16,256]{2,1,0:T(8,128)S(1)}, u32[]{:S(2)}, u32[]{:S(2)}) collective-permute-start(f32[20,16,256]{2,1,0:T(8,128)} %pad_maximum_fusion.2), channel_id=1, source_target_pairs={{4,8},{8,4},{12,16},{16,12},{20,24},{24,20},{5,9},{9,5},{13,17},{1... | collective-permute-start | bytes 983048 | tf_op jit(solution)/shard_map/ppermute | solution.py:46
  17.0 0.8 %pad_maximum_fusion = f32[64,16,128]{2,1,0:T(8,128)} fusion(f32[32,16,128]{2,1,0:T(8,128)S(1)} %bitcast.31, f32[32,16,128]{2,1,0:T(8,128)S(1)} %bitcast.32), kind=kLoop, calls=%fused_computation.1 | loop fusion | flops 131072 | bytes 1048576 | tf_op jit(solution)/shard_map/concatenate | solution.py:40
  17.8 2.1 %collective-permute-start = (f32[64,16,128]{2,1,0:T(8,128)}, f32[64,16,128]{2,1,0:T(8,128)S(1)}, u32[]{:S(2)}, u32[]{:S(2)}) collective-permute-start(f32[64,16,128]{2,1,0:T(8,128)} %pad_maximum_fusion), channel_id=1, source_target_pairs={{0,1},{1,0},{2,3},{3,2},{4,5},{5,4},{6,7},{7,6},{8,9},{9,8},{10,11... | collective-permute-start | bytes 1572872 | tf_op jit(solution)/shard_map/ppermute | solution.py:47
  20.5 1.4 %reduce.3 = s32[3072]{0:T(1024)S(1)} reduce(s32[3072,1]{0,1:T(1,128)} %param.8, s32[]{:T(128)} %broadcast.31), dimensions={1}, to_apply=%param.8.reduce_sub_computation.3 | reduce | bytes 24580 | tf_op args[3]
  22.5 1.4 %reshape.61 = s32[16,2,96]{2,1,0:T(2,128)} reshape(s32[3072]{0:T(1024)} %param.9) | data formatting | bytes 24576 | tf_op jit(solution)/shard_map/reshape | solution.py:472
  23.9 1.3 %dynamic-slice_compare_fusion = pred[16,1,96]{2,1,0:T(4,128)(4,1)} fusion(s32[16,2,96]{2,1,0:T(2,128)} %reshape_squeeze.3, s32[]{:T(128)S(6)} %select_n.71, s32[]{:T(128)S(6)} %add.50), kind=kLoop, calls=%fused_computation.10 | loop fusion | flops 1536 | bytes 7688 | tf_op jit(solution)/shard_map/eq | solution.py:473
  25.2 1.3 %dynamic-slice_add_fusion = s32[16,1,96]{2,1,0:T(1,128)} fusion(s32[16,2,96]{2,1,0:T(2,128)} %reshape.61, s32[]{:T(128)S(6)} %select_n.71), kind=kLoop, calls=%fused_computation.9 | loop fusion | flops 1536 | bytes 12292 | tf_op jit(solution)/shard_map/sub | solution.py:479
  28.9 1.0 %select_reduce_fusion.1 = s32[16,12]{0,1:T(8,128)S(1)} fusion(s32[16,96]{1,0:T(8,128)} %bitcast.39, s32[16,96]{1,0:T(8,128)S(1)} %select_reduce_fusion, pred[16,96]{1,0:T(8,128)(4,1)S(1)} %bitcast.41), kind=kLoop, calls=%fused_computation.5 | loop fusion | flops 73536 | bytes 14592 | tf_op jit(solution)/shard_map/reduce_sum | solution.py:479
  30.6 0.8 %add.56.slot_ref = s32[192]{0:T(256)S(1)} reshape(s32[16,12]{1,0:T(8,128)} %copy.6) | data formatting | bytes 1536 | tf_op jit(solution)/shard_map/add | solution.py:479
  31.4 1.6 %shard_map.56 = (f32[1,8,16,256]{3,2,1,0:T(8,128)S(1)}, f32[4,8,256]{2,1,0:T(8,128)S(1)}, f32[2,16,256]{2,1,0:T(8,128)S(1)}, f32[2,16,256]{2,1,0:T(8,128)S(1)}) custom-call(s32[9]{0:T(128)S(1)} %convert_element_type.3.flags, s32[192]{0:T(256)S(1)} %add.56.slot_ref, f32[16,12,8,128]{3,2,1,0:T(8,128)S(1)} %all-to-all-done.rows_ref), custom_call_target="tpu_custom_call" | custom-call | tf_op jit(solution)/shard_map/pallas_call | solution.py:458
  33.0 1.9 %collective-permute-start.4 = (f32[2,16,256]{2,1,0:T(8,128)S(1)}, f32[2,16,256]{2,1,0:T(8,128)S(1)}, u32[]{:S(2)}, u32[]{:S(2)}) collective-permute-start(f32[2,16,256]{2,1,0:T(8,128)S(1)} %get-tuple-element.32), channel_id=1, source_target_pairs={{0,4},{4,0},{8,12},{12,8},{16,20},{20,16},{24,28},{28,24},{1,5},{5... | collective-permute-start | bytes 98312 | tf_op jit(solution)/shard_map/ppermute | solution.py:47
  34.9 2.3 %collective-permute-start.5 = (f32[2,16,256]{2,1,0:T(8,128)S(1)}, f32[2,16,256]{2,1,0:T(8,128)S(1)}, u32[]{:S(2)}, u32[]{:S(2)}) collective-permute-start(f32[2,16,256]{2,1,0:T(8,128)S(1)} %get-tuple-element.33), channel_id=1, source_target_pairs={{4,8},{8,4},{12,16},{16,12},{20,24},{24,20},{5,9},{9,5},{13,17},{1... | collective-permute-start | bytes 98312 | tf_op jit(solution)/shard_map/ppermute | solution.py:46
  37.2 3.2 %collective-permute-done.5.refs_1_.refs_2_ = f32[2,16,256]{2,1,0:T(8,128)S(1)} collective-permute-done((f32[2,16,256]{2,1,0:T(8,128)S(1)}, f32[2,16,256]{2,1,0:T(8,128)S(1)}, u32[]{:S(2)}, u32[]{:S(2)}) %collective-permute-start.5) | collective-permute-done | bytes 32800 | tf_op jit(solution)/shard_map/ppermute | solution.py:46
  41.8 2.9 %collective-permute-done.6.refs_6_ = f32[52,2,256]{2,1,0:T(2,128)S(1)} collective-permute-done((f32[52,2,256]{2,1,0:T(2,128)S(1)}, f32[52,2,256]{2,1,0:T(2,128)S(1)}, u32[]{:S(2)}, u32[]{:S(2)}) %collective-permute-start.6) | collective-permute-done | bytes 106528 | tf_op jit(solution)/shard_map/ppermute | solution.py:47
  45.3 2.7 %collective-permute-start.7 = (f32[81,16,128]{2,1,0:T(8,128)S(1)}, f32[81,16,128]{2,1,0:T(8,128)S(1)}, u32[]{:S(2)}, u32[]{:S(2)}) collective-permute-start(f32[81,16,128]{2,1,0:T(8,128)S(1)} %shard_map.58), channel_id=1, source_target_pairs={{0,1},{1,0},{2,3},{3,2},{4,5},{5,4},{6,7},{7,6},{8,9},{9,8},{10,11... | collective-permute-start | bytes 1990664 | tf_op jit(solution)/shard_map/ppermute | solution.py:47
  48.1 1.7 %collective-permute-done.7.refs_7_ = f32[81,16,128]{2,1,0:T(8,128)S(1)} collective-permute-done((f32[81,16,128]{2,1,0:T(8,128)S(1)}, f32[81,16,128]{2,1,0:T(8,128)S(1)}, u32[]{:S(2)}, u32[]{:S(2)}) %collective-permute-start.7) | collective-permute-done | bytes 663584 | tf_op jit(solution)/shard_map/ppermute | solution.py:47
  49.8 4.1 %shard_map.59 = (f32[4,12,24,384]{3,2,1,0:T(8,128)S(1)}, f32[4,12,24,384]{3,2,1,0:T(8,128)S(1)}, f32[12,24,384]{2,1,0:T(8,128)S(1)}, f32[36,8,128]{2,1,0:T(8,128...) custom-call(s32[9]{0:T(128)S(1)} %convert_element_type.3.flags, ...), custom_call_target="tpu_custom_call" | custom-call | tf_op jit(solution)/shard_map/pallas_call | solution.py:458
  54.4 1.9 %collective-permute-start.9 = (f32[36,8,128]{2,1,0:T(8,128)S(1)}, f32[36,8,128]{2,1,0:T(8,128)S(1)}, u32[]{:S(2)}, u32[]{:S(2)}) collective-permute-start(f32[36,8,128]{2,1,0:T(8,128)S(1)} %get-tuple-element.44), channel_id=1, source_target_pairs={{4,8},{8,4},{12,16},{16,12},{20,24},{24,20},{5,9},{9,5},{13,17},{1... | collective-permute-start | bytes 442376 | tf_op jit(solution)/shard_map/ppermute | solution.py:46
  56.3 2.7 %collective-permute-done.8.refs_2_.refs_1_.refs_0_ = f32[36,8,128]{2,1,0:T(8,128)S(1)} collective-permute-done((f32[36,8,128]{2,1,0:T(8,128)S(1)}, f32[36,8,128]{2,1,0:T(8,128)S(1)}, u32[]{:S(2)}, u32[]{:S(2)}) %collective-permute-start.8) | collective-permute-done | bytes 147488 | tf_op jit(solution)/shard_map/ppermute | solution.py:47
  59.0 2.9 %collective-permute-done.9.refs_1_.refs_2_ = f32[36,8,128]{2,1,0:T(8,128)S(1)} collective-permute-done((f32[36,8,128]{2,1,0:T(8,128)S(1)}, f32[36,8,128]{2,1,0:T(8,128)S(1)}, u32[]{:S(2)}, u32[]{:S(2)}) %collective-permute-start.9) | collective-permute-done | bytes 147488 | tf_op jit(solution)/shard_map/ppermute | solution.py:46
  63.0 3.7 %collective-permute-done.10.refs_3_.refs_2_ = f32[80,4,128]{2,1,0:T(4,128)S(1)} collective-permute-done((f32[80,4,128]{2,1,0:T(4,128)S(1)}, f32[80,4,128]{2,1,0:T(4,128)S(1)}, u32[]{:S(2)}, u32[]{:S(2)}) %collective-permute-start.10) | collective-permute-done | bytes 163872 | tf_op jit(solution)/shard_map/ppermute | solution.py:47
  67.3 2.7 %collective-permute-start.11 = (f32[210,8,128]{2,1,0:T(8,128)S(1)}, f32[210,8,128]{2,1,0:T(8,128)S(1)}, u32[]{:S(2)}, u32[]{:S(2)}) collective-permute-start(f32[210,8,128]{2,1,0:T(8,128)S(1)} %shard_map.61), channel_id=1, source_target_pairs={{0,1},{1,0},{2,3},{3,2},{4,5},{5,4},{6,7},{7,6},{8,9},{9,8},{10,11... | collective-permute-start | bytes 2580488 | tf_op jit(solution)/shard_map/ppermute | solution.py:47
  70.1 2.0 %collective-permute-done.11.refs_3_ = f32[210,8,128]{2,1,0:T(8,128)S(1)} collective-permute-done((f32[210,8,128]{2,1,0:T(8,128)S(1)}, f32[210,8,128]{2,1,0:T(8,128)S(1)}, u32[]{:S(2)}, u32[]{:S(2)}) %collective-permute-start.11) | collective-permute-done | bytes 860192 | tf_op jit(solution)/shard_map/ppermute | solution.py:47
  72.1 5.1 %shard_map.62 = f32[4,8,16,256]{3,2,1,0:T(8,128)} custom-call(s32[9]{0:T(128)S(1)} %convert_element_type.3.flags, f32[36,8,128]{2,1,0:T(8,128)S(1)} %get-tuple-element.40.refs_0_.own, f32[4,12,24,384]{3,2,1,0:T(8,128)S(1)} %get-tuple-element.41.state, f32[12,24,384]{2,1,0:T(8,128)S(1)} %get-tuple-element.42.weight, ...), custom_call_target="tpu_custom_call" | custom-call | tf_op jit(solution)/shard_map/pallas_call | solution.py:458
  (34 shorter events, 8.7 us)
Async XLA Ops:
  0.0 10.5 %copy-start = (f32[4,8,16,256]{3,2,1,0:T(8,128)S(1)}, f32[4,8,16,256]{3,2,1,0:T(8,128)}, u32[]{:S(2)}) copy-start(f32[4,8,16,256]{3,2,1,0:T(8,128)} %start_field) | copy-start | bytes 1572868
  0.0 10.5 %copy-start.1 = (f32[4,8,16,256]{3,2,1,0:T(8,128)S(1)}, f32[4,8,16,256]{3,2,1,0:T(8,128)}, u32[]{:S(2)}) copy-start(f32[4,8,16,256]{3,2,1,0:T(8,128)} %right_side) | copy-start | bytes 1572868
  0.8 1.0 %copy-start.2 = (f32[96,1024]{1,0:T(8,128)S(1)}, f32[96,1024]{1,0:T(8,128)}, u32[]{:S(2)}) copy-start(f32[96,1024]{1,0:T(8,128)} %mask_ref.1) | copy-start | bytes 1179652
  3.9 27.5 %all-to-all-start = ((f32[16,12,8,128]{3,2,1,0:T(8,128)}), f32[16,12,8,128]{3,2,1,0:T(8,128)S(1)}, u32[]{:S(2)}, u32[]{:S(2)}) async-start(f32[16,12,8,128]{3,2,1,0:T(8,128)} %shard_map.55), calls=%async_computation | async-start | bytes 1572864 | tf_op jit(solution)/shard_map/all_to_all | solution.py:508
  10.7 26.5 %collective-permute-start.3 = (f32[64,3,256]{2,1,0:T(4,128)S(1)}, f32[64,3,256]{2,1,0:T(4,128)S(1)}, u32[]{:S(2)}, u32[]{:S(2)}) collective-permute-start(f32[64,3,256]{2,1,0:T(4,128)S(1)} %pad_maximum_fusion.3), channel_id=1, source_target_pairs={{0,2},{2,0},{1,3},{3,1},{4,6},{6,4},{5,7},{7,5},{8,10},{10,8},{9,1... | collective-permute-start | bytes 589832 | tf_op jit(solution)/shard_map/ppermute | solution.py:47
  12.8 24.4 %collective-permute-start.1 = (f32[20,16,256]{2,1,0:T(8,128)}, f32[20,16,256]{2,1,0:T(8,128)S(1)}, u32[]{:S(2)}, u32[]{:S(2)}) collective-permute-start(f32[20,16,256]{2,1,0:T(8,128)} %pad_maximum_fusion.1), channel_id=1, source_target_pairs={{0,4},{4,0},{8,12},{12,8},{16,20},{20,16},{24,28},{28,24},{1,5},{5... | collective-permute-start | bytes 983048 | tf_op jit(solution)/shard_map/ppermute | solution.py:47
  14.7 22.5 %collective-permute-start.2 = (f32[20,16,256]{2,1,0:T(8,128)}, f32[20,16,256]{2,1,0:T(8,128)S(1)}, u32[]{:S(2)}, u32[]{:S(2)}) collective-permute-start(f32[20,16,256]{2,1,0:T(8,128)} %pad_maximum_fusion.2), channel_id=1, source_target_pairs={{4,8},{8,4},{12,16},{16,12},{20,24},{24,20},{5,9},{9,5},{13,17},{1... | collective-permute-start | bytes 983048 | tf_op jit(solution)/shard_map/ppermute | solution.py:46
  17.8 13.6 %collective-permute-start = (f32[64,16,128]{2,1,0:T(8,128)}, f32[64,16,128]{2,1,0:T(8,128)S(1)}, u32[]{:S(2)}, u32[]{:S(2)}) collective-permute-start(f32[64,16,128]{2,1,0:T(8,128)} %pad_maximum_fusion), channel_id=1, source_target_pairs={{0,1},{1,0},{2,3},{3,2},{4,5},{5,4},{6,7},{7,6},{8,9},{9,8},{10,11... | collective-permute-start | bytes 1572872 | tf_op jit(solution)/shard_map/ppermute | solution.py:47
  33.0 4.2 %collective-permute-start.4 = (f32[2,16,256]{2,1,0:T(8,128)S(1)}, f32[2,16,256]{2,1,0:T(8,128)S(1)}, u32[]{:S(2)}, u32[]{:S(2)}) collective-permute-start(f32[2,16,256]{2,1,0:T(8,128)S(1)} %get-tuple-element.32), channel_id=1, source_target_pairs={{0,4},{4,0},{8,12},{12,8},{16,20},{20,16},{24,28},{28,24},{1,5},{5... | collective-permute-start | bytes 98312 | tf_op jit(solution)/shard_map/ppermute | solution.py:47
  34.9 5.5 %collective-permute-start.5 = (f32[2,16,256]{2,1,0:T(8,128)S(1)}, f32[2,16,256]{2,1,0:T(8,128)S(1)}, u32[]{:S(2)}, u32[]{:S(2)}) collective-permute-start(f32[2,16,256]{2,1,0:T(8,128)S(1)} %get-tuple-element.33), channel_id=1, source_target_pairs={{4,8},{8,4},{12,16},{16,12},{20,24},{24,20},{5,9},{9,5},{13,17},{1... | collective-permute-start | bytes 98312 | tf_op jit(solution)/shard_map/ppermute | solution.py:46
  41.1 3.6 %collective-permute-start.6 = (f32[52,2,256]{2,1,0:T(2,128)S(1)}, f32[52,2,256]{2,1,0:T(2,128)S(1)}, u32[]{:S(2)}, u32[]{:S(2)}) collective-permute-start(f32[52,2,256]{2,1,0:T(2,128)S(1)} %shard_map.57), channel_id=1, source_target_pairs={{0,2},{2,0},{1,3},{3,1},{4,6},{6,4},{5,7},{7,5},{8,10},{10,8},{9,1... | collective-permute-start | bytes 319496 | tf_op jit(solution)/shard_map/ppermute | solution.py:47
  45.3 4.5 %collective-permute-start.7 = (f32[81,16,128]{2,1,0:T(8,128)S(1)}, f32[81,16,128]{2,1,0:T(8,128)S(1)}, u32[]{:S(2)}, u32[]{:S(2)}) collective-permute-start(f32[81,16,128]{2,1,0:T(8,128)S(1)} %shard_map.58), channel_id=1, source_target_pairs={{0,1},{1,0},{2,3},{3,2},{4,5},{5,4},{6,7},{7,6},{8,9},{9,8},{10,11... | collective-permute-start | bytes 1990664 | tf_op jit(solution)/shard_map/ppermute | solution.py:47
  53.9 5.1 %collective-permute-start.8 = (f32[36,8,128]{2,1,0:T(8,128)S(1)}, f32[36,8,128]{2,1,0:T(8,128)S(1)}, u32[]{:S(2)}, u32[]{:S(2)}) collective-permute-start(f32[36,8,128]{2,1,0:T(8,128)S(1)} %get-tuple-element.40.refs_0_.own), channel_id=1, source_target_pairs={{0,4},{4,0},{8,12},{12,8},{16,20},{20,16},{24,28},{28,24},{1,5},{5... | collective-permute-start | bytes 442376 | tf_op jit(solution)/shard_map/ppermute | solution.py:47
  54.4 7.5 %collective-permute-start.9 = (f32[36,8,128]{2,1,0:T(8,128)S(1)}, f32[36,8,128]{2,1,0:T(8,128)S(1)}, u32[]{:S(2)}, u32[]{:S(2)}) collective-permute-start(f32[36,8,128]{2,1,0:T(8,128)S(1)} %get-tuple-element.44), channel_id=1, source_target_pairs={{4,8},{8,4},{12,16},{16,12},{20,24},{24,20},{5,9},{9,5},{13,17},{1... | collective-permute-start | bytes 442376 | tf_op jit(solution)/shard_map/ppermute | solution.py:46
  62.5 4.2 %collective-permute-start.10 = (f32[80,4,128]{2,1,0:T(4,128)S(1)}, f32[80,4,128]{2,1,0:T(4,128)S(1)}, u32[]{:S(2)}, u32[]{:S(2)}) collective-permute-start(f32[80,4,128]{2,1,0:T(4,128)S(1)} %shard_map.60), channel_id=1, source_target_pairs={{0,2},{2,0},{1,3},{3,1},{4,6},{6,4},{5,7},{7,5},{8,10},{10,8},{9,1... | collective-permute-start | bytes 491528 | tf_op jit(solution)/shard_map/ppermute | solution.py:47
  67.3 4.7 %collective-permute-start.11 = (f32[210,8,128]{2,1,0:T(8,128)S(1)}, f32[210,8,128]{2,1,0:T(8,128)S(1)}, u32[]{:S(2)}, u32[]{:S(2)}) collective-permute-start(f32[210,8,128]{2,1,0:T(8,128)S(1)} %shard_map.61), channel_id=1, source_target_pairs={{0,1},{1,0},{2,3},{3,2},{4,5},{5,4},{6,7},{7,6},{8,9},{9,8},{10,11... | collective-permute-start | bytes 2580488 | tf_op jit(solution)/shard_map/ppermute | solution.py:47

commit v9 on v8

--- a/solution.py
+++ b/solution.py
@@ -234,8 +234,7 @@
     return got, refs[at:]
 
 
-def chi_kernel(flags, slot_ref, rows_ref, out, coarse_out, *refs):
-    *x_out, acc, pooled = refs
+def chi_kernel(slot_ref, rows_ref, out, coarse_out, acc, pooled):
     _, planes, rows, lanes = out.shape
     acc[...] = jnp.zeros(acc.shape, jnp.float32)
     per = rows_ref.shape[1]
@@ -259,10 +258,6 @@
                     total = v if total is None else total + v
                 out[0, 2 * qx + i, :, zt * LANES:(zt + 1) * LANES] = pooled[zt]
             coarse_out[qx, :, zt * LANES:(zt + 1) * LANES] = total
-    for n, ref in enumerate(x_out):
-        start = jnp.where((flags[0] == 1) == (n == 0), planes - FINE_W, 0)
-        for j in range(FINE_W):
-            ref[j] = out[0, start + j]
 
 
 def side(up, v, dim, width):
@@ -515,15 +510,16 @@
     first_x = halo_x(groups)
     first_y = swap("gy", lambda up, n: flat([cut(v, 2, START_W, up) for v, _ in groups]))
     first_z = swap("lvl", lambda up, n: flat([cut(v, 3, LANES, up) for v, _ in groups]))
-    first_z, slot_of = lax.optimization_barrier((first_z, slot_of))
-    chi, pooled_chi, *chi_out = call(
+    first_y, first_z, slot_of = lax.optimization_barrier((first_y, first_z, slot_of))
+    chi, pooled_chi = call(
         chi_kernel,
-        [(1, planes, rows, lanes), (c_planes, c_rows, lanes), *[(FINE_W, rows, lanes)] * pair_counts[0]],
+        [(1, planes, rows, lanes), (c_planes, c_rows, lanes)],
         [pltpu.VMEM(((slots + 1) * 8, LANES), jnp.float32), pltpu.VMEM((lanes // LANES, rows, LANES), jnp.float32)],
-        flags, slot_of, arrived, smem=2,
-    )
-    chi_x = swap("gx", lambda up, n: chi_out[n])
-    first_x, first_y, chi_x = lax.optimization_barrier((first_x, first_y, chi_x))
+        slot_of, arrived,
+    )
+    group = [(chi, FINE_W)]
+    chi_x = halo_x(group)
+    first_x, chi_x = lax.optimization_barrier((first_x, chi_x))
     slabs = lambda v: v.reshape(-1, rows, lanes)
     far_x = len(first_x) * 4 * (START_W + FINE_W)
     chi_slabs = planes + len(chi_x) * FINE_W

time: 78 us -> 77.2 us (0.990)
  waiting for transfers between devices: 19.2 us -> 24.5 us
  local copies, waits for them, and re-layouts: 7.5 us -> 2.95 us
  other arithmetic: 8.39 us -> 4.27 us
  starting transfers between devices: 26.7 us -> 29.5 us
    all_to_all x1, waiting for transfers between devices: 0.01 us -> 6.17 us  [body(): lax.all_to_all(outgoing, ('gx', 'gy'), split_axis=0, concat_axis=0, tiled...]
    ppermute x9, starting transfers between devices: 13.7 us -> 16.3 us  [swap(): got.insert(0, lax.ppermute(message(even, 0), axis, pairs(count, 0)))]
    sub x1, other arithmetic: 1.33 us -> 0.02 us  [routes(): their_slots[:, None, :] - slots]
    eq x1, other arithmetic: 1.33 us -> 0.02 us  [routes(): arriving = their_tiles == my_tile]
    reshape x1, local copies, waits for them, and re-layouts: 1.39 us -> 0.08 us  [routes(): block_slot.reshape(tiles, count_l, per_device)]
    add x2, local copies, waits for them, and re-layouts: 1.46 us -> 0.17 us  [routes(): jnp.sum(jnp.where(hit, their_slots[:, None, :] - slots, 0), axis=2) + slots]
    unnamed x1, other arithmetic: 1.37 us -> 0.58 us
    unnamed x8 -> x12, local copies, waits for them, and re-layouts: 2.28 us -> 1.5 us
  transfers between devices with their start and end apart: 13 -> 13, of which waited for: 7 -> 10; matrix products, arithmetic and copies ran while one was open for 18% -> 7% of each run, Pallas kernels for 2% -> 2%
where the time goes in v9:
time: 77.2 us; the launch traced here: 76.9 us
  starting transfers between devices  29.5 us (38%)
  waiting for transfers between devices  24.5 us (32%)
  Pallas kernels  15.4 us (20%)
  other arithmetic  4.27 us (6%)
  local copies, waits for them, and re-layouts  2.95 us (4%)
    ppermute x9, starting transfers between devices, swap(): got.insert(0, lax.ppermute(message(even, 0), axis, pairs(count, 0)))  16.3 us
    pallas_call x8, Pallas kernels, call(): pl.pallas_call(kernel, out_shape=outs, in_specs=[SMEM] * smem + [VMEM] *...  15.4 us
    ppermute x9, waiting for transfers between devices, swap(): got.insert(0, lax.ppermute(message(even, 0), axis, pairs(count, 0)))  12.8 us
    all_to_all x1, starting transfers between devices, body(): lax.all_to_all(outgoing, ('gx', 'gy'), split_axis=0, concat_axis=0, tiled...  6.64 us
    ppermute x3, starting transfers between devices, swap(): lax.ppermute(message(~even, 1), axis, pairs(count, 1))  6.56 us
    all_to_all x1, waiting for transfers between devices, body(): lax.all_to_all(outgoing, ('gx', 'gy'), split_axis=0, concat_axis=0, tiled...  6.17 us
    ppermute x3, waiting for transfers between devices, swap(): lax.ppermute(message(~even, 1), axis, pairs(count, 1))  5.58 us
    concatenate x4, other arithmetic, flat(): jnp.concatenate([p.reshape(-1, *p.shape[-2:]) for p in parts], axis=0)  3.07 us
  transfers between devices with their start and end apart: 13, of which 10 were waited for; matrix products, arithmetic and copies ran while one was open for 7% of the time, Pallas kernels for 2%

profile of v9, /device:TPU:9, one launch (start us, length us, event | category | flops | bytes accessed | tf_op | source)
XLA Modules:
  0.0 76.9 jit_solution(12156056242012331683)
XLA Ops:
  0.0 0.8 %fusion.1.tile_ref = s32[96]{0:T(128)S(1)} fusion(s32[3072,1]{0,1:T(1,128)} %param.8, s32[]{:T(128)S(6)} %select_n.75), kind=kLoop, calls=%fused_computation.24 | loop fusion | bytes 772 | tf_op jit(solution)/shard_map/dynamic_slice | solution.py:495
  0.8 1.0 %copy-done.2 = f32[96,1024]{1,0:T(8,128)S(1)} copy-done((f32[96,1024]{1,0:T(8,128)S(1)}, f32[96,1024]{1,0:T(8,128)}, u32[]{:S(2)}) %copy-start.2) | copy-done | bytes 393240
  1.8 2.0 %shard_map.55 = f32[16,12,8,128]{3,2,1,0:T(8,128)} custom-call(s32[96]{0:T(128)S(1)} %fusion.1.tile_ref, f32[96,1024]{1,0:T(8,128)S(1)} %copy-done.2), custom_call_target="tpu_custom_call" | custom-call | tf_op jit(solution)/shard_map/pallas_call | solution.py:453
  3.9 6.6 %all-to-all-start = ((f32[16,12,8,128]{3,2,1,0:T(8,128)}), f32[16,12,8,128]{3,2,1,0:T(8,128)S(1)}, u32[]{:S(2)}, u32[]{:S(2)}) async-start(f32[16,12,8,128]{3,2,1,0:T(8,128)} %shard_map.55), calls=%async_computation | async-start | bytes 1572864 | tf_op jit(solution)/shard_map/all_to_all | solution.py:503
  10.6 0.8 pad_maximum_fusion.3
  11.4 1.2 %collective-permute-start = (f32[64,3,256]{2,1,0:T(4,128)}, f32[64,3,256]{2,1,0:T(4,128)S(1)}, u32[]{:S(2)}, u32[]{:S(2)}) collective-permute-start(f32[64,3,256]{2,1,0:T(4,128)} %pad_maximum_fusion.3), channel_id=1, source_target_pairs={{0,2},{2,0},{1,3},{3,1},{4,6},{6,4},{5,7},{7,5},{8,10},{10,8},{9,1... | collective-permute-start | bytes 589832 | tf_op jit(solution)/shard_map/ppermute | solution.py:47
  12.6 0.7 pad_maximum_fusion.1
  13.4 1.2 %collective-permute-start.2 = (f32[20,16,256]{2,1,0:T(8,128)}, f32[20,16,256]{2,1,0:T(8,128)S(1)}, u32[]{:S(2)}, u32[]{:S(2)}) collective-permute-start(f32[20,16,256]{2,1,0:T(8,128)} %pad_maximum_fusion.1), channel_id=1, source_target_pairs={{0,4},{4,0},{8,12},{12,8},{16,20},{20,16},{24,28},{28,24},{1,5},{5... | collective-permute-start | bytes 983048 | tf_op jit(solution)/shard_map/ppermute | solution.py:47
  14.6 0.7 pad_maximum_fusion.2
  15.3 2.2 %collective-permute-start.3 = (f32[20,16,256]{2,1,0:T(8,128)}, f32[20,16,256]{2,1,0:T(8,128)S(1)}, u32[]{:S(2)}, u32[]{:S(2)}) collective-permute-start(f32[20,16,256]{2,1,0:T(8,128)} %pad_maximum_fusion.2), channel_id=1, source_target_pairs={{4,8},{8,4},{12,16},{16,12},{20,24},{24,20},{5,9},{9,5},{13,17},{1... | collective-permute-start | bytes 983048 | tf_op jit(solution)/shard_map/ppermute | solution.py:46
  17.6 0.8 %pad_maximum_fusion = f32[64,16,128]{2,1,0:T(8,128)} fusion(f32[32,16,128]{2,1,0:T(8,128)S(1)} %bitcast.35, f32[32,16,128]{2,1,0:T(8,128)S(1)} %bitcast.36), kind=kLoop, calls=%fused_computation.1 | loop fusion | flops 131072 | bytes 1048576 | tf_op jit(solution)/shard_map/concatenate | solution.py:40
  18.4 2.1 %collective-permute-start.1 = (f32[64,16,128]{2,1,0:T(8,128)}, f32[64,16,128]{2,1,0:T(8,128)S(1)}, u32[]{:S(2)}, u32[]{:S(2)}) collective-permute-start(f32[64,16,128]{2,1,0:T(8,128)} %pad_maximum_fusion), channel_id=1, source_target_pairs={{0,1},{1,0},{2,3},{3,2},{4,5},{5,4},{6,7},{7,6},{8,9},{9,8},{10,11... | collective-permute-start | bytes 1572872 | tf_op jit(solution)/shard_map/ppermute | solution.py:47
  22.6 1.2 %collective-permute-done.refs_5_.refs_4_ = f32[64,3,256]{2,1,0:T(4,128)S(1)} collective-permute-done((f32[64,3,256]{2,1,0:T(4,128)}, f32[64,3,256]{2,1,0:T(4,128)S(1)}, u32[]{:S(2)}, u32[]{:S(2)}) %collective-permute-start) | collective-permute-done | bytes 196640 | tf_op jit(solution)/shard_map/ppermute | solution.py:47
  23.8 6.2 %all-to-all-done.rows_ref = f32[16,12,8,128]{3,2,1,0:T(8,128)S(1)} async-done(((f32[16,12,8,128]{3,2,1,0:T(8,128)}), f32[16,12,8,128]{3,2,1,0:T(8,128)S(1)}, u32[]{:S(2)}, u32[]{:S(2)}) %all-to-all-start) | async-done | bytes 786464 | tf_op jit(solution)/shard_map/all_to_all | solution.py:503
  30.0 1.6 %shard_map.56 = (f32[1,8,16,256]{3,2,1,0:T(8,128)S(1)}, f32[4,8,256]{2,1,0:T(8,128)S(1)}) custom-call(s32[192]{0:T(256)S(1)} %add.59.slot_ref, f32[16,12,8,128]{3,2,1,0:T(8,128)S(1)} %all-to-all-done.rows_ref), custom_call_target="tpu_custom_call" | custom-call | tf_op jit(solution)/shard_map/pallas_call | solution.py:453
  31.6 1.9 %collective-permute-start.5 = (f32[2,16,256]{2,1,0:T(8,128)S(1)}, f32[2,16,256]{2,1,0:T(8,128)S(1)}, u32[]{:S(2)}, u32[]{:S(2)}) collective-permute-start(f32[2,16,256]{2,1,0:T(8,128)S(1)} %get-tuple-element.47), channel_id=1, source_target_pairs={{4,8},{8,4},{12,16},{16,12},{20,24},{24,20},{5,9},{9,5},{13,17},{1... | collective-permute-start | bytes 98312 | tf_op jit(solution)/shard_map/ppermute | solution.py:46
  33.5 1.4 %collective-permute-start.4 = (f32[2,16,256]{2,1,0:T(8,128)S(1)}, f32[2,16,256]{2,1,0:T(8,128)S(1)}, u32[]{:S(2)}, u32[]{:S(2)}) collective-permute-start(f32[2,16,256]{2,1,0:T(8,128)S(1)} %get-tuple-element.48), channel_id=1, source_target_pairs={{0,4},{4,0},{8,12},{12,8},{16,20},{20,16},{24,28},{28,24},{1,5},{5... | collective-permute-start | bytes 98312 | tf_op jit(solution)/shard_map/ppermute | solution.py:47
  35.3 1.9 %collective-permute-done.5.refs_1_.refs_2_ = f32[2,16,256]{2,1,0:T(8,128)S(1)} collective-permute-done((f32[2,16,256]{2,1,0:T(8,128)S(1)}, f32[2,16,256]{2,1,0:T(8,128)S(1)}, u32[]{:S(2)}, u32[]{:S(2)}) %collective-permute-start.5) | collective-permute-done | bytes 32800 | tf_op jit(solution)/shard_map/ppermute | solution.py:46
  37.7 0.9 %collective-permute-start.6 = (f32[52,2,256]{2,1,0:T(2,128)S(1)}, f32[52,2,256]{2,1,0:T(2,128)S(1)}, u32[]{:S(2)}, u32[]{:S(2)}) collective-permute-start(f32[52,2,256]{2,1,0:T(2,128)S(1)} %shard_map.57), channel_id=1, source_target_pairs={{0,2},{2,0},{1,3},{3,1},{4,6},{6,4},{5,7},{7,5},{8,10},{10,8},{9,1... | collective-permute-start | bytes 319496 | tf_op jit(solution)/shard_map/ppermute | solution.py:47
  38.6 2.7 %collective-permute-done.6.refs_6_ = f32[52,2,256]{2,1,0:T(2,128)S(1)} collective-permute-done((f32[52,2,256]{2,1,0:T(2,128)S(1)}, f32[52,2,256]{2,1,0:T(2,128)S(1)}, u32[]{:S(2)}, u32[]{:S(2)}) %collective-permute-start.6) | collective-permute-done | bytes 106528 | tf_op jit(solution)/shard_map/ppermute | solution.py:47
  42.0 4.8 %collective-permute-start.7 = (f32[81,16,128]{2,1,0:T(8,128)S(1)}, f32[81,16,128]{2,1,0:T(8,128)S(1)}, u32[]{:S(2)}, u32[]{:S(2)}) collective-permute-start(f32[81,16,128]{2,1,0:T(8,128)S(1)} %shard_map.58), channel_id=1, source_target_pairs={{0,1},{1,0},{2,3},{3,2},{4,5},{5,4},{6,7},{7,6},{8,9},{9,8},{10,11... | collective-permute-start | bytes 1990664 | tf_op jit(solution)/shard_map/ppermute | solution.py:47
  46.8 1.7 %collective-permute-done.7.refs_7_ = f32[81,16,128]{2,1,0:T(8,128)S(1)} collective-permute-done((f32[81,16,128]{2,1,0:T(8,128)S(1)}, f32[81,16,128]{2,1,0:T(8,128)S(1)}, u32[]{:S(2)}, u32[]{:S(2)}) %collective-permute-start.7) | collective-permute-done | bytes 663584 | tf_op jit(solution)/shard_map/ppermute | solution.py:47
  48.5 4.2 %shard_map.59 = (f32[4,12,24,384]{3,2,1,0:T(8,128)S(1)}, f32[4,12,24,384]{3,2,1,0:T(8,128)S(1)}, f32[12,24,384]{2,1,0:T(8,128)S(1)}, f32[36,8,128]{2,1,0:T(8,128...) custom-call(s32[9]{0:T(128)S(1)} %convert_element_type.3.flags, ...), custom_call_target="tpu_custom_call" | custom-call | tf_op jit(solution)/shard_map/pallas_call | solution.py:453
  52.7 1.3 %collective-permute-start.8 = (f32[36,8,128]{2,1,0:T(8,128)S(1)}, f32[36,8,128]{2,1,0:T(8,128)S(1)}, u32[]{:S(2)}, u32[]{:S(2)}) collective-permute-start(f32[36,8,128]{2,1,0:T(8,128)S(1)} %get-tuple-element.36.refs_0_.own), channel_id=1, source_target_pairs={{0,4},{4,0},{8,12},{12,8},{16,20},{20,16},{24,28},{28,24},{1,5},{5... | collective-permute-start | bytes 442376 | tf_op jit(solution)/shard_map/ppermute | solution.py:47
  54.0 2.5 %collective-permute-start.9 = (f32[36,8,128]{2,1,0:T(8,128)S(1)}, f32[36,8,128]{2,1,0:T(8,128)S(1)}, u32[]{:S(2)}, u32[]{:S(2)}) collective-permute-start(f32[36,8,128]{2,1,0:T(8,128)S(1)} %get-tuple-element.40), channel_id=1, source_target_pairs={{4,8},{8,4},{12,16},{16,12},{20,24},{24,20},{5,9},{9,5},{13,17},{1... | collective-permute-start | bytes 442376 | tf_op jit(solution)/shard_map/ppermute | solution.py:46
  56.5 1.3 %collective-permute-done.8.refs_2_.refs_1_.refs_0_ = f32[36,8,128]{2,1,0:T(8,128)S(1)} collective-permute-done((f32[36,8,128]{2,1,0:T(8,128)S(1)}, f32[36,8,128]{2,1,0:T(8,128)S(1)}, u32[]{:S(2)}, u32[]{:S(2)}) %collective-permute-start.8) | collective-permute-done | bytes 147488 | tf_op jit(solution)/shard_map/ppermute | solution.py:47
  57.8 3.7 %collective-permute-done.9.refs_1_.refs_2_ = f32[36,8,128]{2,1,0:T(8,128)S(1)} collective-permute-done((f32[36,8,128]{2,1,0:T(8,128)S(1)}, f32[36,8,128]{2,1,0:T(8,128)S(1)}, u32[]{:S(2)}, u32[]{:S(2)}) %collective-permute-start.9) | collective-permute-done | bytes 147488 | tf_op jit(solution)/shard_map/ppermute | solution.py:46
  62.1 0.7 collective-permute-start.10
  62.9 3.5 %collective-permute-done.10.refs_3_.refs_2_ = f32[80,4,128]{2,1,0:T(4,128)S(1)} collective-permute-done((f32[80,4,128]{2,1,0:T(4,128)S(1)}, f32[80,4,128]{2,1,0:T(4,128)S(1)}, u32[]{:S(2)}, u32[]{:S(2)}) %collective-permute-start.10) | collective-permute-done | bytes 163872 | tf_op jit(solution)/shard_map/ppermute | solution.py:47
  67.0 2.7 %collective-permute-start.11 = (f32[210,8,128]{2,1,0:T(8,128)S(1)}, f32[210,8,128]{2,1,0:T(8,128)S(1)}, u32[]{:S(2)}, u32[]{:S(2)}) collective-permute-start(f32[210,8,128]{2,1,0:T(8,128)S(1)} %shard_map.61), channel_id=1, source_target_pairs={{0,1},{1,0},{2,3},{3,2},{4,5},{5,4},{6,7},{7,6},{8,9},{9,8},{10,11... | collective-permute-start | bytes 2580488 | tf_op jit(solution)/shard_map/ppermute | solution.py:47
  69.7 2.0 %collective-permute-done.11.refs_3_ = f32[210,8,128]{2,1,0:T(8,128)S(1)} collective-permute-done((f32[210,8,128]{2,1,0:T(8,128)S(1)}, f32[210,8,128]{2,1,0:T(8,128)S(1)}, u32[]{:S(2)}, u32[]{:S(2)}) %collective-permute-start.11) | collective-permute-done | bytes 860192 | tf_op jit(solution)/shard_map/ppermute | solution.py:47
  71.7 5.2 %shard_map.62 = f32[4,8,16,256]{3,2,1,0:T(8,128)} custom-call(s32[9]{0:T(128)S(1)} %convert_element_type.3.flags, f32[36,8,128]{2,1,0:T(8,128)S(1)} %get-tuple-element.36.refs_0_.own, f32[4,12,24,384]{3,2,1,0:T(8,128)S(1)} %get-tuple-element.37.state, f32[12,24,384]{2,1,0:T(8,128)S(1)} %get-tuple-element.38.weight, ...), custom_call_target="tpu_custom_call" | custom-call | tf_op jit(solution)/shard_map/pallas_call | solution.py:453
  (39 shorter events, 4.9 us)
Async XLA Ops:
  0.0 10.5 %copy-start = (f32[4,8,16,256]{3,2,1,0:T(8,128)S(1)}, f32[4,8,16,256]{3,2,1,0:T(8,128)}, u32[]{:S(2)}) copy-start(f32[4,8,16,256]{3,2,1,0:T(8,128)} %start_field) | copy-start | bytes 1572868
  0.0 10.5 %copy-start.1 = (f32[4,8,16,256]{3,2,1,0:T(8,128)S(1)}, f32[4,8,16,256]{3,2,1,0:T(8,128)}, u32[]{:S(2)}) copy-start(f32[4,8,16,256]{3,2,1,0:T(8,128)} %right_side) | copy-start | bytes 1572868
  0.8 1.0 %copy-start.2 = (f32[96,1024]{1,0:T(8,128)S(1)}, f32[96,1024]{1,0:T(8,128)}, u32[]{:S(2)}) copy-start(f32[96,1024]{1,0:T(8,128)} %mask_ref.1) | copy-start | bytes 1179652
  3.9 26.1 %all-to-all-start = ((f32[16,12,8,128]{3,2,1,0:T(8,128)}), f32[16,12,8,128]{3,2,1,0:T(8,128)S(1)}, u32[]{:S(2)}, u32[]{:S(2)}) async-start(f32[16,12,8,128]{3,2,1,0:T(8,128)} %shard_map.55), calls=%async_computation | async-start | bytes 1572864 | tf_op jit(solution)/shard_map/all_to_all | solution.py:503
  11.4 12.4 %collective-permute-start = (f32[64,3,256]{2,1,0:T(4,128)}, f32[64,3,256]{2,1,0:T(4,128)S(1)}, u32[]{:S(2)}, u32[]{:S(2)}) collective-permute-start(f32[64,3,256]{2,1,0:T(4,128)} %pad_maximum_fusion.3), channel_id=1, source_target_pairs={{0,2},{2,0},{1,3},{3,1},{4,6},{6,4},{5,7},{7,5},{8,10},{10,8},{9,1... | collective-permute-start | bytes 589832 | tf_op jit(solution)/shard_map/ppermute | solution.py:47
  12.6 8.4 %copy-start.4 = (s32[3072,1]{0,1:T(1,128)S(1)}, s32[3072,1]{0,1:T(1,128)}, u32[]{:S(2)}) copy-start(s32[3072,1]{0,1:T(1,128)} %param.8) | copy-start | bytes 36868
  12.6 9.0 %copy-start.3 = (s32[3072]{0:T(1024)S(1)}, s32[3072]{0:T(1024)}, u32[]{:S(2)}) copy-start(s32[3072]{0:T(1024)} %param.9) | copy-start | bytes 36868
  13.4 21.9 %collective-permute-start.2 = (f32[20,16,256]{2,1,0:T(8,128)}, f32[20,16,256]{2,1,0:T(8,128)S(1)}, u32[]{:S(2)}, u32[]{:S(2)}) collective-permute-start(f32[20,16,256]{2,1,0:T(8,128)} %pad_maximum_fusion.1), channel_id=1, source_target_pairs={{0,4},{4,0},{8,12},{12,8},{16,20},{20,16},{24,28},{28,24},{1,5},{5... | collective-permute-start | bytes 983048 | tf_op jit(solution)/shard_map/ppermute | solution.py:47
  15.3 19.9 %collective-permute-start.3 = (f32[20,16,256]{2,1,0:T(8,128)}, f32[20,16,256]{2,1,0:T(8,128)S(1)}, u32[]{:S(2)}, u32[]{:S(2)}) collective-permute-start(f32[20,16,256]{2,1,0:T(8,128)} %pad_maximum_fusion.2), channel_id=1, source_target_pairs={{4,8},{8,4},{12,16},{16,12},{20,24},{24,20},{5,9},{9,5},{13,17},{1... | collective-permute-start | bytes 983048 | tf_op jit(solution)/shard_map/ppermute | solution.py:46
  18.4 5.4 %collective-permute-start.1 = (f32[64,16,128]{2,1,0:T(8,128)}, f32[64,16,128]{2,1,0:T(8,128)S(1)}, u32[]{:S(2)}, u32[]{:S(2)}) collective-permute-start(f32[64,16,128]{2,1,0:T(8,128)} %pad_maximum_fusion), channel_id=1, source_target_pairs={{0,1},{1,0},{2,3},{3,2},{4,5},{5,4},{6,7},{7,6},{8,9},{9,8},{10,11... | collective-permute-start | bytes 1572872 | tf_op jit(solution)/shard_map/ppermute | solution.py:47
  31.6 5.6 %collective-permute-start.5 = (f32[2,16,256]{2,1,0:T(8,128)S(1)}, f32[2,16,256]{2,1,0:T(8,128)S(1)}, u32[]{:S(2)}, u32[]{:S(2)}) collective-permute-start(f32[2,16,256]{2,1,0:T(8,128)S(1)} %get-tuple-element.47), channel_id=1, source_target_pairs={{4,8},{8,4},{12,16},{16,12},{20,24},{24,20},{5,9},{9,5},{13,17},{1... | collective-permute-start | bytes 98312 | tf_op jit(solution)/shard_map/ppermute | solution.py:46
  33.5 3.6 %collective-permute-start.4 = (f32[2,16,256]{2,1,0:T(8,128)S(1)}, f32[2,16,256]{2,1,0:T(8,128)S(1)}, u32[]{:S(2)}, u32[]{:S(2)}) collective-permute-start(f32[2,16,256]{2,1,0:T(8,128)S(1)} %get-tuple-element.48), channel_id=1, source_target_pairs={{0,4},{4,0},{8,12},{12,8},{16,20},{20,16},{24,28},{28,24},{1,5},{5... | collective-permute-start | bytes 98312 | tf_op jit(solution)/shard_map/ppermute | solution.py:47
  37.7 3.6 %collective-permute-start.6 = (f32[52,2,256]{2,1,0:T(2,128)S(1)}, f32[52,2,256]{2,1,0:T(2,128)S(1)}, u32[]{:S(2)}, u32[]{:S(2)}) collective-permute-start(f32[52,2,256]{2,1,0:T(2,128)S(1)} %shard_map.57), channel_id=1, source_target_pairs={{0,2},{2,0},{1,3},{3,1},{4,6},{6,4},{5,7},{7,5},{8,10},{10,8},{9,1... | collective-permute-start | bytes 319496 | tf_op jit(solution)/shard_map/ppermute | solution.py:47
  42.0 6.5 %collective-permute-start.7 = (f32[81,16,128]{2,1,0:T(8,128)S(1)}, f32[81,16,128]{2,1,0:T(8,128)S(1)}, u32[]{:S(2)}, u32[]{:S(2)}) collective-permute-start(f32[81,16,128]{2,1,0:T(8,128)S(1)} %shard_map.58), channel_id=1, source_target_pairs={{0,1},{1,0},{2,3},{3,2},{4,5},{5,4},{6,7},{7,6},{8,9},{9,8},{10,11... | collective-permute-start | bytes 1990664 | tf_op jit(solution)/shard_map/ppermute | solution.py:47
  52.7 5.1 %collective-permute-start.8 = (f32[36,8,128]{2,1,0:T(8,128)S(1)}, f32[36,8,128]{2,1,0:T(8,128)S(1)}, u32[]{:S(2)}, u32[]{:S(2)}) collective-permute-start(f32[36,8,128]{2,1,0:T(8,128)S(1)} %get-tuple-element.36.refs_0_.own), channel_id=1, source_target_pairs={{0,4},{4,0},{8,12},{12,8},{16,20},{20,16},{24,28},{28,24},{1,5},{5... | collective-permute-start | bytes 442376 | tf_op jit(solution)/shard_map/ppermute | solution.py:47
  54.0 7.5 %collective-permute-start.9 = (f32[36,8,128]{2,1,0:T(8,128)S(1)}, f32[36,8,128]{2,1,0:T(8,128)S(1)}, u32[]{:S(2)}, u32[]{:S(2)}) collective-permute-start(f32[36,8,128]{2,1,0:T(8,128)S(1)} %get-tuple-element.40), channel_id=1, source_target_pairs={{4,8},{8,4},{12,16},{16,12},{20,24},{24,20},{5,9},{9,5},{13,17},{1... | collective-permute-start | bytes 442376 | tf_op jit(solution)/shard_map/ppermute | solution.py:46
  62.1 4.2 %collective-permute-start.10 = (f32[80,4,128]{2,1,0:T(4,128)S(1)}, f32[80,4,128]{2,1,0:T(4,128)S(1)}, u32[]{:S(2)}, u32[]{:S(2)}) collective-permute-start(f32[80,4,128]{2,1,0:T(4,128)S(1)} %shard_map.60), channel_id=1, source_target_pairs={{0,2},{2,0},{1,3},{3,1},{4,6},{6,4},{5,7},{7,5},{8,10},{10,8},{9,1... | collective-permute-start | bytes 491528 | tf_op jit(solution)/shard_map/ppermute | solution.py:47
  67.0 4.8 %collective-permute-start.11 = (f32[210,8,128]{2,1,0:T(8,128)S(1)}, f32[210,8,128]{2,1,0:T(8,128)S(1)}, u32[]{:S(2)}, u32[]{:S(2)}) collective-permute-start(f32[210,8,128]{2,1,0:T(8,128)S(1)} %shard_map.61), channel_id=1, source_target_pairs={{0,1},{1,0},{2,3},{3,2},{4,5},{5,4},{6,7},{7,6},{8,9},{9,8},{10,11... | collective-permute-start | bytes 2580488 | tf_op jit(solution)/shard_map/ppermute | solution.py:47

commit v10 on v9

--- a/solution.py
+++ b/solution.py
@@ -223,7 +223,7 @@
         out_ref[t, jnp.minimum(n, capacity - 1)] = rows_ref[r]
         return 0
 
-    lax.fori_loop(0, count, row, 0, unroll=8)
+    lax.fori_loop(0, count, row, 0, unroll=32)
 
 
 def split(refs, nums):
@@ -245,7 +245,7 @@
             acc[at, :] = acc[at, :] + rows_ref[s, c]
         return 0
 
-    lax.fori_loop(0, rows_ref.shape[0], add, 0)
+    lax.fori_loop(0, rows_ref.shape[0], add, 0, unroll=4)
     z_tiles = lanes // LANES
     across = rows // 2
     for qx in range(planes // 2):

time: 77.2 us -> 77.3 us (level)
  no operation moved by 1% of the time
where the time goes in v10:
time: 77.3 us; the launch traced here: 76.8 us
  starting transfers between devices  29.5 us (38%)
  waiting for transfers between devices  24.4 us (32%)
  Pallas kernels  15.4 us (20%)
  other arithmetic  4.27 us (6%)
  local copies, waits for them, and re-layouts  2.95 us (4%)
    ppermute x9, starting transfers between devices, swap(): got.insert(0, lax.ppermute(message(even, 0), axis, pairs(count, 0)))  16.2 us
    pallas_call x8, Pallas kernels, call(): pl.pallas_call(kernel, out_shape=outs, in_specs=[SMEM] * smem + [VMEM] *...  15.4 us
    ppermute x9, waiting for transfers between devices, swap(): got.insert(0, lax.ppermute(message(even, 0), axis, pairs(count, 0)))  12.7 us
    ppermute x3, starting transfers between devices, swap(): lax.ppermute(message(~even, 1), axis, pairs(count, 1))  6.66 us
    all_to_all x1, starting transfers between devices, body(): lax.all_to_all(outgoing, ('gx', 'gy'), split_axis=0, concat_axis=0, tiled...  6.64 us
    all_to_all x1, waiting for transfers between devices, body(): lax.all_to_all(outgoing, ('gx', 'gy'), split_axis=0, concat_axis=0, tiled...  6.17 us
    ppermute x3, waiting for transfers between devices, swap(): lax.ppermute(message(~even, 1), axis, pairs(count, 1))  5.59 us
    concatenate x4, other arithmetic, flat(): jnp.concatenate([p.reshape(-1, *p.shape[-2:]) for p in parts], axis=0)  3.07 us
  transfers between devices with their start and end apart: 13, of which 10 were waited for; matrix products, arithmetic and copies ran while one was open for 7% of the time, Pallas kernels for 2%

profile of v10, /device:TPU:9, one launch (start us, length us, event | category | flops | bytes accessed | tf_op | source)
XLA Modules:
  0.0 76.8 jit_solution(56720150758014890)
XLA Ops:
  0.0 0.8 %fusion.1.tile_ref = s32[96]{0:T(128)S(1)} fusion(s32[3072,1]{0,1:T(1,128)} %param.8, s32[]{:T(128)S(6)} %select_n.75), kind=kLoop, calls=%fused_computation.24 | loop fusion | bytes 772 | tf_op jit(solution)/shard_map/dynamic_slice | solution.py:495
  0.8 1.0 %copy-done.2 = f32[96,1024]{1,0:T(8,128)S(1)} copy-done((f32[96,1024]{1,0:T(8,128)S(1)}, f32[96,1024]{1,0:T(8,128)}, u32[]{:S(2)}) %copy-start.2) | copy-done | bytes 393240
  1.8 2.0 %shard_map.55 = f32[16,12,8,128]{3,2,1,0:T(8,128)} custom-call(s32[96]{0:T(128)S(1)} %fusion.1.tile_ref, f32[96,1024]{1,0:T(8,128)S(1)} %copy-done.2), custom_call_target="tpu_custom_call" | custom-call | tf_op jit(solution)/shard_map/pallas_call | solution.py:453
  3.8 6.6 %all-to-all-start = ((f32[16,12,8,128]{3,2,1,0:T(8,128)}), f32[16,12,8,128]{3,2,1,0:T(8,128)S(1)}, u32[]{:S(2)}, u32[]{:S(2)}) async-start(f32[16,12,8,128]{3,2,1,0:T(8,128)} %shard_map.55), calls=%async_computation | async-start | bytes 1572864 | tf_op jit(solution)/shard_map/all_to_all | solution.py:503
  10.6 0.8 pad_maximum_fusion.3
  11.3 1.2 %collective-permute-start = (f32[64,3,256]{2,1,0:T(4,128)}, f32[64,3,256]{2,1,0:T(4,128)S(1)}, u32[]{:S(2)}, u32[]{:S(2)}) collective-permute-start(f32[64,3,256]{2,1,0:T(4,128)} %pad_maximum_fusion.3), channel_id=1, source_target_pairs={{0,2},{2,0},{1,3},{3,1},{4,6},{6,4},{5,7},{7,5},{8,10},{10,8},{9,1... | collective-permute-start | bytes 589832 | tf_op jit(solution)/shard_map/ppermute | solution.py:47
  12.6 0.7 pad_maximum_fusion.1
  13.3 1.2 %collective-permute-start.2 = (f32[20,16,256]{2,1,0:T(8,128)}, f32[20,16,256]{2,1,0:T(8,128)S(1)}, u32[]{:S(2)}, u32[]{:S(2)}) collective-permute-start(f32[20,16,256]{2,1,0:T(8,128)} %pad_maximum_fusion.1), channel_id=1, source_target_pairs={{0,4},{4,0},{8,12},{12,8},{16,20},{20,16},{24,28},{28,24},{1,5},{5... | collective-permute-start | bytes 983048 | tf_op jit(solution)/shard_map/ppermute | solution.py:47
  14.5 0.7 pad_maximum_fusion.2
  15.3 2.2 %collective-permute-start.3 = (f32[20,16,256]{2,1,0:T(8,128)}, f32[20,16,256]{2,1,0:T(8,128)S(1)}, u32[]{:S(2)}, u32[]{:S(2)}) collective-permute-start(f32[20,16,256]{2,1,0:T(8,128)} %pad_maximum_fusion.2), channel_id=1, source_target_pairs={{4,8},{8,4},{12,16},{16,12},{20,24},{24,20},{5,9},{9,5},{13,17},{1... | collective-permute-start | bytes 983048 | tf_op jit(solution)/shard_map/ppermute | solution.py:46
  17.5 0.8 %pad_maximum_fusion = f32[64,16,128]{2,1,0:T(8,128)} fusion(f32[32,16,128]{2,1,0:T(8,128)S(1)} %bitcast.35, f32[32,16,128]{2,1,0:T(8,128)S(1)} %bitcast.36), kind=kLoop, calls=%fused_computation.1 | loop fusion | flops 131072 | bytes 1048576 | tf_op jit(solution)/shard_map/concatenate | solution.py:40
  18.3 2.1 %collective-permute-start.1 = (f32[64,16,128]{2,1,0:T(8,128)}, f32[64,16,128]{2,1,0:T(8,128)S(1)}, u32[]{:S(2)}, u32[]{:S(2)}) collective-permute-start(f32[64,16,128]{2,1,0:T(8,128)} %pad_maximum_fusion), channel_id=1, source_target_pairs={{0,1},{1,0},{2,3},{3,2},{4,5},{5,4},{6,7},{7,6},{8,9},{9,8},{10,11... | collective-permute-start | bytes 1572872 | tf_op jit(solution)/shard_map/ppermute | solution.py:47
  22.5 1.2 %collective-permute-done.refs_5_.refs_4_ = f32[64,3,256]{2,1,0:T(4,128)S(1)} collective-permute-done((f32[64,3,256]{2,1,0:T(4,128)}, f32[64,3,256]{2,1,0:T(4,128)S(1)}, u32[]{:S(2)}, u32[]{:S(2)}) %collective-permute-start) | collective-permute-done | bytes 196640 | tf_op jit(solution)/shard_map/ppermute | solution.py:47
  23.8 6.2 %all-to-all-done.rows_ref = f32[16,12,8,128]{3,2,1,0:T(8,128)S(1)} async-done(((f32[16,12,8,128]{3,2,1,0:T(8,128)}), f32[16,12,8,128]{3,2,1,0:T(8,128)S(1)}, u32[]{:S(2)}, u32[]{:S(2)}) %all-to-all-start) | async-done | bytes 786464 | tf_op jit(solution)/shard_map/all_to_all | solution.py:503
  29.9 1.6 %shard_map.56 = (f32[1,8,16,256]{3,2,1,0:T(8,128)S(1)}, f32[4,8,256]{2,1,0:T(8,128)S(1)}) custom-call(s32[192]{0:T(256)S(1)} %add.59.slot_ref, f32[16,12,8,128]{3,2,1,0:T(8,128)S(1)} %all-to-all-done.rows_ref), custom_call_target="tpu_custom_call" | custom-call | tf_op jit(solution)/shard_map/pallas_call | solution.py:453
  31.6 1.9 %collective-permute-start.5 = (f32[2,16,256]{2,1,0:T(8,128)S(1)}, f32[2,16,256]{2,1,0:T(8,128)S(1)}, u32[]{:S(2)}, u32[]{:S(2)}) collective-permute-start(f32[2,16,256]{2,1,0:T(8,128)S(1)} %get-tuple-element.47), channel_id=1, source_target_pairs={{4,8},{8,4},{12,16},{16,12},{20,24},{24,20},{5,9},{9,5},{13,17},{1... | collective-permute-start | bytes 98312 | tf_op jit(solution)/shard_map/ppermute | solution.py:46
  33.5 1.5 %collective-permute-start.4 = (f32[2,16,256]{2,1,0:T(8,128)S(1)}, f32[2,16,256]{2,1,0:T(8,128)S(1)}, u32[]{:S(2)}, u32[]{:S(2)}) collective-permute-start(f32[2,16,256]{2,1,0:T(8,128)S(1)} %get-tuple-element.48), channel_id=1, source_target_pairs={{0,4},{4,0},{8,12},{12,8},{16,20},{20,16},{24,28},{28,24},{1,5},{5... | collective-permute-start | bytes 98312 | tf_op jit(solution)/shard_map/ppermute | solution.py:47
  35.2 1.9 %collective-permute-done.5.refs_1_.refs_2_ = f32[2,16,256]{2,1,0:T(8,128)S(1)} collective-permute-done((f32[2,16,256]{2,1,0:T(8,128)S(1)}, f32[2,16,256]{2,1,0:T(8,128)S(1)}, u32[]{:S(2)}, u32[]{:S(2)}) %collective-permute-start.5) | collective-permute-done | bytes 32800 | tf_op jit(solution)/shard_map/ppermute | solution.py:46
  37.7 0.8 %collective-permute-start.6 = (f32[52,2,256]{2,1,0:T(2,128)S(1)}, f32[52,2,256]{2,1,0:T(2,128)S(1)}, u32[]{:S(2)}, u32[]{:S(2)}) collective-permute-start(f32[52,2,256]{2,1,0:T(2,128)S(1)} %shard_map.57), channel_id=1, source_target_pairs={{0,2},{2,0},{1,3},{3,1},{4,6},{6,4},{5,7},{7,5},{8,10},{10,8},{9,1... | collective-permute-start | bytes 319496 | tf_op jit(solution)/shard_map/ppermute | solution.py:47
  38.6 2.8 %collective-permute-done.6.refs_6_ = f32[52,2,256]{2,1,0:T(2,128)S(1)} collective-permute-done((f32[52,2,256]{2,1,0:T(2,128)S(1)}, f32[52,2,256]{2,1,0:T(2,128)S(1)}, u32[]{:S(2)}, u32[]{:S(2)}) %collective-permute-start.6) | collective-permute-done | bytes 106528 | tf_op jit(solution)/shard_map/ppermute | solution.py:47
  42.0 4.7 %collective-permute-start.7 = (f32[81,16,128]{2,1,0:T(8,128)S(1)}, f32[81,16,128]{2,1,0:T(8,128)S(1)}, u32[]{:S(2)}, u32[]{:S(2)}) collective-permute-start(f32[81,16,128]{2,1,0:T(8,128)S(1)} %shard_map.58), channel_id=1, source_target_pairs={{0,1},{1,0},{2,3},{3,2},{4,5},{5,4},{6,7},{7,6},{8,9},{9,8},{10,11... | collective-permute-start | bytes 1990664 | tf_op jit(solution)/shard_map/ppermute | solution.py:47
  46.7 1.7 %collective-permute-done.7.refs_7_ = f32[81,16,128]{2,1,0:T(8,128)S(1)} collective-permute-done((f32[81,16,128]{2,1,0:T(8,128)S(1)}, f32[81,16,128]{2,1,0:T(8,128)S(1)}, u32[]{:S(2)}, u32[]{:S(2)}) %collective-permute-start.7) | collective-permute-done | bytes 663584 | tf_op jit(solution)/shard_map/ppermute | solution.py:47
  48.5 4.2 %shard_map.59 = (f32[4,12,24,384]{3,2,1,0:T(8,128)S(1)}, f32[4,12,24,384]{3,2,1,0:T(8,128)S(1)}, f32[12,24,384]{2,1,0:T(8,128)S(1)}, f32[36,8,128]{2,1,0:T(8,128...) custom-call(s32[9]{0:T(128)S(1)} %convert_element_type.3.flags, ...), custom_call_target="tpu_custom_call" | custom-call | tf_op jit(solution)/shard_map/pallas_call | solution.py:453
  52.7 1.3 %collective-permute-start.8 = (f32[36,8,128]{2,1,0:T(8,128)S(1)}, f32[36,8,128]{2,1,0:T(8,128)S(1)}, u32[]{:S(2)}, u32[]{:S(2)}) collective-permute-start(f32[36,8,128]{2,1,0:T(8,128)S(1)} %get-tuple-element.36.refs_0_.own), channel_id=1, source_target_pairs={{0,4},{4,0},{8,12},{12,8},{16,20},{20,16},{24,28},{28,24},{1,5},{5... | collective-permute-start | bytes 442376 | tf_op jit(solution)/shard_map/ppermute | solution.py:47
  53.9 2.6 %collective-permute-start.9 = (f32[36,8,128]{2,1,0:T(8,128)S(1)}, f32[36,8,128]{2,1,0:T(8,128)S(1)}, u32[]{:S(2)}, u32[]{:S(2)}) collective-permute-start(f32[36,8,128]{2,1,0:T(8,128)S(1)} %get-tuple-element.40), channel_id=1, source_target_pairs={{4,8},{8,4},{12,16},{16,12},{20,24},{24,20},{5,9},{9,5},{13,17},{1... | collective-permute-start | bytes 442376 | tf_op jit(solution)/shard_map/ppermute | solution.py:46
  56.5 1.3 %collective-permute-done.8.refs_2_.refs_1_.refs_0_ = f32[36,8,128]{2,1,0:T(8,128)S(1)} collective-permute-done((f32[36,8,128]{2,1,0:T(8,128)S(1)}, f32[36,8,128]{2,1,0:T(8,128)S(1)}, u32[]{:S(2)}, u32[]{:S(2)}) %collective-permute-start.8) | collective-permute-done | bytes 147488 | tf_op jit(solution)/shard_map/ppermute | solution.py:47
  57.8 3.7 %collective-permute-done.9.refs_1_.refs_2_ = f32[36,8,128]{2,1,0:T(8,128)S(1)} collective-permute-done((f32[36,8,128]{2,1,0:T(8,128)S(1)}, f32[36,8,128]{2,1,0:T(8,128)S(1)}, u32[]{:S(2)}, u32[]{:S(2)}) %collective-permute-start.9) | collective-permute-done | bytes 147488 | tf_op jit(solution)/shard_map/ppermute | solution.py:46
  62.0 0.7 collective-permute-start.10
  62.7 3.5 %collective-permute-done.10.refs_3_.refs_2_ = f32[80,4,128]{2,1,0:T(4,128)S(1)} collective-permute-done((f32[80,4,128]{2,1,0:T(4,128)S(1)}, f32[80,4,128]{2,1,0:T(4,128)S(1)}, u32[]{:S(2)}, u32[]{:S(2)}) %collective-permute-start.10) | collective-permute-done | bytes 163872 | tf_op jit(solution)/shard_map/ppermute | solution.py:47
  66.9 2.7 %collective-permute-start.11 = (f32[210,8,128]{2,1,0:T(8,128)S(1)}, f32[210,8,128]{2,1,0:T(8,128)S(1)}, u32[]{:S(2)}, u32[]{:S(2)}) collective-permute-start(f32[210,8,128]{2,1,0:T(8,128)S(1)} %shard_map.61), channel_id=1, source_target_pairs={{0,1},{1,0},{2,3},{3,2},{4,5},{5,4},{6,7},{7,6},{8,9},{9,8},{10,11... | collective-permute-start | bytes 2580488 | tf_op jit(solution)/shard_map/ppermute | solution.py:47
  69.6 2.0 %collective-permute-done.11.refs_3_ = f32[210,8,128]{2,1,0:T(8,128)S(1)} collective-permute-done((f32[210,8,128]{2,1,0:T(8,128)S(1)}, f32[210,8,128]{2,1,0:T(8,128)S(1)}, u32[]{:S(2)}, u32[]{:S(2)}) %collective-permute-start.11) | collective-permute-done | bytes 860192 | tf_op jit(solution)/shard_map/ppermute | solution.py:47
  71.6 5.2 %shard_map.62 = f32[4,8,16,256]{3,2,1,0:T(8,128)} custom-call(s32[9]{0:T(128)S(1)} %convert_element_type.3.flags, f32[36,8,128]{2,1,0:T(8,128)S(1)} %get-tuple-element.36.refs_0_.own, f32[4,12,24,384]{3,2,1,0:T(8,128)S(1)} %get-tuple-element.37.state, f32[12,24,384]{2,1,0:T(8,128)S(1)} %get-tuple-element.38.weight, ...), custom_call_target="tpu_custom_call" | custom-call | tf_op jit(solution)/shard_map/pallas_call | solution.py:453
  (39 shorter events, 4.8 us)
Async XLA Ops:
  0.0 10.5 %copy-start = (f32[4,8,16,256]{3,2,1,0:T(8,128)S(1)}, f32[4,8,16,256]{3,2,1,0:T(8,128)}, u32[]{:S(2)}) copy-start(f32[4,8,16,256]{3,2,1,0:T(8,128)} %start_field) | copy-start | bytes 1572868
  0.0 10.5 %copy-start.1 = (f32[4,8,16,256]{3,2,1,0:T(8,128)S(1)}, f32[4,8,16,256]{3,2,1,0:T(8,128)}, u32[]{:S(2)}) copy-start(f32[4,8,16,256]{3,2,1,0:T(8,128)} %right_side) | copy-start | bytes 1572868
  0.8 1.0 %copy-start.2 = (f32[96,1024]{1,0:T(8,128)S(1)}, f32[96,1024]{1,0:T(8,128)}, u32[]{:S(2)}) copy-start(f32[96,1024]{1,0:T(8,128)} %mask_ref.1) | copy-start | bytes 1179652
  3.8 26.1 %all-to-all-start = ((f32[16,12,8,128]{3,2,1,0:T(8,128)}), f32[16,12,8,128]{3,2,1,0:T(8,128)S(1)}, u32[]{:S(2)}, u32[]{:S(2)}) async-start(f32[16,12,8,128]{3,2,1,0:T(8,128)} %shard_map.55), calls=%async_computation | async-start | bytes 1572864 | tf_op jit(solution)/shard_map/all_to_all | solution.py:503
  11.3 12.4 %collective-permute-start = (f32[64,3,256]{2,1,0:T(4,128)}, f32[64,3,256]{2,1,0:T(4,128)S(1)}, u32[]{:S(2)}, u32[]{:S(2)}) collective-permute-start(f32[64,3,256]{2,1,0:T(4,128)} %pad_maximum_fusion.3), channel_id=1, source_target_pairs={{0,2},{2,0},{1,3},{3,1},{4,6},{6,4},{5,7},{7,5},{8,10},{10,8},{9,1... | collective-permute-start | bytes 589832 | tf_op jit(solution)/shard_map/ppermute | solution.py:47
  12.6 8.4 %copy-start.4 = (s32[3072,1]{0,1:T(1,128)S(1)}, s32[3072,1]{0,1:T(1,128)}, u32[]{:S(2)}) copy-start(s32[3072,1]{0,1:T(1,128)} %param.8) | copy-start | bytes 36868
  12.6 9.0 %copy-start.3 = (s32[3072]{0:T(1024)S(1)}, s32[3072]{0:T(1024)}, u32[]{:S(2)}) copy-start(s32[3072]{0:T(1024)} %param.9) | copy-start | bytes 36868
  13.3 21.9 %collective-permute-start.2 = (f32[20,16,256]{2,1,0:T(8,128)}, f32[20,16,256]{2,1,0:T(8,128)S(1)}, u32[]{:S(2)}, u32[]{:S(2)}) collective-permute-start(f32[20,16,256]{2,1,0:T(8,128)} %pad_maximum_fusion.1), channel_id=1, source_target_pairs={{0,4},{4,0},{8,12},{12,8},{16,20},{20,16},{24,28},{28,24},{1,5},{5... | collective-permute-start | bytes 983048 | tf_op jit(solution)/shard_map/ppermute | solution.py:47
  15.3 19.9 %collective-permute-start.3 = (f32[20,16,256]{2,1,0:T(8,128)}, f32[20,16,256]{2,1,0:T(8,128)S(1)}, u32[]{:S(2)}, u32[]{:S(2)}) collective-permute-start(f32[20,16,256]{2,1,0:T(8,128)} %pad_maximum_fusion.2), channel_id=1, source_target_pairs={{4,8},{8,4},{12,16},{16,12},{20,24},{24,20},{5,9},{9,5},{13,17},{1... | collective-permute-start | bytes 983048 | tf_op jit(solution)/shard_map/ppermute | solution.py:46
  18.3 5.4 %collective-permute-start.1 = (f32[64,16,128]{2,1,0:T(8,128)}, f32[64,16,128]{2,1,0:T(8,128)S(1)}, u32[]{:S(2)}, u32[]{:S(2)}) collective-permute-start(f32[64,16,128]{2,1,0:T(8,128)} %pad_maximum_fusion), channel_id=1, source_target_pairs={{0,1},{1,0},{2,3},{3,2},{4,5},{5,4},{6,7},{7,6},{8,9},{9,8},{10,11... | collective-permute-start | bytes 1572872 | tf_op jit(solution)/shard_map/ppermute | solution.py:47
  31.6 5.6 %collective-permute-start.5 = (f32[2,16,256]{2,1,0:T(8,128)S(1)}, f32[2,16,256]{2,1,0:T(8,128)S(1)}, u32[]{:S(2)}, u32[]{:S(2)}) collective-permute-start(f32[2,16,256]{2,1,0:T(8,128)S(1)} %get-tuple-element.47), channel_id=1, source_target_pairs={{4,8},{8,4},{12,16},{16,12},{20,24},{24,20},{5,9},{9,5},{13,17},{1... | collective-permute-start | bytes 98312 | tf_op jit(solution)/shard_map/ppermute | solution.py:46
  33.5 3.6 %collective-permute-start.4 = (f32[2,16,256]{2,1,0:T(8,128)S(1)}, f32[2,16,256]{2,1,0:T(8,128)S(1)}, u32[]{:S(2)}, u32[]{:S(2)}) collective-permute-start(f32[2,16,256]{2,1,0:T(8,128)S(1)} %get-tuple-element.48), channel_id=1, source_target_pairs={{0,4},{4,0},{8,12},{12,8},{16,20},{20,16},{24,28},{28,24},{1,5},{5... | collective-permute-start | bytes 98312 | tf_op jit(solution)/shard_map/ppermute | solution.py:47
  37.7 3.6 %collective-permute-start.6 = (f32[52,2,256]{2,1,0:T(2,128)S(1)}, f32[52,2,256]{2,1,0:T(2,128)S(1)}, u32[]{:S(2)}, u32[]{:S(2)}) collective-permute-start(f32[52,2,256]{2,1,0:T(2,128)S(1)} %shard_map.57), channel_id=1, source_target_pairs={{0,2},{2,0},{1,3},{3,1},{4,6},{6,4},{5,7},{7,5},{8,10},{10,8},{9,1... | collective-permute-start | bytes 319496 | tf_op jit(solution)/shard_map/ppermute | solution.py:47
  42.0 6.4 %collective-permute-start.7 = (f32[81,16,128]{2,1,0:T(8,128)S(1)}, f32[81,16,128]{2,1,0:T(8,128)S(1)}, u32[]{:S(2)}, u32[]{:S(2)}) collective-permute-start(f32[81,16,128]{2,1,0:T(8,128)S(1)} %shard_map.58), channel_id=1, source_target_pairs={{0,1},{1,0},{2,3},{3,2},{4,5},{5,4},{6,7},{7,6},{8,9},{9,8},{10,11... | collective-permute-start | bytes 1990664 | tf_op jit(solution)/shard_map/ppermute | solution.py:47
  52.7 5.1 %collective-permute-start.8 = (f32[36,8,128]{2,1,0:T(8,128)S(1)}, f32[36,8,128]{2,1,0:T(8,128)S(1)}, u32[]{:S(2)}, u32[]{:S(2)}) collective-permute-start(f32[36,8,128]{2,1,0:T(8,128)S(1)} %get-tuple-element.36.refs_0_.own), channel_id=1, source_target_pairs={{0,4},{4,0},{8,12},{12,8},{16,20},{20,16},{24,28},{28,24},{1,5},{5... | collective-permute-start | bytes 442376 | tf_op jit(solution)/shard_map/ppermute | solution.py:47
  53.9 7.5 %collective-permute-start.9 = (f32[36,8,128]{2,1,0:T(8,128)S(1)}, f32[36,8,128]{2,1,0:T(8,128)S(1)}, u32[]{:S(2)}, u32[]{:S(2)}) collective-permute-start(f32[36,8,128]{2,1,0:T(8,128)S(1)} %get-tuple-element.40), channel_id=1, source_target_pairs={{4,8},{8,4},{12,16},{16,12},{20,24},{24,20},{5,9},{9,5},{13,17},{1... | collective-permute-start | bytes 442376 | tf_op jit(solution)/shard_map/ppermute | solution.py:46
  62.0 4.2 %collective-permute-start.10 = (f32[80,4,128]{2,1,0:T(4,128)S(1)}, f32[80,4,128]{2,1,0:T(4,128)S(1)}, u32[]{:S(2)}, u32[]{:S(2)}) collective-permute-start(f32[80,4,128]{2,1,0:T(4,128)S(1)} %shard_map.60), channel_id=1, source_target_pairs={{0,2},{2,0},{1,3},{3,1},{4,6},{6,4},{5,7},{7,5},{8,10},{10,8},{9,1... | collective-permute-start | bytes 491528 | tf_op jit(solution)/shard_map/ppermute | solution.py:47
  66.9 4.8 %collective-permute-start.11 = (f32[210,8,128]{2,1,0:T(8,128)S(1)}, f32[210,8,128]{2,1,0:T(8,128)S(1)}, u32[]{:S(2)}, u32[]{:S(2)}) collective-permute-start(f32[210,8,128]{2,1,0:T(8,128)S(1)} %shard_map.61), channel_id=1, source_target_pairs={{0,1},{1,0},{2,3},{3,2},{4,5},{5,4},{6,7},{7,6},{8,9},{9,8},{10,11... | collective-permute-start | bytes 2580488 | tf_op jit(solution)/shard_map/ppermute | solution.py:47
